TPU v7x, 256 devices: a whole 4x4x8 slice. The times are simulated.
256 devices in a mesh: row: 8 (over y, core), col: 32 (over x, z).
Axes of the slice: x: 4, y: 4, z: 8, core: 2. Of those that a mesh axis runs over, the one named last changes fastest.
Arguments:
- adjoint: bfloat16 [16384, 16384], P('row', 'col'), may hold values from -1 to 1, as said below
- taper: int32 [64, 64], replicated, may hold values from 0 to 1, as said below
- panel_two: bfloat16 [16384, 1024], P(('row', 'col')), may hold values from -6 to 6
- panel_one: bfloat16 [16384, 1024], P(('row', 'col')), may hold values from -6 to 6
- incoming: float32 [16384, 1024], P('col', 'row'), may hold values from -6 to 6
- inverse_factor: bfloat16 [1024, 1024], P('row'), may hold values from -1 to 1, as said below
Outputs:
- second_grad: float32 [16384, 1024], P('col', 'row')
- first_grad: float32 [16384, 1024], P('col', 'row')
Inputs may be any that keep to these rules, and one draw needn't show every extreme that they name: `taper`: symmetric in its two indices; every entry with |a - b| <= 1 is 1. `adjoint`: symmetric. `inverse_factor`: lower triangular with a positive diagonal.
All inputs are finite; a program needn't handle non-finite values.
Results may differ from a plain program's by a relative error of at most 0.0025.
Values may be sent and summed in bfloat16 or wider, within the bound.
No kernel may reach another device: no remote copies, remote signals or barrier semaphores. Data moves between devices by JAX's collectives and lax.ppermute only.
A program may use at most 64 MiB of HBM per device.

v0:
```python
import jax
import jax.numpy as jnp
from jax import lax
from jax.sharding import PartitionSpec as P

BLK = 256


def broadcast(value, axis, source):
    kept = jnp.where(lax.axis_index(axis) == source, value, 0).astype(value.dtype)
    return lax.psum(kept, axis)


def mask_tiles(taper, row_tiles, col_tiles):
    first_row = lax.axis_index("row") * row_tiles
    first_col = lax.axis_index("col") * col_tiles
    return lax.dynamic_slice(taper, (first_row, first_col), (row_tiles, col_tiles))


def masked_local(adjoint, mask_block, tile_size):
    row_count, col_count = adjoint.shape
    shaped = adjoint.reshape(row_count // tile_size, tile_size, col_count // tile_size, tile_size)
    keep_mask = mask_block.astype(adjoint.dtype)[:, None, :, None]
    return (shaped * keep_mask).reshape(row_count, col_count)


def local(adjoint, taper, panel_two, panel_one, incoming, inverse_factor):
    tile_size = BLK
    row_tiles = adjoint.shape[0] // tile_size
    col_tiles = adjoint.shape[1] // tile_size
    mask_block = mask_tiles(taper, row_tiles, col_tiles)

    def gather_rows(panel):
        return lax.all_gather(panel, "col", axis=0, tiled=True)

    def spread(mirror_term):
        return lax.psum_scatter(mirror_term, "row", scatter_dimension=1, tiled=True)

    masked = masked_local(adjoint, mask_block, tile_size)

    def mirror(gathered):
        return lax.dot_general(
            masked, gathered, (((0,), (0,)), ((), ())), preferred_element_type=jnp.float32
        )

    rows_second = gather_rows(panel_two)
    second_grad = incoming + spread(-2.0 * mirror(rows_second))
    second_rounded = second_grad.astype(jnp.bfloat16)
    rows_first = gather_rows(panel_one)
    panel_width = panel_one.shape[1]
    diagonal_block = broadcast(rows_first[:panel_width], "row", 0)
    first_term = -2.0 * mirror(rows_first)
    partial_value = jnp.dot(second_rounded, inverse_factor, preferred_element_type=jnp.float32)
    carried = lax.psum(partial_value, "row")
    slab_rows = inverse_factor.shape[0]
    columns = lax.dynamic_slice_in_dim(
        diagonal_block, lax.axis_index("row") * slab_rows, slab_rows, 1
    ).astype(jnp.float32)
    carried_term = jnp.dot(
        carried, columns, precision=lax.Precision.HIGHEST, preferred_element_type=jnp.float32
    )
    first_grad = spread(first_term) - carried_term
    return (second_grad, first_grad)


def solution(mesh):
    in_specs = (
        P("row", "col"),
        P(),
        P(("row", "col"), None),
        P(("row", "col"), None),
        P("col", "row"),
        P("row", None),
    )
    out_specs = (P("col", "row"), P("col", "row"))
    return jax.shard_map(local, mesh=mesh, in_specs=in_specs, out_specs=out_specs, check_vma=False)
```

profile of v0, /device:TPU:1, one launch (start us, length us, event | category | flops | bytes accessed | tf_op | source)
XLA Modules:
  0.0 404.1 jit_solution(9717838235637787397)
XLA Ops:
  7.2 0.0 all-gather.3.cloned.1.call-start
  7.2 0.7 all-gather.3.cloned.1.call-update
  7.9 0.0 all-gather.5.cloned.1.call-start
  8.0 0.7 all-gather.5.cloned.1.call-update
  8.7 0.0 reduce-scatter.3.cloned.1.call-start
  8.7 0.8 dynamic-slice_convert_fusion
  9.5 1.1 mul.28
  10.6 0.5 copy.8
  11.1 82.4 %all-gather.3.cloned.1.call-done = bf16[2048,1024]{1,0:T(8,128)(2,1)} async-done(((bf16[64,1024]{1,0:T(8,128)(2,1)}), bf16[2048,1024]{1,0:T(8,128)(2,1)}) %all-gather.3.cloned.1.call-update) | async-done | bytes 4194320 | tf_op jit(solution)/shard_map/all_gather | solution.py:34
  93.5 6.5 %convolution_multiply_fusion.1 = f32[512,1024]{1,0:T(8,128)} fusion(bf16[2048,1024]{1,0:T(8,128)(2,1)} %all-gather.3.cloned.1.call-done, bf16[2048,512]{1,0:T(8,128)(2,1)} %param.6, bf16[2048,512]{1,0:T(8,128)(2,1)S(1)} %bitcast.8), kind=kOutput, calls=%fused_computation.2 | convolution fusion | flops 2149056512 | bytes 10485760 | tf_op jit(solution)/shard_map/dot_general | solution.py:42
  100.1 0.0 all-reduce.5.cloned.1.call-start
  100.2 75.0 %all-gather.5.cloned.1.call-done = bf16[2048,1024]{1,0:T(8,128)(2,1)} async-done(((bf16[64,1024]{1,0:T(8,128)(2,1)}), bf16[2048,1024]{1,0:T(8,128)(2,1)}) %all-gather.5.cloned.1.call-update) | async-done | bytes 4194320 | tf_op jit(solution)/shard_map/all_gather | solution.py:34
  175.2 3.1 slice_select_fusion
  178.2 0.0 all-reduce.5.cloned.1.call-update
  178.3 0.0 reduce-scatter.5.cloned.1.call-start
  178.3 6.5 %convolution_multiply_fusion = f32[512,1024]{1,0:T(8,128)} fusion(bf16[2048,1024]{1,0:T(8,128)(2,1)} %all-gather.5.cloned.1.call-done, bf16[2048,512]{1,0:T(8,128)(2,1)} %param.6, bf16[2048,512]{1,0:T(8,128)(2,1)S(1)} %bitcast.9), kind=kOutput, calls=%fused_computation.1 | convolution fusion | flops 2149056512 | bytes 10485760 | tf_op jit(solution)/shard_map/dot_general | solution.py:42
  184.9 0.0 all-reduce.3.cloned.1.call-start
  184.9 26.3 %reduce-scatter.3.cloned.1.call-done = f32[512,128]{1,0:T(8,128)} async-done(((f32[512,1024]{1,0:T(8,128)}), f32[512,128]{1,0:T(8,128)}) %reduce-scatter.3.cloned.1.call-update) | async-done | bytes 262160 | tf_op jit(solution)/shard_map/reduce_scatter | solution.py:37
  211.3 1.0 add.22
  212.3 1.8 fusion.3
  214.1 69.8 %all-reduce.5.cloned.1.call-done = bf16[1024,1024]{1,0:T(8,128)(2,1)} async-done(((bf16[1024,1024]{1,0:T(8,128)(2,1)}), bf16[1024,1024]{1,0:T(8,128)(2,1)}) %all-reduce.5.cloned.1.call-update) | async-done | bytes 2097168 | tf_op jit(solution)/shard_map/psum | solution.py:11
  283.8 37.5 %reduce-scatter.5.cloned.1.call-done = f32[512,128]{1,0:T(8,128)} async-done(((f32[512,1024]{1,0:T(8,128)}), f32[512,128]{1,0:T(8,128)}) %reduce-scatter.5.cloned.1.call-update) | async-done | bytes 262160 | tf_op jit(solution)/shard_map/reduce_scatter | solution.py:37
  321.3 72.6 %all-reduce.3.cloned.1.call-done = f32[512,1024]{1,0:T(8,128)} async-done(((f32[512,1024]{1,0:T(8,128)}), f32[512,1024]{1,0:T(8,128)}) %all-reduce.3.cloned.1.call-update) | async-done | bytes 2097168 | tf_op jit(solution)/shard_map/psum | solution.py:54
  393.9 3.4 convolution_subtract_fusion
  (9 shorter events, 0.1 us)
Async XLA Ops:
  7.2 205.1 %copy-start = (bf16[128,1024]{1,0:T(8,128)(2,1)S(1)}, bf16[128,1024]{1,0:T(8,128)(2,1)}, u32[]{:S(2)}) copy-start(bf16[128,1024]{1,0:T(8,128)(2,1)} %param.11) | copy-start | bytes 786436
  7.2 86.4 %all-gather.3.cloned.1.call-start = ((), (), s32[]{:S(2)}) async-start(), calls=%async_computation.2 | async-start | bytes 4325376 | tf_op jit(solution)/shard_map/all_gather | solution.py:34
  7.9 167.2 %all-gather.5.cloned.1.call-start = ((), (), s32[]{:S(2)}) async-start(), calls=%async_computation.4 | async-start | bytes 4325376 | tf_op jit(solution)/shard_map/all_gather | solution.py:34
  8.7 202.6 %reduce-scatter.3.cloned.1.call-start = ((), (), s32[]{:S(2)}) async-start(), calls=%async_computation.3 | async-start | bytes 2359296 | tf_op jit(solution)/shard_map/reduce_scatter | solution.py:37
  100.1 183.7 %all-reduce.5.cloned.1.call-start = ((), (), s32[]{:S(2)}) async-start(), calls=%async_computation.7 | async-start | bytes 4194304 | tf_op jit(solution)/shard_map/psum | solution.py:11
  178.3 143.0 %reduce-scatter.5.cloned.1.call-start = ((), (), s32[]{:S(2)}) async-start(), calls=%async_computation.5 | async-start | bytes 2359296 | tf_op jit(solution)/shard_map/reduce_scatter | solution.py:37
  184.8 26.4 %copy-start.2 = (f32[512,128]{1,0:T(8,128)S(1)}, f32[512,128]{1,0:T(8,128)}, u32[]{:S(2)}) copy-start(f32[512,128]{1,0:T(8,128)} %param.10) | copy-start | bytes 786436
  184.9 209.0 %all-reduce.3.cloned.1.call-start = ((), (), s32[]{:S(2)}) async-start(), calls=%async_computation.6 | async-start | bytes 4194304 | tf_op jit(solution)/shard_map/psum | solution.py:54
  212.2 1.8 copy-start.1
Sparse Core Ops, SparseCore 0:
  10.6 82.8 all-gather.2
  96.1 78.9 all-gather.4
  177.7 33.4 reduce-scatter.2
  213.5 70.2 all-reduce.4
  286.2 35.0 reduce-scatter.4
  323.5 70.2 all-reduce.2
where the time goes:
time: 405 us; the launch traced here: 404 us
  waiting for transfers between devices  365 us (90%)
  matrix products  18.3 us (5%)
  between operations  14.2 us (4%)
  other arithmetic  4.82 us (1%)
    all_gather x2, waiting for transfers between devices, gather_rows(): return lax.all_gather(panel, 'col', axis=0, tiled=True)  157 us
    psum x1, waiting for transfers between devices, local(): carried = lax.psum(partial_value, 'row')  72.6 us
    psum x1, waiting for transfers between devices, broadcast(): return lax.psum(kept, axis)  69.8 us
    reduce_scatter x2, waiting for transfers between devices, spread(): return lax.psum_scatter(mirror_term, 'row', scatter_dimension=1, tiled=True)  63.8 us
    dot_general x2, matrix products, mirror(): lax.dot_general(masked, gathered, (((0,), (0,)), ((), ())), preferred_ele...  13.1 us
  transfers between devices with their start and end apart: 6, of which 6 were waited for; matrix products, arithmetic and copies ran while one was open for 5% of the time, Pallas kernels for 0%

commit v1 on v0

v1 whole, which is shorter than its diff:
```python
import jax
import jax.numpy as jnp
from jax import lax
from jax.experimental import pallas as pl
from jax.experimental.pallas import tpu as pltpu
from jax.sharding import PartitionSpec as P

BLK = 256
NX, NZ, NY = 4, 8, 4
SUB = 64
PAIR = 2 * SUB
HALF = 512
F32, BF16 = jnp.float32, jnp.bfloat16
VMEM = pl.BlockSpec(memory_space=pltpu.VMEM)
SMEM = pl.BlockSpec(memory_space=pltpu.SMEM)
ANY = pl.BlockSpec(memory_space=pl.ANY)
BIG = pltpu.CompilerParams(vmem_limit_bytes=40 * 2**20)


def shift(value, core, dx, dz):
    pairs = []
    for y in range(NY):
        row = y * 2 + core
        for x in range(NX):
            for z in range(NZ):
                target = (x + dx) % NX * NZ + (z + dz) % NZ
                pairs.append((row * NX * NZ + x * NZ + z, row * NX * NZ + target))
    return lax.ppermute(value, ("row", "col"), pairs)


def y_shift(value, dy):
    pairs = [(y * 2 + k, (y + dy) % NY * 2 + k) for y in range(NY) for k in range(2)]
    return lax.ppermute(value, "row", pairs)


def core_swap(value):
    return lax.ppermute(value, "row", [(r, r ^ 1) for r in range(2 * NY)])


def x_all(value, core):
    return [value] + [shift(value, core, d, 0) for d in (1, -1, 2)]


def z_ring(value, core, turn):
    down1, up1 = shift(value, core, 0, 1), shift(value, core, 0, -1)
    down2, up2 = shift(down1, core, 0, 1), shift(up1, core, 0, -1)
    down3, up3 = shift(down2, core, 0, 1), shift(up2, core, 0, -1)
    far = shift(down3, core, 0, 1) if turn > 0 else shift(up3, core, 0, -1)
    return [value, down1, up1, down2, up2, down3, up3, far]


def offset(n):
    return ((n + 1) // 2) * (1 - 2 * (n % 2))


def source(pos, b, t):
    first = pos[3] == 0
    i = jnp.where(first, t, b // 2)
    j = jnp.where(first, b, b % 2 * 4 + t)
    return (pos[0] + offset(i) + NX) % NX, (pos[1] + offset(j) + NZ) % NZ


def pack_kernel(pos, two, one, own, give):
    first = pos[3] == 0
    for n, panel in enumerate((two, one)):
        for q in range(NY):
            left = panel[:, q * 256:q * 256 + 128]
            right = panel[:, q * 256 + 128:q * 256 + 256]
            at = slice(q * 128, q * 128 + 128)
            own[n, :, at] = jnp.where(first, left, right)
            give[n, :, at] = jnp.where(first, right, left)


def pack(pos, two, one):
    return pl.pallas_call(
        pack_kernel,
        out_shape=(jax.ShapeDtypeStruct((2, SUB, HALF), BF16),) * 2,
        in_specs=[SMEM, VMEM, VMEM],
        out_specs=(VMEM, VMEM),
        compiler_params=BIG,
        name="pack_columns",
    )(pos, two, one)


def diagonal_shard_kernel(pos, own, taken, gathered, out):
    out[:SUB] = own[1]
    out[SUB:PAIR] = taken[1]
    column = pl.multiple_of(pos[2] * 128, 128)
    for q in range(NY):
        out[PAIR:, q * 128:(q + 1) * 128] = gathered[q * 16:(q + 1) * 16, pl.ds(column, 128)]


def diagonal_shard(pos, own, taken, gathered):
    return pl.pallas_call(
        diagonal_shard_kernel,
        out_shape=jax.ShapeDtypeStruct((PAIR + 16, HALF), BF16),
        in_specs=[SMEM] + [VMEM] * 3,
        out_specs=VMEM,
        compiler_params=BIG,
        name="shard_with_diagonal",
    )(pos, own, taken, gathered)


def join(pos, parts, core, extra):
    count = len(parts)

    def kernel(pos, *refs):
        out, sems = refs[count], refs[count + 1]

        @pl.when(pos[3] == core)
        def _():
            copies = []
            for n in range(count):
                copies.append(pltpu.make_async_copy(
                    refs[n].at[:PAIR], out.at[pl.ds(n * PAIR, PAIR)], sems.at[n]))
                if extra:
                    copies.append(pltpu.make_async_copy(
                        refs[n].at[PAIR:], out.at[pl.ds(count * PAIR + n * 16, 16)], sems.at[count + n]))
            for copy in copies:
                copy.start()
            for copy in copies:
                copy.wait()

    rows = count * (PAIR + (16 if extra else 0))
    return pl.pallas_call(
        kernel,
        out_shape=jax.ShapeDtypeStruct((rows, HALF), BF16),
        in_specs=[SMEM] + [ANY] * count,
        out_specs=ANY,
        scratch_shapes=[pltpu.SemaphoreType.DMA((2 * count,))],
        name="join_parts",
    )(pos, *parts)


def gather(pos, shard, extra):
    by_z = z_ring(join(pos, x_all(shard, 0), 0, extra), 0, 1)
    by_x = x_all(join(pos, z_ring(shard, 1, -1), 1, extra), 1)
    return by_z + by_x


def prepare_kernel(pos, taper, mine, other, out, rows):
    lane = lax.broadcasted_iota(jnp.int32, (SUB, 2 * BLK), 1)
    first_col = (pos[0] * NZ + pos[1]) * 2

    def block(b, carry):
        for t in range(4):
            x, z = source(pos, b, t)
            row = pl.multiple_of((x * NZ + z) * SUB, SUB)
            for h, ref in enumerate((mine, other)):
                core = pos[3] if h == 0 else 1 - pos[3]
                tile = (pos[2] * 2 + core) * 8 + x * 2 + z // 4
                left = taper[tile, first_col].astype(F32)
                right = taper[tile, first_col + 1].astype(F32)
                keep = jnp.where(lane < BLK, left, right)
                at = t * PAIR + h * SUB
                rows[at:at + SUB, :] = (ref[pl.ds(row, SUB), :].astype(F32) * keep).astype(BF16)
        out[b] = rows[...].T
        return carry

    lax.fori_loop(0, 8, block, 0)


def prepare(pos, taper, mine, other):
    return pl.pallas_call(
        prepare_kernel,
        out_shape=jax.ShapeDtypeStruct((8, 512, 512), BF16),
        in_specs=[SMEM, SMEM, VMEM, VMEM],
        out_specs=VMEM,
        scratch_shapes=[pltpu.VMEM((512, 512), BF16)],
        compiler_params=BIG,
        name="prepare_adjoint",
    )(pos, taper, mine, other)


def block_refs(refs, core, first_row, rows, width):
    if core == 0:
        return [refs[b].at[pl.ds(first_row, rows)] for b in range(NZ)]
    return [
        refs[NZ + b // 2].at[pl.ds(2 * first_row + b % 2 * rows, rows)] for b in range(NZ)
    ]


def load_blocks(pos, refs, held, sems, first_row, rows):
    for core in range(2):
        @pl.when(pos[3] == core)
        def _(core=core):
            for b, ref in enumerate(block_refs(refs, core, first_row, rows, HALF)):
                pltpu.make_async_copy(ref, held.at[b], sems.at[b]).start()


def product_kernel(pos, adjoint, *refs):
    panels, outs, held, total, sems = refs[:12], refs[12:16], refs[16], refs[17], refs[18]
    load_blocks(pos, panels, held, sems, 0, 512)
    total[...] = jnp.zeros_like(total)

    def block(b, carry):
        pltpu.make_async_copy(held.at[b], held.at[b], sems.at[b]).wait()
        total[...] += jnp.dot(adjoint[b], held[b], preferred_element_type=F32)
        return carry

    lax.fori_loop(0, 8, block, 0)
    for d, out in enumerate(outs):
        column = pl.multiple_of((pos[2] + d) % NY * 128, 128)
        out[...] = (-2.0 * total[:, pl.ds(column, 128)]).astype(out.dtype)


def product(pos, adjoint, panels, kind):
    return pl.pallas_call(
        product_kernel,
        out_shape=(jax.ShapeDtypeStruct((512, 128), F32),) + (jax.ShapeDtypeStruct((512, 128), kind),) * 3,
        in_specs=[SMEM, VMEM] + [ANY] * 12,
        out_specs=(VMEM,) * 4,
        scratch_shapes=[
            pltpu.VMEM((8, 512, HALF), BF16),
            pltpu.VMEM((512, HALF), F32),
            pltpu.SemaphoreType.DMA((8,)),
        ],
        compiler_params=BIG,
        name="masked_product",
    )(pos, adjoint, *panels)


def factor_kernel(pos, inverse, *refs):
    panels, out, held, diagonal, sems = refs[:12], refs[12], refs[13], refs[14], refs[15]
    load_blocks(pos, panels, held, sems, 512, 64)

    def block(b, carry):
        pltpu.make_async_copy(held.at[b], held.at[b], sems.at[b]).wait()
        for t in range(4):
            x, z = source(pos, b, t)
            row = (x * NZ + z) * SUB
            for q in range(NY):
                at = pl.multiple_of(row + q * 16, 16)
                diagonal[pl.ds(at, 16), :] = held[b, t * 16:(t + 1) * 16, q * 128:(q + 1) * 128]
        return carry

    lax.fori_loop(0, 8, block, 0)
    value = jnp.dot(inverse[...], diagonal[:1024, :], preferred_element_type=F32)
    high = value.astype(BF16)
    out[:, :128] = high
    out[:, 128:] = (value - high.astype(F32)).astype(BF16)


def factor(pos, inverse, panels):
    return pl.pallas_call(
        factor_kernel,
        out_shape=jax.ShapeDtypeStruct((1024, 256), BF16),
        in_specs=[SMEM, VMEM] + [ANY] * 12,
        out_specs=VMEM,
        scratch_shapes=[
            pltpu.VMEM((8, 64, HALF), BF16),
            pltpu.VMEM((2048, 128), BF16),
            pltpu.SemaphoreType.DMA((8,)),
        ],
        compiler_params=BIG,
        name="inverse_times_diagonal",
    )(pos, inverse, *panels)


def carried_kernel(pos, mine, other, factors, out, total):
    first = pos[3] == 0
    total[...] = jnp.zeros_like(total)

    def block(d, carry):
        y = (pos[2] - d + NY) % NY
        a, b = mine[d], other[d]
        pair = jnp.concatenate([jnp.where(first, a, b), jnp.where(first, b, a)], axis=1)
        rows = pl.multiple_of(y * 256, 256)
        total[...] += jnp.dot(pair, factors[pl.ds(rows, 256), :], preferred_element_type=F32)
        return carry

    lax.fori_loop(0, NY, block, 0)
    out[...] = total[:, :128] + total[:, 128:]


def carried(pos, mine, other, factors):
    return pl.pallas_call(
        carried_kernel,
        out_shape=jax.ShapeDtypeStruct((512, 128), F32),
        in_specs=[SMEM] + [VMEM] * 3,
        out_specs=VMEM,
        scratch_shapes=[pltpu.VMEM((512, 256), F32)],
        compiler_params=BIG,
        name="carried_term",
    )(pos, mine, other, factors)


def after(value, *others):
    return lax.optimization_barrier((value,) + others)[0]


def local(adjoint, taper, panel_two, panel_one, incoming, inverse_factor):
    row, col = lax.axis_index("row"), lax.axis_index("col")
    pos = jnp.stack([col // NZ, col % NZ, row // 2, row % 2]).astype(jnp.int32)

    own, give = pack(pos, panel_two, panel_one)
    taken = core_swap(give)
    same_core = [[2 * y + k for y in range(NY)] for k in range(2)]
    top = jnp.where(pos[3] == 0, own[1], taken[1])
    diagonal = lax.all_gather(top, "row", axis_index_groups=same_core, axis=0, tiled=True)
    inverse = lax.all_gather(after(inverse_factor, diagonal), "row", axis=0, tiled=True)

    two = gather(pos, jnp.concatenate([own[0], taken[0]], axis=0), False)
    one = gather(pos, diagonal_shard(pos, own, taken, diagonal), True)
    masked = prepare(pos, taper, adjoint, core_swap(adjoint))

    mine, *sent = product(pos, masked, two, F32)
    r1, r2, r3 = [y_shift(part, d + 1) for d, part in enumerate(sent)]
    second_grad = incoming + ((mine + r1) + (r2 + r3))
    rounded = second_grad.astype(BF16)
    column = jnp.stack([rounded, y_shift(rounded, 1), y_shift(rounded, 2), y_shift(rounded, 3)])
    other = core_swap(column)

    factors = factor(pos, inverse, one)
    mine, *sent = product(pos, masked, one, BF16)
    r1, r2, r3 = [y_shift(part, d + 1) for d, part in enumerate(sent)]
    term = carried(pos, column, other, factors)
    first_grad = ((mine + r1.astype(F32)) + (r2.astype(F32) + r3.astype(F32))) - term
    return second_grad, first_grad


def solution(mesh):
    in_specs = (
        P("row", "col"),
        P(),
        P(("row", "col"), None),
        P(("row", "col"), None),
        P("col", "row"),
        P("row", None),
    )
    out_specs = (P("col", "row"), P("col", "row"))
    return jax.shard_map(local, mesh=mesh, in_specs=in_specs, out_specs=out_specs, check_vma=False)
```

time: 405 us -> 309 us (0.76)
  waiting for transfers between devices: 365 us -> 47.4 us
  starting transfers between devices: 0.24 us -> 117 us
  Pallas kernels: 0 us -> 93.4 us
  matrix products: 18.3 us -> 0 us
  local copies, waits for them, and re-layouts: 1.65 us -> 19.8 us
  blocking collectives: 0 us -> 9.89 us
    all_gather x2 -> x1, waiting for transfers between devices: 157 us -> 0.01 us  [local(): lax.all_gather(after(inverse_factor, diagonal), 'row', axis=0, tiled=True)]
    psum x2 -> x0, waiting for transfers between devices: 142 us -> none  [the longest x1 72.6 us: local(): carried = lax.psum(partial_value, 'row')]
    ppermute x0 -> x52, starting transfers between devices: none -> 117 us  [the longest x40 79.1 us: shift(): return lax.ppermute(value, ('row', 'col'), pairs)]
    pallas_call x0 -> x11, Pallas kernels: none -> 93.4 us  [the longest x4 72.8 us: join(): pl.pallas_call(kernel, out_shape=jax.ShapeDtypeStruct((rows, HALF), BF16)...]
    reduce_scatter x2 -> x0, waiting for transfers between devices: 63.8 us -> none  [spread(): return lax.psum_scatter(mirror_term, 'row', scatter_dimension=1, tiled=True)]
    ppermute x0 -> x52, waiting for transfers between devices: none -> 47.4 us  [the longest x40 37.8 us: shift(): return lax.ppermute(value, ('row', 'col'), pairs)]
    unnamed x7 -> x92, local copies, waits for them, and re-layouts: 0.5 us -> 19.8 us
    dot_general x4 -> x0, matrix products: 18.3 us -> none  [the longest x2 13.1 us: mirror(): lax.dot_general(masked, gathered, (((0,), (0,)), ((), ())), preferred_ele...]
  transfers between devices with their start and end apart: 6 -> 53, of which waited for: 6 -> 11; matrix products, arithmetic and copies ran while one was open for 5% -> 1% of each run, Pallas kernels for 0% -> 30%
where the time goes in v1:
time: 309 us; the launch traced here: 307 us
  starting transfers between devices  117 us (38%)
  Pallas kernels  93.4 us (30%)
  waiting for transfers between devices  47.4 us (15%)
  local copies, waits for them, and re-layouts  19.8 us (6%)
  between operations  15.1 us (5%)
  blocking collectives  9.89 us (3%)
  other arithmetic  4.67 us (2%)
    ppermute x40, starting transfers between devices, shift(): return lax.ppermute(value, ('row', 'col'), pairs)  79.1 us
    pallas_call x4, Pallas kernels, join(): pl.pallas_call(kernel, out_shape=jax.ShapeDtypeStruct((rows, HALF), BF16)...  72.8 us
    ppermute x40, waiting for transfers between devices, shift(): return lax.ppermute(value, ('row', 'col'), pairs)  37.8 us
    ppermute x3, starting transfers between devices, core_swap(): return lax.ppermute(value, 'row', [(r, r ^ 1) for r in range(2 * NY)])  26 us
    unnamed x92, local copies, waits for them, and re-layouts  19.8 us
    ppermute x9, starting transfers between devices, y_shift(): return lax.ppermute(value, 'row', pairs)  12.1 us
    pallas_call x2, Pallas kernels, product(): pl.pallas_call(product_kernel, out_shape=(jax.ShapeDtypeStruct((512, 128)...  10.7 us
    all_gather x1, blocking collectives, local(): lax.all_gather(top, 'row', axis_index_groups=same_core, axis=0, tiled=True)  9.89 us
  transfers between devices with their start and end apart: 53, of which 11 were waited for; matrix products, arithmetic and copies ran while one was open for 1% of the time, Pallas kernels for 30%

profile of v1, /device:TPU:1, one launch (start us, length us, event | category | flops | bytes accessed | tf_op | source)
XLA Modules:
  0.0 307.5 jit_solution(9128736609550868985)
XLA Ops:
  9.7 3.3 %collective-permute-start.1 = (bf16[2,64,512]{2,1,0:T(8,128)(2,1)S(1)}, bf16[2,64,512]{2,1,0:T(8,128)(2,1)S(1)}, u32[]{:S(2)}, u32[]{:S(2)}) collective-permute-start(bf16[2,64,512]{2,1,0:T(8,128)(2,1)S(1)} %get-tuple-element.14), channel_id=1, source_target_pairs={{0,32},{32,0},{64,96},{96,64},{128,160},{160,128},{192,224},{224,1... | collective-permute-start | bytes 393224 | tf_op jit(solution)/shard_map/ppermute | solution.py:37
  16.1 5.7 %collective-permute-start.13 = (bf16[128,512]{1,0:T(8,128)(2,1)S(1)}, bf16[128,512]{1,0:T(8,128)(2,1)S(1)}, u32[]{:S(2)}, u32[]{:S(2)}) collective-permute-start(bf16[128,512]{1,0:T(8,128)(2,1)S(1)} %pad_maximum_fusion.1.refs_0_), channel_id=1, source_target_pairs={{32,39},{33,32},{34,33},{35,34},{36,35},{37,36},{38,37},{39,38},{4... | collective-permute-start | bytes 393224 | tf_op jit(solution)/shard_map/ppermute | solution.py:28
  26.8 9.9 %all-gather = bf16[1,256,512]{2,1,0:T(8,128)(2,1)S(1)} all-gather(bf16[1,64,512]{2,1,0:T(8,128)(2,1)S(1)} %get-tuple-element.26), channel_id=2, replica_groups={{0,64,128,192},{32,96,160,224},{1,65,129,193},{33,97,161,225},{2,66,130..., dimensions={1}, use_global_device_ids=true | all-gather | bytes 327680 | tf_op jit(solution)/shard_map/all_gather | solution.py:300
  37.8 4.6 %collective-permute-start.36 = (bf16[144,512]{1,0:T(8,128)(2,1)S(1)}, bf16[144,512]{1,0:T(8,128)(2,1)S(1)}, u32[]{:S(2)}, u32[]{:S(2)}) collective-permute-start(bf16[144,512]{1,0:T(8,128)(2,1)S(1)} %shard_with_diagonal.1.refs_0_), channel_id=1, source_target_pairs={{32,39},{33,32},{34,33},{35,34},{36,35},{37,36},{38,37},{39,38},{4... | collective-permute-start | bytes 442376 | tf_op jit(solution)/shard_map/ppermute | solution.py:28
  46.4 3.1 collective-permute-done.35.refs_1_
  51.4 3.4 %collective-permute-start.14 = (bf16[128,512]{1,0:T(8,128)(2,1)S(1)}, bf16[128,512]{1,0:T(8,128)(2,1)}, u32[]{:S(2)}, u32[]{:S(2)}) collective-permute-start(bf16[128,512]{1,0:T(8,128)(2,1)S(1)} %collective-permute-done.12.refs_1_), channel_id=1, source_target_pairs={{32,33},{33,34},{34,35},{35,36},{36,37},{37,38},{38,39},{39,32},{4... | collective-permute-start | bytes 393224 | tf_op jit(solution)/shard_map/ppermute | solution.py:28
  54.8 3.1 %collective-permute-start.38 = (bf16[144,512]{1,0:T(8,128)(2,1)S(1)}, bf16[144,512]{1,0:T(8,128)(2,1)S(1)}, u32[]{:S(2)}, u32[]{:S(2)}) collective-permute-start(bf16[144,512]{1,0:T(8,128)(2,1)S(1)} %collective-permute-done.36.refs_2_), channel_id=1, source_target_pairs={{32,39},{33,32},{34,33},{35,34},{36,35},{37,36},{38,37},{39,38},{4... | collective-permute-start | bytes 442376 | tf_op jit(solution)/shard_map/ppermute | solution.py:28
  60.2 22.6 %collective-permute-start = (bf16[2048,512]{1,0:T(8,128)(2,1)}, bf16[2048,512]{1,0:T(8,128)(2,1)}, u32[]{:S(2)}, u32[]{:S(2)}) collective-permute-start(bf16[2048,512]{1,0:T(8,128)(2,1)} %mine.1), channel_id=1, source_target_pairs={{0,32},{32,0},{64,96},{96,64},{128,160},{160,128},{192,224},{224,1... | collective-permute-start | bytes 6291464 | tf_op jit(solution)/shard_map/ppermute | solution.py:37
  82.8 5.6 %collective-permute-start.17 = (bf16[128,512]{1,0:T(8,128)(2,1)S(1)}, bf16[128,512]{1,0:T(8,128)(2,1)}, u32[]{:S(2)}, u32[]{:S(2)}) collective-permute-start(bf16[128,512]{1,0:T(8,128)(2,1)S(1)} %collective-permute-done.15.refs_4_), channel_id=1, source_target_pairs={{32,39},{33,32},{34,33},{35,34},{36,35},{37,36},{38,37},{39,38},{4... | collective-permute-start | bytes 393224 | tf_op jit(solution)/shard_map/ppermute | solution.py:28
  98.1 3.6 %collective-permute-done.18.refs_7_ = bf16[128,512]{1,0:T(8,128)(2,1)} collective-permute-done((bf16[128,512]{1,0:T(8,128)(2,1)}, bf16[128,512]{1,0:T(8,128)(2,1)}, u32[]{:S(2)}, u32[]{:S(2)}) %collective-permute-start.18) | collective-permute-done | bytes 131104 | tf_op jit(solution)/shard_map/ppermute | solution.py:28
  101.7 3.6 %collective-permute-start.40 = (bf16[144,512]{1,0:T(8,128)(2,1)S(1)}, bf16[144,512]{1,0:T(8,128)(2,1)}, u32[]{:S(2)}, u32[]{:S(2)}) collective-permute-start(bf16[144,512]{1,0:T(8,128)(2,1)S(1)} %collective-permute-done.38.refs_4_), channel_id=1, source_target_pairs={{32,39},{33,32},{34,33},{35,34},{36,35},{37,36},{38,37},{39,38},{4... | collective-permute-start | bytes 442376 | tf_op jit(solution)/shard_map/ppermute | solution.py:28
  105.3 33.7 %join_parts.5.refs_8_ = bf16[1024,512]{1,0:T(8,128)(2,1)} custom-call(s32[4]{0:T(128)} %copy-done.26, bf16[128,512]{1,0:T(8,128)(2,1)} %copy-done.33, bf16[128,512]{1,0:T(8,128)(2,1)} %copy-done.41, bf16[128,512]{1,0:T(8,128)(2,1)} %copy-done.40, bf16[128,512]{1,0:T(8,128)(2,1)} %collective-permute-done.14.refs_3_, bf16[128,512]{1,0:T(8,128)(2,1)} %copy-done.42, ...), custom_call_target="tpu_custom_call" | custom-call | tf_op jit(solution)/shard_map/join_parts/pallas_call | solution.py:125
  141.8 4.6 %collective-permute-start.20 = (bf16[1024,512]{1,0:T(8,128)(2,1)}, bf16[1024,512]{1,0:T(8,128)(2,1)S(1)}, u32[]{:S(2)}, u32[]{:S(2)}) collective-permute-start(bf16[1024,512]{1,0:T(8,128)(2,1)} %join_parts.5.refs_8_), channel_id=1, source_target_pairs={{32,56},{33,57},{34,58},{35,59},{36,60},{37,61},{38,62},{39,63},{4... | collective-permute-start | bytes 3145736 | tf_op jit(solution)/shard_map/ppermute | solution.py:28
  149.0 18.3 %collective-permute-done.19.refs_9_ = bf16[1024,512]{1,0:T(8,128)(2,1)S(1)} collective-permute-done((bf16[1024,512]{1,0:T(8,128)(2,1)}, bf16[1024,512]{1,0:T(8,128)(2,1)S(1)}, u32[]{:S(2)}, u32[]{:S(2)}) %collective-permute-start.19) | collective-permute-done | bytes 1048608 | tf_op jit(solution)/shard_map/ppermute | solution.py:28
  174.5 4.6 %collective-permute-start.41 = (bf16[144,512]{1,0:T(8,128)(2,1)}, bf16[144,512]{1,0:T(8,128)(2,1)}, u32[]{:S(2)}, u32[]{:S(2)}) collective-permute-start(bf16[144,512]{1,0:T(8,128)(2,1)} %collective-permute-done.40.refs_6_), channel_id=1, source_target_pairs={{32,39},{33,32},{34,33},{35,34},{36,35},{37,36},{38,37},{39,38},{4... | collective-permute-start | bytes 442376 | tf_op jit(solution)/shard_map/ppermute | solution.py:28
  180.7 3.6 %prepare_adjoint.1.adjoint = bf16[8,512,512]{2,1,0:T(8,128)(2,1)S(1)} custom-call(s32[4]{0:T(128)S(1)} %copy-done.28, s32[64,64]{1,0:T(8,128)S(1)} %copy-done.30, bf16[2048,512]{1,0:T(8,128)(2,1)S(1)} %copy-done.18, bf16[2048,512]{1,0:T(8,128)(2,1)} %collective-permute-done.other), custom_call_target="tpu_custom_call" | custom-call | tf_op jit(solution)/shard_map/prepare_adjoint/pallas_call | solution.py:164
  184.4 5.3 %masked_product.2 = (f32[512,128]{1,0:T(8,128)S(1)}, f32[512,128]{1,0:T(8,128)}, f32[512,128]{1,0:T(8,128)S(1)}, f32[512,128]{1,0:T(8,128)S(1)}) custom-call(s32[4]{0:T(128)S(1)} %copy-done.28, bf16[8,512,512]{2,1,0:T(8,128)(2,1)S(1)} %prepare_adjoint.1.adjoint, bf16[512,512]{1,0:T(8,128)(2,1)S(1)} %copy-done.17, ...), custom_call_target="tpu_custom_call" | custom-call | tf_op jit(solution)/shard_map/masked_product/pallas_call | solution.py:208
  192.8 37.6 %join_parts.7.refs_8_ = bf16[1152,512]{1,0:T(8,128)(2,1)} custom-call(s32[4]{0:T(128)} %copy-done.26, bf16[144,512]{1,0:T(8,128)(2,1)} %copy-done.20, bf16[144,512]{1,0:T(8,128)(2,1)} %copy-done.35, bf16[144,512]{1,0:T(8,128)(2,1)} %copy-done.34, bf16[144,512]{1,0:T(8,128)(2,1)} %collective-permute-done.37.refs_3_, bf16[144,512]{1,0:T(8,128)(2,1)} %copy-done.36, ...), custom_call_target="tpu_custom_call" | custom-call | tf_op jit(solution)/shard_map/join_parts/pallas_call | solution.py:125
  236.5 3.8 %collective-permute-done.23 = f32[512,128]{1,0:T(8,128)S(1)} collective-permute-done((f32[512,128]{1,0:T(8,128)}, f32[512,128]{1,0:T(8,128)S(1)}, u32[]{:S(2)}, u32[]{:S(2)}) %collective-permute-start.23) | collective-permute-done | bytes 262176 | tf_op jit(solution)/shard_map/ppermute | solution.py:33
  240.3 4.9 %collective-permute-start.43 = (bf16[1152,512]{1,0:T(8,128)(2,1)}, bf16[1152,512]{1,0:T(8,128)(2,1)S(1)}, u32[]{:S(2)}, u32[]{:S(2)}) collective-permute-start(bf16[1152,512]{1,0:T(8,128)(2,1)} %join_parts.7.refs_8_), channel_id=1, source_target_pairs={{32,56},{33,57},{34,58},{35,59},{36,60},{37,61},{38,62},{39,63},{4... | collective-permute-start | bytes 3538952 | tf_op jit(solution)/shard_map/ppermute | solution.py:28
  245.2 3.3 %collective-permute-start.44 = (bf16[1152,512]{1,0:T(8,128)(2,1)}, bf16[1152,512]{1,0:T(8,128)(2,1)S(1)}, u32[]{:S(2)}, u32[]{:S(2)}) collective-permute-start(bf16[1152,512]{1,0:T(8,128)(2,1)} %join_parts.7.refs_8_), channel_id=1, source_target_pairs={{32,48},{33,49},{34,50},{35,51},{36,52},{37,53},{38,54},{39,55},{4... | collective-permute-start | bytes 3538952 | tf_op jit(solution)/shard_map/ppermute | solution.py:28
  261.6 9.7 %collective-permute-done.43.refs_10_ = bf16[1152,512]{1,0:T(8,128)(2,1)S(1)} collective-permute-done((bf16[1152,512]{1,0:T(8,128)(2,1)}, bf16[1152,512]{1,0:T(8,128)(2,1)S(1)}, u32[]{:S(2)}, u32[]{:S(2)}) %collective-permute-start.43) | collective-permute-done | bytes 1179680 | tf_op jit(solution)/shard_map/ppermute | solution.py:28
  271.4 3.2 %copy-done.1 = bf16[8,512,512]{2,1,0:T(8,128)(2,1)S(1)} copy-done((bf16[8,512,512]{2,1,0:T(8,128)(2,1)S(1)}, bf16[8,512,512]{2,1,0:T(8,128)(2,1)}, u32[]{:S(2)}) %copy-start.1) | copy-done | bytes 4194328
  274.6 5.4 %masked_product.3 = (f32[512,128]{1,0:T(8,128)S(1)}, bf16[512,128]{1,0:T(8,128)(2,1)}, bf16[512,128]{1,0:T(8,128)(2,1)}, bf16[512,128]{1,0:T(8,128)(2,1)}) custom-call(s32[4]{0:T(128)S(1)} %copy-done.29, bf16[8,512,512]{2,1,0:T(8,128)(2,1)S(1)} %copy-done.1, bf16[576,512]{1,0:T(8,128)(2,1)S(1)} %copy-done.3, ...), custom_call_target="tpu_custom_call" | custom-call | tf_op jit(solution)/shard_map/masked_product/pallas_call | solution.py:208
  (193 shorter events, 85.9 us)
Async XLA Ops:
  7.2 278.0 %all-gather.3.cloned.1.call-start = ((), (), s32[]{:S(2)}) async-start(), calls=%async_computation | async-start | bytes 2359296 | tf_op jit(solution)/shard_map/all_gather | solution.py:301
  16.1 28.2 %collective-permute-start.13 = (bf16[128,512]{1,0:T(8,128)(2,1)S(1)}, bf16[128,512]{1,0:T(8,128)(2,1)S(1)}, u32[]{:S(2)}, u32[]{:S(2)}) collective-permute-start(bf16[128,512]{1,0:T(8,128)(2,1)S(1)} %pad_maximum_fusion.1.refs_0_), channel_id=1, source_target_pairs={{32,39},{33,32},{34,33},{35,34},{36,35},{37,36},{38,37},{39,38},{4... | collective-permute-start | bytes 393224 | tf_op jit(solution)/shard_map/ppermute | solution.py:28
  21.9 23.1 %collective-permute-start.12 = (bf16[128,512]{1,0:T(8,128)(2,1)S(1)}, bf16[128,512]{1,0:T(8,128)(2,1)S(1)}, u32[]{:S(2)}, u32[]{:S(2)}) collective-permute-start(bf16[128,512]{1,0:T(8,128)(2,1)S(1)} %pad_maximum_fusion.1.refs_0_), channel_id=1, source_target_pairs={{32,33},{33,34},{34,35},{35,36},{36,37},{37,38},{38,39},{39,32},{4... | collective-permute-start | bytes 393224 | tf_op jit(solution)/shard_map/ppermute | solution.py:28
  25.9 66.8 %collective-permute-start.5 = (bf16[512,512]{1,0:T(8,128)(2,1)}, bf16[512,512]{1,0:T(8,128)(2,1)S(1)}, u32[]{:S(2)}, u32[]{:S(2)}) collective-permute-start(bf16[512,512]{1,0:T(8,128)(2,1)} %join_parts.4.refs_0_), channel_id=1, source_target_pairs={{0,1},{1,2},{2,3},{3,4},{4,5},{5,6},{6,7},{7,0},{8,9},{9,10},{10,1... | collective-permute-start | bytes 1572872 | tf_op jit(solution)/shard_map/ppermute | solution.py:28
  51.4 31.4 %collective-permute-start.14 = (bf16[128,512]{1,0:T(8,128)(2,1)S(1)}, bf16[128,512]{1,0:T(8,128)(2,1)}, u32[]{:S(2)}, u32[]{:S(2)}) collective-permute-start(bf16[128,512]{1,0:T(8,128)(2,1)S(1)} %collective-permute-done.12.refs_1_), channel_id=1, source_target_pairs={{32,33},{33,34},{34,35},{35,36},{36,37},{37,38},{38,39},{39,32},{4... | collective-permute-start | bytes 393224 | tf_op jit(solution)/shard_map/ppermute | solution.py:28
  54.8 33.6 %collective-permute-start.38 = (bf16[144,512]{1,0:T(8,128)(2,1)S(1)}, bf16[144,512]{1,0:T(8,128)(2,1)S(1)}, u32[]{:S(2)}, u32[]{:S(2)}) collective-permute-start(bf16[144,512]{1,0:T(8,128)(2,1)S(1)} %collective-permute-done.36.refs_2_), channel_id=1, source_target_pairs={{32,39},{33,32},{34,33},{35,34},{36,35},{37,36},{38,37},{39,38},{4... | collective-permute-start | bytes 442376 | tf_op jit(solution)/shard_map/ppermute | solution.py:28
  58.0 33.2 %collective-permute-start.37 = (bf16[144,512]{1,0:T(8,128)(2,1)S(1)}, bf16[144,512]{1,0:T(8,128)(2,1)}, u32[]{:S(2)}, u32[]{:S(2)}) collective-permute-start(bf16[144,512]{1,0:T(8,128)(2,1)S(1)} %collective-permute-done.35.refs_1_), channel_id=1, source_target_pairs={{32,33},{33,34},{34,35},{35,36},{36,37},{37,38},{38,39},{39,32},{4... | collective-permute-start | bytes 442376 | tf_op jit(solution)/shard_map/ppermute | solution.py:28
  60.2 114.4 %collective-permute-start = (bf16[2048,512]{1,0:T(8,128)(2,1)}, bf16[2048,512]{1,0:T(8,128)(2,1)}, u32[]{:S(2)}, u32[]{:S(2)}) collective-permute-start(bf16[2048,512]{1,0:T(8,128)(2,1)} %mine.1), channel_id=1, source_target_pairs={{0,32},{32,0},{64,96},{96,64},{128,160},{160,128},{192,224},{224,1... | collective-permute-start | bytes 6291464 | tf_op jit(solution)/shard_map/ppermute | solution.py:37
  91.2 50.6 %collective-permute-start.28 = (bf16[576,512]{1,0:T(8,128)(2,1)}, bf16[576,512]{1,0:T(8,128)(2,1)S(1)}, u32[]{:S(2)}, u32[]{:S(2)}) collective-permute-start(bf16[576,512]{1,0:T(8,128)(2,1)} %join_parts.6.refs_0_), channel_id=1, source_target_pairs={{0,1},{1,2},{2,3},{3,4},{4,5},{5,6},{6,7},{7,0},{8,9},{9,10},{10,1... | collective-permute-start | bytes 1769480 | tf_op jit(solution)/shard_map/ppermute | solution.py:28
  92.1 49.0 %collective-permute-start.6 = (bf16[512,512]{1,0:T(8,128)(2,1)S(1)}, bf16[512,512]{1,0:T(8,128)(2,1)S(1)}, u32[]{:S(2)}, u32[]{:S(2)}) collective-permute-start(bf16[512,512]{1,0:T(8,128)(2,1)S(1)} %copy-done.17), channel_id=1, source_target_pairs={{0,7},{1,0},{2,1},{3,2},{4,3},{5,4},{6,5},{7,6},{8,15},{9,8},{10,9... | collective-permute-start | bytes 1572872 | tf_op jit(solution)/shard_map/ppermute | solution.py:28
  92.8 53.6 %collective-permute-start.7 = (bf16[512,512]{1,0:T(8,128)(2,1)S(1)}, bf16[512,512]{1,0:T(8,128)(2,1)S(1)}, u32[]{:S(2)}, u32[]{:S(2)}) collective-permute-start(bf16[512,512]{1,0:T(8,128)(2,1)S(1)} %collective-permute-done.5.refs_1_), channel_id=1, source_target_pairs={{0,1},{1,2},{2,3},{3,4},{4,5},{5,6},{6,7},{7,0},{8,9},{9,10},{10,1... | collective-permute-start | bytes 1572872 | tf_op jit(solution)/shard_map/ppermute | solution.py:28
  101.7 37.3 %collective-permute-start.40 = (bf16[144,512]{1,0:T(8,128)(2,1)S(1)}, bf16[144,512]{1,0:T(8,128)(2,1)}, u32[]{:S(2)}, u32[]{:S(2)}) collective-permute-start(bf16[144,512]{1,0:T(8,128)(2,1)S(1)} %collective-permute-done.38.refs_4_), channel_id=1, source_target_pairs={{32,39},{33,32},{34,33},{35,34},{36,35},{37,36},{38,37},{39,38},{4... | collective-permute-start | bytes 442376 | tf_op jit(solution)/shard_map/ppermute | solution.py:28
  139.0 28.3 %collective-permute-start.19 = (bf16[1024,512]{1,0:T(8,128)(2,1)}, bf16[1024,512]{1,0:T(8,128)(2,1)S(1)}, u32[]{:S(2)}, u32[]{:S(2)}) collective-permute-start(bf16[1024,512]{1,0:T(8,128)(2,1)} %join_parts.5.refs_8_), channel_id=1, source_target_pairs={{32,40},{33,41},{34,42},{35,43},{36,44},{37,45},{38,46},{39,47},{4... | collective-permute-start | bytes 3145736 | tf_op jit(solution)/shard_map/ppermute | solution.py:28
  141.8 27.9 %collective-permute-start.20 = (bf16[1024,512]{1,0:T(8,128)(2,1)}, bf16[1024,512]{1,0:T(8,128)(2,1)S(1)}, u32[]{:S(2)}, u32[]{:S(2)}) collective-permute-start(bf16[1024,512]{1,0:T(8,128)(2,1)} %join_parts.5.refs_8_), channel_id=1, source_target_pairs={{32,56},{33,57},{34,58},{35,59},{36,60},{37,61},{38,62},{39,63},{4... | collective-permute-start | bytes 3145736 | tf_op jit(solution)/shard_map/ppermute | solution.py:28
  146.4 24.7 %collective-permute-start.21 = (bf16[1024,512]{1,0:T(8,128)(2,1)}, bf16[1024,512]{1,0:T(8,128)(2,1)S(1)}, u32[]{:S(2)}, u32[]{:S(2)}) collective-permute-start(bf16[1024,512]{1,0:T(8,128)(2,1)} %join_parts.5.refs_8_), channel_id=1, source_target_pairs={{32,48},{33,49},{34,50},{35,51},{36,52},{37,53},{38,54},{39,55},{4... | collective-permute-start | bytes 3145736 | tf_op jit(solution)/shard_map/ppermute | solution.py:28
  148.3 19.7 %collective-permute-start.9 = (bf16[512,512]{1,0:T(8,128)(2,1)S(1)}, bf16[512,512]{1,0:T(8,128)(2,1)S(1)}, u32[]{:S(2)}, u32[]{:S(2)}) collective-permute-start(bf16[512,512]{1,0:T(8,128)(2,1)S(1)} %collective-permute-done.7.refs_3_), channel_id=1, source_target_pairs={{0,1},{1,2},{2,3},{3,4},{4,5},{5,6},{6,7},{7,0},{8,9},{9,10},{10,1... | collective-permute-start | bytes 1572872 | tf_op jit(solution)/shard_map/ppermute | solution.py:28
  169.6 62.9 %collective-permute-start.29 = (bf16[576,512]{1,0:T(8,128)(2,1)S(1)}, bf16[576,512]{1,0:T(8,128)(2,1)}, u32[]{:S(2)}, u32[]{:S(2)}) collective-permute-start(bf16[576,512]{1,0:T(8,128)(2,1)S(1)} %copy-done.3), channel_id=1, source_target_pairs={{0,7},{1,0},{2,1},{3,2},{4,3},{5,4},{6,5},{7,6},{8,15},{9,8},{10,9... | collective-permute-start | bytes 1769480 | tf_op jit(solution)/shard_map/ppermute | solution.py:28
  171.1 64.7 %collective-permute-start.30 = (bf16[576,512]{1,0:T(8,128)(2,1)S(1)}, bf16[576,512]{1,0:T(8,128)(2,1)}, u32[]{:S(2)}, u32[]{:S(2)}) collective-permute-start(bf16[576,512]{1,0:T(8,128)(2,1)S(1)} %collective-permute-done.28.refs_1_), channel_id=1, source_target_pairs={{0,1},{1,2},{2,3},{3,4},{4,5},{5,6},{6,7},{7,0},{8,9},{9,10},{10,1... | collective-permute-start | bytes 1769480 | tf_op jit(solution)/shard_map/ppermute | solution.py:28
  172.6 20.2 %collective-permute-start.39 = (bf16[144,512]{1,0:T(8,128)(2,1)}, bf16[144,512]{1,0:T(8,128)(2,1)}, u32[]{:S(2)}, u32[]{:S(2)}) collective-permute-start(bf16[144,512]{1,0:T(8,128)(2,1)} %collective-permute-done.37.refs_3_), channel_id=1, source_target_pairs={{32,33},{33,34},{34,35},{35,36},{36,37},{37,38},{38,39},{39,32},{4... | collective-permute-start | bytes 442376 | tf_op jit(solution)/shard_map/ppermute | solution.py:28
  191.8 44.0 %collective-permute-start.22 = (f32[512,128]{1,0:T(8,128)}, f32[512,128]{1,0:T(8,128)}, u32[]{:S(2)}, u32[]{:S(2)}) collective-permute-start(f32[512,128]{1,0:T(8,128)} %get-tuple-element.16), channel_id=1, source_target_pairs={{0,64},{32,96},{64,128},{96,160},{128,192},{160,224},{192,0},{224,... | collective-permute-start | bytes 786440 | tf_op jit(solution)/shard_map/ppermute | solution.py:33
  230.5 31.1 %collective-permute-start.42 = (bf16[1152,512]{1,0:T(8,128)(2,1)}, bf16[1152,512]{1,0:T(8,128)(2,1)S(1)}, u32[]{:S(2)}, u32[]{:S(2)}) collective-permute-start(bf16[1152,512]{1,0:T(8,128)(2,1)} %join_parts.7.refs_8_), channel_id=1, source_target_pairs={{32,40},{33,41},{34,42},{35,43},{36,44},{37,45},{38,46},{39,47},{4... | collective-permute-start | bytes 3538952 | tf_op jit(solution)/shard_map/ppermute | solution.py:28
  240.3 31.0 %collective-permute-start.43 = (bf16[1152,512]{1,0:T(8,128)(2,1)}, bf16[1152,512]{1,0:T(8,128)(2,1)S(1)}, u32[]{:S(2)}, u32[]{:S(2)}) collective-permute-start(bf16[1152,512]{1,0:T(8,128)(2,1)} %join_parts.7.refs_8_), channel_id=1, source_target_pairs={{32,56},{33,57},{34,58},{35,59},{36,60},{37,61},{38,62},{39,63},{4... | collective-permute-start | bytes 3538952 | tf_op jit(solution)/shard_map/ppermute | solution.py:28
  245.2 26.1 %collective-permute-start.44 = (bf16[1152,512]{1,0:T(8,128)(2,1)}, bf16[1152,512]{1,0:T(8,128)(2,1)S(1)}, u32[]{:S(2)}, u32[]{:S(2)}) collective-permute-start(bf16[1152,512]{1,0:T(8,128)(2,1)} %join_parts.7.refs_8_), channel_id=1, source_target_pairs={{32,48},{33,49},{34,50},{35,51},{36,52},{37,53},{38,54},{39,55},{4... | collective-permute-start | bytes 3538952 | tf_op jit(solution)/shard_map/ppermute | solution.py:28
  261.6 35.0 %collective-permute-start.51 = (bf16[4,512,128]{2,1,0:T(8,128)(2,1)}, bf16[4,512,128]{2,1,0:T(8,128)(2,1)}, u32[]{:S(2)}, u32[]{:S(2)}) collective-permute-start(bf16[4,512,128]{2,1,0:T(8,128)(2,1)} %pad_maximum_fusion.mine), channel_id=1, source_target_pairs={{0,32},{32,0},{64,96},{96,64},{128,160},{160,128},{192,224},{224,1... | collective-permute-start | bytes 1572872 | tf_op jit(solution)/shard_map/ppermute | solution.py:37
  (75 other events, 1502.0 us)
Sparse Core Ops, SparseCore 0:
  98.2 44.6 all-gather.2

commit v2 on v1

v2 whole, which is shorter than its diff:
```python
import functools

import jax
import jax.numpy as jnp
from jax import lax
from jax.experimental import pallas as pl
from jax.experimental.pallas import tpu as pltpu
from jax.sharding import PartitionSpec as P

BLK = 256
NX, NZ, NY = 4, 8, 4
SUB = 64
PAIR = 2 * SUB
HALF = 512
F32, BF16 = jnp.float32, jnp.bfloat16
VMEM = pl.BlockSpec(memory_space=pltpu.VMEM)
SMEM = pl.BlockSpec(memory_space=pltpu.SMEM)
ANY = pl.BlockSpec(memory_space=pl.ANY)
BIG = pltpu.CompilerParams(vmem_limit_bytes=40 * 2**20)


def x_shift(value, dx):
    pairs = [(x * NZ + z, (x + dx) % NX * NZ + z) for x in range(NX) for z in range(NZ)]
    return lax.ppermute(value, "col", pairs)


def z_shift(value, dz):
    pairs = [(x * NZ + z, x * NZ + (z + dz) % NZ) for x in range(NX) for z in range(NZ)]
    return lax.ppermute(value, "col", pairs)


def y_shift(value, dy):
    pairs = [(y * 2 + k, (y + dy) % NY * 2 + k) for y in range(NY) for k in range(2)]
    return lax.ppermute(value, "row", pairs)


def y_first(value, y):
    return lax.ppermute(value, "row", [(k, y * 2 + k) for k in range(2)])


def core_swap(value):
    return lax.ppermute(value, "row", [(r, r ^ 1) for r in range(2 * NY)])


def gather_xz(part):
    block = jnp.concatenate([part] + [x_shift(part, d) for d in (1, -1, 2)], axis=0)
    down1, up1 = z_shift(block, 1), z_shift(block, -1)
    down2, up2 = z_shift(down1, 1), z_shift(up1, -1)
    down3, up3 = z_shift(down2, 1), z_shift(up2, -1)
    return [block, down1, up1, down2, up2, down3, up3, z_shift(down3, 1)]


def after(value, *others):
    return lax.optimization_barrier((value,) + others)[0]


def gather_zx(part, earlier):
    same_x = [[x * NZ + z for z in range(NZ)] for x in range(NX)]
    block = lax.all_gather(part, "col", axis_index_groups=same_x, axis=0, tiled=True)
    block = after(block, earlier)
    down, up = x_shift(block, 1), x_shift(block, -1)
    return [block, down, up, x_shift(down[:HALF], 1), x_shift(up[HALF:], -1)]


def offset(n):
    return ((n + 1) // 2) * (1 - 2 * (n % 2))


def source_xz(pos, b, t):
    return (pos[0] + offset(t) + NX) % NX, (pos[1] + offset(b) + NZ) % NZ


def source_zx(pos, b, t):
    return (pos[0] + offset(b // 2) + NX) % NX, b % 2 * 4 + t


def pack_kernel(pos, two, one, own, give):
    first = pos[3] == 0
    for n, panel in enumerate((two, one)):
        for q in range(NY):
            left = panel[:, q * 256:q * 256 + 128]
            right = panel[:, q * 256 + 128:q * 256 + 256]
            at = slice(q * 128, q * 128 + 128)
            own[n, :, at] = jnp.where(first, left, right)
            give[n, :, at] = jnp.where(first, right, left)


def pack(pos, two, one):
    return pl.pallas_call(
        pack_kernel,
        out_shape=(jax.ShapeDtypeStruct((2, SUB, HALF), BF16),) * 2,
        in_specs=[SMEM, VMEM, VMEM],
        out_specs=(VMEM, VMEM),
        compiler_params=BIG,
        name="pack_columns",
    )(pos, two, one)


def prepare_kernel(pos, taper, mine, other, for_two, for_one, rows):
    lane = lax.broadcasted_iota(jnp.int32, (SUB, 2 * BLK), 1)
    first_col = (pos[0] * NZ + pos[1]) * 2

    for out, source in ((for_two, source_xz), (for_one, source_zx)):
        def block(b, carry, out=out, source=source):
            for t in range(4):
                x, z = source(pos, b, t)
                row = pl.multiple_of((x * NZ + z) * SUB, SUB)
                for h, ref in enumerate((mine, other)):
                    core = pos[3] if h == 0 else 1 - pos[3]
                    tile = (pos[2] * 2 + core) * 8 + x * 2 + z // 4
                    left = taper[tile, first_col].astype(F32)
                    right = taper[tile, first_col + 1].astype(F32)
                    keep = jnp.where(lane < BLK, left, right)
                    at = t * PAIR + h * SUB
                    rows[at:at + SUB, :] = (ref[pl.ds(row, SUB), :].astype(F32) * keep).astype(BF16)
            out[b] = rows[...].T
            return carry

        lax.fori_loop(0, 8, block, 0)


def prepare(pos, taper, mine, other):
    return pl.pallas_call(
        prepare_kernel,
        out_shape=(jax.ShapeDtypeStruct((8, 512, 512), BF16),) * 2,
        in_specs=[SMEM, SMEM, VMEM, VMEM],
        out_specs=(VMEM, VMEM),
        scratch_shapes=[pltpu.VMEM((512, 512), BF16)],
        compiler_params=BIG,
        name="prepare_adjoint",
    )(pos, taper, mine, other)


def windows(refs):
    if len(refs) == 8:
        return list(refs)
    halves = [ref.at[pl.ds(h * HALF, HALF)] for ref in refs[:3] for h in range(2)]
    return halves + list(refs[3:])


def product_kernel(count, pos, adjoint, *refs):
    panels, outs, held, total, sems = refs[:count], refs[count:count + 4], refs[-3], refs[-2], refs[-1]
    copies = [
        pltpu.make_async_copy(ref, held.at[b], sems.at[b]) for b, ref in enumerate(windows(panels))
    ]
    for copy in copies:
        copy.start()
    total[...] = jnp.zeros_like(total)

    def block(b, carry):
        pltpu.make_async_copy(held.at[b], held.at[b], sems.at[b]).wait()
        total[...] += jnp.dot(adjoint[b], held[b], preferred_element_type=F32)
        return carry

    lax.fori_loop(0, 8, block, 0)
    for d, out in enumerate(outs):
        column = pl.multiple_of((pos[2] + d) % NY * 128, 128)
        out[...] = (-2.0 * total[:, pl.ds(column, 128)]).astype(out.dtype)


def product(pos, adjoint, panels, kind):
    count = len(panels)
    return pl.pallas_call(
        functools.partial(product_kernel, count),
        out_shape=(jax.ShapeDtypeStruct((512, 128), F32),) + (jax.ShapeDtypeStruct((512, 128), kind),) * 3,
        in_specs=[SMEM, VMEM] + [ANY] * count,
        out_specs=(VMEM,) * 4,
        scratch_shapes=[
            pltpu.VMEM((8, 512, HALF), BF16),
            pltpu.VMEM((512, HALF), F32),
            pltpu.SemaphoreType.DMA((8,)),
        ],
        compiler_params=BIG,
        name="masked_product",
    )(pos, adjoint, *panels)


def diagonal_kernel(pos, block, down, up, far_low, far_high, own, one, two, three, held, sems):
    panels = (block, down, up, far_low, far_high)
    copies = [
        pltpu.make_async_copy(ref, held.at[b], sems.at[b]) for b, ref in enumerate(windows(panels))
    ]
    for copy in copies:
        copy.start()
    half = jnp.where(pos[3] == 0, 0, SUB)

    def fill(b, carry):
        pltpu.make_async_copy(held.at[b], held.at[b], sems.at[b]).wait()
        x, z = source_zx(pos, b, 0)

        @pl.when(x < 2)
        def _():
            for t in range(4):
                from_row = pl.multiple_of(half + t * PAIR, SUB)
                to_row = pl.multiple_of((x * NZ + z + t) * SUB, SUB)
                for d, out in enumerate((own, one, two, three)):
                    out[pl.ds(to_row, SUB), :] = held[b, pl.ds(from_row, SUB), d * 128:(d + 1) * 128]
        return carry

    lax.fori_loop(0, 8, fill, 0)


def diagonal(pos, panels):
    return pl.pallas_call(
        diagonal_kernel,
        out_shape=(jax.ShapeDtypeStruct((1024, 128), BF16),) * 4,
        in_specs=[SMEM] + [ANY] * 5,
        out_specs=(VMEM,) * 4,
        scratch_shapes=[pltpu.VMEM((8, 512, HALF), BF16), pltpu.SemaphoreType.DMA((8,))],
        compiler_params=BIG,
        name="diagonal_columns",
    )(pos, *panels)


def factor_kernel(pos, inverse, own, one, two, three, out):
    sent = (one[...] + two[...]) + three[...]
    columns = jnp.where(pos[2] == 0, own[...], sent)
    value = jnp.dot(inverse[...], columns, preferred_element_type=F32)
    high = value.astype(BF16)
    out[:, :128] = high
    out[:, 128:] = (value - high.astype(F32)).astype(BF16)


def factor(pos, inverse, parts):
    return pl.pallas_call(
        factor_kernel,
        out_shape=jax.ShapeDtypeStruct((1024, 256), BF16),
        in_specs=[SMEM] + [VMEM] * 5,
        out_specs=VMEM,
        compiler_params=BIG,
        name="inverse_times_diagonal",
    )(pos, inverse, *parts)


def carried_kernel(pos, mine, other, factors, out, total):
    first = pos[3] == 0
    total[...] = jnp.zeros_like(total)

    def block(d, carry):
        y = (pos[2] - d + NY) % NY
        a, b = mine[d], other[d]
        pair = jnp.concatenate([jnp.where(first, a, b), jnp.where(first, b, a)], axis=1)
        rows = pl.multiple_of(y * 256, 256)
        total[...] += jnp.dot(pair, factors[pl.ds(rows, 256), :], preferred_element_type=F32)
        return carry

    lax.fori_loop(0, NY, block, 0)
    out[...] = total[:, :128] + total[:, 128:]


def carried(pos, mine, other, factors):
    return pl.pallas_call(
        carried_kernel,
        out_shape=jax.ShapeDtypeStruct((512, 128), F32),
        in_specs=[SMEM] + [VMEM] * 3,
        out_specs=VMEM,
        scratch_shapes=[pltpu.VMEM((512, 256), F32)],
        compiler_params=BIG,
        name="carried_term",
    )(pos, mine, other, factors)


def local(adjoint, taper, panel_two, panel_one, incoming, inverse_factor):
    row, col = lax.axis_index("row"), lax.axis_index("col")
    pos = jnp.stack([col // NZ, col % NZ, row // 2, row % 2]).astype(jnp.int32)

    own, give = pack(pos, panel_two, panel_one)
    taken = core_swap(give)
    shards = jnp.concatenate([own, taken], axis=1)
    two = gather_xz(shards[0])
    one = gather_zx(shards[1], two[4])
    inverse = lax.all_gather(after(inverse_factor, two[4]), "row", axis=0, tiled=True)
    masked_two, masked_one = prepare(pos, taper, adjoint, core_swap(adjoint))

    mine, *sent = product(pos, masked_two, two, F32)
    r1, r2, r3 = [y_shift(part, d + 1) for d, part in enumerate(sent)]
    second_grad = incoming + ((mine + r1) + (r2 + r3))
    rounded = second_grad.astype(BF16)
    column = jnp.stack([rounded, y_shift(rounded, 1), y_shift(rounded, 2), y_shift(rounded, 3)])
    other = core_swap(column)

    mine, *sent = product(pos, masked_one, one, BF16)
    r1, r2, r3 = [y_shift(part, d + 1) for d, part in enumerate(sent)]
    first, *rest = diagonal(pos, one)
    factors = factor(pos, inverse, [first] + [y_first(part, d + 1) for d, part in enumerate(rest)])
    term = carried(pos, column, other, factors)
    first_grad = ((mine + r1.astype(F32)) + (r2.astype(F32) + r3.astype(F32))) - term
    return second_grad, first_grad


def solution(mesh):
    in_specs = (
        P("row", "col"),
        P(),
        P(("row", "col"), None),
        P(("row", "col"), None),
        P("col", "row"),
        P("row", None),
    )
    out_specs = (P("col", "row"), P("col", "row"))
    return jax.shard_map(local, mesh=mesh, in_specs=in_specs, out_specs=out_specs, check_vma=False)
```

time: 309 us -> 178 us (0.58)
  Pallas kernels: 93.4 us -> 19 us
  starting transfers between devices: 117 us -> 43.3 us
  waiting for transfers between devices: 47.4 us -> 92.8 us
  local copies, waits for them, and re-layouts: 19.8 us -> 5.11 us
  blocking collectives: 9.89 us -> 0 us
    pallas_call x8 -> x4, Pallas kernels: 87.6 us -> 15.6 us  [the longest x2 9.14 us: product(): pl.pallas_call(functools.partial(product_kernel, count), out_shape=(jax.S...]
    ppermute x40 -> x17, starting transfers between devices: 79.1 us -> 24.8 us  [the longest x7 10.6 us: z_shift(): return lax.ppermute(value, 'col', pairs)]
    ppermute x40 -> x17, waiting for transfers between devices: 37.8 us -> 79.4 us  [the longest x7 68.8 us: z_shift(): return lax.ppermute(value, 'col', pairs)]
    ppermute x3, starting transfers between devices: 26 us -> 9.74 us  [core_swap(): return lax.ppermute(value, 'row', [(r, r ^ 1) for r in range(2 * NY)])]
    unnamed x92 -> x19, local copies, waits for them, and re-layouts: 19.8 us -> 4.36 us
    all_gather x1 -> x0, blocking collectives: 9.89 us -> none  [local(): lax.all_gather(top, 'row', axis_index_groups=same_core, axis=0, tiled=True)]
    ppermute x9, waiting for transfers between devices: 8.64 us -> 12.5 us  [y_shift(): return lax.ppermute(value, 'row', pairs)]
    ppermute x9, starting transfers between devices: 12.1 us -> 8.64 us  [y_shift(): return lax.ppermute(value, 'row', pairs)]
  transfers between devices with their start and end apart: 53 -> 31, of which waited for: 11 -> 17; matrix products, arithmetic and copies ran while one was open for 1% -> 1% of each run, Pallas kernels for 30% -> 10%
where the time goes in v2:
time: 178 us; the launch traced here: 176 us
  waiting for transfers between devices  92.8 us (52%)
  starting transfers between devices  43.3 us (24%)
  Pallas kernels  19 us (11%)
  between operations  14.3 us (8%)
  local copies, waits for them, and re-layouts  5.11 us (3%)
    ppermute x7, waiting for transfers between devices, z_shift(): return lax.ppermute(value, 'col', pairs)  68.8 us
    ppermute x9, waiting for transfers between devices, y_shift(): return lax.ppermute(value, 'row', pairs)  12.5 us
    ppermute x7, starting transfers between devices, z_shift(): return lax.ppermute(value, 'col', pairs)  10.6 us
    ppermute x7, starting transfers between devices, x_shift(): return lax.ppermute(value, 'col', pairs)  10.1 us
    ppermute x3, starting transfers between devices, core_swap(): return lax.ppermute(value, 'row', [(r, r ^ 1) for r in range(2 * NY)])  9.74 us
    pallas_call x2, Pallas kernels, product(): pl.pallas_call(functools.partial(product_kernel, count), out_shape=(jax.S...  9.14 us
    ppermute x9, starting transfers between devices, y_shift(): return lax.ppermute(value, 'row', pairs)  8.64 us
    ppermute x7, waiting for transfers between devices, x_shift(): return lax.ppermute(value, 'col', pairs)  6.84 us
  transfers between devices with their start and end apart: 31, of which 17 were waited for; matrix products, arithmetic and copies ran while one was open for 1% of the time, Pallas kernels for 10%

profile of v2, /device:TPU:1, one launch (start us, length us, event | category | flops | bytes accessed | tf_op | source)
XLA Modules:
  0.0 176.3 jit_solution(14976119352967367113)
XLA Ops:
  9.9 3.3 %collective-permute-start.1 = (bf16[2,64,512]{2,1,0:T(8,128)(2,1)S(1)}, bf16[2,64,512]{2,1,0:T(8,128)(2,1)S(1)}, u32[]{:S(2)}, u32[]{:S(2)}) collective-permute-start(bf16[2,64,512]{2,1,0:T(8,128)(2,1)S(1)} %get-tuple-element.22), channel_id=1, source_target_pairs={{0,32},{32,0},{64,96},{96,64},{128,160},{160,128},{192,224},{224,1... | collective-permute-start | bytes 393224 | tf_op jit(solution)/shard_map/ppermute | solution.py:42
  17.5 3.8 %collective-permute-done.4 = bf16[128,512]{1,0:T(8,128)(2,1)S(1)} collective-permute-done((bf16[128,512]{1,0:T(8,128)(2,1)S(1)}, bf16[128,512]{1,0:T(8,128)(2,1)S(1)}, u32[]{:S(2)}, u32[]{:S(2)}) %collective-permute-start.4) | collective-permute-done | bytes 131104 | tf_op jit(solution)/shard_map/ppermute | solution.py:24
  22.4 1.9 %collective-permute-done.2 = bf16[128,512]{1,0:T(8,128)(2,1)S(1)} collective-permute-done((bf16[128,512]{1,0:T(8,128)(2,1)S(1)}, bf16[128,512]{1,0:T(8,128)(2,1)S(1)}, u32[]{:S(2)}, u32[]{:S(2)}) %collective-permute-start.2) | collective-permute-done | bytes 131104 | tf_op jit(solution)/shard_map/ppermute | solution.py:24
  24.4 3.8 %collective-permute-start.6 = (bf16[512,512]{1,0:T(8,128)(2,1)S(1)}, bf16[512,512]{1,0:T(8,128)(2,1)S(1)}, u32[]{:S(2)}, u32[]{:S(2)}) collective-permute-start(bf16[512,512]{1,0:T(8,128)(2,1)S(1)} %pad_maximum_fusion.refs_0_), channel_id=1, source_target_pairs={{0,7},{1,0},{2,1},{3,2},{4,3},{5,4},{6,5},{7,6},{8,15},{9,8},{10,9... | collective-permute-start | bytes 1572872 | tf_op jit(solution)/shard_map/ppermute | solution.py:29
  28.2 13.5 %collective-permute-done.6.refs_2_ = bf16[512,512]{1,0:T(8,128)(2,1)S(1)} collective-permute-done((bf16[512,512]{1,0:T(8,128)(2,1)S(1)}, bf16[512,512]{1,0:T(8,128)(2,1)S(1)}, u32[]{:S(2)}, u32[]{:S(2)}) %collective-permute-start.6) | collective-permute-done | bytes 524320 | tf_op jit(solution)/shard_map/ppermute | solution.py:29
  41.6 4.2 %collective-permute-start.8 = (bf16[512,512]{1,0:T(8,128)(2,1)S(1)}, bf16[512,512]{1,0:T(8,128)(2,1)}, u32[]{:S(2)}, u32[]{:S(2)}) collective-permute-start(bf16[512,512]{1,0:T(8,128)(2,1)S(1)} %collective-permute-done.6.refs_2_), channel_id=1, source_target_pairs={{0,7},{1,0},{2,1},{3,2},{4,3},{5,4},{6,5},{7,6},{8,15},{9,8},{10,9... | collective-permute-start | bytes 1572872 | tf_op jit(solution)/shard_map/ppermute | solution.py:29
  45.9 12.0 %collective-permute-done.8.refs_4_ = bf16[512,512]{1,0:T(8,128)(2,1)} collective-permute-done((bf16[512,512]{1,0:T(8,128)(2,1)S(1)}, bf16[512,512]{1,0:T(8,128)(2,1)}, u32[]{:S(2)}, u32[]{:S(2)}) %collective-permute-start.8) | collective-permute-done | bytes 524320 | tf_op jit(solution)/shard_map/ppermute | solution.py:29
  57.9 2.7 %collective-permute-start = (bf16[2048,512]{1,0:T(8,128)(2,1)S(1)}, bf16[2048,512]{1,0:T(8,128)(2,1)}, u32[]{:S(2)}, u32[]{:S(2)}) collective-permute-start(bf16[2048,512]{1,0:T(8,128)(2,1)S(1)} %copy-done.1), channel_id=1, source_target_pairs={{0,32},{32,0},{64,96},{96,64},{128,160},{160,128},{192,224},{224,1... | collective-permute-start | bytes 6291464 | tf_op jit(solution)/shard_map/ppermute | solution.py:42
  60.6 15.7 %collective-permute-done.5.refs_1_ = bf16[512,512]{1,0:T(8,128)(2,1)S(1)} collective-permute-done((bf16[512,512]{1,0:T(8,128)(2,1)S(1)}, bf16[512,512]{1,0:T(8,128)(2,1)S(1)}, u32[]{:S(2)}, u32[]{:S(2)}) %collective-permute-start.5) | collective-permute-done | bytes 524320 | tf_op jit(solution)/shard_map/ppermute | solution.py:29
  77.1 13.3 %collective-permute-done.7.refs_3_ = bf16[512,512]{1,0:T(8,128)(2,1)} collective-permute-done((bf16[512,512]{1,0:T(8,128)(2,1)S(1)}, bf16[512,512]{1,0:T(8,128)(2,1)}, u32[]{:S(2)}, u32[]{:S(2)}) %collective-permute-start.7) | collective-permute-done | bytes 524320 | tf_op jit(solution)/shard_map/ppermute | solution.py:29
  90.4 2.5 %collective-permute-start.15 = (bf16[1024,512]{1,0:T(8,128)(2,1)}, bf16[1024,512]{1,0:T(8,128)(2,1)S(1)}, u32[]{:S(2)}, u32[]{:S(2)}) collective-permute-start(bf16[1024,512]{1,0:T(8,128)(2,1)} %bitcast.11), channel_id=1, source_target_pairs={{0,8},{1,9},{2,10},{3,11},{4,12},{5,13},{6,14},{7,15},{8,16},{9,17... | collective-permute-start | bytes 3145736 | tf_op jit(solution)/shard_map/ppermute | solution.py:24
  94.2 2.5 %collective-permute-start.10 = (bf16[512,512]{1,0:T(8,128)(2,1)}, bf16[512,512]{1,0:T(8,128)(2,1)S(1)}, u32[]{:S(2)}, u32[]{:S(2)}) collective-permute-start(bf16[512,512]{1,0:T(8,128)(2,1)} %collective-permute-done.8.refs_4_), channel_id=1, source_target_pairs={{0,7},{1,0},{2,1},{3,2},{4,3},{5,4},{6,5},{7,6},{8,15},{9,8},{10,9... | collective-permute-start | bytes 1572872 | tf_op jit(solution)/shard_map/ppermute | solution.py:29
  96.8 7.1 %collective-permute-done.9.refs_5_ = bf16[512,512]{1,0:T(8,128)(2,1)} collective-permute-done((bf16[512,512]{1,0:T(8,128)(2,1)}, bf16[512,512]{1,0:T(8,128)(2,1)}, u32[]{:S(2)}, u32[]{:S(2)}) %collective-permute-start.9) | collective-permute-done | bytes 524320 | tf_op jit(solution)/shard_map/ppermute | solution.py:29
  103.8 5.1 %prepare_adjoint.1 = (bf16[8,512,512]{2,1,0:T(8,128)(2,1)S(1)}, bf16[8,512,512]{2,1,0:T(8,128)(2,1)S(1)}) custom-call(s32[4]{0:T(128)S(1)} %pad_add_fusion.pos, s32[64,64]{1,0:T(8,128)S(1)} %copy-done.7, bf16[2048,512]{1,0:T(8,128)(2,1)S(1)} %copy-done.1, bf16[2048,512]{1,0:T(8,128)(2,1)} %collective-permute-done.other), custom_call_target="tpu_custom_call" | custom-call | tf_op jit(solution)/shard_map/prepare_adjoint/pallas_call | solution.py:123
  109.0 7.2 %collective-permute-done.11.refs_7_ = bf16[512,512]{1,0:T(8,128)(2,1)S(1)} collective-permute-done((bf16[512,512]{1,0:T(8,128)(2,1)}, bf16[512,512]{1,0:T(8,128)(2,1)S(1)}, u32[]{:S(2)}, u32[]{:S(2)}) %collective-permute-start.11) | collective-permute-done | bytes 524320 | tf_op jit(solution)/shard_map/ppermute | solution.py:29
  116.2 4.5 %masked_product.2 = (f32[512,128]{1,0:T(8,128)S(1)}, f32[512,128]{1,0:T(8,128)S(1)}, f32[512,128]{1,0:T(8,128)S(1)}, f32[512,128]{1,0:T(8,128)S(1)}) custom-call(s32[4]{0:T(128)S(1)} %pad_add_fusion.pos, bf16[8,512,512]{2,1,0:T(8,128)(2,1)S(1)} %get-tuple-element.20.adjoint, bf16[512,512]{1,0:T(8,128)(2,1)S(1)} %pad_maximum_fusion.refs_0_, ...), custom_call_target="tpu_custom_call" | custom-call | tf_op jit(solution)/shard_map/masked_product/pallas_call | solution.py:163
  120.7 3.1 %collective-permute-start.13 = (f32[512,128]{1,0:T(8,128)S(1)}, f32[512,128]{1,0:T(8,128)S(1)}, u32[]{:S(2)}, u32[]{:S(2)}) collective-permute-start(f32[512,128]{1,0:T(8,128)S(1)} %get-tuple-element.25), channel_id=1, source_target_pairs={{0,128},{32,160},{64,192},{96,224},{128,0},{160,32},{192,64},{224,... | collective-permute-start | bytes 786440 | tf_op jit(solution)/shard_map/ppermute | solution.py:34
  125.4 2.3 %collective-permute-start.17 = (bf16[512,512]{1,0:T(8,128)(2,1)S(1)}, bf16[512,512]{1,0:T(8,128)(2,1)S(1)}, u32[]{:S(2)}, u32[]{:S(2)}) collective-permute-start(bf16[512,512]{1,0:T(8,128)(2,1)S(1)} %slice.18), channel_id=1, source_target_pairs={{0,8},{1,9},{2,10},{3,11},{4,12},{5,13},{6,14},{7,15},{8,16},{9,17... | collective-permute-start | bytes 1572872 | tf_op jit(solution)/shard_map/ppermute | solution.py:24
  129.1 5.0 %collective-permute-done.14 = f32[512,128]{1,0:T(8,128)S(1)} collective-permute-done((f32[512,128]{1,0:T(8,128)S(1)}, f32[512,128]{1,0:T(8,128)S(1)}, u32[]{:S(2)}, u32[]{:S(2)}) %collective-permute-start.14) | collective-permute-done | bytes 262176 | tf_op jit(solution)/shard_map/ppermute | solution.py:34
  135.3 3.1 %collective-permute-start.24 = (bf16[512,128]{1,0:T(8,128)(2,1)S(1)}, bf16[512,128]{1,0:T(8,128)(2,1)S(1)}, u32[]{:S(2)}, u32[]{:S(2)}) collective-permute-start(bf16[512,128]{1,0:T(8,128)(2,1)S(1)} %get-tuple-element.38), channel_id=1, source_target_pairs={{0,192},{32,224},{64,0},{96,32},{128,64},{160,96},{192,128},{224,1... | collective-permute-start | bytes 393224 | tf_op jit(solution)/shard_map/ppermute | solution.py:34
  139.2 2.8 %collective-permute-done.24 = bf16[512,128]{1,0:T(8,128)(2,1)S(1)} collective-permute-done((bf16[512,128]{1,0:T(8,128)(2,1)S(1)}, bf16[512,128]{1,0:T(8,128)(2,1)S(1)}, u32[]{:S(2)}, u32[]{:S(2)}) %collective-permute-start.24) | collective-permute-done | bytes 131104 | tf_op jit(solution)/shard_map/ppermute | solution.py:34
  145.1 3.7 %collective-permute-start.25 = (bf16[4,512,128]{2,1,0:T(8,128)(2,1)S(1)}, bf16[4,512,128]{2,1,0:T(8,128)(2,1)S(1)}, u32[]{:S(2)}, u32[]{:S(2)}) collective-permute-start(bf16[4,512,128]{2,1,0:T(8,128)(2,1)S(1)} %pad_maximum_fusion.1.mine), channel_id=1, source_target_pairs={{0,32},{32,0},{64,96},{96,64},{128,160},{160,128},{192,224},{224,1... | collective-permute-start | bytes 1572872 | tf_op jit(solution)/shard_map/ppermute | solution.py:42
  154.5 4.6 %masked_product.3 = (f32[512,128]{1,0:T(8,128)S(1)}, bf16[512,128]{1,0:T(8,128)(2,1)S(1)}, bf16[512,128]{1,0:T(8,128)(2,1)S(1)}, bf16[512,128]{1,0:T(8,128)(2,1)S(1)}) custom-call(s32[4]{0:T(128)S(1)} %pad_add_fusion.pos, bf16[8,512,512]{2,1,0:T(8,128)(2,1)S(1)} %get-tuple-element.27.adjoint, bf16[1024,512]{1,0:T(8,128)(2,1)S(1)} %bitcast.14, ...), custom_call_target="tpu_custom_call" | custom-call | tf_op jit(solution)/shard_map/masked_product/pallas_call | solution.py:163
  159.3 3.7 %collective-permute-done.27.two = bf16[1024,128]{1,0:T(8,128)(2,1)S(1)} collective-permute-done((bf16[1024,128]{1,0:T(8,128)(2,1)S(1)}, bf16[1024,128]{1,0:T(8,128)(2,1)S(1)}, u32[]{:S(2)}, u32[]{:S(2)}) %collective-permute-start.27) | collective-permute-done | bytes 262176 | tf_op jit(solution)/shard_map/ppermute | solution.py:38
  (75 shorter events, 30.5 us)
Async XLA Ops:
  7.2 83.2 %all-gather.6.cloned.1.call-start = ((), (), s32[]{:S(2)}) async-start(), calls=%async_computation.1 | async-start | bytes 1179648 | tf_op jit(solution)/shard_map/all_gather | solution.py:59
  14.9 148.2 %all-gather.4.cloned.1.call-start = ((), (), s32[]{:S(2)}) async-start(), calls=%async_computation | async-start | bytes 2359296 | tf_op jit(solution)/shard_map/all_gather | solution.py:272
  16.9 7.4 %collective-permute-start.2 = (bf16[128,512]{1,0:T(8,128)(2,1)S(1)}, bf16[128,512]{1,0:T(8,128)(2,1)S(1)}, u32[]{:S(2)}, u32[]{:S(2)}) collective-permute-start(bf16[128,512]{1,0:T(8,128)(2,1)S(1)} %get-tuple-element.41), channel_id=1, source_target_pairs={{0,8},{1,9},{2,10},{3,11},{4,12},{5,13},{6,14},{7,15},{8,16},{9,17... | collective-permute-start | bytes 393224 | tf_op jit(solution)/shard_map/ppermute | solution.py:24
  24.4 17.2 %collective-permute-start.6 = (bf16[512,512]{1,0:T(8,128)(2,1)S(1)}, bf16[512,512]{1,0:T(8,128)(2,1)S(1)}, u32[]{:S(2)}, u32[]{:S(2)}) collective-permute-start(bf16[512,512]{1,0:T(8,128)(2,1)S(1)} %pad_maximum_fusion.refs_0_), channel_id=1, source_target_pairs={{0,7},{1,0},{2,1},{3,2},{4,3},{5,4},{6,5},{7,6},{8,15},{9,8},{10,9... | collective-permute-start | bytes 1572872 | tf_op jit(solution)/shard_map/ppermute | solution.py:29
  41.6 16.2 %collective-permute-start.8 = (bf16[512,512]{1,0:T(8,128)(2,1)S(1)}, bf16[512,512]{1,0:T(8,128)(2,1)}, u32[]{:S(2)}, u32[]{:S(2)}) collective-permute-start(bf16[512,512]{1,0:T(8,128)(2,1)S(1)} %collective-permute-done.6.refs_2_), channel_id=1, source_target_pairs={{0,7},{1,0},{2,1},{3,2},{4,3},{5,4},{6,5},{7,6},{8,15},{9,8},{10,9... | collective-permute-start | bytes 1572872 | tf_op jit(solution)/shard_map/ppermute | solution.py:29
  57.9 45.9 %collective-permute-start = (bf16[2048,512]{1,0:T(8,128)(2,1)S(1)}, bf16[2048,512]{1,0:T(8,128)(2,1)}, u32[]{:S(2)}, u32[]{:S(2)}) collective-permute-start(bf16[2048,512]{1,0:T(8,128)(2,1)S(1)} %copy-done.1), channel_id=1, source_target_pairs={{0,32},{32,0},{64,96},{96,64},{128,160},{160,128},{192,224},{224,1... | collective-permute-start | bytes 6291464 | tf_op jit(solution)/shard_map/ppermute | solution.py:42
  60.6 15.7 %collective-permute-start.5 = (bf16[512,512]{1,0:T(8,128)(2,1)S(1)}, bf16[512,512]{1,0:T(8,128)(2,1)S(1)}, u32[]{:S(2)}, u32[]{:S(2)}) collective-permute-start(bf16[512,512]{1,0:T(8,128)(2,1)S(1)} %pad_maximum_fusion.refs_0_), channel_id=1, source_target_pairs={{0,1},{1,2},{2,3},{3,4},{4,5},{5,6},{6,7},{7,0},{8,9},{9,10},{10,1... | collective-permute-start | bytes 1572872 | tf_op jit(solution)/shard_map/ppermute | solution.py:29
  76.3 14.1 %collective-permute-start.7 = (bf16[512,512]{1,0:T(8,128)(2,1)S(1)}, bf16[512,512]{1,0:T(8,128)(2,1)}, u32[]{:S(2)}, u32[]{:S(2)}) collective-permute-start(bf16[512,512]{1,0:T(8,128)(2,1)S(1)} %collective-permute-done.5.refs_1_), channel_id=1, source_target_pairs={{0,1},{1,2},{2,3},{3,4},{4,5},{5,6},{6,7},{7,0},{8,9},{9,10},{10,1... | collective-permute-start | bytes 1572872 | tf_op jit(solution)/shard_map/ppermute | solution.py:29
  90.4 13.4 %collective-permute-start.9 = (bf16[512,512]{1,0:T(8,128)(2,1)}, bf16[512,512]{1,0:T(8,128)(2,1)}, u32[]{:S(2)}, u32[]{:S(2)}) collective-permute-start(bf16[512,512]{1,0:T(8,128)(2,1)} %collective-permute-done.7.refs_3_), channel_id=1, source_target_pairs={{0,1},{1,2},{2,3},{3,4},{4,5},{5,6},{6,7},{7,0},{8,9},{9,10},{10,1... | collective-permute-start | bytes 1572872 | tf_op jit(solution)/shard_map/ppermute | solution.py:29
  90.4 34.9 %collective-permute-start.15 = (bf16[1024,512]{1,0:T(8,128)(2,1)}, bf16[1024,512]{1,0:T(8,128)(2,1)S(1)}, u32[]{:S(2)}, u32[]{:S(2)}) collective-permute-start(bf16[1024,512]{1,0:T(8,128)(2,1)} %bitcast.11), channel_id=1, source_target_pairs={{0,8},{1,9},{2,10},{3,11},{4,12},{5,13},{6,14},{7,15},{8,16},{9,17... | collective-permute-start | bytes 3145736 | tf_op jit(solution)/shard_map/ppermute | solution.py:24
  92.9 34.9 %collective-permute-start.16 = (bf16[1024,512]{1,0:T(8,128)(2,1)}, bf16[1024,512]{1,0:T(8,128)(2,1)S(1)}, u32[]{:S(2)}, u32[]{:S(2)}) collective-permute-start(bf16[1024,512]{1,0:T(8,128)(2,1)} %bitcast.12), channel_id=1, source_target_pairs={{0,24},{1,25},{2,26},{3,27},{4,28},{5,29},{6,30},{7,31},{8,0},{9,1... | collective-permute-start | bytes 3145736 | tf_op jit(solution)/shard_map/ppermute | solution.py:24
  94.2 14.7 %collective-permute-start.10 = (bf16[512,512]{1,0:T(8,128)(2,1)}, bf16[512,512]{1,0:T(8,128)(2,1)S(1)}, u32[]{:S(2)}, u32[]{:S(2)}) collective-permute-start(bf16[512,512]{1,0:T(8,128)(2,1)} %collective-permute-done.8.refs_4_), channel_id=1, source_target_pairs={{0,7},{1,0},{2,1},{3,2},{4,3},{5,4},{6,5},{7,6},{8,15},{9,8},{10,9... | collective-permute-start | bytes 1572872 | tf_op jit(solution)/shard_map/ppermute | solution.py:29
  103.8 12.4 %collective-permute-start.11 = (bf16[512,512]{1,0:T(8,128)(2,1)}, bf16[512,512]{1,0:T(8,128)(2,1)S(1)}, u32[]{:S(2)}, u32[]{:S(2)}) collective-permute-start(bf16[512,512]{1,0:T(8,128)(2,1)} %collective-permute-done.9.refs_5_), channel_id=1, source_target_pairs={{0,1},{1,2},{2,3},{3,4},{4,5},{5,6},{6,7},{7,0},{8,9},{9,10},{10,1... | collective-permute-start | bytes 1572872 | tf_op jit(solution)/shard_map/ppermute | solution.py:29
  120.7 8.4 %collective-permute-start.13 = (f32[512,128]{1,0:T(8,128)S(1)}, f32[512,128]{1,0:T(8,128)S(1)}, u32[]{:S(2)}, u32[]{:S(2)}) collective-permute-start(f32[512,128]{1,0:T(8,128)S(1)} %get-tuple-element.25), channel_id=1, source_target_pairs={{0,128},{32,160},{64,192},{96,224},{128,0},{160,32},{192,64},{224,... | collective-permute-start | bytes 786440 | tf_op jit(solution)/shard_map/ppermute | solution.py:34
  123.9 10.2 %collective-permute-start.14 = (f32[512,128]{1,0:T(8,128)S(1)}, f32[512,128]{1,0:T(8,128)S(1)}, u32[]{:S(2)}, u32[]{:S(2)}) collective-permute-start(f32[512,128]{1,0:T(8,128)S(1)} %get-tuple-element.26), channel_id=1, source_target_pairs={{0,192},{32,224},{64,0},{96,32},{128,64},{160,96},{192,128},{224,1... | collective-permute-start | bytes 786440 | tf_op jit(solution)/shard_map/ppermute | solution.py:34
  124.6 10.0 %collective-permute-start.12 = (f32[512,128]{1,0:T(8,128)S(1)}, f32[512,128]{1,0:T(8,128)S(1)}, u32[]{:S(2)}, u32[]{:S(2)}) collective-permute-start(f32[512,128]{1,0:T(8,128)S(1)} %get-tuple-element.24), channel_id=1, source_target_pairs={{0,64},{32,96},{64,128},{96,160},{128,192},{160,224},{192,0},{224,... | collective-permute-start | bytes 786440 | tf_op jit(solution)/shard_map/ppermute | solution.py:34
  125.4 23.5 %collective-permute-start.17 = (bf16[512,512]{1,0:T(8,128)(2,1)S(1)}, bf16[512,512]{1,0:T(8,128)(2,1)S(1)}, u32[]{:S(2)}, u32[]{:S(2)}) collective-permute-start(bf16[512,512]{1,0:T(8,128)(2,1)S(1)} %slice.18), channel_id=1, source_target_pairs={{0,8},{1,9},{2,10},{3,11},{4,12},{5,13},{6,14},{7,15},{8,16},{9,17... | collective-permute-start | bytes 1572872 | tf_op jit(solution)/shard_map/ppermute | solution.py:24
  127.8 21.1 %collective-permute-start.18 = (bf16[512,512]{1,0:T(8,128)(2,1)S(1)}, bf16[512,512]{1,0:T(8,128)(2,1)S(1)}, u32[]{:S(2)}, u32[]{:S(2)}) collective-permute-start(bf16[512,512]{1,0:T(8,128)(2,1)S(1)} %slice.19), channel_id=1, source_target_pairs={{0,24},{1,25},{2,26},{3,27},{4,28},{5,29},{6,30},{7,31},{8,0},{9,1... | collective-permute-start | bytes 1572872 | tf_op jit(solution)/shard_map/ppermute | solution.py:24
  145.1 20.8 %collective-permute-start.25 = (bf16[4,512,128]{2,1,0:T(8,128)(2,1)S(1)}, bf16[4,512,128]{2,1,0:T(8,128)(2,1)S(1)}, u32[]{:S(2)}, u32[]{:S(2)}) collective-permute-start(bf16[4,512,128]{2,1,0:T(8,128)(2,1)S(1)} %pad_maximum_fusion.1.mine), channel_id=1, source_target_pairs={{0,32},{32,0},{64,96},{96,64},{128,160},{160,128},{192,224},{224,1... | collective-permute-start | bytes 1572872 | tf_op jit(solution)/shard_map/ppermute | solution.py:42
  150.2 9.0 %collective-permute-start.26 = (bf16[1024,128]{1,0:T(8,128)(2,1)S(1)}, bf16[1024,128]{1,0:T(8,128)(2,1)S(1)}, u32[]{:S(2)}, u32[]{:S(2)}) collective-permute-start(bf16[1024,128]{1,0:T(8,128)(2,1)S(1)} %get-tuple-element.35), channel_id=1, source_target_pairs={{0,64},{32,96},{1,65},{33,97},{2,66},{34,98},{3,67},{35,99},{4,68}... | collective-permute-start | bytes 786440 | tf_op jit(solution)/shard_map/ppermute | solution.py:38
  151.6 11.5 %collective-permute-start.27 = (bf16[1024,128]{1,0:T(8,128)(2,1)S(1)}, bf16[1024,128]{1,0:T(8,128)(2,1)S(1)}, u32[]{:S(2)}, u32[]{:S(2)}) collective-permute-start(bf16[1024,128]{1,0:T(8,128)(2,1)S(1)} %get-tuple-element.36), channel_id=1, source_target_pairs={{0,128},{32,160},{1,129},{33,161},{2,130},{34,162},{3,131},{35,163... | collective-permute-start | bytes 786440 | tf_op jit(solution)/shard_map/ppermute | solution.py:38
  153.2 9.9 %collective-permute-start.28 = (bf16[1024,128]{1,0:T(8,128)(2,1)S(1)}, bf16[1024,128]{1,0:T(8,128)(2,1)S(1)}, u32[]{:S(2)}, u32[]{:S(2)}) collective-permute-start(bf16[1024,128]{1,0:T(8,128)(2,1)S(1)} %get-tuple-element.37), channel_id=1, source_target_pairs={{0,192},{32,224},{1,193},{33,225},{2,194},{34,226},{3,195},{35,227... | collective-permute-start | bytes 786440 | tf_op jit(solution)/shard_map/ppermute | solution.py:38
  159.1 8.4 %collective-permute-start.21 = (bf16[512,128]{1,0:T(8,128)(2,1)S(1)}, bf16[512,128]{1,0:T(8,128)(2,1)S(1)}, u32[]{:S(2)}, u32[]{:S(2)}) collective-permute-start(bf16[512,128]{1,0:T(8,128)(2,1)S(1)} %get-tuple-element.32), channel_id=1, source_target_pairs={{0,192},{32,224},{64,0},{96,32},{128,64},{160,96},{192,128},{224,1... | collective-permute-start | bytes 393224 | tf_op jit(solution)/shard_map/ppermute | solution.py:34
  159.2 8.3 %collective-permute-start.20 = (bf16[512,128]{1,0:T(8,128)(2,1)S(1)}, bf16[512,128]{1,0:T(8,128)(2,1)S(1)}, u32[]{:S(2)}, u32[]{:S(2)}) collective-permute-start(bf16[512,128]{1,0:T(8,128)(2,1)S(1)} %get-tuple-element.31), channel_id=1, source_target_pairs={{0,128},{32,160},{64,192},{96,224},{128,0},{160,32},{192,64},{224,... | collective-permute-start | bytes 393224 | tf_op jit(solution)/shard_map/ppermute | solution.py:34
  (16 other events, 253.8 us)
Sparse Core Ops, SparseCore 0:
  15.0 38.0 all-gather.5
  58.0 32.0 all-gather.3

commit v3 on v2

--- a/solution.py
+++ b/solution.py
@@ -9,6 +9,8 @@
 
 BLK = 256
 NX, NZ, NY = 4, 8, 4
+SAME_CORE = [[2 * y + k for y in range(NY)] for k in range(2)]
+SAME_X = [[x * NZ + z for z in range(NZ)] for x in range(NX)]
 SUB = 64
 PAIR = 2 * SUB
 HALF = 512
@@ -16,7 +18,8 @@
 VMEM = pl.BlockSpec(memory_space=pltpu.VMEM)
 SMEM = pl.BlockSpec(memory_space=pltpu.SMEM)
 ANY = pl.BlockSpec(memory_space=pl.ANY)
-BIG = pltpu.CompilerParams(vmem_limit_bytes=40 * 2**20)
+BIG = pltpu.CompilerParams(vmem_limit_bytes=24 * 2**20)
+SMALL = pltpu.CompilerParams(vmem_limit_bytes=12 * 2**20)
 
 
 def x_shift(value, dx):
@@ -42,24 +45,12 @@
     return lax.ppermute(value, "row", [(r, r ^ 1) for r in range(2 * NY)])
 
 
-def gather_xz(part):
-    block = jnp.concatenate([part] + [x_shift(part, d) for d in (1, -1, 2)], axis=0)
-    down1, up1 = z_shift(block, 1), z_shift(block, -1)
-    down2, up2 = z_shift(down1, 1), z_shift(up1, -1)
-    down3, up3 = z_shift(down2, 1), z_shift(up2, -1)
-    return [block, down1, up1, down2, up2, down3, up3, z_shift(down3, 1)]
-
-
-def after(value, *others):
-    return lax.optimization_barrier((value,) + others)[0]
-
-
-def gather_zx(part, earlier):
-    same_x = [[x * NZ + z for z in range(NZ)] for x in range(NX)]
-    block = lax.all_gather(part, "col", axis_index_groups=same_x, axis=0, tiled=True)
-    block = after(block, earlier)
-    down, up = x_shift(block, 1), x_shift(block, -1)
-    return [block, down, up, x_shift(down[:HALF], 1), x_shift(up[HALF:], -1)]
+def together(*values):
+    return lax.optimization_barrier(values)
+
+
+def y_exchange(value):
+    return lax.all_to_all(value, "row", 0, 0, axis_index_groups=SAME_CORE, tiled=True)
 
 
 def offset(n):
@@ -91,7 +82,7 @@
         out_shape=(jax.ShapeDtypeStruct((2, SUB, HALF), BF16),) * 2,
         in_specs=[SMEM, VMEM, VMEM],
         out_specs=(VMEM, VMEM),
-        compiler_params=BIG,
+        compiler_params=SMALL,
         name="pack_columns",
     )(pos, two, one)
 
@@ -132,47 +123,60 @@
 
 
 def windows(refs):
-    if len(refs) == 8:
-        return list(refs)
-    halves = [ref.at[pl.ds(h * HALF, HALF)] for ref in refs[:3] for h in range(2)]
-    return halves + list(refs[3:])
-
-
-def product_kernel(count, pos, adjoint, *refs):
-    panels, outs, held, total, sems = refs[:count], refs[count:count + 4], refs[-3], refs[-2], refs[-1]
-    copies = [
-        pltpu.make_async_copy(ref, held.at[b], sems.at[b]) for b, ref in enumerate(windows(panels))
-    ]
+    return [ref.at[pl.ds(h * HALF, HALF)] for ref in refs for h in range(ref.shape[0] // HALF)]
+
+
+def product_kernel(count, first_block, scale, pos, adjoint, *refs):
+    panels = refs[:count]
+    held, sems = refs[-2], refs[-1]
+    total = refs[-3]
+    copies, rows = [], 0
+    for n, ref in enumerate(panels):
+        size = ref.shape[0]
+        copies.append(pltpu.make_async_copy(ref, held.at[pl.ds(rows, size)], sems.at[n]))
+        rows += size
     for copy in copies:
         copy.start()
-    total[...] = jnp.zeros_like(total)
+    if first_block == 0:
+        total[...] = jnp.zeros_like(total)
+    else:
+        total[...] = refs[count][...]
+    for copy in copies:
+        copy.wait()
 
     def block(b, carry):
-        pltpu.make_async_copy(held.at[b], held.at[b], sems.at[b]).wait()
-        total[...] += jnp.dot(adjoint[b], held[b], preferred_element_type=F32)
+        at = pl.multiple_of(b * HALF, HALF)
+        total[...] += jnp.dot(
+            adjoint[first_block + b], held[pl.ds(at, HALF), :], preferred_element_type=F32)
         return carry
 
-    lax.fori_loop(0, 8, block, 0)
-    for d, out in enumerate(outs):
-        column = pl.multiple_of((pos[2] + d) % NY * 128, 128)
-        out[...] = (-2.0 * total[:, pl.ds(column, 128)]).astype(out.dtype)
-
-
-def product(pos, adjoint, panels, kind):
+    lax.fori_loop(0, rows // HALF, block, 0)
+    if scale is not None:
+        out = refs[count + 1]
+        for t in range(NY):
+            out[t] = (scale * total[:, t * 128:(t + 1) * 128]).astype(out.dtype)
+
+
+def product(pos, adjoint, panels, first_block, before=None, kind=None):
     count = len(panels)
-    return pl.pallas_call(
-        functools.partial(product_kernel, count),
-        out_shape=(jax.ShapeDtypeStruct((512, 128), F32),) + (jax.ShapeDtypeStruct((512, 128), kind),) * 3,
-        in_specs=[SMEM, VMEM] + [ANY] * count,
-        out_specs=(VMEM,) * 4,
-        scratch_shapes=[
-            pltpu.VMEM((8, 512, HALF), BF16),
-            pltpu.VMEM((512, HALF), F32),
-            pltpu.SemaphoreType.DMA((8,)),
-        ],
-        compiler_params=BIG,
+    rows = sum(panel.shape[0] for panel in panels)
+    last = kind is not None
+    scratch = [pltpu.VMEM((rows, HALF), BF16), pltpu.SemaphoreType.DMA((count,))]
+    if last:
+        scratch = [pltpu.VMEM((512, HALF), F32)] + scratch
+        shape = jax.ShapeDtypeStruct((NY, 512, 128), kind)
+    else:
+        shape = jax.ShapeDtypeStruct((512, HALF), F32)
+    extra = [] if before is None else [before]
+    return pl.pallas_call(
+        functools.partial(product_kernel, count, first_block, -2.0 if last else None),
+        out_shape=shape,
+        in_specs=[SMEM, VMEM] + [ANY] * count + [VMEM] * len(extra),
+        out_specs=VMEM,
+        scratch_shapes=scratch,
+        compiler_params=SMALL,
         name="masked_product",
-    )(pos, adjoint, *panels)
+    )(pos, adjoint, *panels, *extra)
 
 
 def diagonal_kernel(pos, block, down, up, far_low, far_high, own, one, two, three, held, sems):
@@ -207,7 +211,7 @@
         in_specs=[SMEM] + [ANY] * 5,
         out_specs=(VMEM,) * 4,
         scratch_shapes=[pltpu.VMEM((8, 512, HALF), BF16), pltpu.SemaphoreType.DMA((8,))],
-        compiler_params=BIG,
+        compiler_params=SMALL,
         name="diagonal_columns",
     )(pos, *panels)
 
@@ -227,7 +231,7 @@
         out_shape=jax.ShapeDtypeStruct((1024, 256), BF16),
         in_specs=[SMEM] + [VMEM] * 5,
         out_specs=VMEM,
-        compiler_params=BIG,
+        compiler_params=SMALL,
         name="inverse_times_diagonal",
     )(pos, inverse, *parts)
 
@@ -236,9 +240,8 @@
     first = pos[3] == 0
     total[...] = jnp.zeros_like(total)
 
-    def block(d, carry):
-        y = (pos[2] - d + NY) % NY
-        a, b = mine[d], other[d]
+    def block(y, carry):
+        a, b = mine[y], other[y]
         pair = jnp.concatenate([jnp.where(first, a, b), jnp.where(first, b, a)], axis=1)
         rows = pl.multiple_of(y * 256, 256)
         total[...] += jnp.dot(pair, factors[pl.ds(rows, 256), :], preferred_element_type=F32)
@@ -255,7 +258,7 @@
         in_specs=[SMEM] + [VMEM] * 3,
         out_specs=VMEM,
         scratch_shapes=[pltpu.VMEM((512, 256), F32)],
-        compiler_params=BIG,
+        compiler_params=SMALL,
         name="carried_term",
     )(pos, mine, other, factors)
 
@@ -266,25 +269,36 @@
 
     own, give = pack(pos, panel_two, panel_one)
     taken = core_swap(give)
-    shards = jnp.concatenate([own, taken], axis=1)
-    two = gather_xz(shards[0])
-    one = gather_zx(shards[1], two[4])
-    inverse = lax.all_gather(after(inverse_factor, two[4]), "row", axis=0, tiled=True)
-    masked_two, masked_one = prepare(pos, taper, adjoint, core_swap(adjoint))
-
-    mine, *sent = product(pos, masked_two, two, F32)
-    r1, r2, r3 = [y_shift(part, d + 1) for d, part in enumerate(sent)]
-    second_grad = incoming + ((mine + r1) + (r2 + r3))
+    shard_two = jnp.concatenate([own[0], taken[0]], axis=0)
+    shard_one = jnp.concatenate([own[1], taken[1]], axis=0)
+
+    block = jnp.concatenate([shard_two] + [x_shift(shard_two, d) for d in (1, -1, 2)], axis=0)
+    one = lax.all_gather(shard_one, "col", axis_index_groups=SAME_X, axis=0, tiled=True)
+    down1, up1, swapped = together(z_shift(block, 1), z_shift(block, -1), core_swap(adjoint))
+    for_two, for_one = prepare(pos, taper, adjoint, swapped)
+    down2, up2, for_two, for_one = together(z_shift(down1, 1), z_shift(up1, -1), for_two, for_one)
+    sum_two = product(pos, for_two, [block, down1, up1, down2, up2], 0)
+    one, down2, up2 = together(one, down2, up2)
+    down3, up3, sum_two = together(z_shift(down2, 1), z_shift(up2, -1), sum_two)
+    far = [z_shift(down3[:256], 1), z_shift(up3[256:], -1)]
+    sum_two = product(pos, for_two, [down3, up3], 5, sum_two)
+
+    down, up = x_shift(one, 1), x_shift(one, -1)
+    inverse = lax.all_gather(together(inverse_factor, up2)[0], "row", axis=0, tiled=True)
+    far_one = [x_shift(down[:HALF], 1), x_shift(up[HALF:], -1)]
+    sum_one = product(pos, for_one, [one, down, up], 0)
+
+    sums = product(pos, for_two, far, 7, sum_two, F32)
+    second_grad = incoming + jnp.sum(y_exchange(sums), axis=0)
     rounded = second_grad.astype(BF16)
-    column = jnp.stack([rounded, y_shift(rounded, 1), y_shift(rounded, 2), y_shift(rounded, 3)])
+    column = y_exchange(jnp.broadcast_to(rounded, (NY, 512, 128)))
     other = core_swap(column)
 
-    mine, *sent = product(pos, masked_one, one, BF16)
-    r1, r2, r3 = [y_shift(part, d + 1) for d, part in enumerate(sent)]
-    first, *rest = diagonal(pos, one)
+    first, *rest = diagonal(pos, [one, down, up] + far_one)
     factors = factor(pos, inverse, [first] + [y_first(part, d + 1) for d, part in enumerate(rest)])
+    sums = product(pos, for_one, far_one, 6, sum_one, BF16)
     term = carried(pos, column, other, factors)
-    first_grad = ((mine + r1.astype(F32)) + (r2.astype(F32) + r3.astype(F32))) - term
+    first_grad = jnp.sum(y_exchange(sums).astype(F32), axis=0) - term
     return second_grad, first_grad
 
 

time: 178 us -> 162 us (0.910)
  waiting for transfers between devices: 92.8 us -> 44.4 us
  local copies, waits for them, and re-layouts: 5.11 us -> 19.3 us
  starting transfers between devices: 43.3 us -> 51.8 us
  Pallas kernels: 19 us -> 25 us
  other arithmetic: 1.73 us -> 5.63 us
    ppermute x7 -> x8, waiting for transfers between devices: 68.8 us -> 24.2 us  [z_shift(): return lax.ppermute(value, 'col', pairs)]
    all_to_all x0 -> x3, starting transfers between devices: none -> 13 us  [y_exchange(): lax.all_to_all(value, 'row', 0, 0, axis_index_groups=SAME_CORE, tiled=True)]
    ppermute x9 -> x0, waiting for transfers between devices: 12.5 us -> none  [y_shift(): return lax.ppermute(value, 'row', pairs)]
    unnamed x19 -> x38, local copies, waits for them, and re-layouts: 4.36 us -> 16.5 us
    ppermute x9 -> x0, starting transfers between devices: 8.64 us -> none  [y_shift(): return lax.ppermute(value, 'row', pairs)]
    all_to_all x0 -> x3, waiting for transfers between devices: none -> 6.63 us  [y_exchange(): lax.all_to_all(value, 'row', 0, 0, axis_index_groups=SAME_CORE, tiled=True)]
    pallas_call x2 -> x5, Pallas kernels: 9.14 us -> 12.9 us  [product(): pl.pallas_call(functools.partial(product_kernel, count, first_block, -2.0...]
    ppermute x7 -> x8, starting transfers between devices: 10.6 us -> 14.2 us  [z_shift(): return lax.ppermute(value, 'col', pairs)]
  transfers between devices with their start and end apart: 31 -> 26, of which waited for: 17 -> 11; matrix products, arithmetic and copies ran while one was open for 1% -> 5% of each run, Pallas kernels for 10% -> 14%
where the time goes in v3:
time: 162 us; the launch traced here: 160 us
  starting transfers between devices  51.8 us (32%)
  waiting for transfers between devices  44.4 us (27%)
  Pallas kernels  25 us (15%)
  local copies, waits for them, and re-layouts  19.3 us (12%)
  between operations  14.4 us (9%)
  other arithmetic  5.63 us (3%)
    ppermute x8, waiting for transfers between devices, z_shift(): return lax.ppermute(value, 'col', pairs)  24.2 us
    unnamed x38, local copies, waits for them, and re-layouts  16.5 us
    ppermute x8, starting transfers between devices, z_shift(): return lax.ppermute(value, 'col', pairs)  14.2 us
    all_to_all x3, starting transfers between devices, y_exchange(): lax.all_to_all(value, 'row', 0, 0, axis_index_groups=SAME_CORE, tiled=True)  13 us
    pallas_call x5, Pallas kernels, product(): pl.pallas_call(functools.partial(product_kernel, count, first_block, -2.0...  12.9 us
    ppermute x3, starting transfers between devices, core_swap(): return lax.ppermute(value, 'row', [(r, r ^ 1) for r in range(2 * NY)])  9.25 us
    ppermute x7, starting transfers between devices, x_shift(): return lax.ppermute(value, 'col', pairs)  8.1 us
    ppermute x3, starting transfers between devices, y_first(): return lax.ppermute(value, 'row', [(k, y * 2 + k) for k in range(2)])  7.15 us
  transfers between devices with their start and end apart: 26, of which 11 were waited for; matrix products, arithmetic and copies ran while one was open for 5% of the time, Pallas kernels for 14%

profile of v3, /device:TPU:1, one launch (start us, length us, event | category | flops | bytes accessed | tf_op | source)
XLA Modules:
  0.0 160.4 jit_solution(6211191857996626084)
XLA Ops:
  7.2 3.3 %collective-permute-start.6 = (bf16[2048,512]{1,0:T(8,128)(2,1)}, bf16[2048,512]{1,0:T(8,128)(2,1)}, u32[]{:S(2)}, u32[]{:S(2)}) collective-permute-start(bf16[2048,512]{1,0:T(8,128)(2,1)} %mine.1), channel_id=1, source_target_pairs={{0,32},{32,0},{64,96},{96,64},{128,160},{160,128},{192,224},{224,1... | collective-permute-start | bytes 6291464 | tf_op jit(solution)/shard_map/ppermute | solution.py:45
  15.4 2.7 %collective-permute-start.2 = (bf16[128,512]{1,0:T(8,128)(2,1)S(1)}, bf16[128,512]{1,0:T(8,128)(2,1)S(1)}, u32[]{:S(2)}, u32[]{:S(2)}) collective-permute-start(bf16[128,512]{1,0:T(8,128)(2,1)S(1)} %pad_maximum_fusion), channel_id=1, source_target_pairs={{0,24},{1,25},{2,26},{3,27},{4,28},{5,29},{6,30},{7,31},{8,0},{9,1... | collective-permute-start | bytes 393224 | tf_op jit(solution)/shard_map/ppermute | solution.py:27
  18.1 3.2 %collective-permute-done.1 = bf16[128,512]{1,0:T(8,128)(2,1)S(1)} collective-permute-done((bf16[128,512]{1,0:T(8,128)(2,1)S(1)}, bf16[128,512]{1,0:T(8,128)(2,1)S(1)}, u32[]{:S(2)}, u32[]{:S(2)}) %collective-permute-start.1) | collective-permute-done | bytes 131104 | tf_op jit(solution)/shard_map/ppermute | solution.py:27
  25.1 4.0 %collective-permute-start.5 = (bf16[512,512]{1,0:T(8,128)(2,1)S(1)}, bf16[512,512]{1,0:T(8,128)(2,1)S(1)}, u32[]{:S(2)}, u32[]{:S(2)}) collective-permute-start(bf16[512,512]{1,0:T(8,128)(2,1)S(1)} %constant_dynamic-update-slice_fusion.refs_0_), channel_id=1, source_target_pairs={{0,7},{1,0},{2,1},{3,2},{4,3},{5,4},{6,5},{7,6},{8,15},{9,8},{10,9... | collective-permute-start | bytes 1572872 | tf_op jit(solution)/shard_map/ppermute | solution.py:32
  29.1 17.3 %collective-permute-done.4.refs_1_ = bf16[512,512]{1,0:T(8,128)(2,1)S(1)} collective-permute-done((bf16[512,512]{1,0:T(8,128)(2,1)S(1)}, bf16[512,512]{1,0:T(8,128)(2,1)S(1)}, u32[]{:S(2)}, u32[]{:S(2)}) %collective-permute-start.4) | collective-permute-done | bytes 524320 | tf_op jit(solution)/shard_map/ppermute | solution.py:32
  46.5 2.7 %collective-permute-start.8 = (bf16[512,512]{1,0:T(8,128)(2,1)S(1)}, bf16[512,512]{1,0:T(8,128)(2,1)S(1)}, u32[]{:S(2)}, u32[]{:S(2)}) collective-permute-start(bf16[512,512]{1,0:T(8,128)(2,1)S(1)} %collective-permute-done.5.refs_2_), channel_id=1, source_target_pairs={{0,7},{1,0},{2,1},{3,2},{4,3},{5,4},{6,5},{7,6},{8,15},{9,8},{10,9... | collective-permute-start | bytes 1572872 | tf_op jit(solution)/shard_map/ppermute | solution.py:32
  49.2 5.1 %prepare_adjoint.1 = (bf16[8,512,512]{2,1,0:T(8,128)(2,1)S(1)}, bf16[8,512,512]{2,1,0:T(8,128)(2,1)S(1)}) custom-call(s32[4]{0:T(128)S(1)} %pad_add_fusion.pos, s32[64,64]{1,0:T(8,128)S(1)} %copy-done.16, bf16[2048,512]{1,0:T(8,128)(2,1)S(1)} %copy-done.5, bf16[2048,512]{1,0:T(8,128)(2,1)} %collective-permute-done.6.other), custom_call_target="tpu_custom_call" | custom-call | tf_op jit(solution)/shard_map/prepare_adjoint/pallas_call | solution.py:114
  58.3 3.6 %collective-permute-done.7.refs_3_ = bf16[512,512]{1,0:T(8,128)(2,1)S(1)} collective-permute-done((bf16[512,512]{1,0:T(8,128)(2,1)S(1)}, bf16[512,512]{1,0:T(8,128)(2,1)S(1)}, u32[]{:S(2)}, u32[]{:S(2)}) %collective-permute-start.7) | collective-permute-done | bytes 524320 | tf_op jit(solution)/shard_map/ppermute | solution.py:32
  66.9 2.3 %collective-permute-start.15 = (bf16[1024,512]{1,0:T(8,128)(2,1)}, bf16[1024,512]{1,0:T(8,128)(2,1)S(1)}, u32[]{:S(2)}, u32[]{:S(2)}) collective-permute-start(bf16[1024,512]{1,0:T(8,128)(2,1)} %all-gather.3.cloned.1.call-done.refs_0_.block), channel_id=1, source_target_pairs={{0,24},{1,25},{2,26},{3,27},{4,28},{5,29},{6,30},{7,31},{8,0},{9,1... | collective-permute-start | bytes 3145736 | tf_op jit(solution)/shard_map/ppermute | solution.py:27
  74.5 3.0 %masked_product.5.refs_2_ = f32[512,512]{1,0:T(8,128)S(1)} custom-call(s32[4]{0:T(128)S(1)} %pad_add_fusion.pos, bf16[8,512,512]{2,1,0:T(8,128)(2,1)S(1)} %copy-done.1, bf16[512,512]{1,0:T(8,128)(2,1)S(1)} %constant_dynamic-update-slice_fusion.refs_0_, bf16[512,512]{1,0:T(8,128)(2,1)S(1)} %collective-permute-done.4.refs_1_, bf16[512,512]{1,0:T(8,128)(2,1)S(1)} %copy-done.9, ...), custom_call_target="tpu_custom_call" | custom-call | tf_op jit(solution)/shard_map/masked_product/pallas_call | solution.py:171
  77.8 2.9 %collective-permute-start.12 = (bf16[256,512]{1,0:T(8,128)(2,1)S(1)}, bf16[256,512]{1,0:T(8,128)(2,1)S(1)}, u32[]{:S(2)}, u32[]{:S(2)}) collective-permute-start(bf16[256,512]{1,0:T(8,128)(2,1)S(1)} %slice.29), channel_id=1, source_target_pairs={{0,7},{1,0},{2,1},{3,2},{4,3},{5,4},{6,5},{7,6},{8,15},{9,8},{10,9... | collective-permute-start | bytes 786440 | tf_op jit(solution)/shard_map/ppermute | solution.py:32
  82.3 2.3 %collective-permute-done.11.refs_0_ = bf16[256,512]{1,0:T(8,128)(2,1)S(1)} collective-permute-done((bf16[256,512]{1,0:T(8,128)(2,1)S(1)}, bf16[256,512]{1,0:T(8,128)(2,1)S(1)}, u32[]{:S(2)}, u32[]{:S(2)}) %collective-permute-start.11) | collective-permute-done | bytes 262176 | tf_op jit(solution)/shard_map/ppermute | solution.py:32
  86.6 4.7 %all-to-all-start = ((f32[4,512,128]{2,1,0:T(8,128)}), f32[4,512,128]{2,1,0:T(8,128)}, u32[]{:S(2)}, u32[]{:S(2)}) async-start(f32[4,512,128]{2,1,0:T(8,128)} %masked_product.7), calls=%async_computation | async-start | bytes 2097152 | tf_op jit(solution)/shard_map/all_to_all | solution.py:53
  93.1 2.7 %collective-permute-start.16 = (bf16[512,512]{1,0:T(8,128)(2,1)}, bf16[512,512]{1,0:T(8,128)(2,1)}, u32[]{:S(2)}, u32[]{:S(2)}) collective-permute-start(bf16[512,512]{1,0:T(8,128)(2,1)} %slice.35), channel_id=1, source_target_pairs={{0,24},{1,25},{2,26},{3,27},{4,28},{5,29},{6,30},{7,31},{8,0},{9,1... | collective-permute-start | bytes 1572872 | tf_op jit(solution)/shard_map/ppermute | solution.py:27
  95.7 6.6 %all-to-all-done = f32[4,512,128]{2,1,0:T(8,128)} async-done(((f32[4,512,128]{2,1,0:T(8,128)}), f32[4,512,128]{2,1,0:T(8,128)}, u32[]{:S(2)}, u32[]{:S(2)}) %all-to-all-start) | async-done | bytes 1048608 | tf_op jit(solution)/shard_map/all_to_all | solution.py:53
  106.3 4.1 %all-to-all-start.2 = ((bf16[4,512,128]{2,1,0:T(8,128)(2,1)}), bf16[4,512,128]{2,1,0:T(8,128)(2,1)}, u32[]{:S(2)}, u32[]{:S(2)}) async-start(bf16[4,512,128]{2,1,0:T(8,128)(2,1)} %broadcast_in_dim.3), calls=%async_computation.2 | async-start | bytes 1048576 | tf_op jit(solution)/shard_map/all_to_all | solution.py:53
  112.6 3.5 %masked_product.8.refs_2_ = f32[512,512]{1,0:T(8,128)S(1)} custom-call(s32[4]{0:T(128)S(1)} %pad_add_fusion.pos, bf16[8,512,512]{2,1,0:T(8,128)(2,1)S(1)} %copy-done.3, bf16[1024,512]{1,0:T(8,128)(2,1)S(1)} %copy-done.4, bf16[1024,512]{1,0:T(8,128)(2,1)S(1)} %collective-permute-done.13.refs_1_.down, bf16[1024,512]{1,0:T(8,128)(2,1)S(1)} %collective-permute-done.15.refs_2_.up), custom_call_target="tpu_custom_call" | custom-call | tf_op jit(solution)/shard_map/masked_product/pallas_call | solution.py:171
  116.1 2.7 %masked_product.9 = bf16[4,512,128]{2,1,0:T(8,128)(2,1)S(1)} custom-call(s32[4]{0:T(128)S(1)} %pad_add_fusion.pos, bf16[8,512,512]{2,1,0:T(8,128)(2,1)S(1)} %copy-done.3, bf16[512,512]{1,0:T(8,128)(2,1)} %collective-permute-done.14.refs_0_.far_low, bf16[512,512]{1,0:T(8,128)(2,1)} %collective-permute-done.16.refs_1_.far_high, ...), custom_call_target="tpu_custom_call" | custom-call | tf_op jit(solution)/shard_map/masked_product/pallas_call | solution.py:171
  119.7 4.2 %all-to-all-start.1 = ((bf16[4,512,128]{2,1,0:T(8,128)(2,1)}), bf16[4,512,128]{2,1,0:T(8,128)(2,1)}, u32[]{:S(2)}, u32[]{:S(2)}) async-start(bf16[4,512,128]{2,1,0:T(8,128)(2,1)} %copy-done.7), calls=%async_computation.1 | async-start | bytes 1048576 | tf_op jit(solution)/shard_map/all_to_all | solution.py:53
  123.9 5.7 %collective-permute-start.17 = (bf16[4,512,128]{2,1,0:T(8,128)(2,1)}, bf16[4,512,128]{2,1,0:T(8,128)(2,1)}, u32[]{:S(2)}, u32[]{:S(2)}) collective-permute-start(bf16[4,512,128]{2,1,0:T(8,128)(2,1)} %all-to-all-done.2.mine), channel_id=1, source_target_pairs={{0,32},{32,0},{64,96},{96,64},{128,160},{160,128},{192,224},{224,1... | collective-permute-start | bytes 1572872 | tf_op jit(solution)/shard_map/ppermute | solution.py:45
  129.5 2.9 %diagonal_columns.1 = (bf16[1024,128]{1,0:T(8,128)(2,1)S(1)}, bf16[1024,128]{1,0:T(8,128)(2,1)}, bf16[1024,128]{1,0:T(8,128)(2,1)}, bf16[1024,128]{1,0:T(8,128)(2,1)}) custom-call(s32[4]{0:T(128)S(1)} %pad_add_fusion.pos, bf16[1024,512]{1,0:T(8,128)(2,1)S(1)} %copy-done.4, bf16[1024,512]{1,0:T(8,128)(2,1)S(1)} %collective-permute-done.13.refs_1_.down, ...), custom_call_target="tpu_custom_call" | custom-call | tf_op jit(solution)/shard_map/diagonal_columns/pallas_call | solution.py:208
  132.4 3.7 %collective-permute-start.18 = (bf16[1024,128]{1,0:T(8,128)(2,1)}, bf16[1024,128]{1,0:T(8,128)(2,1)S(1)}, u32[]{:S(2)}, u32[]{:S(2)}) collective-permute-start(bf16[1024,128]{1,0:T(8,128)(2,1)} %get-tuple-element.43), channel_id=1, source_target_pairs={{0,64},{32,96},{1,65},{33,97},{2,66},{34,98},{3,67},{35,99},{4,68}... | collective-permute-start | bytes 786440 | tf_op jit(solution)/shard_map/ppermute | solution.py:41
  142.1 5.6 %collective-permute-done.19.two = bf16[1024,128]{1,0:T(8,128)(2,1)S(1)} collective-permute-done((bf16[1024,128]{1,0:T(8,128)(2,1)}, bf16[1024,128]{1,0:T(8,128)(2,1)S(1)}, u32[]{:S(2)}, u32[]{:S(2)}) %collective-permute-start.19) | collective-permute-done | bytes 262176 | tf_op jit(solution)/shard_map/ppermute | solution.py:41
  150.6 2.2 %carried_term.1 = f32[512,128]{1,0:T(8,128)S(1)} custom-call(s32[4]{0:T(128)S(1)} %pad_add_fusion.pos, bf16[4,512,128]{2,1,0:T(8,128)(2,1)} %all-to-all-done.2.mine, bf16[4,512,128]{2,1,0:T(8,128)(2,1)} %collective-permute-done.17.other, bf16[1024,256]{1,0:T(8,128)(2,1)S(1)} %inverse_times_diagonal.1.factors), custom_call_target="tpu_custom_call" | custom-call | tf_op jit(solution)/shard_map/carried_term/pallas_call | solution.py:255
  (93 shorter events, 45.0 us)
Async XLA Ops:
  7.2 56.6 %all-gather.3.cloned.1.call-start = ((), (), s32[]{:S(2)}) async-start(), calls=%async_computation.3 | async-start | bytes 1179648 | tf_op jit(solution)/shard_map/all_gather | solution.py:276
  7.2 39.2 %collective-permute-start.6 = (bf16[2048,512]{1,0:T(8,128)(2,1)}, bf16[2048,512]{1,0:T(8,128)(2,1)}, u32[]{:S(2)}, u32[]{:S(2)}) collective-permute-start(bf16[2048,512]{1,0:T(8,128)(2,1)} %mine.1), channel_id=1, source_target_pairs={{0,32},{32,0},{64,96},{96,64},{128,160},{160,128},{192,224},{224,1... | collective-permute-start | bytes 6291464 | tf_op jit(solution)/shard_map/ppermute | solution.py:45
  15.2 132.5 %all-gather.5.cloned.1.call-start = ((), (), s32[]{:S(2)}) async-start(), calls=%async_computation.4 | async-start | bytes 2359296 | tf_op jit(solution)/shard_map/all_gather | solution.py:287
  15.3 6.0 %collective-permute-start.1 = (bf16[128,512]{1,0:T(8,128)(2,1)S(1)}, bf16[128,512]{1,0:T(8,128)(2,1)S(1)}, u32[]{:S(2)}, u32[]{:S(2)}) collective-permute-start(bf16[128,512]{1,0:T(8,128)(2,1)S(1)} %pad_maximum_fusion), channel_id=1, source_target_pairs={{0,8},{1,9},{2,10},{3,11},{4,12},{5,13},{6,14},{7,15},{8,16},{9,17... | collective-permute-start | bytes 393224 | tf_op jit(solution)/shard_map/ppermute | solution.py:27
  15.4 7.8 %collective-permute-start.2 = (bf16[128,512]{1,0:T(8,128)(2,1)S(1)}, bf16[128,512]{1,0:T(8,128)(2,1)S(1)}, u32[]{:S(2)}, u32[]{:S(2)}) collective-permute-start(bf16[128,512]{1,0:T(8,128)(2,1)S(1)} %pad_maximum_fusion), channel_id=1, source_target_pairs={{0,24},{1,25},{2,26},{3,27},{4,28},{5,29},{6,30},{7,31},{8,0},{9,1... | collective-permute-start | bytes 393224 | tf_op jit(solution)/shard_map/ppermute | solution.py:27
  23.4 23.0 %collective-permute-start.4 = (bf16[512,512]{1,0:T(8,128)(2,1)S(1)}, bf16[512,512]{1,0:T(8,128)(2,1)S(1)}, u32[]{:S(2)}, u32[]{:S(2)}) collective-permute-start(bf16[512,512]{1,0:T(8,128)(2,1)S(1)} %constant_dynamic-update-slice_fusion.refs_0_), channel_id=1, source_target_pairs={{0,1},{1,2},{2,3},{3,4},{4,5},{5,6},{6,7},{7,0},{8,9},{9,10},{10,1... | collective-permute-start | bytes 1572872 | tf_op jit(solution)/shard_map/ppermute | solution.py:32
  25.1 21.3 %collective-permute-start.5 = (bf16[512,512]{1,0:T(8,128)(2,1)S(1)}, bf16[512,512]{1,0:T(8,128)(2,1)S(1)}, u32[]{:S(2)}, u32[]{:S(2)}) collective-permute-start(bf16[512,512]{1,0:T(8,128)(2,1)S(1)} %constant_dynamic-update-slice_fusion.refs_0_), channel_id=1, source_target_pairs={{0,7},{1,0},{2,1},{3,2},{4,3},{5,4},{6,5},{7,6},{8,15},{9,8},{10,9... | collective-permute-start | bytes 1572872 | tf_op jit(solution)/shard_map/ppermute | solution.py:32
  46.4 15.5 %collective-permute-start.7 = (bf16[512,512]{1,0:T(8,128)(2,1)S(1)}, bf16[512,512]{1,0:T(8,128)(2,1)S(1)}, u32[]{:S(2)}, u32[]{:S(2)}) collective-permute-start(bf16[512,512]{1,0:T(8,128)(2,1)S(1)} %collective-permute-done.4.refs_1_), channel_id=1, source_target_pairs={{0,1},{1,2},{2,3},{3,4},{4,5},{5,6},{6,7},{7,0},{8,9},{9,10},{10,1... | collective-permute-start | bytes 1572872 | tf_op jit(solution)/shard_map/ppermute | solution.py:32
  46.5 16.5 %collective-permute-start.8 = (bf16[512,512]{1,0:T(8,128)(2,1)S(1)}, bf16[512,512]{1,0:T(8,128)(2,1)S(1)}, u32[]{:S(2)}, u32[]{:S(2)}) collective-permute-start(bf16[512,512]{1,0:T(8,128)(2,1)S(1)} %collective-permute-done.5.refs_2_), channel_id=1, source_target_pairs={{0,7},{1,0},{2,1},{3,2},{4,3},{5,4},{6,5},{7,6},{8,15},{9,8},{10,9... | collective-permute-start | bytes 1572872 | tf_op jit(solution)/shard_map/ppermute | solution.py:32
  63.8 13.8 %collective-permute-start.9 = (bf16[512,512]{1,0:T(8,128)(2,1)}, bf16[512,512]{1,0:T(8,128)(2,1)S(1)}, u32[]{:S(2)}, u32[]{:S(2)}) collective-permute-start(bf16[512,512]{1,0:T(8,128)(2,1)} %copy-done.10), channel_id=1, source_target_pairs={{0,1},{1,2},{2,3},{3,4},{4,5},{5,6},{6,7},{7,0},{8,9},{9,10},{10,1... | collective-permute-start | bytes 1572872 | tf_op jit(solution)/shard_map/ppermute | solution.py:32
  64.4 13.2 %collective-permute-start.10 = (bf16[512,512]{1,0:T(8,128)(2,1)}, bf16[512,512]{1,0:T(8,128)(2,1)S(1)}, u32[]{:S(2)}, u32[]{:S(2)}) collective-permute-start(bf16[512,512]{1,0:T(8,128)(2,1)} %copy-done.12), channel_id=1, source_target_pairs={{0,7},{1,0},{2,1},{3,2},{4,3},{5,4},{6,5},{7,6},{8,15},{9,8},{10,9... | collective-permute-start | bytes 1572872 | tf_op jit(solution)/shard_map/ppermute | solution.py:32
  66.5 24.7 %collective-permute-start.13 = (bf16[1024,512]{1,0:T(8,128)(2,1)}, bf16[1024,512]{1,0:T(8,128)(2,1)S(1)}, u32[]{:S(2)}, u32[]{:S(2)}) collective-permute-start(bf16[1024,512]{1,0:T(8,128)(2,1)} %all-gather.3.cloned.1.call-done.refs_0_.block), channel_id=1, source_target_pairs={{0,8},{1,9},{2,10},{3,11},{4,12},{5,13},{6,14},{7,15},{8,16},{9,17... | collective-permute-start | bytes 3145736 | tf_op jit(solution)/shard_map/ppermute | solution.py:27
  66.9 25.3 %collective-permute-start.15 = (bf16[1024,512]{1,0:T(8,128)(2,1)}, bf16[1024,512]{1,0:T(8,128)(2,1)S(1)}, u32[]{:S(2)}, u32[]{:S(2)}) collective-permute-start(bf16[1024,512]{1,0:T(8,128)(2,1)} %all-gather.3.cloned.1.call-done.refs_0_.block), channel_id=1, source_target_pairs={{0,24},{1,25},{2,26},{3,27},{4,28},{5,29},{6,30},{7,31},{8,0},{9,1... | collective-permute-start | bytes 3145736 | tf_op jit(solution)/shard_map/ppermute | solution.py:27
  77.6 6.9 %collective-permute-start.11 = (bf16[256,512]{1,0:T(8,128)(2,1)S(1)}, bf16[256,512]{1,0:T(8,128)(2,1)S(1)}, u32[]{:S(2)}, u32[]{:S(2)}) collective-permute-start(bf16[256,512]{1,0:T(8,128)(2,1)S(1)} %slice.28), channel_id=1, source_target_pairs={{0,1},{1,2},{2,3},{3,4},{4,5},{5,6},{6,7},{7,0},{8,9},{9,10},{10,1... | collective-permute-start | bytes 786440 | tf_op jit(solution)/shard_map/ppermute | solution.py:32
  77.8 6.8 %collective-permute-start.12 = (bf16[256,512]{1,0:T(8,128)(2,1)S(1)}, bf16[256,512]{1,0:T(8,128)(2,1)S(1)}, u32[]{:S(2)}, u32[]{:S(2)}) collective-permute-start(bf16[256,512]{1,0:T(8,128)(2,1)S(1)} %slice.29), channel_id=1, source_target_pairs={{0,7},{1,0},{2,1},{3,2},{4,3},{5,4},{6,5},{7,6},{8,15},{9,8},{10,9... | collective-permute-start | bytes 786440 | tf_op jit(solution)/shard_map/ppermute | solution.py:32
  86.6 15.7 %all-to-all-start = ((f32[4,512,128]{2,1,0:T(8,128)}), f32[4,512,128]{2,1,0:T(8,128)}, u32[]{:S(2)}, u32[]{:S(2)}) async-start(f32[4,512,128]{2,1,0:T(8,128)} %masked_product.7), calls=%async_computation | async-start | bytes 2097152 | tf_op jit(solution)/shard_map/all_to_all | solution.py:53
  92.2 23.9 %collective-permute-start.14 = (bf16[512,512]{1,0:T(8,128)(2,1)}, bf16[512,512]{1,0:T(8,128)(2,1)}, u32[]{:S(2)}, u32[]{:S(2)}) collective-permute-start(bf16[512,512]{1,0:T(8,128)(2,1)} %slice.34), channel_id=1, source_target_pairs={{0,8},{1,9},{2,10},{3,11},{4,12},{5,13},{6,14},{7,15},{8,16},{9,17... | collective-permute-start | bytes 1572872 | tf_op jit(solution)/shard_map/ppermute | solution.py:27
  93.1 23.1 %collective-permute-start.16 = (bf16[512,512]{1,0:T(8,128)(2,1)}, bf16[512,512]{1,0:T(8,128)(2,1)}, u32[]{:S(2)}, u32[]{:S(2)}) collective-permute-start(bf16[512,512]{1,0:T(8,128)(2,1)} %slice.35), channel_id=1, source_target_pairs={{0,24},{1,25},{2,26},{3,27},{4,28},{5,29},{6,30},{7,31},{8,0},{9,1... | collective-permute-start | bytes 1572872 | tf_op jit(solution)/shard_map/ppermute | solution.py:27
  106.3 13.4 %all-to-all-start.2 = ((bf16[4,512,128]{2,1,0:T(8,128)(2,1)}), bf16[4,512,128]{2,1,0:T(8,128)(2,1)}, u32[]{:S(2)}, u32[]{:S(2)}) async-start(bf16[4,512,128]{2,1,0:T(8,128)(2,1)} %broadcast_in_dim.3), calls=%async_computation.2 | async-start | bytes 1048576 | tf_op jit(solution)/shard_map/all_to_all | solution.py:53
  119.7 19.9 %all-to-all-start.1 = ((bf16[4,512,128]{2,1,0:T(8,128)(2,1)}), bf16[4,512,128]{2,1,0:T(8,128)(2,1)}, u32[]{:S(2)}, u32[]{:S(2)}) async-start(bf16[4,512,128]{2,1,0:T(8,128)(2,1)} %copy-done.7), calls=%async_computation.1 | async-start | bytes 1048576 | tf_op jit(solution)/shard_map/all_to_all | solution.py:53
  123.9 26.7 %collective-permute-start.17 = (bf16[4,512,128]{2,1,0:T(8,128)(2,1)}, bf16[4,512,128]{2,1,0:T(8,128)(2,1)}, u32[]{:S(2)}, u32[]{:S(2)}) collective-permute-start(bf16[4,512,128]{2,1,0:T(8,128)(2,1)} %all-to-all-done.2.mine), channel_id=1, source_target_pairs={{0,32},{32,0},{64,96},{96,64},{128,160},{160,128},{192,224},{224,1... | collective-permute-start | bytes 1572872 | tf_op jit(solution)/shard_map/ppermute | solution.py:45
  132.4 9.7 %collective-permute-start.18 = (bf16[1024,128]{1,0:T(8,128)(2,1)}, bf16[1024,128]{1,0:T(8,128)(2,1)S(1)}, u32[]{:S(2)}, u32[]{:S(2)}) collective-permute-start(bf16[1024,128]{1,0:T(8,128)(2,1)} %get-tuple-element.43), channel_id=1, source_target_pairs={{0,64},{32,96},{1,65},{33,97},{2,66},{34,98},{3,67},{35,99},{4,68}... | collective-permute-start | bytes 786440 | tf_op jit(solution)/shard_map/ppermute | solution.py:41
  136.1 11.6 %collective-permute-start.19 = (bf16[1024,128]{1,0:T(8,128)(2,1)}, bf16[1024,128]{1,0:T(8,128)(2,1)S(1)}, u32[]{:S(2)}, u32[]{:S(2)}) collective-permute-start(bf16[1024,128]{1,0:T(8,128)(2,1)} %get-tuple-element.44), channel_id=1, source_target_pairs={{0,128},{32,160},{1,129},{33,161},{2,130},{34,162},{3,131},{35,163... | collective-permute-start | bytes 786440 | tf_op jit(solution)/shard_map/ppermute | solution.py:41
  138.3 9.4 %collective-permute-start.20 = (bf16[1024,128]{1,0:T(8,128)(2,1)}, bf16[1024,128]{1,0:T(8,128)(2,1)S(1)}, u32[]{:S(2)}, u32[]{:S(2)}) collective-permute-start(bf16[1024,128]{1,0:T(8,128)(2,1)} %get-tuple-element.45), channel_id=1, source_target_pairs={{0,192},{32,224},{1,193},{33,225},{2,194},{34,226},{3,195},{35,227... | collective-permute-start | bytes 786440 | tf_op jit(solution)/shard_map/ppermute | solution.py:41
  (19 other events, 128.3 us)
Sparse Core Ops, SparseCore 0:
  15.3 38.7 all-gather.2
  63.9 28.2 all-gather.4

commit v4 on v0

v4 whole, which is shorter than its diff:
```python
import functools

import jax
import jax.numpy as jnp
from jax import lax
from jax.experimental import pallas as pl
from jax.experimental.pallas import tpu as pltpu
from jax.sharding import PartitionSpec as P

BLK = 256
NX, NZ, NY = 4, 8, 4
SAME_X = [[x * NZ + z for z in range(NZ)] for x in range(NX)]
SUB = 64
PAIR = 2 * SUB
HALF = 512
WIDE = 384
F32, BF16 = jnp.float32, jnp.bfloat16
VMEM = pl.BlockSpec(memory_space=pltpu.VMEM)
SMEM = pl.BlockSpec(memory_space=pltpu.SMEM)
ANY = pl.BlockSpec(memory_space=pl.ANY)
BIG = pltpu.CompilerParams(vmem_limit_bytes=24 * 2**20)
SMALL = pltpu.CompilerParams(vmem_limit_bytes=16 * 2**20)


def x_shift(value, dx):
    pairs = [(x * NZ + z, (x + dx) % NX * NZ + z) for x in range(NX) for z in range(NZ)]
    return lax.ppermute(value, "col", pairs)


def z_shift(value, dz):
    pairs = [(x * NZ + z, x * NZ + (z + dz) % NZ) for x in range(NX) for z in range(NZ)]
    return lax.ppermute(value, "col", pairs)


def y_shift(value, dy):
    pairs = [(y * 2 + k, (y + dy) % NY * 2 + k) for y in range(NY) for k in range(2)]
    return lax.ppermute(value, "row", pairs)


def to_first(value):
    sent = [lax.ppermute(value, "row", [(y * 2 + k, k) for k in range(2)]) for y in range(1, NY)]
    return jnp.stack([value] + sent)


def swap_first(value):
    return lax.ppermute(value, "row", [(0, 1), (1, 0)])


def core_swap(value):
    return lax.ppermute(value, "row", [(r, r ^ 1) for r in range(2 * NY)])


def together(*values):
    return lax.optimization_barrier(values)


def offset(n):
    return ((n + 1) // 2) * (1 - 2 * (n % 2))


def source_xz(pos, b, t):
    return (pos[0] + offset(t) + NX) % NX, (pos[1] + offset(b) + NZ) % NZ


def source_zx(pos, b, t):
    return (pos[0] + offset(b // 2) + NX) % NX, b % 2 * 4 + t


def pack_kernel(pos, two, one, own, give):
    first = pos[3] == 0
    for q in range(NY):
        at = slice(q * 128, q * 128 + 128)
        for n, panel in enumerate((two, one) if q < 3 else (one, two)):
            left = panel[:, q * 256:q * 256 + 128]
            right = panel[:, q * 256 + 128:q * 256 + 256]
            own[n, :, at] = jnp.where(first, left, right)
            give[n, :, at] = jnp.where(first, right, left)


def pack(pos, two, one):
    return pl.pallas_call(
        pack_kernel,
        out_shape=(jax.ShapeDtypeStruct((2, SUB, HALF), BF16),) * 2,
        in_specs=[SMEM, VMEM, VMEM],
        out_specs=(VMEM, VMEM),
        compiler_params=SMALL,
        name="pack_columns",
    )(pos, two, one)


def join_kernel(own, down, up, far, main, rest):
    for n, part in enumerate((own, down, up, far)):
        main[n] = part[:, :WIDE]
        rest[n] = part[:, WIDE:]


def join(*parts):
    return pl.pallas_call(
        join_kernel,
        out_shape=(
            jax.ShapeDtypeStruct((NX, PAIR, WIDE), BF16),
            jax.ShapeDtypeStruct((NX, PAIR, HALF - WIDE), BF16),
        ),
        in_specs=[VMEM] * NX,
        out_specs=(VMEM, VMEM),
        compiler_params=SMALL,
        name="join_parts",
    )(*parts)


def prepare_kernel(pos, taper, mine, other, out_xz, out_zx, rows, held, sems):
    lane = lax.broadcasted_iota(jnp.int32, (SUB, 2 * BLK), 1)
    first_col = (pos[0] * NZ + pos[1]) * 2

    for out, source in ((out_xz, source_xz), (out_zx, source_zx)):
        def block(b, carry, out=out, source=source):
            for t in range(4):
                x, z = source(pos, b, t)
                row = pl.multiple_of((x * NZ + z) * SUB, SUB)
                for h, ref in enumerate((mine, other)):
                    core = pos[3] if h == 0 else 1 - pos[3]
                    tile = (pos[2] * 2 + core) * 8 + x * 2 + z // 4
                    left = taper[tile, first_col].astype(F32)
                    right = taper[tile, first_col + 1].astype(F32)
                    keep = jnp.where(lane < BLK, left, right)
                    at = t * PAIR + h * SUB
                    rows[at:at + SUB, :] = (ref[pl.ds(row, SUB), :].astype(F32) * keep).astype(BF16)
            held[b] = rows[...].T
            pltpu.make_async_copy(held.at[b], out.at[b], sems.at[b]).start()
            return carry

        lax.fori_loop(0, 8, block, 0)
        for b in range(8):
            pltpu.make_async_copy(held.at[b], out.at[b], sems.at[b]).wait()


def prepare(pos, taper, mine, other):
    return pl.pallas_call(
        prepare_kernel,
        out_shape=(jax.ShapeDtypeStruct((8, 512, 512), BF16),) * 2,
        in_specs=[SMEM, SMEM, VMEM, VMEM],
        out_specs=(pl.BlockSpec(memory_space=pltpu.HBM),) * 2,
        scratch_shapes=[
            pltpu.VMEM((512, 512), BF16),
            pltpu.VMEM((8, 512, 512), BF16),
            pltpu.SemaphoreType.DMA((8,)),
        ],
        compiler_params=BIG,
        name="prepare_adjoint",
    )(pos, taper, mine, other)


def product_kernel(count, wide, narrow, first, last, diagonal, pos, by_xz, by_zx, *refs):
    panels, refs = refs[:count], list(refs[count:])
    before = None if first else refs.pop(0)
    pieces = (refs.pop(0), refs.pop(0)) if diagonal else None
    outs = [refs.pop(0) for _ in range(NY)] if last else None
    total = refs.pop(0)
    left, main, rest, sems = refs[:4]
    items = list(wide) + list(narrow)
    for n, (which, b, parts) in enumerate(items):
        pltpu.make_async_copy((by_xz, by_zx)[which].at[b], left.at[n], sems.at[0, n]).start()
        held, at = (main, n) if n < len(wide) else (rest, n - len(wide))
        to = 0
        for index, start, size in parts:
            begin = start(pos) if callable(start) else start
            pltpu.make_async_copy(
                panels[index].at[pl.ds(begin, size)], held.at[at, pl.ds(to, size)], sems.at[1, n]
            ).start()
            to += size

    if diagonal:
        top, top_rest, top_sems = refs[4:7]
        half = jnp.where(pos[3] == 0, 0, SUB)

        @pl.when(pos[2] == 0)
        def _():
            for i in range(NX):
                x = (pos[0] + offset(i) + NX) % NX
                sources = ((panels[i], 0),) if i < 3 else ((panels[3], 0), (panels[4], 4))

                @pl.when(x < 2)
                def _(i=i, x=x, sources=sources):
                    for ref, z in sources:
                        pltpu.make_async_copy(
                            ref.at[:, pl.ds(half, SUB), :],
                            top.at[pl.ds(x * NZ + z, ref.shape[0])], top_sems.at[0]).start()
                    pltpu.make_async_copy(
                        panels[5].at[:, i, pl.ds(half, SUB), :],
                        top_rest.at[pl.ds(x * NZ, NZ)], top_sems.at[1]).start()

    if first:
        total[...] = jnp.zeros_like(total)
    else:
        total[...] = before[...]

    def step(n, held, at, columns):
        pltpu.make_async_copy(left.at[n], left.at[n], sems.at[0, n]).wait()
        pltpu.make_async_copy(held.at[at], held.at[at], sems.at[1, n]).wait()
        block = held[at].reshape(NX * PAIR, held.shape[-1])
        total[:, columns] += jnp.dot(left[n], block, preferred_element_type=F32)

    def wide_step(n, carry):
        step(n, main, n, slice(0, WIDE))
        return carry

    def narrow_step(n, carry):
        step(n + len(wide), rest, n, slice(WIDE, HALF))
        return carry

    if wide:
        lax.fori_loop(0, len(wide), wide_step, 0)
    if narrow:
        lax.fori_loop(0, len(narrow), narrow_step, 0)

    if diagonal:
        @pl.when(pos[2] == 0)
        def _():
            for n, (held, columns) in enumerate(((top, slice(0, WIDE)), (top_rest, slice(WIDE, HALF)))):
                pltpu.make_async_copy(held, held, top_sems.at[n]).wait()
                rows = held[...].reshape(2 * NZ * SUB, held.shape[-1])
                total[:, columns] += jnp.dot(pieces[0][...], rows, preferred_element_type=F32)
                total[:, columns] += jnp.dot(pieces[1][...], rows, preferred_element_type=F32)

    if last:
        for d, out in enumerate(outs):
            column = pl.multiple_of((pos[2] + d) % NY * 128, 128)
            out[...] = (-2.0 * total[:, pl.ds(column, 128)]).astype(out.dtype)


def product(pos, adjoint, panels, wide, narrow, before=None, pieces=(), kind=None):
    last = kind is not None
    column = jax.ShapeDtypeStruct((512, 128), F32)
    sums = jax.ShapeDtypeStruct((512, HALF), F32)
    count = len(wide) + len(narrow)
    scratch = [pltpu.VMEM((512, HALF), F32)] if last else []
    scratch += [
        pltpu.VMEM((max(count, 1), 512, 512), BF16),
        pltpu.VMEM((max(len(wide), 1), NX, PAIR, WIDE), BF16),
        pltpu.VMEM((max(len(narrow), 1), NX, PAIR, HALF - WIDE), BF16),
        pltpu.SemaphoreType.DMA((2, max(count, 1))),
    ]
    if pieces:
        scratch += [
            pltpu.VMEM((2 * NZ, SUB, WIDE), BF16),
            pltpu.VMEM((2 * NZ, SUB, HALF - WIDE), BF16),
            pltpu.SemaphoreType.DMA((2,)),
        ]
    extra = ([] if before is None else [before]) + list(pieces)
    kernel = functools.partial(
        product_kernel, len(panels), tuple(wide), tuple(narrow), before is None, last, bool(pieces))
    return pl.pallas_call(
        kernel,
        out_shape=(column,) + (jax.ShapeDtypeStruct((512, 128), kind),) * 3 if last else sums,
        in_specs=[SMEM, ANY, ANY] + [ANY] * len(panels) + [VMEM] * len(extra),
        out_specs=(VMEM,) * 4 if last else VMEM,
        scratch_shapes=scratch,
        compiler_params=SMALL,
        name="masked_product",
    )(pos, *adjoint, *panels, *extra)


def carried_kernel(pos, mine, other, factor, factor_other, high, low, total):
    @pl.when(pos[2] == 0)
    def _():
        total[...] = jnp.zeros_like(total)

        def block(y, carry):
            left = jnp.concatenate([mine[y], other[y]], axis=1)
            right = jnp.concatenate([factor[y], factor_other[y]], axis=0)
            total[...] += jnp.dot(left, right, preferred_element_type=F32)
            return carry

        lax.fori_loop(0, NY, block, 0)
        value = 0.5 * total[...]
        top = value.astype(BF16)
        high[...] = top
        low[...] = (value - top.astype(F32)).astype(BF16)


def carried(pos, mine, other, factor, factor_other):
    return pl.pallas_call(
        carried_kernel,
        out_shape=(jax.ShapeDtypeStruct((512, 1024), BF16),) * 2,
        in_specs=[SMEM] + [VMEM] * 4,
        out_specs=(VMEM, VMEM),
        scratch_shapes=[pltpu.VMEM((512, 1024), F32)],
        compiler_params=SMALL,
        name="carried_half",
    )(pos, mine, other, factor, factor_other)


def local(adjoint, taper, panel_two, panel_one, incoming, inverse_factor):
    row, col = lax.axis_index("row"), lax.axis_index("col")
    pos = jnp.stack([col // NZ, col % NZ, row // 2, row % 2]).astype(jnp.int32)

    own, give = pack(pos, panel_two, panel_one)
    taken = core_swap(give)
    x_first = jnp.concatenate([own[0], taken[0]], axis=0)
    z_first = jnp.concatenate([own[1], taken[1]], axis=0)

    over_z = lax.all_gather(z_first, "col", axis_index_groups=SAME_X, axis=0, tiled=True)
    block, rest_one = join(x_first, *[x_shift(x_first, d) for d in (1, -1, 2)])
    rest_one = lax.all_gather(rest_one, "col", axis_index_groups=SAME_X, axis=0)

    factor = to_first(inverse_factor)
    down1, up1, swapped, factor = together(
        z_shift(block, 1), z_shift(block, -1), core_swap(adjoint), factor)
    masked = prepare(pos, taper, adjoint, swapped)
    down2, up2, factor_other, *masked = together(
        z_shift(down1, 1), z_shift(up1, -1), swap_first(factor), *masked)
    sums = product(
        pos, masked, [block, down1, up1, down2, up2], [(0, b, [(b, 0, 4)]) for b in range(5)], [])
    over_z, down2, up2 = together(over_z, down2, up2)
    rest_two = over_z[:, WIDE:].reshape(NZ, PAIR, HALF - WIDE)
    rest_two = [rest_two] + [x_shift(rest_two, d) for d in (1, -1, 2)]
    down3, up3, sums = together(z_shift(down2, 1), z_shift(up2, -1), sums)
    far = [z_shift(down3[:2], 1), z_shift(up3[2:], -1)]

    main = over_z[:, :WIDE].reshape(NZ, PAIR, WIDE)
    main, *rest_two = together(main, *rest_two)
    down, up = x_shift(main, 1), x_shift(main, -1)
    sums = product(
        pos, masked, [down3, up3] + rest_two, [(0, 5 + b, [(b, 0, 4)]) for b in range(2)],
        [(1, b, [(2 + b // 2, b % 2 * 4, 4)]) for b in range(8)], sums)
    mine, *sent = product(
        pos, masked, far, [(0, 7, [(0, 0, 2), (1, 0, 2)])], [], sums, kind=F32)
    r1, r2, r3 = [y_shift(part, d + 1) for d, part in enumerate(sent)]
    far_one = [x_shift(down[:4], 1), x_shift(up[4:], -1)]
    second_grad = incoming + ((mine + r1) + (r2 + r3))
    rounded = to_first(second_grad.astype(BF16))
    rounded_other = swap_first(rounded)

    sums = product(
        pos, masked, [main, down, up], [(1, b, [(b // 2, b % 2 * 4, 4)]) for b in range(6)], [])
    pieces = carried(pos, rounded, rounded_other, factor, factor_other)

    def of_z(b):
        return lambda pos: source_xz(pos, b, 0)[1] * NX

    rest_flat = rest_one.reshape(NZ * NX, PAIR, HALF - WIDE)
    sums = product(
        pos, masked, far_one + [rest_flat], [(1, 6 + b, [(b, 0, 4)]) for b in range(2)],
        [(0, b, [(2, of_z(b), 4)]) for b in range(8)], sums)
    mine, *sent = product(
        pos, masked, [main, down, up] + far_one + [rest_one], [], [], sums, pieces, BF16)
    r1, r2, r3 = [y_shift(part, d + 1).astype(F32) for d, part in enumerate(sent)]
    return second_grad, (mine + r1) + (r2 + r3)


def solution(mesh):
    in_specs = (
        P("row", "col"),
        P(),
        P(("row", "col"), None),
        P(("row", "col"), None),
        P("col", "row"),
        P("row", None),
    )
    out_specs = (P("col", "row"), P("col", "row"))
    return jax.shard_map(local, mesh=mesh, in_specs=in_specs, out_specs=out_specs, check_vma=False)
```

time: 405 us -> 179 us (0.44)
  waiting for transfers between devices: 365 us -> 47.2 us
  starting transfers between devices: 0.24 us -> 51.5 us
  Pallas kernels: 0 us -> 37.6 us
  local copies, waits for them, and re-layouts: 1.65 us -> 23 us
  matrix products: 18.3 us -> 0 us
    all_gather x2, waiting for transfers between devices: 157 us -> 0.02 us  [the longest x1 0.02 us: local(): rest_one = lax.all_gather(rest_one, 'col', axis_index_groups=SAME_X, axis=0)]
    psum x2 -> x0, waiting for transfers between devices: 142 us -> none  [the longest x1 72.6 us: local(): carried = lax.psum(partial_value, 'row')]
    reduce_scatter x2 -> x0, waiting for transfers between devices: 63.8 us -> none  [spread(): return lax.psum_scatter(mirror_term, 'row', scatter_dimension=1, tiled=True)]
    ppermute x0 -> x34, starting transfers between devices: none -> 51.4 us  [the longest x8 13.1 us: z_shift(): return lax.ppermute(value, 'col', pairs)]
    ppermute x0 -> x34, waiting for transfers between devices: none -> 47.2 us  [the longest x6 15.1 us: y_shift(): return lax.ppermute(value, 'row', pairs)]
    pallas_call x0 -> x10, Pallas kernels: none -> 37.6 us  [the longest x6 26.5 us: product(): pl.pallas_call(kernel, out_shape=(column,) + (jax.ShapeDtypeStruct((512,...]
    unnamed x7 -> x48, local copies, waits for them, and re-layouts: 0.5 us -> 20.3 us
    dot_general x4 -> x0, matrix products: 18.3 us -> none  [the longest x2 13.1 us: mirror(): lax.dot_general(masked, gathered, (((0,), (0,)), ((), ())), preferred_ele...]
  transfers between devices with their start and end apart: 6 -> 36, of which waited for: 6 -> 12; matrix products, arithmetic and copies ran while one was open for 5% -> 3% of each run, Pallas kernels for 0% -> 17%
where the time goes in v4:
time: 179 us; the launch traced here: 178 us
  starting transfers between devices  51.5 us (29%)
  waiting for transfers between devices  47.2 us (26%)
  Pallas kernels  37.6 us (21%)
  local copies, waits for them, and re-layouts  23 us (13%)
  between operations  14.5 us (8%)
  other arithmetic  4.26 us (2%)
    pallas_call x6, Pallas kernels, product(): pl.pallas_call(kernel, out_shape=(column,) + (jax.ShapeDtypeStruct((512,...  26.5 us
    unnamed x48, local copies, waits for them, and re-layouts  20.3 us
    ppermute x6, waiting for transfers between devices, y_shift(): return lax.ppermute(value, 'row', pairs)  15.1 us
    ppermute x8, starting transfers between devices, z_shift(): return lax.ppermute(value, 'col', pairs)  13.1 us
    ppermute x10, starting transfers between devices, x_shift(): return lax.ppermute(value, 'col', pairs)  12 us
    ppermute x6, waiting for transfers between devices, to_first(): lax.ppermute(value, 'row', [(y * 2 + k, k) for k in range(2)])  11.4 us
    ppermute x10, waiting for transfers between devices, x_shift(): return lax.ppermute(value, 'col', pairs)  11.4 us
    ppermute x2, starting transfers between devices, swap_first(): return lax.ppermute(value, 'row', [(0, 1), (1, 0)])  9.4 us
  transfers between devices with their start and end apart: 36, of which 12 were waited for; matrix products, arithmetic and copies ran while one was open for 3% of the time, Pallas kernels for 17%

profile of v4, /device:TPU:1, one launch (start us, length us, event | category | flops | bytes accessed | tf_op | source)
XLA Modules:
  0.0 178.0 jit_solution(143430764873841419)
XLA Ops:
  7.2 3.3 %collective-permute-start.6 = (bf16[2048,512]{1,0:T(8,128)(2,1)}, bf16[2048,512]{1,0:T(8,128)(2,1)}, u32[]{:S(2)}, u32[]{:S(2)}) collective-permute-start(bf16[2048,512]{1,0:T(8,128)(2,1)} %mine.1), channel_id=1, source_target_pairs={{0,32},{32,0},{64,96},{96,64},{128,160},{160,128},{192,224},{224,1... | collective-permute-start | bytes 6291464 | tf_op jit(solution)/shard_map/ppermute | solution.py:50
  19.2 3.7 %collective-permute-done.3.far = bf16[128,512]{1,0:T(8,128)(2,1)S(1)} collective-permute-done((bf16[128,512]{1,0:T(8,128)(2,1)S(1)}, bf16[128,512]{1,0:T(8,128)(2,1)S(1)}, u32[]{:S(2)}, u32[]{:S(2)}) %collective-permute-start.3) | collective-permute-done | bytes 131104 | tf_op jit(solution)/shard_map/ppermute | solution.py:27
  26.7 5.0 %collective-permute-start.5 = (bf16[4,128,384]{2,1,0:T(8,128)(2,1)S(1)}, bf16[4,128,384]{2,1,0:T(8,128)(2,1)S(1)}, u32[]{:S(2)}, u32[]{:S(2)}) collective-permute-start(bf16[4,128,384]{2,1,0:T(8,128)(2,1)S(1)} %get-tuple-element.40.refs_0_), channel_id=1, source_target_pairs={{0,7},{1,0},{2,1},{3,2},{4,3},{5,4},{6,5},{7,6},{8,15},{9,8},{10,9... | collective-permute-start | bytes 1179656 | tf_op jit(solution)/shard_map/ppermute | solution.py:32
  31.6 6.7 %collective-permute-done.9 = bf16[128,1024]{1,0:T(8,128)(2,1)S(1)} collective-permute-done((bf16[128,1024]{1,0:T(8,128)(2,1)}, bf16[128,1024]{1,0:T(8,128)(2,1)S(1)}, u32[]{:S(2)}, u32[]{:S(2)}) %collective-permute-start.9) | collective-permute-done | bytes 262176 | tf_op jit(solution)/shard_map/ppermute | solution.py:41
  39.5 5.1 %collective-permute-done.5.refs_2_ = bf16[4,128,384]{2,1,0:T(8,128)(2,1)S(1)} collective-permute-done((bf16[4,128,384]{2,1,0:T(8,128)(2,1)S(1)}, bf16[4,128,384]{2,1,0:T(8,128)(2,1)S(1)}, u32[]{:S(2)}, u32[]{:S(2)}) %collective-permute-start.5) | collective-permute-done | bytes 393248 | tf_op jit(solution)/shard_map/ppermute | solution.py:32
  44.6 2.9 %collective-permute-done.4.refs_1_ = bf16[4,128,384]{2,1,0:T(8,128)(2,1)S(1)} collective-permute-done((bf16[4,128,384]{2,1,0:T(8,128)(2,1)S(1)}, bf16[4,128,384]{2,1,0:T(8,128)(2,1)S(1)}, u32[]{:S(2)}, u32[]{:S(2)}) %collective-permute-start.4) | collective-permute-done | bytes 393248 | tf_op jit(solution)/shard_map/ppermute | solution.py:32
  47.5 4.1 %collective-permute-start.12 = (bf16[4,128,1024]{2,1,0:T(8,128)(2,1)S(1)}, bf16[4,128,1024]{2,1,0:T(8,128)(2,1)S(1)}, u32[]{:S(2)}, u32[]{:S(2)}) collective-permute-start(bf16[4,128,1024]{2,1,0:T(8,128)(2,1)S(1)} %pad_maximum_fusion.factor), channel_id=1, source_target_pairs={{0,32},{32,0},{1,33},{33,1},{2,34},{34,2},{3,35},{35,3},{4,36},{36... | collective-permute-start | bytes 3145736 | tf_op jit(solution)/shard_map/ppermute | solution.py:46
  51.7 2.7 %collective-permute-start.11 = (bf16[4,128,384]{2,1,0:T(8,128)(2,1)S(1)}, bf16[4,128,384]{2,1,0:T(8,128)(2,1)S(1)}, u32[]{:S(2)}, u32[]{:S(2)}) collective-permute-start(bf16[4,128,384]{2,1,0:T(8,128)(2,1)S(1)} %collective-permute-done.5.refs_2_), channel_id=1, source_target_pairs={{0,7},{1,0},{2,1},{3,2},{4,3},{5,4},{6,5},{7,6},{8,15},{9,8},{10,9... | collective-permute-start | bytes 1179656 | tf_op jit(solution)/shard_map/ppermute | solution.py:32
  55.1 5.9 %prepare_adjoint.1 = (bf16[8,512,512]{2,1,0:T(8,128)(2,1)S(1)}, bf16[8,512,512]{2,1,0:T(8,128)(2,1)S(1)}) custom-call(s32[4]{0:T(128)S(1)} %pad_add_fusion.pos, s32[64,64]{1,0:T(8,128)S(1)} %copy-done.21, bf16[2048,512]{1,0:T(8,128)(2,1)S(1)} %copy-done.12, bf16[2048,512]{1,0:T(8,128)(2,1)} %collective-permute-done.6.other), custom_call_target="tpu_custom_call" | custom-call | tf_op jit(solution)/shard_map/prepare_adjoint/pallas_call | solution.py:138
  66.8 2.7 %collective-permute-start.14 = (bf16[4,128,384]{2,1,0:T(8,128)(2,1)}, bf16[4,128,384]{2,1,0:T(8,128)(2,1)S(1)}, u32[]{:S(2)}, u32[]{:S(2)}) collective-permute-start(bf16[4,128,384]{2,1,0:T(8,128)(2,1)} %copy-done.17), channel_id=1, source_target_pairs={{0,7},{1,0},{2,1},{3,2},{4,3},{5,4},{6,5},{7,6},{8,15},{9,8},{10,9... | collective-permute-start | bytes 1179656 | tf_op jit(solution)/shard_map/ppermute | solution.py:32
  80.9 4.0 %masked_product.6.refs_6_ = f32[512,512]{1,0:T(8,128)S(1)} custom-call(s32[4]{0:T(128)S(1)} %pad_add_fusion.pos, bf16[8,512,512]{2,1,0:T(8,128)(2,1)S(1)} %copy-done.1, bf16[8,512,512]{2,1,0:T(8,128)(2,1)S(1)} %copy-done.5, bf16[4,128,384]{2,1,0:T(8,128)(2,1)S(1)} %get-tuple-element.40.refs_0_, bf16[4,128,384]{2,1,0:T(8,128)(2,1)S(1)} %collective-permute-done.4.refs_1_, ...), custom_call_target="tpu_custom_call" | custom-call | tf_op jit(solution)/shard_map/masked_product/pallas_call | solution.py:252
  87.8 6.2 %masked_product.7.refs_2_ = f32[512,512]{1,0:T(8,128)S(1)} custom-call(s32[4]{0:T(128)S(1)} %pad_add_fusion.pos, bf16[8,512,512]{2,1,0:T(8,128)(2,1)S(1)} %copy-done.1, bf16[8,512,512]{2,1,0:T(8,128)(2,1)S(1)} %copy-done.5, bf16[4,128,384]{2,1,0:T(8,128)(2,1)S(1)} %collective-permute-done.13.refs_0_, ...), custom_call_target="tpu_custom_call" | custom-call | tf_op jit(solution)/shard_map/masked_product/pallas_call | solution.py:252
  98.6 2.7 %collective-permute-start.24 = (bf16[8,128,384]{2,1,0:T(8,128)(2,1)S(1)}, bf16[8,128,384]{2,1,0:T(8,128)(2,1)S(1)}, u32[]{:S(2)}, u32[]{:S(2)}) collective-permute-start(bf16[8,128,384]{2,1,0:T(8,128)(2,1)S(1)} %bitcast.23), channel_id=1, source_target_pairs={{0,24},{1,25},{2,26},{3,27},{4,28},{5,29},{6,30},{7,31},{8,0},{9,1... | collective-permute-start | bytes 2359304 | tf_op jit(solution)/shard_map/ppermute | solution.py:27
  101.2 8.8 %collective-permute-done.20 = f32[512,128]{1,0:T(8,128)S(1)} collective-permute-done((f32[512,128]{1,0:T(8,128)S(1)}, f32[512,128]{1,0:T(8,128)S(1)}, u32[]{:S(2)}, u32[]{:S(2)}) %collective-permute-start.20) | collective-permute-done | bytes 262176 | tf_op jit(solution)/shard_map/ppermute | solution.py:37
  114.7 3.3 %collective-permute-done.29 = bf16[512,128]{1,0:T(8,128)(2,1)S(1)} collective-permute-done((bf16[512,128]{1,0:T(8,128)(2,1)S(1)}, bf16[512,128]{1,0:T(8,128)(2,1)S(1)}, u32[]{:S(2)}, u32[]{:S(2)}) %collective-permute-start.29) | collective-permute-done | bytes 131104 | tf_op jit(solution)/shard_map/ppermute | solution.py:41
  120.3 5.3 %collective-permute-start.30 = (bf16[4,512,128]{2,1,0:T(8,128)(2,1)}, bf16[4,512,128]{2,1,0:T(8,128)(2,1)}, u32[]{:S(2)}, u32[]{:S(2)}) collective-permute-start(bf16[4,512,128]{2,1,0:T(8,128)(2,1)} %pad_maximum_fusion.1.mine), channel_id=1, source_target_pairs={{0,32},{32,0},{1,33},{33,1},{2,34},{34,2},{3,35},{35,3},{4,36},{36... | collective-permute-start | bytes 1572872 | tf_op jit(solution)/shard_map/ppermute | solution.py:46
  126.4 2.8 %collective-permute-start.26 = (bf16[4,128,384]{2,1,0:T(8,128)(2,1)}, bf16[4,128,384]{2,1,0:T(8,128)(2,1)}, u32[]{:S(2)}, u32[]{:S(2)}) collective-permute-start(bf16[4,128,384]{2,1,0:T(8,128)(2,1)} %slice.43), channel_id=1, source_target_pairs={{0,24},{1,25},{2,26},{3,27},{4,28},{5,29},{6,30},{7,31},{8,0},{9,1... | collective-permute-start | bytes 1179656 | tf_op jit(solution)/shard_map/ppermute | solution.py:27
  130.0 4.7 %masked_product.9.refs_3_ = f32[512,512]{1,0:T(8,128)S(1)} custom-call(s32[4]{0:T(128)S(1)} %pad_add_fusion.pos, bf16[8,512,512]{2,1,0:T(8,128)(2,1)S(1)} %copy-done.1, bf16[8,512,512]{2,1,0:T(8,128)(2,1)S(1)} %copy-done.5, bf16[8,128,384]{2,1,0:T(8,128)(2,1)S(1)} %bitcast.25, bf16[8,128,384]{2,1,0:T(8,128)(2,1)S(1)} %collective-permute-done.23.refs_1_, ...), custom_call_target="tpu_custom_call" | custom-call | tf_op jit(solution)/shard_map/masked_product/pallas_call | solution.py:252
  134.7 3.3 %collective-permute-done.26.refs_1_.refs_4_ = bf16[4,128,384]{2,1,0:T(8,128)(2,1)} collective-permute-done((bf16[4,128,384]{2,1,0:T(8,128)(2,1)}, bf16[4,128,384]{2,1,0:T(8,128)(2,1)}, u32[]{:S(2)}, u32[]{:S(2)}) %collective-permute-start.26) | collective-permute-done | bytes 393248 | tf_op jit(solution)/shard_map/ppermute | solution.py:27
  138.0 3.9 %collective-permute-done.25.refs_0_.refs_3_ = bf16[4,128,384]{2,1,0:T(8,128)(2,1)} collective-permute-done((bf16[4,128,384]{2,1,0:T(8,128)(2,1)}, bf16[4,128,384]{2,1,0:T(8,128)(2,1)}, u32[]{:S(2)}, u32[]{:S(2)}) %collective-permute-start.25) | collective-permute-done | bytes 393248 | tf_op jit(solution)/shard_map/ppermute | solution.py:27
  147.5 5.9 %masked_product.10.refs_6_ = f32[512,512]{1,0:T(8,128)S(1)} custom-call(s32[4]{0:T(128)S(1)} %pad_add_fusion.pos, bf16[8,512,512]{2,1,0:T(8,128)(2,1)S(1)} %copy-done.2, bf16[8,512,512]{2,1,0:T(8,128)(2,1)S(1)} %copy-done.6, bf16[4,128,384]{2,1,0:T(8,128)(2,1)} %collective-permute-done.25.refs_0_.refs_3_, ...), custom_call_target="tpu_custom_call" | custom-call | tf_op jit(solution)/shard_map/masked_product/pallas_call | solution.py:252
  153.4 3.9 %carried_half.1 = (bf16[512,1024]{1,0:T(8,128)(2,1)S(1)}, bf16[512,1024]{1,0:T(8,128)(2,1)S(1)}) custom-call(s32[4]{0:T(128)S(1)} %pad_add_fusion.pos, bf16[4,512,128]{2,1,0:T(8,128)(2,1)} %pad_maximum_fusion.1.mine, bf16[4,512,128]{2,1,0:T(8,128)(2,1)} %collective-permute-done.30.other, bf16[4,128,1024]{2,1,0:T(8,128)(2,1)S(1)} %copy-done.11, ...), custom_call_target="tpu_custom_call" | custom-call | tf_op jit(solution)/shard_map/carried_half/pallas_call | solution.py:282
  157.3 4.0 %masked_product.11 = (f32[512,128]{1,0:T(8,128)S(1)}, bf16[512,128]{1,0:T(8,128)(2,1)S(1)}, bf16[512,128]{1,0:T(8,128)(2,1)S(1)}, bf16[512,128]{1,0:T(8,128)(2,1)S(1)}) custom-call(s32[4]{0:T(128)S(1)} %pad_add_fusion.pos, bf16[8,512,512]{2,1,0:T(8,128)(2,1)S(1)} %copy-done.3, bf16[8,512,512]{2,1,0:T(8,128)(2,1)S(1)} %copy-done.7, ...), custom_call_target="tpu_custom_call" | custom-call | tf_op jit(solution)/shard_map/masked_product/pallas_call | solution.py:252
  164.1 6.3 %collective-permute-done.31 = bf16[512,128]{1,0:T(8,128)(2,1)S(1)} collective-permute-done((bf16[512,128]{1,0:T(8,128)(2,1)S(1)}, bf16[512,128]{1,0:T(8,128)(2,1)S(1)}, u32[]{:S(2)}, u32[]{:S(2)}) %collective-permute-start.31) | collective-permute-done | bytes 131104 | tf_op jit(solution)/shard_map/ppermute | solution.py:37
  (123 shorter events, 56.4 us)
Async XLA Ops:
  7.2 59.6 %all-gather.4.cloned.1.call-start = ((), (), s32[]{:S(2)}) async-start(), calls=%async_computation | async-start | bytes 1179648 | tf_op jit(solution)/shard_map/all_gather | solution.py:302
  7.2 40.3 %collective-permute-start.6 = (bf16[2048,512]{1,0:T(8,128)(2,1)}, bf16[2048,512]{1,0:T(8,128)(2,1)}, u32[]{:S(2)}, u32[]{:S(2)}) collective-permute-start(bf16[2048,512]{1,0:T(8,128)(2,1)} %mine.1), channel_id=1, source_target_pairs={{0,32},{32,0},{64,96},{96,64},{128,160},{160,128},{192,224},{224,1... | collective-permute-start | bytes 6291464 | tf_op jit(solution)/shard_map/ppermute | solution.py:50
  15.2 119.5 %all-gather.6.cloned.1.call-start = ((), (), s32[]{:S(2)}) async-start(), calls=%async_computation.1 | async-start | bytes 1179648 | tf_op jit(solution)/shard_map/all_gather | solution.py:304
  15.3 16.4 %collective-permute-start.7 = (bf16[128,1024]{1,0:T(8,128)(2,1)}, bf16[128,1024]{1,0:T(8,128)(2,1)S(1)}, u32[]{:S(2)}, u32[]{:S(2)}) collective-permute-start(bf16[128,1024]{1,0:T(8,128)(2,1)} %param.11), channel_id=1, source_target_pairs={{64,0},{96,32},{65,1},{97,33},{66,2},{98,34},{67,3},{99,35},{68,4}... | collective-permute-start | bytes 786440 | tf_op jit(solution)/shard_map/ppermute | solution.py:41
  22.9 15.5 %collective-permute-start.9 = (bf16[128,1024]{1,0:T(8,128)(2,1)}, bf16[128,1024]{1,0:T(8,128)(2,1)S(1)}, u32[]{:S(2)}, u32[]{:S(2)}) collective-permute-start(bf16[128,1024]{1,0:T(8,128)(2,1)} %param.11), channel_id=1, source_target_pairs={{192,0},{224,32},{193,1},{225,33},{194,2},{226,34},{195,3},{227,35... | collective-permute-start | bytes 786440 | tf_op jit(solution)/shard_map/ppermute | solution.py:41
  24.2 14.2 %collective-permute-start.8 = (bf16[128,1024]{1,0:T(8,128)(2,1)}, bf16[128,1024]{1,0:T(8,128)(2,1)S(1)}, u32[]{:S(2)}, u32[]{:S(2)}) collective-permute-start(bf16[128,1024]{1,0:T(8,128)(2,1)} %param.11), channel_id=1, source_target_pairs={{128,0},{160,32},{129,1},{161,33},{130,2},{162,34},{131,3},{163,35... | collective-permute-start | bytes 786440 | tf_op jit(solution)/shard_map/ppermute | solution.py:41
  26.7 17.9 %collective-permute-start.5 = (bf16[4,128,384]{2,1,0:T(8,128)(2,1)S(1)}, bf16[4,128,384]{2,1,0:T(8,128)(2,1)S(1)}, u32[]{:S(2)}, u32[]{:S(2)}) collective-permute-start(bf16[4,128,384]{2,1,0:T(8,128)(2,1)S(1)} %get-tuple-element.40.refs_0_), channel_id=1, source_target_pairs={{0,7},{1,0},{2,1},{3,2},{4,3},{5,4},{6,5},{7,6},{8,15},{9,8},{10,9... | collective-permute-start | bytes 1179656 | tf_op jit(solution)/shard_map/ppermute | solution.py:32
  31.6 15.8 %collective-permute-start.4 = (bf16[4,128,384]{2,1,0:T(8,128)(2,1)S(1)}, bf16[4,128,384]{2,1,0:T(8,128)(2,1)S(1)}, u32[]{:S(2)}, u32[]{:S(2)}) collective-permute-start(bf16[4,128,384]{2,1,0:T(8,128)(2,1)S(1)} %get-tuple-element.40.refs_0_), channel_id=1, source_target_pairs={{0,1},{1,2},{2,3},{3,4},{4,5},{5,6},{6,7},{7,0},{8,9},{9,10},{10,1... | collective-permute-start | bytes 1179656 | tf_op jit(solution)/shard_map/ppermute | solution.py:32
  47.5 17.6 %collective-permute-start.12 = (bf16[4,128,1024]{2,1,0:T(8,128)(2,1)S(1)}, bf16[4,128,1024]{2,1,0:T(8,128)(2,1)S(1)}, u32[]{:S(2)}, u32[]{:S(2)}) collective-permute-start(bf16[4,128,1024]{2,1,0:T(8,128)(2,1)S(1)} %pad_maximum_fusion.factor), channel_id=1, source_target_pairs={{0,32},{32,0},{1,33},{33,1},{2,34},{34,2},{3,35},{35,3},{4,36},{36... | collective-permute-start | bytes 3145736 | tf_op jit(solution)/shard_map/ppermute | solution.py:46
  51.6 13.5 %collective-permute-start.10 = (bf16[4,128,384]{2,1,0:T(8,128)(2,1)S(1)}, bf16[4,128,384]{2,1,0:T(8,128)(2,1)S(1)}, u32[]{:S(2)}, u32[]{:S(2)}) collective-permute-start(bf16[4,128,384]{2,1,0:T(8,128)(2,1)S(1)} %collective-permute-done.4.refs_1_), channel_id=1, source_target_pairs={{0,1},{1,2},{2,3},{3,4},{4,5},{5,6},{6,7},{7,0},{8,9},{9,10},{10,1... | collective-permute-start | bytes 1179656 | tf_op jit(solution)/shard_map/ppermute | solution.py:32
  51.7 13.4 %collective-permute-start.11 = (bf16[4,128,384]{2,1,0:T(8,128)(2,1)S(1)}, bf16[4,128,384]{2,1,0:T(8,128)(2,1)S(1)}, u32[]{:S(2)}, u32[]{:S(2)}) collective-permute-start(bf16[4,128,384]{2,1,0:T(8,128)(2,1)S(1)} %collective-permute-done.5.refs_2_), channel_id=1, source_target_pairs={{0,7},{1,0},{2,1},{3,2},{4,3},{5,4},{6,5},{7,6},{8,15},{9,8},{10,9... | collective-permute-start | bytes 1179656 | tf_op jit(solution)/shard_map/ppermute | solution.py:32
  66.8 18.1 %collective-permute-start.13 = (bf16[4,128,384]{2,1,0:T(8,128)(2,1)}, bf16[4,128,384]{2,1,0:T(8,128)(2,1)S(1)}, u32[]{:S(2)}, u32[]{:S(2)}) collective-permute-start(bf16[4,128,384]{2,1,0:T(8,128)(2,1)} %copy-done.15), channel_id=1, source_target_pairs={{0,1},{1,2},{2,3},{3,4},{4,5},{5,6},{6,7},{7,0},{8,9},{9,10},{10,1... | collective-permute-start | bytes 1179656 | tf_op jit(solution)/shard_map/ppermute | solution.py:32
  66.8 18.1 %collective-permute-start.14 = (bf16[4,128,384]{2,1,0:T(8,128)(2,1)}, bf16[4,128,384]{2,1,0:T(8,128)(2,1)S(1)}, u32[]{:S(2)}, u32[]{:S(2)}) collective-permute-start(bf16[4,128,384]{2,1,0:T(8,128)(2,1)} %copy-done.17), channel_id=1, source_target_pairs={{0,7},{1,0},{2,1},{3,2},{4,3},{5,4},{6,5},{7,6},{8,15},{9,8},{10,9... | collective-permute-start | bytes 1179656 | tf_op jit(solution)/shard_map/ppermute | solution.py:32
  70.5 17.3 %collective-permute-start.19 = (bf16[8,128,128]{2,1,0:T(8,128)(2,1)S(1)}, bf16[8,128,128]{2,1,0:T(8,128)(2,1)S(1)}, u32[]{:S(2)}, u32[]{:S(2)}) collective-permute-start(bf16[8,128,128]{2,1,0:T(8,128)(2,1)S(1)} %bitcast.28), channel_id=1, source_target_pairs={{0,16},{1,17},{2,18},{3,19},{4,20},{5,21},{6,22},{7,23},{8,24},{9,... | collective-permute-start | bytes 786440 | tf_op jit(solution)/shard_map/ppermute | solution.py:27
  72.9 14.9 %collective-permute-start.18 = (bf16[8,128,128]{2,1,0:T(8,128)(2,1)S(1)}, bf16[8,128,128]{2,1,0:T(8,128)(2,1)S(1)}, u32[]{:S(2)}, u32[]{:S(2)}) collective-permute-start(bf16[8,128,128]{2,1,0:T(8,128)(2,1)S(1)} %bitcast.29), channel_id=1, source_target_pairs={{0,24},{1,25},{2,26},{3,27},{4,28},{5,29},{6,30},{7,31},{8,0},{9,1... | collective-permute-start | bytes 786440 | tf_op jit(solution)/shard_map/ppermute | solution.py:27
  74.5 13.3 %collective-permute-start.17 = (bf16[8,128,128]{2,1,0:T(8,128)(2,1)S(1)}, bf16[8,128,128]{2,1,0:T(8,128)(2,1)S(1)}, u32[]{:S(2)}, u32[]{:S(2)}) collective-permute-start(bf16[8,128,128]{2,1,0:T(8,128)(2,1)S(1)} %bitcast.30), channel_id=1, source_target_pairs={{0,8},{1,9},{2,10},{3,11},{4,12},{5,13},{6,14},{7,15},{8,16},{9,17... | collective-permute-start | bytes 786440 | tf_op jit(solution)/shard_map/ppermute | solution.py:27
  95.8 14.2 %collective-permute-start.20 = (f32[512,128]{1,0:T(8,128)S(1)}, f32[512,128]{1,0:T(8,128)S(1)}, u32[]{:S(2)}, u32[]{:S(2)}) collective-permute-start(f32[512,128]{1,0:T(8,128)S(1)} %get-tuple-element.62), channel_id=1, source_target_pairs={{0,64},{32,96},{64,128},{96,160},{128,192},{160,224},{192,0},{224,... | collective-permute-start | bytes 786440 | tf_op jit(solution)/shard_map/ppermute | solution.py:37
  95.9 14.1 %collective-permute-start.21 = (f32[512,128]{1,0:T(8,128)S(1)}, f32[512,128]{1,0:T(8,128)S(1)}, u32[]{:S(2)}, u32[]{:S(2)}) collective-permute-start(f32[512,128]{1,0:T(8,128)S(1)} %get-tuple-element.63), channel_id=1, source_target_pairs={{0,128},{32,160},{64,192},{96,224},{128,0},{160,32},{192,64},{224,... | collective-permute-start | bytes 786440 | tf_op jit(solution)/shard_map/ppermute | solution.py:37
  96.5 13.5 %collective-permute-start.22 = (f32[512,128]{1,0:T(8,128)S(1)}, f32[512,128]{1,0:T(8,128)S(1)}, u32[]{:S(2)}, u32[]{:S(2)}) collective-permute-start(f32[512,128]{1,0:T(8,128)S(1)} %get-tuple-element.64), channel_id=1, source_target_pairs={{0,192},{32,224},{64,0},{96,32},{128,64},{160,96},{192,128},{224,1... | collective-permute-start | bytes 786440 | tf_op jit(solution)/shard_map/ppermute | solution.py:37
  98.6 27.0 %collective-permute-start.24 = (bf16[8,128,384]{2,1,0:T(8,128)(2,1)S(1)}, bf16[8,128,384]{2,1,0:T(8,128)(2,1)S(1)}, u32[]{:S(2)}, u32[]{:S(2)}) collective-permute-start(bf16[8,128,384]{2,1,0:T(8,128)(2,1)S(1)} %bitcast.23), channel_id=1, source_target_pairs={{0,24},{1,25},{2,26},{3,27},{4,28},{5,29},{6,30},{7,31},{8,0},{9,1... | collective-permute-start | bytes 2359304 | tf_op jit(solution)/shard_map/ppermute | solution.py:27
  101.2 27.9 %collective-permute-start.23 = (bf16[8,128,384]{2,1,0:T(8,128)(2,1)S(1)}, bf16[8,128,384]{2,1,0:T(8,128)(2,1)S(1)}, u32[]{:S(2)}, u32[]{:S(2)}) collective-permute-start(bf16[8,128,384]{2,1,0:T(8,128)(2,1)S(1)} %bitcast.24), channel_id=1, source_target_pairs={{0,8},{1,9},{2,10},{3,11},{4,12},{5,13},{6,14},{7,15},{8,16},{9,17... | collective-permute-start | bytes 2359304 | tf_op jit(solution)/shard_map/ppermute | solution.py:27
  120.3 33.1 %collective-permute-start.30 = (bf16[4,512,128]{2,1,0:T(8,128)(2,1)}, bf16[4,512,128]{2,1,0:T(8,128)(2,1)}, u32[]{:S(2)}, u32[]{:S(2)}) collective-permute-start(bf16[4,512,128]{2,1,0:T(8,128)(2,1)} %pad_maximum_fusion.1.mine), channel_id=1, source_target_pairs={{0,32},{32,0},{1,33},{33,1},{2,34},{34,2},{3,35},{35,3},{4,36},{36... | collective-permute-start | bytes 1572872 | tf_op jit(solution)/shard_map/ppermute | solution.py:46
  126.4 11.6 %collective-permute-start.26 = (bf16[4,128,384]{2,1,0:T(8,128)(2,1)}, bf16[4,128,384]{2,1,0:T(8,128)(2,1)}, u32[]{:S(2)}, u32[]{:S(2)}) collective-permute-start(bf16[4,128,384]{2,1,0:T(8,128)(2,1)} %slice.43), channel_id=1, source_target_pairs={{0,24},{1,25},{2,26},{3,27},{4,28},{5,29},{6,30},{7,31},{8,0},{9,1... | collective-permute-start | bytes 1179656 | tf_op jit(solution)/shard_map/ppermute | solution.py:27
  130.0 11.9 %collective-permute-start.25 = (bf16[4,128,384]{2,1,0:T(8,128)(2,1)}, bf16[4,128,384]{2,1,0:T(8,128)(2,1)}, u32[]{:S(2)}, u32[]{:S(2)}) collective-permute-start(bf16[4,128,384]{2,1,0:T(8,128)(2,1)} %slice.42), channel_id=1, source_target_pairs={{0,8},{1,9},{2,10},{3,11},{4,12},{5,13},{6,14},{7,15},{8,16},{9,17... | collective-permute-start | bytes 1179656 | tf_op jit(solution)/shard_map/ppermute | solution.py:27
  (36 other events, 242.0 us)
Sparse Core Ops, SparseCore 0:
  15.3 37.0 all-gather.3
  69.6 33.2 all-gather.5

commit v5 on v0

v5 whole, which is shorter than its diff:
```python
import functools

import jax
import jax.numpy as jnp
from jax import lax
from jax.experimental import pallas as pl
from jax.experimental.pallas import tpu as pltpu
from jax.sharding import PartitionSpec as P

BLK = 256
NX, NZ, NY = 4, 8, 4
SUB = 64
PAIR = 2 * SUB
HALF = 512
F32, BF16 = jnp.float32, jnp.bfloat16
VMEM = pl.BlockSpec(memory_space=pltpu.VMEM)
SMEM = pl.BlockSpec(memory_space=pltpu.SMEM)
ANY = pl.BlockSpec(memory_space=pl.ANY)
BIG = pltpu.CompilerParams(vmem_limit_bytes=24 * 2**20)
SMALL = pltpu.CompilerParams(vmem_limit_bytes=16 * 2**20)


def x_shift(value, dx):
    pairs = [(x * NZ + z, (x + dx) % NX * NZ + z) for x in range(NX) for z in range(NZ)]
    return lax.ppermute(value, "col", pairs)


def z_shift(value, dz):
    pairs = [(x * NZ + z, x * NZ + (z + dz) % NZ) for x in range(NX) for z in range(NZ)]
    return lax.ppermute(value, "col", pairs)


def y_shift(value, dy):
    pairs = [(y * 2 + k, (y + dy) % NY * 2 + k) for y in range(NY) for k in range(2)]
    return lax.ppermute(value, "row", pairs)


def y_first(value, y):
    return lax.ppermute(value, "row", [(k, y * 2 + k) for k in range(2)])


def y_all(value):
    return jnp.stack([value] + [y_shift(value, d) for d in range(1, NY)])


def core_swap(value):
    return lax.ppermute(value, "row", [(r, r ^ 1) for r in range(2 * NY)])


def together(*values):
    return lax.optimization_barrier(values)


def offset(n):
    return ((n + 1) // 2) * (1 - 2 * (n % 2))


def source(pos, i, j):
    return (pos[0] + offset(i) + NX) % NX, (pos[1] + offset(j) + NZ) % NZ


def pack_kernel(pos, two, one, own, give):
    first = pos[3] == 0
    for q in range(NY):
        at = slice(q * 128, q * 128 + 128)
        for n, panel in enumerate((two, one)):
            left = panel[:, q * 256:q * 256 + 128]
            right = panel[:, q * 256 + 128:q * 256 + 256]
            own[n, :, at] = jnp.where(first, left, right)
            give[n, :, at] = jnp.where(first, right, left)


def pack(pos, two, one):
    return pl.pallas_call(
        pack_kernel,
        out_shape=(jax.ShapeDtypeStruct((2, SUB, HALF), BF16),) * 2,
        in_specs=[SMEM, VMEM, VMEM],
        out_specs=(VMEM, VMEM),
        compiler_params=SMALL,
        name="pack_columns",
    )(pos, two, one)


def join_kernel(picks, *refs):
    for n, pick in enumerate(picks):
        refs[-1][n] = refs[n][...] if pick is None else refs[n][pick]


def join(parts, picks):
    return pl.pallas_call(
        functools.partial(join_kernel, picks),
        out_shape=jax.ShapeDtypeStruct((len(parts), PAIR, HALF), BF16),
        in_specs=[VMEM] * len(parts),
        out_specs=VMEM,
        compiler_params=SMALL,
        name="join_parts",
    )(*parts)


def prepare_kernel(pos, taper, mine, other, out, rows):
    lane = lax.broadcasted_iota(jnp.int32, (SUB, 2 * BLK), 1)
    first_col = (pos[0] * NZ + pos[1]) * 2

    def block(j, carry):
        for i in range(NX):
            x, z = source(pos, i, j)
            row = pl.multiple_of((x * NZ + z) * SUB, SUB)
            for h, ref in enumerate((mine, other)):
                core = pos[3] if h == 0 else 1 - pos[3]
                tile = (pos[2] * 2 + core) * 8 + x * 2 + z // 4
                left = taper[tile, first_col].astype(F32)
                right = taper[tile, first_col + 1].astype(F32)
                keep = jnp.where(lane < BLK, left, right)
                at = i * PAIR + h * SUB
                rows[at:at + SUB, :] = (ref[pl.ds(row, SUB), :].astype(F32) * keep).astype(BF16)
        out[j] = rows[...].T
        return carry

    lax.fori_loop(0, NZ, block, 0)


def prepare(pos, taper, mine, other):
    return pl.pallas_call(
        prepare_kernel,
        out_shape=jax.ShapeDtypeStruct((NZ, 512, 512), BF16),
        in_specs=[SMEM, SMEM, VMEM, VMEM],
        out_specs=VMEM,
        scratch_shapes=[pltpu.VMEM((512, 512), BF16)],
        compiler_params=SMALL,
        name="prepare_adjoint",
    )(pos, taper, mine, other)


def product_kernel(count, items, first, last, pos, adjoint, *refs):
    panels, refs = refs[:count], list(refs[count:])
    before = None if first else refs.pop(0)
    outs = [refs.pop(0) for _ in range(NY)] if last else None
    total, held, sems = refs
    for n, (_, parts) in enumerate(items):
        to = 0
        for index, start, size in parts:
            pltpu.make_async_copy(
                panels[index].at[pl.ds(start, size)], held.at[n, pl.ds(to, size)], sems.at[n]).start()
            to += size
    if first:
        total[...] = jnp.zeros_like(total)
    else:
        total[...] = before[...]
    begin = items[0][0]

    def step(n, carry):
        pltpu.make_async_copy(held.at[n], held.at[n], sems.at[n]).wait()
        total[...] += jnp.dot(
            adjoint[begin + n], held[n].reshape(NX * PAIR, HALF), preferred_element_type=F32)
        return carry

    lax.fori_loop(0, len(items), step, 0)
    if last:
        for d, out in enumerate(outs):
            column = pl.multiple_of((pos[2] + d) % NY * 128, 128)
            out[...] = (-2.0 * total[:, pl.ds(column, 128)]).astype(out.dtype)


def product(pos, adjoint, panels, items, before=None, kind=None):
    last = kind is not None
    column = jax.ShapeDtypeStruct((512, 128), F32)
    scratch = [pltpu.VMEM((512, HALF), F32)] if last else []
    scratch += [
        pltpu.VMEM((len(items), NX, PAIR, HALF), BF16),
        pltpu.SemaphoreType.DMA((len(items),)),
    ]
    extra = [] if before is None else [before]
    kernel = functools.partial(product_kernel, len(panels), tuple(items), before is None, last)
    return pl.pallas_call(
        kernel,
        out_shape=(column,) + (jax.ShapeDtypeStruct((512, 128), kind),) * 3
        if last else jax.ShapeDtypeStruct((512, HALF), F32),
        in_specs=[SMEM, VMEM] + [ANY] * len(panels) + [VMEM] * len(extra),
        out_specs=(VMEM,) * 4 if last else VMEM,
        scratch_shapes=scratch,
        compiler_params=SMALL,
        name="masked_product",
    )(pos, adjoint, *panels, *extra)


def diagonal_kernel(where, pos, *refs):
    panels, outs, held, sem = refs[:-6], refs[-6:-2], refs[-2], refs[-1]
    half = jnp.where(pos[3] == 0, 0, SUB)

    @pl.when(pos[2] == 0)
    def _():
        for i in range(NX):
            x = source(pos, i, 0)[0]

            @pl.when(x < 2)
            def _(i=i, x=x):
                for j in range(NZ):
                    index, at = where[i][j]
                    z = source(pos, i, j)[1]
                    pltpu.make_async_copy(
                        panels[index].at[at, pl.ds(half, SUB), :], held.at[x * NZ + z], sem.at[0]
                    ).start()

        pltpu.make_async_copy(held, held, sem.at[0]).wait()
        for d, out in enumerate(outs):
            out[...] = held[:, :, d * 128:(d + 1) * 128].reshape(2 * NZ * SUB, 128)


def diagonal(pos, panels, where):
    return pl.pallas_call(
        functools.partial(diagonal_kernel, where),
        out_shape=(jax.ShapeDtypeStruct((1024, 128), BF16),) * 4,
        in_specs=[SMEM] + [ANY] * len(panels),
        out_specs=(VMEM,) * 4,
        scratch_shapes=[pltpu.VMEM((2 * NZ, SUB, HALF), BF16), pltpu.SemaphoreType.DMA((1,))],
        compiler_params=SMALL,
        name="diagonal_columns",
    )(pos, *panels)


def factor_kernel(pos, inverse, inverse_other, own, one, two, three, out, out_other):
    sent = (one[...] + two[...]) + three[...]
    columns = jnp.where(pos[2] == 0, own[...], sent)
    for left, result in ((inverse, out), (inverse_other, out_other)):
        def block(d, carry, left=left, result=result):
            value = jnp.dot(left[d], columns, preferred_element_type=F32)
            high = value.astype(BF16)
            result[d, :, :128] = high
            result[d, :, 128:] = (value - high.astype(F32)).astype(BF16)
            return carry

        lax.fori_loop(0, NY, block, 0)


def factor(pos, inverse, inverse_other, parts):
    return pl.pallas_call(
        factor_kernel,
        out_shape=(jax.ShapeDtypeStruct((NY, 128, 256), BF16),) * 2,
        in_specs=[SMEM] + [VMEM] * 6,
        out_specs=(VMEM, VMEM),
        compiler_params=SMALL,
        name="inverse_times_diagonal",
    )(pos, inverse, inverse_other, *parts)


def carried_kernel(mine, other, factors, factors_other, out, total):
    total[...] = jnp.zeros_like(total)

    def block(d, carry):
        left = jnp.concatenate([mine[d], other[d]], axis=1)
        right = jnp.concatenate([factors[d], factors_other[d]], axis=0)
        total[...] += jnp.dot(left, right, preferred_element_type=F32)
        return carry

    lax.fori_loop(0, NY, block, 0)
    out[...] = total[:, :128] + total[:, 128:]


def carried(mine, other, factors, factors_other):
    return pl.pallas_call(
        carried_kernel,
        out_shape=jax.ShapeDtypeStruct((512, 128), F32),
        in_specs=[VMEM] * 4,
        out_specs=VMEM,
        scratch_shapes=[pltpu.VMEM((512, 256), F32)],
        compiler_params=SMALL,
        name="carried_term",
    )(mine, other, factors, factors_other)


def local(adjoint, taper, panel_two, panel_one, incoming, inverse_factor):
    row, col = lax.axis_index("row"), lax.axis_index("col")
    pos = jnp.stack([col // NZ, col % NZ, row // 2, row % 2]).astype(jnp.int32)

    own, give = pack(pos, panel_two, panel_one)
    taken = core_swap(give)
    shards = jnp.concatenate([own, taken], axis=1)

    first_x = [shards] + [x_shift(shards, d) for d in (1, -1, 2)]
    own = join(first_x + [shards], (0, 0, 0, 0, 1))
    inverse = y_all(inverse_factor)
    down1, up1, inverse, swapped = together(
        z_shift(own, 1), z_shift(own, -1), inverse, core_swap(adjoint))

    def x_others(*messages):
        part = join(messages, (4,) * len(messages)) if len(messages) > 1 else messages[0][-1:]
        return [part] + [x_shift(part, d) for d in (1, -1, 2)]

    masked = prepare(pos, taper, adjoint, swapped)
    down2, up2, masked, inverse_other, *near = together(
        z_shift(down1, 1), z_shift(up1, -1), masked, core_swap(inverse), *x_others(down1, up1))
    sums = product(
        pos, masked, [own, down1, up1, down2, up2], [(j, [(j, 0, 4)]) for j in range(5)])
    down3, up3, sums, *middle = together(
        z_shift(down2, 1), z_shift(up2, -1), sums, *x_others(down2, up2))
    sums = product(pos, masked, [down3, up3], [(5 + j, [(j, 0, 4)]) for j in range(2)], sums)
    sums_one = product(
        pos, masked, first_x + near + middle,
        [(0, [(i, 1, 1) for i in range(NX)])]
        + [(1 + j, [(NX * (1 + j // 2) + i, j % 2, 1) for i in range(NX)]) for j in range(4)])
    far_low, far_high, sums, sums_one, *third = together(
        z_shift(down3[:2], 1), z_shift(up3[2:], -1), sums, sums_one, *x_others(down3, up3))
    last = x_others(far_high)

    mine, *sent = product(
        pos, masked, [far_low, far_high], [(7, [(0, 0, 2), (1, 0, 2)])], sums, F32)
    r1, r2, r3 = [y_shift(part, d + 1) for d, part in enumerate(sent)]
    second_grad = incoming + ((mine + r1) + (r2 + r3))
    rounded = y_all(second_grad.astype(BF16))
    rounded_other = core_swap(rounded)

    where = tuple(
        ((i, 1),) + tuple((NX * (1 + j // 2) + i, j % 2) for j in range(7)) for i in range(NX))
    first, *rest = diagonal(pos, first_x + near + middle + third + last, where)
    rest = [y_first(part, d + 1) for d, part in enumerate(rest)]
    mine, *sent = product(
        pos, masked, third + last,
        [(5 + j, [(NX * (j // 2) + i, j % 2, 1) for i in range(NX)]) for j in range(3)],
        sums_one, BF16)
    r1, r2, r3 = [y_shift(part, d + 1).astype(F32) for d, part in enumerate(sent)]
    factors = factor(pos, inverse, inverse_other, [first] + rest)
    term = carried(rounded, rounded_other, *factors)
    return second_grad, (mine + r1) + (r2 + r3) - term


def solution(mesh):
    in_specs = (
        P("row", "col"),
        P(),
        P(("row", "col"), None),
        P(("row", "col"), None),
        P("col", "row"),
        P("row", None),
    )
    out_specs = (P("col", "row"), P("col", "row"))
    return jax.shard_map(local, mesh=mesh, in_specs=in_specs, out_specs=out_specs, check_vma=False)
```

time: 405 us -> 152 us (0.38)
  the two profiles are of different devices: /device:TPU:1 before, /device:TPU:16 now
where the time goes in v5:
time: 152 us
  waiting for transfers between devices  63.3 us (42%)
  starting transfers between devices  60.3 us (40%)
  Pallas kernels  23.9 us (16%)
  local copies, waits for them, and re-layouts  1.91 us (1%)
  other arithmetic  1.83 us (1%)
    ppermute x15, waiting for transfers between devices, x_shift(): return lax.ppermute(value, 'col', pairs)  29.3 us
    ppermute x15, starting transfers between devices, x_shift(): return lax.ppermute(value, 'col', pairs)  25.2 us
    ppermute x12, waiting for transfers between devices, y_shift(): return lax.ppermute(value, 'row', pairs)  19.6 us
    ppermute x12, starting transfers between devices, y_shift(): return lax.ppermute(value, 'row', pairs)  16.4 us
    pallas_call x5, Pallas kernels, product(): pl.pallas_call(kernel, out_shape=(column,) + (jax.ShapeDtypeStruct((512,...  16.2 us
    ppermute x8, starting transfers between devices, z_shift(): return lax.ppermute(value, 'col', pairs)  15.4 us
    ppermute x8, waiting for transfers between devices, z_shift(): return lax.ppermute(value, 'col', pairs)  7.83 us
    ppermute x3, waiting for transfers between devices, y_first(): return lax.ppermute(value, 'row', [(k, y * 2 + k) for k in range(2)])  5.26 us
  transfers between devices with their start and end apart: 42, of which 23 were waited for; matrix products, arithmetic and copies ran while one was open for 0% of the time, Pallas kernels for 15%

profile of v5, /device:TPU:16, one launch (start us, length us, event | category | flops | bytes accessed | tf_op | source)
XLA Modules:
  0.0 152.2 jit_solution(3481152343219166350)
XLA Ops:
  5.1 3.1 %collective-permute-start.3 = (bf16[2,128,512]{2,1,0:T(8,128)(2,1)S(1)}, bf16[2,128,512]{2,1,0:T(8,128)(2,1)S(1)}, u32[]{:S(2)}, u32[]{:S(2)}) collective-permute-start(bf16[2,128,512]{2,1,0:T(8,128)(2,1)S(1)} %constant_dynamic-update-slice_fusion.refs_0_.refs_4_), channel_id=1, source_target_pairs={{0,16},{1,17},{2,18},{3,19},{4,20},{5,21},{6,22},{7,23},{8,24},{9,... | collective-permute-start | bytes 786440 | tf_op jit(solution)/shard_map/ppermute | solution.py:25
  11.5 4.3 %collective-permute-done.3.refs_3_ = bf16[2,128,512]{2,1,0:T(8,128)(2,1)S(1)} collective-permute-done((bf16[2,128,512]{2,1,0:T(8,128)(2,1)S(1)}, bf16[2,128,512]{2,1,0:T(8,128)(2,1)S(1)}, u32[]{:S(2)}, u32[]{:S(2)}) %collective-permute-start.3) | collective-permute-done | bytes 262176 | tf_op jit(solution)/shard_map/ppermute | solution.py:25
  15.8 4.9 %collective-permute-done.2.refs_2_ = bf16[2,128,512]{2,1,0:T(8,128)(2,1)S(1)} collective-permute-done((bf16[2,128,512]{2,1,0:T(8,128)(2,1)S(1)}, bf16[2,128,512]{2,1,0:T(8,128)(2,1)S(1)}, u32[]{:S(2)}, u32[]{:S(2)}) %collective-permute-start.2) | collective-permute-done | bytes 262176 | tf_op jit(solution)/shard_map/ppermute | solution.py:25
  20.8 5.9 %collective-permute-start.5 = (bf16[5,128,512]{2,1,0:T(8,128)(2,1)S(1)}, bf16[5,128,512]{2,1,0:T(8,128)(2,1)S(1)}, u32[]{:S(2)}, u32[]{:S(2)}) collective-permute-start(bf16[5,128,512]{2,1,0:T(8,128)(2,1)S(1)} %join_parts.4.refs_0_), channel_id=1, source_target_pairs={{0,7},{1,0},{2,1},{3,2},{4,3},{5,4},{6,5},{7,6},{8,15},{9,8},{10,9... | collective-permute-start | bytes 1966088 | tf_op jit(solution)/shard_map/ppermute | solution.py:30
  27.2 2.9 %collective-permute-start.7 = (bf16[128,1024]{1,0:T(8,128)(2,1)S(1)}, bf16[128,1024]{1,0:T(8,128)(2,1)S(1)}, u32[]{:S(2)}, u32[]{:S(2)}) collective-permute-start(bf16[128,1024]{1,0:T(8,128)(2,1)S(1)} %copy-done.5), channel_id=1, source_target_pairs={{0,128},{32,160},{64,192},{96,224},{128,0},{160,32},{192,64},{224,... | collective-permute-start | bytes 786440 | tf_op jit(solution)/shard_map/ppermute | solution.py:35
  30.1 5.9 %collective-permute-done.8 = bf16[128,1024]{1,0:T(8,128)(2,1)S(1)} collective-permute-done((bf16[128,1024]{1,0:T(8,128)(2,1)S(1)}, bf16[128,1024]{1,0:T(8,128)(2,1)S(1)}, u32[]{:S(2)}, u32[]{:S(2)}) %collective-permute-start.8) | collective-permute-done | bytes 262176 | tf_op jit(solution)/shard_map/ppermute | solution.py:35
  36.4 4.4 %collective-permute-done.5.refs_1_.refs_2_ = bf16[5,128,512]{2,1,0:T(8,128)(2,1)S(1)} collective-permute-done((bf16[5,128,512]{2,1,0:T(8,128)(2,1)S(1)}, bf16[5,128,512]{2,1,0:T(8,128)(2,1)S(1)}, u32[]{:S(2)}, u32[]{:S(2)}) %collective-permute-start.5) | collective-permute-done | bytes 655392 | tf_op jit(solution)/shard_map/ppermute | solution.py:30
  40.8 3.4 %collective-permute-done.4.refs_0_.refs_1_ = bf16[5,128,512]{2,1,0:T(8,128)(2,1)S(1)} collective-permute-done((bf16[5,128,512]{2,1,0:T(8,128)(2,1)S(1)}, bf16[5,128,512]{2,1,0:T(8,128)(2,1)S(1)}, u32[]{:S(2)}, u32[]{:S(2)}) %collective-permute-start.4) | collective-permute-done | bytes 655392 | tf_op jit(solution)/shard_map/ppermute | solution.py:30
  44.2 3.2 %collective-permute-start.11 = (bf16[5,128,512]{2,1,0:T(8,128)(2,1)S(1)}, bf16[5,128,512]{2,1,0:T(8,128)(2,1)S(1)}, u32[]{:S(2)}, u32[]{:S(2)}) collective-permute-start(bf16[5,128,512]{2,1,0:T(8,128)(2,1)S(1)} %collective-permute-done.5.refs_1_.refs_2_), channel_id=1, source_target_pairs={{0,7},{1,0},{2,1},{3,2},{4,3},{5,4},{6,5},{7,6},{8,15},{9,8},{10,9... | collective-permute-start | bytes 1966088 | tf_op jit(solution)/shard_map/ppermute | solution.py:30
  47.5 3.1 %collective-permute-start.15 = (bf16[2,128,512]{2,1,0:T(8,128)(2,1)S(1)}, bf16[2,128,512]{2,1,0:T(8,128)(2,1)S(1)}, u32[]{:S(2)}, u32[]{:S(2)}) collective-permute-start(bf16[2,128,512]{2,1,0:T(8,128)(2,1)S(1)} %join_parts.5.refs_4_), channel_id=1, source_target_pairs={{0,16},{1,17},{2,18},{3,19},{4,20},{5,21},{6,22},{7,23},{8,24},{9,... | collective-permute-start | bytes 786440 | tf_op jit(solution)/shard_map/ppermute | solution.py:25
  51.7 5.5 %collective-permute-done.15.refs_7_ = bf16[2,128,512]{2,1,0:T(8,128)(2,1)S(1)} collective-permute-done((bf16[2,128,512]{2,1,0:T(8,128)(2,1)S(1)}, bf16[2,128,512]{2,1,0:T(8,128)(2,1)S(1)}, u32[]{:S(2)}, u32[]{:S(2)}) %collective-permute-start.15) | collective-permute-done | bytes 262176 | tf_op jit(solution)/shard_map/ppermute | solution.py:25
  59.8 2.9 %prepare_adjoint.1.adjoint = bf16[8,512,512]{2,1,0:T(8,128)(2,1)S(1)} custom-call(s32[4]{0:T(128)S(1)} %pad_add_fusion.pos, s32[64,64]{1,0:T(8,128)S(1)} %copy-done.3, bf16[2048,512]{1,0:T(8,128)(2,1)S(1)} %copy-done, bf16[2048,512]{1,0:T(8,128)(2,1)S(1)} %collective-permute-done.9.other), custom_call_target="tpu_custom_call" | custom-call | tf_op jit(solution)/shard_map/prepare_adjoint/pallas_call | solution.py:123
  63.0 2.8 %collective-permute-done.13.refs_5_ = bf16[2,128,512]{2,1,0:T(8,128)(2,1)S(1)} collective-permute-done((bf16[2,128,512]{2,1,0:T(8,128)(2,1)S(1)}, bf16[2,128,512]{2,1,0:T(8,128)(2,1)S(1)}, u32[]{:S(2)}, u32[]{:S(2)}) %collective-permute-start.13) | collective-permute-done | bytes 262176 | tf_op jit(solution)/shard_map/ppermute | solution.py:25
  66.0 3.2 %collective-permute-start.17 = (bf16[5,128,512]{2,1,0:T(8,128)(2,1)S(1)}, bf16[5,128,512]{2,1,0:T(8,128)(2,1)S(1)}, u32[]{:S(2)}, u32[]{:S(2)}) collective-permute-start(bf16[5,128,512]{2,1,0:T(8,128)(2,1)S(1)} %collective-permute-done.11.refs_4_.refs_1_), channel_id=1, source_target_pairs={{0,7},{1,0},{2,1},{3,2},{4,3},{5,4},{6,5},{7,6},{8,15},{9,8},{10,9... | collective-permute-start | bytes 1966088 | tf_op jit(solution)/shard_map/ppermute | solution.py:30
  73.2 3.0 %masked_product.5.refs_2_ = f32[512,512]{1,0:T(8,128)S(1)} custom-call(s32[4]{0:T(128)S(1)} %pad_add_fusion.pos, bf16[8,512,512]{2,1,0:T(8,128)(2,1)S(1)} %prepare_adjoint.1.adjoint, bf16[5,128,512]{2,1,0:T(8,128)(2,1)S(1)} %join_parts.4.refs_0_, bf16[5,128,512]{2,1,0:T(8,128)(2,1)S(1)} %collective-permute-done.4.refs_0_.refs_1_, ...), custom_call_target="tpu_custom_call" | custom-call | tf_op jit(solution)/shard_map/masked_product/pallas_call | solution.py:174
  76.3 2.8 %collective-permute-done.20.refs_11_ = bf16[2,128,512]{2,1,0:T(8,128)(2,1)S(1)} collective-permute-done((bf16[2,128,512]{2,1,0:T(8,128)(2,1)S(1)}, bf16[2,128,512]{2,1,0:T(8,128)(2,1)S(1)}, u32[]{:S(2)}, u32[]{:S(2)}) %collective-permute-start.20) | collective-permute-done | bytes 262176 | tf_op jit(solution)/shard_map/ppermute | solution.py:25
  81.8 2.7 %collective-permute-start.22 = (bf16[3,128,512]{2,1,0:T(8,128)(2,1)S(1)}, bf16[3,128,512]{2,1,0:T(8,128)(2,1)S(1)}, u32[]{:S(2)}, u32[]{:S(2)}) collective-permute-start(bf16[3,128,512]{2,1,0:T(8,128)(2,1)S(1)} %slice.10), channel_id=1, source_target_pairs={{0,7},{1,0},{2,1},{3,2},{4,3},{5,4},{6,5},{7,6},{8,15},{9,8},{10,9... | collective-permute-start | bytes 1179656 | tf_op jit(solution)/shard_map/ppermute | solution.py:30
  90.8 6.2 %masked_product.7.refs_8_ = f32[512,512]{1,0:T(8,128)S(1)} custom-call(s32[4]{0:T(128)S(1)} %pad_add_fusion.pos, bf16[8,512,512]{2,1,0:T(8,128)(2,1)S(1)} %prepare_adjoint.1.adjoint, bf16[2,128,512]{2,1,0:T(8,128)(2,1)S(1)} %constant_dynamic-update-slice_fusion.refs_0_.refs_4_, bf16[2,128,512]{2,1,0:T(8,128)(2,1)S(1)} %collective-permute-done.1.refs_1_, ...), custom_call_target="tpu_custom_call" | custom-call | tf_op jit(solution)/shard_map/masked_product/pallas_call | solution.py:174
  102.3 9.3 %collective-permute-done.26 = f32[512,128]{1,0:T(8,128)S(1)} collective-permute-done((f32[512,128]{1,0:T(8,128)S(1)}, f32[512,128]{1,0:T(8,128)S(1)}, u32[]{:S(2)}, u32[]{:S(2)}) %collective-permute-start.26) | collective-permute-done | bytes 262176 | tf_op jit(solution)/shard_map/ppermute | solution.py:35
  126.0 2.7 %collective-permute-done.29.refs_5_.refs_17_ = bf16[1,128,512]{2,1,0:T(8,128)(2,1)S(1)} collective-permute-done((bf16[1,128,512]{2,1,0:T(8,128)(2,1)S(1)}, bf16[1,128,512]{2,1,0:T(8,128)(2,1)S(1)}, u32[]{:S(2)}, u32[]{:S(2)}) %collective-permute-start.29) | collective-permute-done | bytes 131104 | tf_op jit(solution)/shard_map/ppermute | solution.py:25
  132.0 4.1 %masked_product.9 = (f32[512,128]{1,0:T(8,128)S(1)}, bf16[512,128]{1,0:T(8,128)(2,1)S(1)}, bf16[512,128]{1,0:T(8,128)(2,1)S(1)}, bf16[512,128]{1,0:T(8,128)(2,1)S(1)}) custom-call(s32[4]{0:T(128)S(1)} %pad_add_fusion.pos, bf16[8,512,512]{2,1,0:T(8,128)(2,1)S(1)} %prepare_adjoint.1.adjoint, bf16[2,128,512]{2,1,0:T(8,128)(2,1)S(1)} %join_parts.7.refs_0_.refs_12_, ...), custom_call_target="tpu_custom_call" | custom-call | tf_op jit(solution)/shard_map/masked_product/pallas_call | solution.py:174
  138.0 3.2 %collective-permute-start.33 = (bf16[512,128]{1,0:T(8,128)(2,1)S(1)}, bf16[512,128]{1,0:T(8,128)(2,1)S(1)}, u32[]{:S(2)}, u32[]{:S(2)}) collective-permute-start(bf16[512,128]{1,0:T(8,128)(2,1)S(1)} %get-tuple-element.79), channel_id=1, source_target_pairs={{0,128},{32,160},{64,192},{96,224},{128,0},{160,32},{192,64},{224,... | collective-permute-start | bytes 393224 | tf_op jit(solution)/shard_map/ppermute | solution.py:35
  141.2 5.3 %collective-permute-done.40.two = bf16[1024,128]{1,0:T(8,128)(2,1)S(1)} collective-permute-done((bf16[1024,128]{1,0:T(8,128)(2,1)S(1)}, bf16[1024,128]{1,0:T(8,128)(2,1)S(1)}, u32[]{:S(2)}, u32[]{:S(2)}) %collective-permute-start.40) | collective-permute-done | bytes 262176 | tf_op jit(solution)/shard_map/ppermute | solution.py:39
  146.5 2.6 %inverse_times_diagonal.1 = (bf16[4,128,256]{2,1,0:T(8,128)(2,1)S(1)}, bf16[4,128,256]{2,1,0:T(8,128)(2,1)S(1)}) custom-call(s32[4]{0:T(128)S(1)} %pad_add_fusion.pos, bf16[4,128,1024]{2,1,0:T(8,128)(2,1)S(1)} %pad_maximum_fusion.inverse, bf16[4,128,1024]{2,1,0:T(8,128)(2,1)S(1)} %collective-permute-done.12.inverse_other, ...), custom_call_target="tpu_custom_call" | custom-call | tf_op jit(solution)/shard_map/inverse_times_diagonal/pallas_call | solution.py:236
  (96 shorter events, 53.8 us)
Async XLA Ops:
  0.6 43.6 %collective-permute-start.9 = (bf16[2048,512]{1,0:T(8,128)(2,1)}, bf16[2048,512]{1,0:T(8,128)(2,1)S(1)}, u32[]{:S(2)}, u32[]{:S(2)}) collective-permute-start(bf16[2048,512]{1,0:T(8,128)(2,1)} %mine.1), channel_id=1, source_target_pairs={{0,32},{32,0},{64,96},{96,64},{128,160},{160,128},{192,224},{224,1... | collective-permute-start | bytes 6291464 | tf_op jit(solution)/shard_map/ppermute | solution.py:47
  5.1 10.7 %collective-permute-start.3 = (bf16[2,128,512]{2,1,0:T(8,128)(2,1)S(1)}, bf16[2,128,512]{2,1,0:T(8,128)(2,1)S(1)}, u32[]{:S(2)}, u32[]{:S(2)}) collective-permute-start(bf16[2,128,512]{2,1,0:T(8,128)(2,1)S(1)} %constant_dynamic-update-slice_fusion.refs_0_.refs_4_), channel_id=1, source_target_pairs={{0,16},{1,17},{2,18},{3,19},{4,20},{5,21},{6,22},{7,23},{8,24},{9,... | collective-permute-start | bytes 786440 | tf_op jit(solution)/shard_map/ppermute | solution.py:25
  8.2 12.6 %collective-permute-start.2 = (bf16[2,128,512]{2,1,0:T(8,128)(2,1)S(1)}, bf16[2,128,512]{2,1,0:T(8,128)(2,1)S(1)}, u32[]{:S(2)}, u32[]{:S(2)}) collective-permute-start(bf16[2,128,512]{2,1,0:T(8,128)(2,1)S(1)} %constant_dynamic-update-slice_fusion.refs_0_.refs_4_), channel_id=1, source_target_pairs={{0,24},{1,25},{2,26},{3,27},{4,28},{5,29},{6,30},{7,31},{8,0},{9,1... | collective-permute-start | bytes 786440 | tf_op jit(solution)/shard_map/ppermute | solution.py:25
  9.3 11.4 %collective-permute-start.1 = (bf16[2,128,512]{2,1,0:T(8,128)(2,1)S(1)}, bf16[2,128,512]{2,1,0:T(8,128)(2,1)S(1)}, u32[]{:S(2)}, u32[]{:S(2)}) collective-permute-start(bf16[2,128,512]{2,1,0:T(8,128)(2,1)S(1)} %constant_dynamic-update-slice_fusion.refs_0_.refs_4_), channel_id=1, source_target_pairs={{0,8},{1,9},{2,10},{3,11},{4,12},{5,13},{6,14},{7,15},{8,16},{9,17... | collective-permute-start | bytes 786440 | tf_op jit(solution)/shard_map/ppermute | solution.py:25
  10.2 17.0 %collective-permute-start.6 = (bf16[128,1024]{1,0:T(8,128)(2,1)}, bf16[128,1024]{1,0:T(8,128)(2,1)S(1)}, u32[]{:S(2)}, u32[]{:S(2)}) collective-permute-start(bf16[128,1024]{1,0:T(8,128)(2,1)} %param.11), channel_id=1, source_target_pairs={{0,64},{32,96},{64,128},{96,160},{128,192},{160,224},{192,0},{224,... | collective-permute-start | bytes 786440 | tf_op jit(solution)/shard_map/ppermute | solution.py:35
  20.8 20.0 %collective-permute-start.5 = (bf16[5,128,512]{2,1,0:T(8,128)(2,1)S(1)}, bf16[5,128,512]{2,1,0:T(8,128)(2,1)S(1)}, u32[]{:S(2)}, u32[]{:S(2)}) collective-permute-start(bf16[5,128,512]{2,1,0:T(8,128)(2,1)S(1)} %join_parts.4.refs_0_), channel_id=1, source_target_pairs={{0,7},{1,0},{2,1},{3,2},{4,3},{5,4},{6,5},{7,6},{8,15},{9,8},{10,9... | collective-permute-start | bytes 1966088 | tf_op jit(solution)/shard_map/ppermute | solution.py:30
  26.8 17.5 %collective-permute-start.4 = (bf16[5,128,512]{2,1,0:T(8,128)(2,1)S(1)}, bf16[5,128,512]{2,1,0:T(8,128)(2,1)S(1)}, u32[]{:S(2)}, u32[]{:S(2)}) collective-permute-start(bf16[5,128,512]{2,1,0:T(8,128)(2,1)S(1)} %join_parts.4.refs_0_), channel_id=1, source_target_pairs={{0,1},{1,2},{2,3},{3,4},{4,5},{5,6},{6,7},{7,0},{8,9},{9,10},{10,1... | collective-permute-start | bytes 1966088 | tf_op jit(solution)/shard_map/ppermute | solution.py:30
  44.2 21.5 %collective-permute-start.12 = (bf16[4,128,1024]{2,1,0:T(8,128)(2,1)S(1)}, bf16[4,128,1024]{2,1,0:T(8,128)(2,1)S(1)}, u32[]{:S(2)}, u32[]{:S(2)}) collective-permute-start(bf16[4,128,1024]{2,1,0:T(8,128)(2,1)S(1)} %pad_maximum_fusion.inverse), channel_id=1, source_target_pairs={{0,32},{32,0},{64,96},{96,64},{128,160},{160,128},{192,224},{224,1... | collective-permute-start | bytes 3145736 | tf_op jit(solution)/shard_map/ppermute | solution.py:47
  44.2 21.5 %collective-permute-start.10 = (bf16[5,128,512]{2,1,0:T(8,128)(2,1)S(1)}, bf16[5,128,512]{2,1,0:T(8,128)(2,1)S(1)}, u32[]{:S(2)}, u32[]{:S(2)}) collective-permute-start(bf16[5,128,512]{2,1,0:T(8,128)(2,1)S(1)} %collective-permute-done.4.refs_0_.refs_1_), channel_id=1, source_target_pairs={{0,1},{1,2},{2,3},{3,4},{4,5},{5,6},{6,7},{7,0},{8,9},{9,10},{10,1... | collective-permute-start | bytes 1966088 | tf_op jit(solution)/shard_map/ppermute | solution.py:30
  44.2 21.5 %collective-permute-start.11 = (bf16[5,128,512]{2,1,0:T(8,128)(2,1)S(1)}, bf16[5,128,512]{2,1,0:T(8,128)(2,1)S(1)}, u32[]{:S(2)}, u32[]{:S(2)}) collective-permute-start(bf16[5,128,512]{2,1,0:T(8,128)(2,1)S(1)} %collective-permute-done.5.refs_1_.refs_2_), channel_id=1, source_target_pairs={{0,7},{1,0},{2,1},{3,2},{4,3},{5,4},{6,5},{7,6},{8,15},{9,8},{10,9... | collective-permute-start | bytes 1966088 | tf_op jit(solution)/shard_map/ppermute | solution.py:30
  50.6 12.4 %collective-permute-start.14 = (bf16[2,128,512]{2,1,0:T(8,128)(2,1)S(1)}, bf16[2,128,512]{2,1,0:T(8,128)(2,1)S(1)}, u32[]{:S(2)}, u32[]{:S(2)}) collective-permute-start(bf16[2,128,512]{2,1,0:T(8,128)(2,1)S(1)} %join_parts.5.refs_4_), channel_id=1, source_target_pairs={{0,24},{1,25},{2,26},{3,27},{4,28},{5,29},{6,30},{7,31},{8,0},{9,1... | collective-permute-start | bytes 786440 | tf_op jit(solution)/shard_map/ppermute | solution.py:25
  65.8 16.0 %collective-permute-start.16 = (bf16[5,128,512]{2,1,0:T(8,128)(2,1)S(1)}, bf16[5,128,512]{2,1,0:T(8,128)(2,1)S(1)}, u32[]{:S(2)}, u32[]{:S(2)}) collective-permute-start(bf16[5,128,512]{2,1,0:T(8,128)(2,1)S(1)} %collective-permute-done.10.refs_3_.refs_0_), channel_id=1, source_target_pairs={{0,1},{1,2},{2,3},{3,4},{4,5},{5,6},{6,7},{7,0},{8,9},{9,10},{10,1... | collective-permute-start | bytes 1966088 | tf_op jit(solution)/shard_map/ppermute | solution.py:30
  66.0 15.8 %collective-permute-start.17 = (bf16[5,128,512]{2,1,0:T(8,128)(2,1)S(1)}, bf16[5,128,512]{2,1,0:T(8,128)(2,1)S(1)}, u32[]{:S(2)}, u32[]{:S(2)}) collective-permute-start(bf16[5,128,512]{2,1,0:T(8,128)(2,1)S(1)} %collective-permute-done.11.refs_4_.refs_1_), channel_id=1, source_target_pairs={{0,7},{1,0},{2,1},{3,2},{4,3},{5,4},{6,5},{7,6},{8,15},{9,8},{10,9... | collective-permute-start | bytes 1966088 | tf_op jit(solution)/shard_map/ppermute | solution.py:30
  81.8 16.2 %collective-permute-start.22 = (bf16[3,128,512]{2,1,0:T(8,128)(2,1)S(1)}, bf16[3,128,512]{2,1,0:T(8,128)(2,1)S(1)}, u32[]{:S(2)}, u32[]{:S(2)}) collective-permute-start(bf16[3,128,512]{2,1,0:T(8,128)(2,1)S(1)} %slice.10), channel_id=1, source_target_pairs={{0,7},{1,0},{2,1},{3,2},{4,3},{5,4},{6,5},{7,6},{8,15},{9,8},{10,9... | collective-permute-start | bytes 1179656 | tf_op jit(solution)/shard_map/ppermute | solution.py:30
  84.5 12.5 %collective-permute-start.21 = (bf16[2,128,512]{2,1,0:T(8,128)(2,1)S(1)}, bf16[2,128,512]{2,1,0:T(8,128)(2,1)S(1)}, u32[]{:S(2)}, u32[]{:S(2)}) collective-permute-start(bf16[2,128,512]{2,1,0:T(8,128)(2,1)S(1)} %slice.9), channel_id=1, source_target_pairs={{0,1},{1,2},{2,3},{3,4},{4,5},{5,6},{6,7},{7,0},{8,9},{9,10},{10,1... | collective-permute-start | bytes 786440 | tf_op jit(solution)/shard_map/ppermute | solution.py:30
  84.6 12.4 %collective-permute-start.25 = (bf16[2,128,512]{2,1,0:T(8,128)(2,1)S(1)}, bf16[2,128,512]{2,1,0:T(8,128)(2,1)S(1)}, u32[]{:S(2)}, u32[]{:S(2)}) collective-permute-start(bf16[2,128,512]{2,1,0:T(8,128)(2,1)S(1)} %join_parts.7.refs_0_.refs_12_), channel_id=1, source_target_pairs={{0,16},{1,17},{2,18},{3,19},{4,20},{5,21},{6,22},{7,23},{8,24},{9,... | collective-permute-start | bytes 786440 | tf_op jit(solution)/shard_map/ppermute | solution.py:25
  99.3 12.3 %collective-permute-start.26 = (f32[512,128]{1,0:T(8,128)S(1)}, f32[512,128]{1,0:T(8,128)S(1)}, u32[]{:S(2)}, u32[]{:S(2)}) collective-permute-start(f32[512,128]{1,0:T(8,128)S(1)} %get-tuple-element.69), channel_id=1, source_target_pairs={{0,64},{32,96},{64,128},{96,160},{128,192},{160,224},{192,0},{224,... | collective-permute-start | bytes 786440 | tf_op jit(solution)/shard_map/ppermute | solution.py:35
  100.6 11.0 %collective-permute-start.27 = (f32[512,128]{1,0:T(8,128)S(1)}, f32[512,128]{1,0:T(8,128)S(1)}, u32[]{:S(2)}, u32[]{:S(2)}) collective-permute-start(f32[512,128]{1,0:T(8,128)S(1)} %get-tuple-element.70), channel_id=1, source_target_pairs={{0,128},{32,160},{64,192},{96,224},{128,0},{160,32},{192,64},{224,... | collective-permute-start | bytes 786440 | tf_op jit(solution)/shard_map/ppermute | solution.py:35
  101.3 12.2 %collective-permute-start.28 = (f32[512,128]{1,0:T(8,128)S(1)}, f32[512,128]{1,0:T(8,128)S(1)}, u32[]{:S(2)}, u32[]{:S(2)}) collective-permute-start(f32[512,128]{1,0:T(8,128)S(1)} %get-tuple-element.71), channel_id=1, source_target_pairs={{0,192},{32,224},{64,0},{96,32},{128,64},{160,96},{192,128},{224,1... | collective-permute-start | bytes 786440 | tf_op jit(solution)/shard_map/ppermute | solution.py:35
  123.7 25.4 %collective-permute-start.38 = (bf16[4,512,128]{2,1,0:T(8,128)(2,1)S(1)}, bf16[4,512,128]{2,1,0:T(8,128)(2,1)S(1)}, u32[]{:S(2)}, u32[]{:S(2)}) collective-permute-start(bf16[4,512,128]{2,1,0:T(8,128)(2,1)S(1)} %pad_maximum_fusion.1.mine), channel_id=1, source_target_pairs={{0,32},{32,0},{64,96},{96,64},{128,160},{160,128},{192,224},{224,1... | collective-permute-start | bytes 1572872 | tf_op jit(solution)/shard_map/ppermute | solution.py:47
  130.0 16.5 %collective-permute-start.40 = (bf16[1024,128]{1,0:T(8,128)(2,1)S(1)}, bf16[1024,128]{1,0:T(8,128)(2,1)S(1)}, u32[]{:S(2)}, u32[]{:S(2)}) collective-permute-start(bf16[1024,128]{1,0:T(8,128)(2,1)S(1)} %get-tuple-element.84), channel_id=1, source_target_pairs={{0,128},{32,160},{1,129},{33,161},{2,130},{34,162},{3,131},{35,163... | collective-permute-start | bytes 786440 | tf_op jit(solution)/shard_map/ppermute | solution.py:39
  131.3 15.2 %collective-permute-start.41 = (bf16[1024,128]{1,0:T(8,128)(2,1)S(1)}, bf16[1024,128]{1,0:T(8,128)(2,1)S(1)}, u32[]{:S(2)}, u32[]{:S(2)}) collective-permute-start(bf16[1024,128]{1,0:T(8,128)(2,1)S(1)} %get-tuple-element.85), channel_id=1, source_target_pairs={{0,192},{32,224},{1,193},{33,225},{2,194},{34,226},{3,195},{35,227... | collective-permute-start | bytes 786440 | tf_op jit(solution)/shard_map/ppermute | solution.py:39
  136.1 14.0 %collective-permute-start.32 = (bf16[512,128]{1,0:T(8,128)(2,1)S(1)}, bf16[512,128]{1,0:T(8,128)(2,1)S(1)}, u32[]{:S(2)}, u32[]{:S(2)}) collective-permute-start(bf16[512,128]{1,0:T(8,128)(2,1)S(1)} %get-tuple-element.78), channel_id=1, source_target_pairs={{0,64},{32,96},{64,128},{96,160},{128,192},{160,224},{192,0},{224,... | collective-permute-start | bytes 393224 | tf_op jit(solution)/shard_map/ppermute | solution.py:35
  138.0 12.1 %collective-permute-start.33 = (bf16[512,128]{1,0:T(8,128)(2,1)S(1)}, bf16[512,128]{1,0:T(8,128)(2,1)S(1)}, u32[]{:S(2)}, u32[]{:S(2)}) collective-permute-start(bf16[512,128]{1,0:T(8,128)(2,1)S(1)} %get-tuple-element.79), channel_id=1, source_target_pairs={{0,128},{32,160},{64,192},{96,224},{128,0},{160,32},{192,64},{224,... | collective-permute-start | bytes 393224 | tf_op jit(solution)/shard_map/ppermute | solution.py:35
  (24 other events, 263.5 us)

commit v6 on v5

--- a/solution.py
+++ b/solution.py
@@ -59,13 +59,17 @@
     return (pos[0] + offset(i) + NX) % NX, (pos[1] + offset(j) + NZ) % NZ
 
 
-def pack_kernel(pos, two, one, own, give):
+def pack_kernel(pos, two, one, own, give, held, sems):
+    copies = [pltpu.make_async_copy(ref, held.at[n], sems.at[n]) for n, ref in enumerate((two, one))]
+    for copy in copies:
+        copy.start()
     first = pos[3] == 0
-    for q in range(NY):
-        at = slice(q * 128, q * 128 + 128)
-        for n, panel in enumerate((two, one)):
-            left = panel[:, q * 256:q * 256 + 128]
-            right = panel[:, q * 256 + 128:q * 256 + 256]
+    for n, copy in enumerate(copies):
+        copy.wait()
+        for q in range(NY):
+            at = slice(q * 128, q * 128 + 128)
+            left = held[n, :, q * 256:q * 256 + 128]
+            right = held[n, :, q * 256 + 128:q * 256 + 256]
             own[n, :, at] = jnp.where(first, left, right)
             give[n, :, at] = jnp.where(first, right, left)
 
@@ -74,8 +78,9 @@
     return pl.pallas_call(
         pack_kernel,
         out_shape=(jax.ShapeDtypeStruct((2, SUB, HALF), BF16),) * 2,
-        in_specs=[SMEM, VMEM, VMEM],
+        in_specs=[SMEM, ANY, ANY],
         out_specs=(VMEM, VMEM),
+        scratch_shapes=[pltpu.VMEM((2, SUB, 2 * HALF), BF16), pltpu.SemaphoreType.DMA((2,))],
         compiler_params=SMALL,
         name="pack_columns",
     )(pos, two, one)
@@ -97,35 +102,49 @@
     )(*parts)
 
 
-def prepare_kernel(pos, taper, mine, other, out, rows):
+def prepare_kernel(pos, taper, mine, other, for_two, for_one, rows):
     lane = lax.broadcasted_iota(jnp.int32, (SUB, 2 * BLK), 1)
     first_col = (pos[0] * NZ + pos[1]) * 2
 
-    def block(j, carry):
+    def put(at, i, j):
+        x, z = source(pos, i, j)
+        row = pl.multiple_of((x * NZ + z) * SUB, SUB)
+        for h, ref in enumerate((mine, other)):
+            core = pos[3] if h == 0 else 1 - pos[3]
+            tile = (pos[2] * 2 + core) * 8 + x * 2 + z // 4
+            left = taper[tile, first_col].astype(F32)
+            right = taper[tile, first_col + 1].astype(F32)
+            keep = jnp.where(lane < BLK, left, right)
+            rows[at + h * SUB:at + h * SUB + SUB, :] = (
+                ref[pl.ds(row, SUB), :].astype(F32) * keep).astype(BF16)
+
+    def block_two(j, carry):
         for i in range(NX):
-            x, z = source(pos, i, j)
-            row = pl.multiple_of((x * NZ + z) * SUB, SUB)
-            for h, ref in enumerate((mine, other)):
-                core = pos[3] if h == 0 else 1 - pos[3]
-                tile = (pos[2] * 2 + core) * 8 + x * 2 + z // 4
-                left = taper[tile, first_col].astype(F32)
-                right = taper[tile, first_col + 1].astype(F32)
-                keep = jnp.where(lane < BLK, left, right)
-                at = i * PAIR + h * SUB
-                rows[at:at + SUB, :] = (ref[pl.ds(row, SUB), :].astype(F32) * keep).astype(BF16)
-        out[j] = rows[...].T
+            put(i * PAIR, i, j)
+        for_two[j] = rows[:512].T
         return carry
 
-    lax.fori_loop(0, NZ, block, 0)
+    def block_one(c, carry):
+        for i in range(NX):
+            for s in range(2):
+                put((2 * i + s) * PAIR, i, jnp.where(c == 0, 7 * s, 2 * c - 1 + s))
+        for_one[c] = rows[...].T
+        return carry
+
+    lax.fori_loop(0, NZ, block_two, 0)
+    lax.fori_loop(0, NZ // 2, block_one, 0)
 
 
 def prepare(pos, taper, mine, other):
     return pl.pallas_call(
         prepare_kernel,
-        out_shape=jax.ShapeDtypeStruct((NZ, 512, 512), BF16),
+        out_shape=(
+            jax.ShapeDtypeStruct((NZ, 512, 512), BF16),
+            jax.ShapeDtypeStruct((NZ // 2, 512, 1024), BF16),
+        ),
         in_specs=[SMEM, SMEM, VMEM, VMEM],
-        out_specs=VMEM,
-        scratch_shapes=[pltpu.VMEM((512, 512), BF16)],
+        out_specs=(VMEM, VMEM),
+        scratch_shapes=[pltpu.VMEM((1024, 512), BF16)],
         compiler_params=SMALL,
         name="prepare_adjoint",
     )(pos, taper, mine, other)
@@ -151,7 +170,7 @@
     def step(n, carry):
         pltpu.make_async_copy(held.at[n], held.at[n], sems.at[n]).wait()
         total[...] += jnp.dot(
-            adjoint[begin + n], held[n].reshape(NX * PAIR, HALF), preferred_element_type=F32)
+            adjoint[begin + n], held[n].reshape(-1, HALF), preferred_element_type=F32)
         return carry
 
     lax.fori_loop(0, len(items), step, 0)
@@ -166,7 +185,7 @@
     column = jax.ShapeDtypeStruct((512, 128), F32)
     scratch = [pltpu.VMEM((512, HALF), F32)] if last else []
     scratch += [
-        pltpu.VMEM((len(items), NX, PAIR, HALF), BF16),
+        pltpu.VMEM((len(items), adjoint.shape[2] // PAIR, PAIR, HALF), BF16),
         pltpu.SemaphoreType.DMA((len(items),)),
     ]
     extra = [] if before is None else [before]
@@ -222,14 +241,11 @@
     sent = (one[...] + two[...]) + three[...]
     columns = jnp.where(pos[2] == 0, own[...], sent)
     for left, result in ((inverse, out), (inverse_other, out_other)):
-        def block(d, carry, left=left, result=result):
-            value = jnp.dot(left[d], columns, preferred_element_type=F32)
-            high = value.astype(BF16)
-            result[d, :, :128] = high
-            result[d, :, 128:] = (value - high.astype(F32)).astype(BF16)
-            return carry
-
-        lax.fori_loop(0, NY, block, 0)
+        value = jnp.dot(left[...].reshape(512, 1024), columns, preferred_element_type=F32)
+        high = value.astype(BF16)
+        low = (value - high.astype(F32)).astype(BF16)
+        result[:, :, :128] = high.reshape(NY, 128, 128)
+        result[:, :, 128:] = low.reshape(NY, 128, 128)
 
 
 def factor(pos, inverse, inverse_other, parts):
@@ -276,47 +292,51 @@
     taken = core_swap(give)
     shards = jnp.concatenate([own, taken], axis=1)
 
-    first_x = [shards] + [x_shift(shards, d) for d in (1, -1, 2)]
-    own = join(first_x + [shards], (0, 0, 0, 0, 1))
+    two, one = shards[0], shards[1]
+
+    def x_all(part):
+        return [part] + [x_shift(part, d) for d in (1, -1, 2)]
+
+    def of_one(*messages):
+        return x_all(join(messages, (NX,) * len(messages)))
+
+    *two, swapped = together(*x_all(two), core_swap(adjoint))
+    own = join(two + [one], (None,) * 5)
     inverse = y_all(inverse_factor)
-    down1, up1, inverse, swapped = together(
-        z_shift(own, 1), z_shift(own, -1), inverse, core_swap(adjoint))
-
-    def x_others(*messages):
-        part = join(messages, (4,) * len(messages)) if len(messages) > 1 else messages[0][-1:]
-        return [part] + [x_shift(part, d) for d in (1, -1, 2)]
-
-    masked = prepare(pos, taper, adjoint, swapped)
-    down2, up2, masked, inverse_other, *near = together(
-        z_shift(down1, 1), z_shift(up1, -1), masked, core_swap(inverse), *x_others(down1, up1))
+    down1, up1, inverse, *first_x = together(
+        z_shift(own, 1), z_shift(own, -1), inverse, *x_all(one[None]))
+
+    for_two, for_one = prepare(pos, taper, adjoint, swapped)
+    down2, up2, for_two, for_one, inverse_other, *near = together(
+        z_shift(down1, 1), z_shift(up1, -1), for_two, for_one, core_swap(inverse),
+        *of_one(down1, up1))
     sums = product(
-        pos, masked, [own, down1, up1, down2, up2], [(j, [(j, 0, 4)]) for j in range(5)])
+        pos, for_two, [own, down1, up1, down2, up2], [(j, [(j, 0, 4)]) for j in range(5)])
     down3, up3, sums, *middle = together(
-        z_shift(down2, 1), z_shift(up2, -1), sums, *x_others(down2, up2))
-    sums = product(pos, masked, [down3, up3], [(5 + j, [(j, 0, 4)]) for j in range(2)], sums)
+        z_shift(down2, 1), z_shift(up2, -1), sums, *of_one(down2, up2))
+    sums = product(pos, for_two, [down3, up3], [(5 + j, [(j, 0, 4)]) for j in range(2)], sums)
     sums_one = product(
-        pos, masked, first_x + near + middle,
-        [(0, [(i, 1, 1) for i in range(NX)])]
-        + [(1 + j, [(NX * (1 + j // 2) + i, j % 2, 1) for i in range(NX)]) for j in range(4)])
+        pos, for_one, near + middle,
+        [(1 + c, [(NX * c + i, 0, 2) for i in range(NX)]) for c in range(2)])
     far_low, far_high, sums, sums_one, *third = together(
-        z_shift(down3[:2], 1), z_shift(up3[2:], -1), sums, sums_one, *x_others(down3, up3))
-    last = x_others(far_high)
+        z_shift(down3[:2], 1), z_shift(up3[2:], -1), sums, sums_one, *of_one(down3, up3))
 
     mine, *sent = product(
-        pos, masked, [far_low, far_high], [(7, [(0, 0, 2), (1, 0, 2)])], sums, F32)
-    r1, r2, r3 = [y_shift(part, d + 1) for d, part in enumerate(sent)]
+        pos, for_two, [far_low, far_high], [(7, [(0, 0, 2), (1, 0, 2)])], sums, F32)
+    sums_one = product(pos, for_one, third, [(3, [(i, 0, 2) for i in range(NX)])], sums_one)
+    r1, r2, r3, sums_one, *last = together(
+        *[y_shift(part, d + 1) for d, part in enumerate(sent)], sums_one, *x_all(far_high[2:]))
     second_grad = incoming + ((mine + r1) + (r2 + r3))
     rounded = y_all(second_grad.astype(BF16))
     rounded_other = core_swap(rounded)
 
     where = tuple(
-        ((i, 1),) + tuple((NX * (1 + j // 2) + i, j % 2) for j in range(7)) for i in range(NX))
+        ((i, 0),) + tuple((NX * (1 + j // 2) + i, j % 2) for j in range(7)) for i in range(NX))
     first, *rest = diagonal(pos, first_x + near + middle + third + last, where)
     rest = [y_first(part, d + 1) for d, part in enumerate(rest)]
     mine, *sent = product(
-        pos, masked, third + last,
-        [(5 + j, [(NX * (j // 2) + i, j % 2, 1) for i in range(NX)]) for j in range(3)],
-        sums_one, BF16)
+        pos, for_one, first_x + last,
+        [(0, [(NX * s + i, 0, 1) for i in range(NX) for s in range(2)])], sums_one, BF16)
     r1, r2, r3 = [y_shift(part, d + 1).astype(F32) for d, part in enumerate(sent)]
     factors = factor(pos, inverse, inverse_other, [first] + rest)
     term = carried(rounded, rounded_other, *factors)

time: 152 us -> 151 us (level)
  the two profiles are of different devices: /device:TPU:16 before, /device:TPU:1 now
where the time goes in v6:
time: 151 us; the launch traced here: 150 us
  starting transfers between devices  61.8 us (41%)
  waiting for transfers between devices  59.6 us (39%)
  Pallas kernels  22.8 us (15%)
  other arithmetic  2.78 us (2%)
  local copies, waits for them, and re-layouts  1.92 us (1%)
    ppermute x18, waiting for transfers between devices, x_shift(): return lax.ppermute(value, 'col', pairs)  36.1 us
    ppermute x18, starting transfers between devices, x_shift(): return lax.ppermute(value, 'col', pairs)  21.9 us
    ppermute x12, waiting for transfers between devices, y_shift(): return lax.ppermute(value, 'row', pairs)  16.3 us
    ppermute x12, starting transfers between devices, y_shift(): return lax.ppermute(value, 'row', pairs)  16 us
    pallas_call x6, Pallas kernels, product(): pl.pallas_call(kernel, out_shape=(column,) + (jax.ShapeDtypeStruct((512,...  12.3 us
    ppermute x8, starting transfers between devices, z_shift(): return lax.ppermute(value, 'col', pairs)  10.8 us
    ppermute x4, starting transfers between devices, core_swap(): return lax.ppermute(value, 'row', [(r, r ^ 1) for r in range(2 * NY)])  9.15 us
    ppermute x3, waiting for transfers between devices, y_first(): return lax.ppermute(value, 'row', [(k, y * 2 + k) for k in range(2)])  5.94 us
  transfers between devices with their start and end apart: 45, of which 26 were waited for; matrix products, arithmetic and copies ran while one was open for 1% of the time, Pallas kernels for 15%

profile of v6, /device:TPU:1, one launch (start us, length us, event | category | flops | bytes accessed | tf_op | source)
XLA Modules:
  0.0 149.8 jit_solution(16024354379151131733)
XLA Ops:
  0.6 3.3 %collective-permute-start.4 = (bf16[2048,512]{1,0:T(8,128)(2,1)}, bf16[2048,512]{1,0:T(8,128)(2,1)}, u32[]{:S(2)}, u32[]{:S(2)}) collective-permute-start(bf16[2048,512]{1,0:T(8,128)(2,1)} %mine.1), channel_id=1, source_target_pairs={{0,32},{32,0},{64,96},{96,64},{128,160},{160,128},{192,224},{224,1... | collective-permute-start | bytes 6291464 | tf_op jit(solution)/shard_map/ppermute | solution.py:47
  10.9 4.0 %collective-permute-done.3.refs_3_ = bf16[128,512]{1,0:T(8,128)(2,1)S(1)} collective-permute-done((bf16[128,512]{1,0:T(8,128)(2,1)S(1)}, bf16[128,512]{1,0:T(8,128)(2,1)S(1)}, u32[]{:S(2)}, u32[]{:S(2)}) %collective-permute-start.3) | collective-permute-done | bytes 131104 | tf_op jit(solution)/shard_map/ppermute | solution.py:25
  18.0 3.7 %collective-permute-start.6 = (bf16[5,128,512]{2,1,0:T(8,128)(2,1)S(1)}, bf16[5,128,512]{2,1,0:T(8,128)(2,1)S(1)}, u32[]{:S(2)}, u32[]{:S(2)}) collective-permute-start(bf16[5,128,512]{2,1,0:T(8,128)(2,1)S(1)} %join_parts.4.refs_0_), channel_id=1, source_target_pairs={{0,7},{1,0},{2,1},{3,2},{4,3},{5,4},{6,5},{7,6},{8,15},{9,8},{10,9... | collective-permute-start | bytes 1966088 | tf_op jit(solution)/shard_map/ppermute | solution.py:30
  26.1 3.3 %collective-permute-done.7 = bf16[128,1024]{1,0:T(8,128)(2,1)S(1)} collective-permute-done((bf16[128,1024]{1,0:T(8,128)(2,1)}, bf16[128,1024]{1,0:T(8,128)(2,1)S(1)}, u32[]{:S(2)}, u32[]{:S(2)}) %collective-permute-start.7) | collective-permute-done | bytes 262176 | tf_op jit(solution)/shard_map/ppermute | solution.py:35
  29.3 4.1 %collective-permute-start.12 = (bf16[1,128,512]{2,1,0:T(8,128)(2,1)S(1)}, bf16[1,128,512]{2,1,0:T(8,128)(2,1)S(1)}, u32[]{:S(2)}, u32[]{:S(2)}) collective-permute-start(bf16[1,128,512]{2,1,0:T(8,128)(2,1)S(1)} %get-tuple-element.106.refs_0_), channel_id=1, source_target_pairs={{0,16},{1,17},{2,18},{3,19},{4,20},{5,21},{6,22},{7,23},{8,24},{9,... | collective-permute-start | bytes 393224 | tf_op jit(solution)/shard_map/ppermute | solution.py:25
  36.1 2.5 %collective-permute-start.10 = (bf16[1,128,512]{2,1,0:T(8,128)(2,1)S(1)}, bf16[1,128,512]{2,1,0:T(8,128)(2,1)S(1)}, u32[]{:S(2)}, u32[]{:S(2)}) collective-permute-start(bf16[1,128,512]{2,1,0:T(8,128)(2,1)S(1)} %get-tuple-element.106.refs_0_), channel_id=1, source_target_pairs={{0,8},{1,9},{2,10},{3,11},{4,12},{5,13},{6,14},{7,15},{8,16},{9,17... | collective-permute-start | bytes 393224 | tf_op jit(solution)/shard_map/ppermute | solution.py:25
  39.7 2.6 %collective-permute-done.10.refs_1_ = bf16[1,128,512]{2,1,0:T(8,128)(2,1)S(1)} collective-permute-done((bf16[1,128,512]{2,1,0:T(8,128)(2,1)S(1)}, bf16[1,128,512]{2,1,0:T(8,128)(2,1)S(1)}, u32[]{:S(2)}, u32[]{:S(2)}) %collective-permute-start.10) | collective-permute-done | bytes 131104 | tf_op jit(solution)/shard_map/ppermute | solution.py:25
  42.3 2.6 %collective-permute-start.15 = (bf16[4,128,1024]{2,1,0:T(8,128)(2,1)S(1)}, bf16[4,128,1024]{2,1,0:T(8,128)(2,1)S(1)}, u32[]{:S(2)}, u32[]{:S(2)}) collective-permute-start(bf16[4,128,1024]{2,1,0:T(8,128)(2,1)S(1)} %pad_maximum_fusion.inverse), channel_id=1, source_target_pairs={{0,32},{32,0},{64,96},{96,64},{128,160},{160,128},{192,224},{224,1... | collective-permute-start | bytes 3145736 | tf_op jit(solution)/shard_map/ppermute | solution.py:47
  44.9 2.7 %collective-permute-start.14 = (bf16[5,128,512]{2,1,0:T(8,128)(2,1)S(1)}, bf16[5,128,512]{2,1,0:T(8,128)(2,1)S(1)}, u32[]{:S(2)}, u32[]{:S(2)}) collective-permute-start(bf16[5,128,512]{2,1,0:T(8,128)(2,1)S(1)} %collective-permute-done.6.refs_1_.refs_2_), channel_id=1, source_target_pairs={{0,7},{1,0},{2,1},{3,2},{4,3},{5,4},{6,5},{7,6},{8,15},{9,8},{10,9... | collective-permute-start | bytes 1966088 | tf_op jit(solution)/shard_map/ppermute | solution.py:30
  50.5 5.9 %collective-permute-done.18.refs_3_.refs_7_ = bf16[2,128,512]{2,1,0:T(8,128)(2,1)S(1)} collective-permute-done((bf16[2,128,512]{2,1,0:T(8,128)(2,1)S(1)}, bf16[2,128,512]{2,1,0:T(8,128)(2,1)S(1)}, u32[]{:S(2)}, u32[]{:S(2)}) %collective-permute-start.18) | collective-permute-done | bytes 262176 | tf_op jit(solution)/shard_map/ppermute | solution.py:25
  56.9 4.9 %prepare_adjoint.1 = (bf16[8,512,512]{2,1,0:T(8,128)(2,1)S(1)}, bf16[4,512,1024]{2,1,0:T(8,128)(2,1)S(1)}) custom-call(s32[4]{0:T(128)S(1)} %pad_add_fusion.pos, s32[64,64]{1,0:T(8,128)S(1)} %copy-done.3, bf16[2048,512]{1,0:T(8,128)(2,1)S(1)} %copy-done, bf16[2048,512]{1,0:T(8,128)(2,1)} %collective-permute-done.4.other), custom_call_target="tpu_custom_call" | custom-call | tf_op jit(solution)/shard_map/prepare_adjoint/pallas_call | solution.py:139
  64.0 2.7 %collective-permute-start.20 = (bf16[5,128,512]{2,1,0:T(8,128)(2,1)S(1)}, bf16[5,128,512]{2,1,0:T(8,128)(2,1)S(1)}, u32[]{:S(2)}, u32[]{:S(2)}) collective-permute-start(bf16[5,128,512]{2,1,0:T(8,128)(2,1)S(1)} %collective-permute-done.14.refs_4_.refs_1_), channel_id=1, source_target_pairs={{0,7},{1,0},{2,1},{3,2},{4,3},{5,4},{6,5},{7,6},{8,15},{9,8},{10,9... | collective-permute-start | bytes 1966088 | tf_op jit(solution)/shard_map/ppermute | solution.py:30
  69.0 3.0 %masked_product.6.refs_2_ = f32[512,512]{1,0:T(8,128)S(1)} custom-call(s32[4]{0:T(128)S(1)} %pad_add_fusion.pos, bf16[8,512,512]{2,1,0:T(8,128)(2,1)S(1)} %get-tuple-element.76.adjoint, bf16[5,128,512]{2,1,0:T(8,128)(2,1)S(1)} %join_parts.4.refs_0_, bf16[5,128,512]{2,1,0:T(8,128)(2,1)S(1)} %collective-permute-done.5.refs_0_.refs_1_, ...), custom_call_target="tpu_custom_call" | custom-call | tf_op jit(solution)/shard_map/masked_product/pallas_call | solution.py:193
  73.6 4.8 %collective-permute-done.22.refs_6_.refs_10_ = bf16[2,128,512]{2,1,0:T(8,128)(2,1)S(1)} collective-permute-done((bf16[2,128,512]{2,1,0:T(8,128)(2,1)S(1)}, bf16[2,128,512]{2,1,0:T(8,128)(2,1)S(1)}, u32[]{:S(2)}, u32[]{:S(2)}) %collective-permute-start.22) | collective-permute-done | bytes 262176 | tf_op jit(solution)/shard_map/ppermute | solution.py:25
  86.5 2.2 %masked_product.8.refs_4_ = f32[512,512]{1,0:T(8,128)S(1)} custom-call(s32[4]{0:T(128)S(1)} %pad_add_fusion.pos, bf16[4,512,1024]{2,1,0:T(8,128)(2,1)S(1)} %get-tuple-element.82.adjoint, bf16[2,128,512]{2,1,0:T(8,128)(2,1)S(1)} %join_parts.5.refs_0_.refs_4_, bf16[2,128,512]{2,1,0:T(8,128)(2,1)S(1)} %collective-permute-done.16.refs_1_.refs_5_, ...), custom_call_target="tpu_custom_call" | custom-call | tf_op jit(solution)/shard_map/masked_product/pallas_call | solution.py:193
  88.9 5.4 %collective-permute-done.27.refs_2_.refs_14_ = bf16[2,128,512]{2,1,0:T(8,128)(2,1)S(1)} collective-permute-done((bf16[2,128,512]{2,1,0:T(8,128)(2,1)S(1)}, bf16[2,128,512]{2,1,0:T(8,128)(2,1)S(1)}, u32[]{:S(2)}, u32[]{:S(2)}) %collective-permute-start.27) | collective-permute-done | bytes 262176 | tf_op jit(solution)/shard_map/ppermute | solution.py:25
  99.4 4.6 %collective-permute-start.30 = (f32[512,128]{1,0:T(8,128)S(1)}, f32[512,128]{1,0:T(8,128)S(1)}, u32[]{:S(2)}, u32[]{:S(2)}) collective-permute-start(f32[512,128]{1,0:T(8,128)S(1)} %get-tuple-element.96), channel_id=1, source_target_pairs={{0,128},{32,160},{64,192},{96,224},{128,0},{160,32},{192,64},{224,... | collective-permute-start | bytes 786440 | tf_op jit(solution)/shard_map/ppermute | solution.py:35
  114.5 3.4 %collective-permute-start.40 = (bf16[512,128]{1,0:T(8,128)(2,1)S(1)}, bf16[512,128]{1,0:T(8,128)(2,1)S(1)}, u32[]{:S(2)}, u32[]{:S(2)}) collective-permute-start(bf16[512,128]{1,0:T(8,128)(2,1)S(1)} %get-tuple-element.126), channel_id=1, source_target_pairs={{0,192},{32,224},{64,0},{96,32},{128,64},{160,96},{192,128},{224,1... | collective-permute-start | bytes 393224 | tf_op jit(solution)/shard_map/ppermute | solution.py:35
  119.1 2.5 %collective-permute-done.40 = bf16[512,128]{1,0:T(8,128)(2,1)S(1)} collective-permute-done((bf16[512,128]{1,0:T(8,128)(2,1)S(1)}, bf16[512,128]{1,0:T(8,128)(2,1)S(1)}, u32[]{:S(2)}, u32[]{:S(2)}) %collective-permute-start.40) | collective-permute-done | bytes 131104 | tf_op jit(solution)/shard_map/ppermute | solution.py:35
  125.3 3.0 %collective-permute-start.41 = (bf16[4,512,128]{2,1,0:T(8,128)(2,1)S(1)}, bf16[4,512,128]{2,1,0:T(8,128)(2,1)S(1)}, u32[]{:S(2)}, u32[]{:S(2)}) collective-permute-start(bf16[4,512,128]{2,1,0:T(8,128)(2,1)S(1)} %pad_maximum_fusion.1.mine), channel_id=1, source_target_pairs={{0,32},{32,0},{64,96},{96,64},{128,160},{160,128},{192,224},{224,1... | collective-permute-start | bytes 1572872 | tf_op jit(solution)/shard_map/ppermute | solution.py:47
  128.3 2.3 %diagonal_columns.1 = (bf16[1024,128]{1,0:T(8,128)(2,1)S(1)}, bf16[1024,128]{1,0:T(8,128)(2,1)S(1)}, bf16[1024,128]{1,0:T(8,128)(2,1)S(1)}, bf16[1024,128]{1,0:T(8,128)(2,1)S(1)}) custom-call(s32[4]{0:T(128)S(1)} %pad_add_fusion.pos, bf16[1,128,512]{2,1,0:T(8,128)(2,1)S(1)} %get-tuple-element.106.refs_0_, ...), custom_call_target="tpu_custom_call" | custom-call | tf_op jit(solution)/shard_map/diagonal_columns/pallas_call | solution.py:229
  134.5 2.8 %masked_product.11 = (f32[512,128]{1,0:T(8,128)S(1)}, bf16[512,128]{1,0:T(8,128)(2,1)S(1)}, bf16[512,128]{1,0:T(8,128)(2,1)S(1)}, bf16[512,128]{1,0:T(8,128)(2,1)S(1)}) custom-call(s32[4]{0:T(128)S(1)} %pad_add_fusion.pos, bf16[4,512,1024]{2,1,0:T(8,128)(2,1)S(1)} %get-tuple-element.82.adjoint, bf16[1,128,512]{2,1,0:T(8,128)(2,1)S(1)} %get-tuple-element.106.refs_0_, ...), custom_call_target="tpu_custom_call" | custom-call | tf_op jit(solution)/shard_map/masked_product/pallas_call | solution.py:193
  137.7 5.6 %collective-permute-done.43.two = bf16[1024,128]{1,0:T(8,128)(2,1)S(1)} collective-permute-done((bf16[1024,128]{1,0:T(8,128)(2,1)S(1)}, bf16[1024,128]{1,0:T(8,128)(2,1)S(1)}, u32[]{:S(2)}, u32[]{:S(2)}) %collective-permute-start.43) | collective-permute-done | bytes 262176 | tf_op jit(solution)/shard_map/ppermute | solution.py:39
  146.5 2.4 %collective-permute-done.36 = bf16[512,128]{1,0:T(8,128)(2,1)S(1)} collective-permute-done((bf16[512,128]{1,0:T(8,128)(2,1)S(1)}, bf16[512,128]{1,0:T(8,128)(2,1)S(1)}, u32[]{:S(2)}, u32[]{:S(2)}) %collective-permute-start.36) | collective-permute-done | bytes 131104 | tf_op jit(solution)/shard_map/ppermute | solution.py:35
  (102 shorter events, 64.6 us)
Async XLA Ops:
  0.6 17.3 %collective-permute-start.4 = (bf16[2048,512]{1,0:T(8,128)(2,1)}, bf16[2048,512]{1,0:T(8,128)(2,1)}, u32[]{:S(2)}, u32[]{:S(2)}) collective-permute-start(bf16[2048,512]{1,0:T(8,128)(2,1)} %mine.1), channel_id=1, source_target_pairs={{0,32},{32,0},{64,96},{96,64},{128,160},{160,128},{192,224},{224,1... | collective-permute-start | bytes 6291464 | tf_op jit(solution)/shard_map/ppermute | solution.py:47
  18.0 24.3 %collective-permute-start.6 = (bf16[5,128,512]{2,1,0:T(8,128)(2,1)S(1)}, bf16[5,128,512]{2,1,0:T(8,128)(2,1)S(1)}, u32[]{:S(2)}, u32[]{:S(2)}) collective-permute-start(bf16[5,128,512]{2,1,0:T(8,128)(2,1)S(1)} %join_parts.4.refs_0_), channel_id=1, source_target_pairs={{0,7},{1,0},{2,1},{3,2},{4,3},{5,4},{6,5},{7,6},{8,15},{9,8},{10,9... | collective-permute-start | bytes 1966088 | tf_op jit(solution)/shard_map/ppermute | solution.py:30
  21.7 20.6 %collective-permute-start.5 = (bf16[5,128,512]{2,1,0:T(8,128)(2,1)S(1)}, bf16[5,128,512]{2,1,0:T(8,128)(2,1)S(1)}, u32[]{:S(2)}, u32[]{:S(2)}) collective-permute-start(bf16[5,128,512]{2,1,0:T(8,128)(2,1)S(1)} %join_parts.4.refs_0_), channel_id=1, source_target_pairs={{0,1},{1,2},{2,3},{3,4},{4,5},{5,6},{6,7},{7,0},{8,9},{9,10},{10,1... | collective-permute-start | bytes 1966088 | tf_op jit(solution)/shard_map/ppermute | solution.py:30
  23.0 10.4 %collective-permute-start.9 = (bf16[128,1024]{1,0:T(8,128)(2,1)}, bf16[128,1024]{1,0:T(8,128)(2,1)S(1)}, u32[]{:S(2)}, u32[]{:S(2)}) collective-permute-start(bf16[128,1024]{1,0:T(8,128)(2,1)} %param.11), channel_id=1, source_target_pairs={{0,192},{32,224},{64,0},{96,32},{128,64},{160,96},{192,128},{224,1... | collective-permute-start | bytes 786440 | tf_op jit(solution)/shard_map/ppermute | solution.py:35
  24.4 11.6 %collective-permute-start.8 = (bf16[128,1024]{1,0:T(8,128)(2,1)}, bf16[128,1024]{1,0:T(8,128)(2,1)S(1)}, u32[]{:S(2)}, u32[]{:S(2)}) collective-permute-start(bf16[128,1024]{1,0:T(8,128)(2,1)} %param.11), channel_id=1, source_target_pairs={{0,128},{32,160},{64,192},{96,224},{128,0},{160,32},{192,64},{224,... | collective-permute-start | bytes 786440 | tf_op jit(solution)/shard_map/ppermute | solution.py:35
  29.3 10.4 %collective-permute-start.12 = (bf16[1,128,512]{2,1,0:T(8,128)(2,1)S(1)}, bf16[1,128,512]{2,1,0:T(8,128)(2,1)S(1)}, u32[]{:S(2)}, u32[]{:S(2)}) collective-permute-start(bf16[1,128,512]{2,1,0:T(8,128)(2,1)S(1)} %get-tuple-element.106.refs_0_), channel_id=1, source_target_pairs={{0,16},{1,17},{2,18},{3,19},{4,20},{5,21},{6,22},{7,23},{8,24},{9,... | collective-permute-start | bytes 393224 | tf_op jit(solution)/shard_map/ppermute | solution.py:25
  42.3 21.6 %collective-permute-start.15 = (bf16[4,128,1024]{2,1,0:T(8,128)(2,1)S(1)}, bf16[4,128,1024]{2,1,0:T(8,128)(2,1)S(1)}, u32[]{:S(2)}, u32[]{:S(2)}) collective-permute-start(bf16[4,128,1024]{2,1,0:T(8,128)(2,1)S(1)} %pad_maximum_fusion.inverse), channel_id=1, source_target_pairs={{0,32},{32,0},{64,96},{96,64},{128,160},{160,128},{192,224},{224,1... | collective-permute-start | bytes 3145736 | tf_op jit(solution)/shard_map/ppermute | solution.py:47
  44.9 19.0 %collective-permute-start.13 = (bf16[5,128,512]{2,1,0:T(8,128)(2,1)S(1)}, bf16[5,128,512]{2,1,0:T(8,128)(2,1)S(1)}, u32[]{:S(2)}, u32[]{:S(2)}) collective-permute-start(bf16[5,128,512]{2,1,0:T(8,128)(2,1)S(1)} %collective-permute-done.5.refs_0_.refs_1_), channel_id=1, source_target_pairs={{0,1},{1,2},{2,3},{3,4},{4,5},{5,6},{6,7},{7,0},{8,9},{9,10},{10,1... | collective-permute-start | bytes 1966088 | tf_op jit(solution)/shard_map/ppermute | solution.py:30
  44.9 19.0 %collective-permute-start.14 = (bf16[5,128,512]{2,1,0:T(8,128)(2,1)S(1)}, bf16[5,128,512]{2,1,0:T(8,128)(2,1)S(1)}, u32[]{:S(2)}, u32[]{:S(2)}) collective-permute-start(bf16[5,128,512]{2,1,0:T(8,128)(2,1)S(1)} %collective-permute-done.6.refs_1_.refs_2_), channel_id=1, source_target_pairs={{0,7},{1,0},{2,1},{3,2},{4,3},{5,4},{6,5},{7,6},{8,15},{9,8},{10,9... | collective-permute-start | bytes 1966088 | tf_op jit(solution)/shard_map/ppermute | solution.py:30
  49.6 12.2 %collective-permute-start.17 = (bf16[2,128,512]{2,1,0:T(8,128)(2,1)S(1)}, bf16[2,128,512]{2,1,0:T(8,128)(2,1)S(1)}, u32[]{:S(2)}, u32[]{:S(2)}) collective-permute-start(bf16[2,128,512]{2,1,0:T(8,128)(2,1)S(1)} %join_parts.5.refs_0_.refs_4_), channel_id=1, source_target_pairs={{0,24},{1,25},{2,26},{3,27},{4,28},{5,29},{6,30},{7,31},{8,0},{9,1... | collective-permute-start | bytes 786440 | tf_op jit(solution)/shard_map/ppermute | solution.py:25
  63.9 16.5 %collective-permute-start.19 = (bf16[5,128,512]{2,1,0:T(8,128)(2,1)S(1)}, bf16[5,128,512]{2,1,0:T(8,128)(2,1)S(1)}, u32[]{:S(2)}, u32[]{:S(2)}) collective-permute-start(bf16[5,128,512]{2,1,0:T(8,128)(2,1)S(1)} %collective-permute-done.13.refs_3_.refs_0_), channel_id=1, source_target_pairs={{0,1},{1,2},{2,3},{3,4},{4,5},{5,6},{6,7},{7,0},{8,9},{9,10},{10,1... | collective-permute-start | bytes 1966088 | tf_op jit(solution)/shard_map/ppermute | solution.py:30
  64.0 16.4 %collective-permute-start.20 = (bf16[5,128,512]{2,1,0:T(8,128)(2,1)S(1)}, bf16[5,128,512]{2,1,0:T(8,128)(2,1)S(1)}, u32[]{:S(2)}, u32[]{:S(2)}) collective-permute-start(bf16[5,128,512]{2,1,0:T(8,128)(2,1)S(1)} %collective-permute-done.14.refs_4_.refs_1_), channel_id=1, source_target_pairs={{0,7},{1,0},{2,1},{3,2},{4,3},{5,4},{6,5},{7,6},{8,15},{9,8},{10,9... | collective-permute-start | bytes 1966088 | tf_op jit(solution)/shard_map/ppermute | solution.py:30
  67.5 10.9 %collective-permute-start.22 = (bf16[2,128,512]{2,1,0:T(8,128)(2,1)S(1)}, bf16[2,128,512]{2,1,0:T(8,128)(2,1)S(1)}, u32[]{:S(2)}, u32[]{:S(2)}) collective-permute-start(bf16[2,128,512]{2,1,0:T(8,128)(2,1)S(1)} %join_parts.6.refs_4_.refs_8_), channel_id=1, source_target_pairs={{0,24},{1,25},{2,26},{3,27},{4,28},{5,29},{6,30},{7,31},{8,0},{9,1... | collective-permute-start | bytes 786440 | tf_op jit(solution)/shard_map/ppermute | solution.py:25
  68.7 11.7 %collective-permute-start.21 = (bf16[2,128,512]{2,1,0:T(8,128)(2,1)S(1)}, bf16[2,128,512]{2,1,0:T(8,128)(2,1)S(1)}, u32[]{:S(2)}, u32[]{:S(2)}) collective-permute-start(bf16[2,128,512]{2,1,0:T(8,128)(2,1)S(1)} %join_parts.6.refs_4_.refs_8_), channel_id=1, source_target_pairs={{0,8},{1,9},{2,10},{3,11},{4,12},{5,13},{6,14},{7,15},{8,16},{9,17... | collective-permute-start | bytes 786440 | tf_op jit(solution)/shard_map/ppermute | solution.py:25
  80.5 14.8 %collective-permute-start.25 = (bf16[3,128,512]{2,1,0:T(8,128)(2,1)S(1)}, bf16[3,128,512]{2,1,0:T(8,128)(2,1)S(1)}, u32[]{:S(2)}, u32[]{:S(2)}) collective-permute-start(bf16[3,128,512]{2,1,0:T(8,128)(2,1)S(1)} %slice.18), channel_id=1, source_target_pairs={{0,7},{1,0},{2,1},{3,2},{4,3},{5,4},{6,5},{7,6},{8,15},{9,8},{10,9... | collective-permute-start | bytes 1179656 | tf_op jit(solution)/shard_map/ppermute | solution.py:30
  83.2 11.1 %collective-permute-start.27 = (bf16[2,128,512]{2,1,0:T(8,128)(2,1)S(1)}, bf16[2,128,512]{2,1,0:T(8,128)(2,1)S(1)}, u32[]{:S(2)}, u32[]{:S(2)}) collective-permute-start(bf16[2,128,512]{2,1,0:T(8,128)(2,1)S(1)} %join_parts.7.refs_0_.refs_12_), channel_id=1, source_target_pairs={{0,24},{1,25},{2,26},{3,27},{4,28},{5,29},{6,30},{7,31},{8,0},{9,1... | collective-permute-start | bytes 786440 | tf_op jit(solution)/shard_map/ppermute | solution.py:25
  84.9 10.4 %collective-permute-start.26 = (bf16[2,128,512]{2,1,0:T(8,128)(2,1)S(1)}, bf16[2,128,512]{2,1,0:T(8,128)(2,1)S(1)}, u32[]{:S(2)}, u32[]{:S(2)}) collective-permute-start(bf16[2,128,512]{2,1,0:T(8,128)(2,1)S(1)} %join_parts.7.refs_0_.refs_12_), channel_id=1, source_target_pairs={{0,8},{1,9},{2,10},{3,11},{4,12},{5,13},{6,14},{7,15},{8,16},{9,17... | collective-permute-start | bytes 786440 | tf_op jit(solution)/shard_map/ppermute | solution.py:25
  95.3 11.6 %collective-permute-start.34 = (bf16[1,128,512]{2,1,0:T(8,128)(2,1)S(1)}, bf16[1,128,512]{2,1,0:T(8,128)(2,1)S(1)}, u32[]{:S(2)}, u32[]{:S(2)}) collective-permute-start(bf16[1,128,512]{2,1,0:T(8,128)(2,1)S(1)} %slice.19.refs_4_.refs_16_), channel_id=1, source_target_pairs={{0,16},{1,17},{2,18},{3,19},{4,20},{5,21},{6,22},{7,23},{8,24},{9,... | collective-permute-start | bytes 393224 | tf_op jit(solution)/shard_map/ppermute | solution.py:25
  98.3 13.6 %collective-permute-start.29 = (f32[512,128]{1,0:T(8,128)S(1)}, f32[512,128]{1,0:T(8,128)S(1)}, u32[]{:S(2)}, u32[]{:S(2)}) collective-permute-start(f32[512,128]{1,0:T(8,128)S(1)} %get-tuple-element.95), channel_id=1, source_target_pairs={{0,64},{32,96},{64,128},{96,160},{128,192},{160,224},{192,0},{224,... | collective-permute-start | bytes 786440 | tf_op jit(solution)/shard_map/ppermute | solution.py:35
  99.4 13.9 %collective-permute-start.30 = (f32[512,128]{1,0:T(8,128)S(1)}, f32[512,128]{1,0:T(8,128)S(1)}, u32[]{:S(2)}, u32[]{:S(2)}) collective-permute-start(f32[512,128]{1,0:T(8,128)S(1)} %get-tuple-element.96), channel_id=1, source_target_pairs={{0,128},{32,160},{64,192},{96,224},{128,0},{160,32},{192,64},{224,... | collective-permute-start | bytes 786440 | tf_op jit(solution)/shard_map/ppermute | solution.py:35
  125.3 19.3 %collective-permute-start.41 = (bf16[4,512,128]{2,1,0:T(8,128)(2,1)S(1)}, bf16[4,512,128]{2,1,0:T(8,128)(2,1)S(1)}, u32[]{:S(2)}, u32[]{:S(2)}) collective-permute-start(bf16[4,512,128]{2,1,0:T(8,128)(2,1)S(1)} %pad_maximum_fusion.1.mine), channel_id=1, source_target_pairs={{0,32},{32,0},{64,96},{96,64},{128,160},{160,128},{192,224},{224,1... | collective-permute-start | bytes 1572872 | tf_op jit(solution)/shard_map/ppermute | solution.py:47
  131.9 11.5 %collective-permute-start.43 = (bf16[1024,128]{1,0:T(8,128)(2,1)S(1)}, bf16[1024,128]{1,0:T(8,128)(2,1)S(1)}, u32[]{:S(2)}, u32[]{:S(2)}) collective-permute-start(bf16[1024,128]{1,0:T(8,128)(2,1)S(1)} %get-tuple-element.122), channel_id=1, source_target_pairs={{0,128},{32,160},{1,129},{33,161},{2,130},{34,162},{3,131},{35,163... | collective-permute-start | bytes 786440 | tf_op jit(solution)/shard_map/ppermute | solution.py:39
  133.2 10.2 %collective-permute-start.44 = (bf16[1024,128]{1,0:T(8,128)(2,1)S(1)}, bf16[1024,128]{1,0:T(8,128)(2,1)S(1)}, u32[]{:S(2)}, u32[]{:S(2)}) collective-permute-start(bf16[1024,128]{1,0:T(8,128)(2,1)S(1)} %get-tuple-element.123), channel_id=1, source_target_pairs={{0,192},{32,224},{1,193},{33,225},{2,194},{34,226},{3,195},{35,227... | collective-permute-start | bytes 786440 | tf_op jit(solution)/shard_map/ppermute | solution.py:39
  137.7 11.2 %collective-permute-start.36 = (bf16[512,128]{1,0:T(8,128)(2,1)S(1)}, bf16[512,128]{1,0:T(8,128)(2,1)S(1)}, u32[]{:S(2)}, u32[]{:S(2)}) collective-permute-start(bf16[512,128]{1,0:T(8,128)(2,1)S(1)} %get-tuple-element.117), channel_id=1, source_target_pairs={{0,128},{32,160},{64,192},{96,224},{128,0},{160,32},{192,64},{224,... | collective-permute-start | bytes 393224 | tf_op jit(solution)/shard_map/ppermute | solution.py:35
  (26 other events, 263.8 us)

commit v7 on v6

--- a/solution.py
+++ b/solution.py
@@ -37,10 +37,6 @@
 
 def y_first(value, y):
     return lax.ppermute(value, "row", [(k, y * 2 + k) for k in range(2)])
-
-
-def y_all(value):
-    return jnp.stack([value] + [y_shift(value, d) for d in range(1, NY)])
 
 
 def core_swap(value):
@@ -300,16 +296,20 @@
     def of_one(*messages):
         return x_all(join(messages, (NX,) * len(messages)))
 
-    *two, swapped = together(*x_all(two), core_swap(adjoint))
+    two, one, swapped = together(two, one, core_swap(adjoint))
+    *two, inverse1, inverse3 = together(
+        *x_all(two), y_shift(inverse_factor, 1), y_shift(inverse_factor, 3))
     own = join(two + [one], (None,) * 5)
-    inverse = y_all(inverse_factor)
+    own, later = together(own, inverse_factor)
+    inverse = jnp.stack([inverse_factor, inverse1, y_shift(later, 2), inverse3])
     down1, up1, inverse, *first_x = together(
         z_shift(own, 1), z_shift(own, -1), inverse, *x_all(one[None]))
 
     for_two, for_one = prepare(pos, taper, adjoint, swapped)
-    down2, up2, for_two, for_one, inverse_other, *near = together(
-        z_shift(down1, 1), z_shift(up1, -1), for_two, for_one, core_swap(inverse),
-        *of_one(down1, up1))
+    down2, up2, for_two, for_one, *near = together(
+        z_shift(down1, 1), z_shift(up1, -1), for_two, for_one, *of_one(down1, up1))
+    inverse, down2, up2 = together(inverse, down2, up2)
+    inverse_other = core_swap(inverse)
     sums = product(
         pos, for_two, [own, down1, up1, down2, up2], [(j, [(j, 0, 4)]) for j in range(5)])
     down3, up3, sums, *middle = together(
@@ -318,25 +318,31 @@
     sums_one = product(
         pos, for_one, near + middle,
         [(1 + c, [(NX * c + i, 0, 2) for i in range(NX)]) for c in range(2)])
-    far_low, far_high, sums, sums_one, *third = together(
-        z_shift(down3[:2], 1), z_shift(up3[2:], -1), sums, sums_one, *of_one(down3, up3))
+    third = of_one(down3, up3)
+    far_low, far_high, sums, sums_one = together(
+        z_shift(down3[:2], 1), z_shift(up3[2:], -1), sums, sums_one)
 
     mine, *sent = product(
         pos, for_two, [far_low, far_high], [(7, [(0, 0, 2), (1, 0, 2)])], sums, F32)
+    last = x_all(far_high[2:])
     sums_one = product(pos, for_one, third, [(3, [(i, 0, 2) for i in range(NX)])], sums_one)
-    r1, r2, r3, sums_one, *last = together(
-        *[y_shift(part, d + 1) for d, part in enumerate(sent)], sums_one, *x_all(far_high[2:]))
-    second_grad = incoming + ((mine + r1) + (r2 + r3))
-    rounded = y_all(second_grad.astype(BF16))
-    rounded_other = core_swap(rounded)
-
     where = tuple(
         ((i, 0),) + tuple((NX * (1 + j // 2) + i, j % 2) for j in range(7)) for i in range(NX))
-    first, *rest = diagonal(pos, first_x + near + middle + third + last, where)
-    rest = [y_first(part, d + 1) for d, part in enumerate(rest)]
-    mine, *sent = product(
+    columns = diagonal(pos, first_x + near + middle + third + last, where)
+    r1, r2, r3, sums_one, *columns = together(
+        *[y_shift(part, d + 1) for d, part in enumerate(sent)], sums_one, *columns)
+    second_grad = incoming + ((mine + r1) + (r2 + r3))
+    rounded = second_grad.astype(BF16)
+
+    sums_one = product(
         pos, for_one, first_x + last,
         [(0, [(NX * s + i, 0, 1) for i in range(NX) for s in range(2)])], sums_one, BF16)
+    first, *rest = columns
+    rest = [y_first(part, d + 1) for d, part in enumerate(rest)]
+    s1, s2, s3, *rest = together(*[y_shift(rounded, d) for d in range(1, NY)], *rest, *sums_one)
+    rest, (mine, *sent) = rest[:3], rest[3:]
+    rounded = jnp.stack([rounded, s1, s2, s3])
+    rounded_other = core_swap(rounded)
     r1, r2, r3 = [y_shift(part, d + 1).astype(F32) for d, part in enumerate(sent)]
     factors = factor(pos, inverse, inverse_other, [first] + rest)
     term = carried(rounded, rounded_other, *factors)

time: 151 us -> 138 us (0.914)
  waiting for transfers between devices: 59.6 us -> 31.8 us
  starting transfers between devices: 61.8 us -> 78 us
    ppermute x18, waiting for transfers between devices: 36.1 us -> 18 us  [x_shift(): return lax.ppermute(value, 'col', pairs)]
    ppermute x18, starting transfers between devices: 21.9 us -> 34 us  [x_shift(): return lax.ppermute(value, 'col', pairs)]
    ppermute x3, starting transfers between devices: 3.92 us -> 11 us  [y_first(): return lax.ppermute(value, 'row', [(k, y * 2 + k) for k in range(2)])]
    ppermute x3, waiting for transfers between devices: 5.94 us -> 0.01 us  [y_first(): return lax.ppermute(value, 'row', [(k, y * 2 + k) for k in range(2)])]
    ppermute x12, waiting for transfers between devices: 16.3 us -> 12.6 us  [y_shift(): return lax.ppermute(value, 'row', pairs)]
    ppermute x12, starting transfers between devices: 16 us -> 13.2 us  [y_shift(): return lax.ppermute(value, 'row', pairs)]
  transfers between devices with their start and end apart: 45 -> 45, of which waited for: 26 -> 17; matrix products, arithmetic and copies ran while one was open for 1% -> 1% of each run, Pallas kernels for 15% -> 16%
where the time goes in v7:
time: 138 us
  starting transfers between devices  78 us (57%)
  waiting for transfers between devices  31.8 us (23%)
  Pallas kernels  22.8 us (17%)
  other arithmetic  2.78 us (2%)
  local copies, waits for them, and re-layouts  1.92 us (1%)
    ppermute x18, starting transfers between devices, x_shift(): return lax.ppermute(value, 'col', pairs)  34 us
    ppermute x18, waiting for transfers between devices, x_shift(): return lax.ppermute(value, 'col', pairs)  18 us
    ppermute x12, starting transfers between devices, y_shift(): return lax.ppermute(value, 'row', pairs)  13.2 us
    ppermute x12, waiting for transfers between devices, y_shift(): return lax.ppermute(value, 'row', pairs)  12.6 us
    pallas_call x6, Pallas kernels, product(): pl.pallas_call(kernel, out_shape=(column,) + (jax.ShapeDtypeStruct((512,...  12.3 us
    ppermute x8, starting transfers between devices, z_shift(): return lax.ppermute(value, 'col', pairs)  11.8 us
    ppermute x3, starting transfers between devices, y_first(): return lax.ppermute(value, 'row', [(k, y * 2 + k) for k in range(2)])  11 us
    ppermute x4, starting transfers between devices, core_swap(): return lax.ppermute(value, 'row', [(r, r ^ 1) for r in range(2 * NY)])  7.93 us
  transfers between devices with their start and end apart: 45, of which 17 were waited for; matrix products, arithmetic and copies ran while one was open for 1% of the time, Pallas kernels for 16%

profile of v7, /device:TPU:1, one launch (start us, length us, event | category | flops | bytes accessed | tf_op | source)
XLA Modules:
  0.0 138.2 jit_solution(251878938441804467)
XLA Ops:
  0.6 3.3 %collective-permute-start.1 = (bf16[2048,512]{1,0:T(8,128)(2,1)}, bf16[2048,512]{1,0:T(8,128)(2,1)}, u32[]{:S(2)}, u32[]{:S(2)}) collective-permute-start(bf16[2048,512]{1,0:T(8,128)(2,1)} %mine.1), channel_id=1, source_target_pairs={{0,32},{32,0},{64,96},{96,64},{128,160},{160,128},{192,224},{224,1... | collective-permute-start | bytes 6291464 | tf_op jit(solution)/shard_map/ppermute | solution.py:43
  18.2 4.9 %collective-permute-start.8 = (bf16[5,128,512]{2,1,0:T(8,128)(2,1)S(1)}, bf16[5,128,512]{2,1,0:T(8,128)(2,1)S(1)}, u32[]{:S(2)}, u32[]{:S(2)}) collective-permute-start(bf16[5,128,512]{2,1,0:T(8,128)(2,1)S(1)} %join_parts.4.refs_0_), channel_id=1, source_target_pairs={{0,7},{1,0},{2,1},{3,2},{4,3},{5,4},{6,5},{7,6},{8,15},{9,8},{10,9... | collective-permute-start | bytes 1966088 | tf_op jit(solution)/shard_map/ppermute | solution.py:30
  24.5 3.1 %collective-permute-start.12 = (bf16[1,128,512]{2,1,0:T(8,128)(2,1)S(1)}, bf16[1,128,512]{2,1,0:T(8,128)(2,1)S(1)}, u32[]{:S(2)}, u32[]{:S(2)}) collective-permute-start(bf16[1,128,512]{2,1,0:T(8,128)(2,1)S(1)} %bitcast.17), channel_id=1, source_target_pairs={{0,16},{1,17},{2,18},{3,19},{4,20},{5,21},{6,22},{7,23},{8,24},{9,... | collective-permute-start | bytes 393224 | tf_op jit(solution)/shard_map/ppermute | solution.py:25
  30.5 3.1 %collective-permute-start.10 = (bf16[1,128,512]{2,1,0:T(8,128)(2,1)S(1)}, bf16[1,128,512]{2,1,0:T(8,128)(2,1)S(1)}, u32[]{:S(2)}, u32[]{:S(2)}) collective-permute-start(bf16[1,128,512]{2,1,0:T(8,128)(2,1)S(1)} %bitcast.19), channel_id=1, source_target_pairs={{0,8},{1,9},{2,10},{3,11},{4,12},{5,13},{6,14},{7,15},{8,16},{9,17... | collective-permute-start | bytes 393224 | tf_op jit(solution)/shard_map/ppermute | solution.py:25
  34.7 2.5 %collective-permute-done.10.refs_1_ = bf16[1,128,512]{2,1,0:T(8,128)(2,1)S(1)} collective-permute-done((bf16[1,128,512]{2,1,0:T(8,128)(2,1)S(1)}, bf16[1,128,512]{2,1,0:T(8,128)(2,1)S(1)}, u32[]{:S(2)}, u32[]{:S(2)}) %collective-permute-start.10) | collective-permute-done | bytes 131104 | tf_op jit(solution)/shard_map/ppermute | solution.py:25
  38.4 2.7 %collective-permute-start.14 = (bf16[5,128,512]{2,1,0:T(8,128)(2,1)S(1)}, bf16[5,128,512]{2,1,0:T(8,128)(2,1)S(1)}, u32[]{:S(2)}, u32[]{:S(2)}) collective-permute-start(bf16[5,128,512]{2,1,0:T(8,128)(2,1)S(1)} %collective-permute-done.8.refs_1_.refs_2_), channel_id=1, source_target_pairs={{0,7},{1,0},{2,1},{3,2},{4,3},{5,4},{6,5},{7,6},{8,15},{9,8},{10,9... | collective-permute-start | bytes 1966088 | tf_op jit(solution)/shard_map/ppermute | solution.py:30
  41.1 4.4 %collective-permute-start.17 = (bf16[2,128,512]{2,1,0:T(8,128)(2,1)S(1)}, bf16[2,128,512]{2,1,0:T(8,128)(2,1)S(1)}, u32[]{:S(2)}, u32[]{:S(2)}) collective-permute-start(bf16[2,128,512]{2,1,0:T(8,128)(2,1)S(1)} %join_parts.5.refs_0_.refs_4_), channel_id=1, source_target_pairs={{0,16},{1,17},{2,18},{3,19},{4,20},{5,21},{6,22},{7,23},{8,24},{9,... | collective-permute-start | bytes 786440 | tf_op jit(solution)/shard_map/ppermute | solution.py:25
  47.0 4.9 %prepare_adjoint.1 = (bf16[8,512,512]{2,1,0:T(8,128)(2,1)S(1)}, bf16[4,512,1024]{2,1,0:T(8,128)(2,1)S(1)}) custom-call(s32[4]{0:T(128)S(1)} %pad_add_fusion.pos, s32[64,64]{1,0:T(8,128)S(1)} %copy-done.3, bf16[2048,512]{1,0:T(8,128)(2,1)S(1)} %copy-done, bf16[2048,512]{1,0:T(8,128)(2,1)} %collective-permute-done.1.other), custom_call_target="tpu_custom_call" | custom-call | tf_op jit(solution)/shard_map/prepare_adjoint/pallas_call | solution.py:135
  51.9 4.7 %collective-permute-done.16.refs_2_.refs_6_ = bf16[2,128,512]{2,1,0:T(8,128)(2,1)S(1)} collective-permute-done((bf16[2,128,512]{2,1,0:T(8,128)(2,1)S(1)}, bf16[2,128,512]{2,1,0:T(8,128)(2,1)S(1)}, u32[]{:S(2)}, u32[]{:S(2)}) %collective-permute-start.16) | collective-permute-done | bytes 262176 | tf_op jit(solution)/shard_map/ppermute | solution.py:25
  56.8 2.7 %collective-permute-start.19 = (bf16[5,128,512]{2,1,0:T(8,128)(2,1)S(1)}, bf16[5,128,512]{2,1,0:T(8,128)(2,1)S(1)}, u32[]{:S(2)}, u32[]{:S(2)}) collective-permute-start(bf16[5,128,512]{2,1,0:T(8,128)(2,1)S(1)} %collective-permute-done.14.refs_4_.refs_1_), channel_id=1, source_target_pairs={{0,7},{1,0},{2,1},{3,2},{4,3},{5,4},{6,5},{7,6},{8,15},{9,8},{10,9... | collective-permute-start | bytes 1966088 | tf_op jit(solution)/shard_map/ppermute | solution.py:30
  59.5 3.5 %collective-permute-start.22 = (bf16[2,128,512]{2,1,0:T(8,128)(2,1)S(1)}, bf16[2,128,512]{2,1,0:T(8,128)(2,1)S(1)}, u32[]{:S(2)}, u32[]{:S(2)}) collective-permute-start(bf16[2,128,512]{2,1,0:T(8,128)(2,1)S(1)} %join_parts.6.refs_4_.refs_8_), channel_id=1, source_target_pairs={{0,16},{1,17},{2,18},{3,19},{4,20},{5,21},{6,22},{7,23},{8,24},{9,... | collective-permute-start | bytes 786440 | tf_op jit(solution)/shard_map/ppermute | solution.py:25
  64.9 3.0 %masked_product.6.refs_2_ = f32[512,512]{1,0:T(8,128)S(1)} custom-call(s32[4]{0:T(128)S(1)} %pad_add_fusion.pos, bf16[8,512,512]{2,1,0:T(8,128)(2,1)S(1)} %get-tuple-element.95.adjoint, bf16[5,128,512]{2,1,0:T(8,128)(2,1)S(1)} %join_parts.4.refs_0_, bf16[5,128,512]{2,1,0:T(8,128)(2,1)S(1)} %collective-permute-done.7.refs_0_.refs_1_, ...), custom_call_target="tpu_custom_call" | custom-call | tf_op jit(solution)/shard_map/masked_product/pallas_call | solution.py:189
  67.9 6.9 %collective-permute-done.21.refs_6_.refs_10_ = bf16[2,128,512]{2,1,0:T(8,128)(2,1)S(1)} collective-permute-done((bf16[2,128,512]{2,1,0:T(8,128)(2,1)S(1)}, bf16[2,128,512]{2,1,0:T(8,128)(2,1)S(1)}, u32[]{:S(2)}, u32[]{:S(2)}) %collective-permute-start.21) | collective-permute-done | bytes 262176 | tf_op jit(solution)/shard_map/ppermute | solution.py:25
  76.8 3.3 %collective-permute-start.30 = (bf16[2,128,512]{2,1,0:T(8,128)(2,1)S(1)}, bf16[2,128,512]{2,1,0:T(8,128)(2,1)S(1)}, u32[]{:S(2)}, u32[]{:S(2)}) collective-permute-start(bf16[2,128,512]{2,1,0:T(8,128)(2,1)S(1)} %join_parts.7.refs_0_.refs_12_), channel_id=1, source_target_pairs={{0,16},{1,17},{2,18},{3,19},{4,20},{5,21},{6,22},{7,23},{8,24},{9,... | collective-permute-start | bytes 786440 | tf_op jit(solution)/shard_map/ppermute | solution.py:25
  85.6 3.1 %collective-permute-start.33 = (bf16[1,128,512]{2,1,0:T(8,128)(2,1)S(1)}, bf16[1,128,512]{2,1,0:T(8,128)(2,1)S(1)}, u32[]{:S(2)}, u32[]{:S(2)}) collective-permute-start(bf16[1,128,512]{2,1,0:T(8,128)(2,1)S(1)} %slice.19.refs_16_.refs_4_), channel_id=1, source_target_pairs={{0,16},{1,17},{2,18},{3,19},{4,20},{5,21},{6,22},{7,23},{8,24},{9,... | collective-permute-start | bytes 393224 | tf_op jit(solution)/shard_map/ppermute | solution.py:25
  90.0 2.5 %collective-permute-start.26 = (f32[512,128]{1,0:T(8,128)S(1)}, f32[512,128]{1,0:T(8,128)S(1)}, u32[]{:S(2)}, u32[]{:S(2)}) collective-permute-start(f32[512,128]{1,0:T(8,128)S(1)} %get-tuple-element.118), channel_id=1, source_target_pairs={{0,128},{32,160},{64,192},{96,224},{128,0},{160,32},{192,64},{224,... | collective-permute-start | bytes 786440 | tf_op jit(solution)/shard_map/ppermute | solution.py:35
  93.1 3.6 %collective-permute-start.32 = (bf16[1,128,512]{2,1,0:T(8,128)(2,1)S(1)}, bf16[1,128,512]{2,1,0:T(8,128)(2,1)S(1)}, u32[]{:S(2)}, u32[]{:S(2)}) collective-permute-start(bf16[1,128,512]{2,1,0:T(8,128)(2,1)S(1)} %slice.19.refs_16_.refs_4_), channel_id=1, source_target_pairs={{0,24},{1,25},{2,26},{3,27},{4,28},{5,29},{6,30},{7,31},{8,0},{9,1... | collective-permute-start | bytes 393224 | tf_op jit(solution)/shard_map/ppermute | solution.py:25
  105.3 3.4 %collective-permute-start.36 = (bf16[512,128]{1,0:T(8,128)(2,1)S(1)}, bf16[512,128]{1,0:T(8,128)(2,1)S(1)}, u32[]{:S(2)}, u32[]{:S(2)}) collective-permute-start(bf16[512,128]{1,0:T(8,128)(2,1)S(1)} %get-tuple-element.154), channel_id=1, source_target_pairs={{0,192},{32,224},{64,0},{96,32},{128,64},{160,96},{192,128},{224,1... | collective-permute-start | bytes 393224 | tf_op jit(solution)/shard_map/ppermute | solution.py:35
  108.8 2.5 %collective-permute-start.37 = (bf16[1024,128]{1,0:T(8,128)(2,1)S(1)}, bf16[1024,128]{1,0:T(8,128)(2,1)S(1)}, u32[]{:S(2)}, u32[]{:S(2)}) collective-permute-start(bf16[1024,128]{1,0:T(8,128)(2,1)S(1)} %get-tuple-element.132), channel_id=1, source_target_pairs={{0,64},{32,96},{1,65},{33,97},{2,66},{34,98},{3,67},{35,99},{4,68}... | collective-permute-start | bytes 786440 | tf_op jit(solution)/shard_map/ppermute | solution.py:39
  111.2 3.1 %collective-permute-start.38 = (bf16[1024,128]{1,0:T(8,128)(2,1)S(1)}, bf16[1024,128]{1,0:T(8,128)(2,1)S(1)}, u32[]{:S(2)}, u32[]{:S(2)}) collective-permute-start(bf16[1024,128]{1,0:T(8,128)(2,1)S(1)} %get-tuple-element.133), channel_id=1, source_target_pairs={{0,128},{32,160},{1,129},{33,161},{2,130},{34,162},{3,131},{35,163... | collective-permute-start | bytes 786440 | tf_op jit(solution)/shard_map/ppermute | solution.py:39
  114.3 5.5 %collective-permute-start.39 = (bf16[1024,128]{1,0:T(8,128)(2,1)S(1)}, bf16[1024,128]{1,0:T(8,128)(2,1)S(1)}, u32[]{:S(2)}, u32[]{:S(2)}) collective-permute-start(bf16[1024,128]{1,0:T(8,128)(2,1)S(1)} %get-tuple-element.134), channel_id=1, source_target_pairs={{0,192},{32,224},{1,193},{33,225},{2,194},{34,226},{3,195},{35,227... | collective-permute-start | bytes 786440 | tf_op jit(solution)/shard_map/ppermute | solution.py:39
  119.9 2.8 %masked_product.11 = (f32[512,128]{1,0:T(8,128)S(1)}, bf16[512,128]{1,0:T(8,128)(2,1)S(1)}, bf16[512,128]{1,0:T(8,128)(2,1)S(1)}, bf16[512,128]{1,0:T(8,128)(2,1)S(1)}) custom-call(s32[4]{0:T(128)S(1)} %pad_add_fusion.pos, bf16[4,512,1024]{2,1,0:T(8,128)(2,1)S(1)} %get-tuple-element.104.adjoint, bf16[1,128,512]{2,1,0:T(8,128)(2,1)S(1)} %bitcast.21, ...), custom_call_target="tpu_custom_call" | custom-call | tf_op jit(solution)/shard_map/masked_product/pallas_call | solution.py:189
  122.7 2.4 %collective-permute-done.34 = bf16[512,128]{1,0:T(8,128)(2,1)S(1)} collective-permute-done((bf16[512,128]{1,0:T(8,128)(2,1)S(1)}, bf16[512,128]{1,0:T(8,128)(2,1)S(1)}, u32[]{:S(2)}, u32[]{:S(2)}) %collective-permute-start.34) | collective-permute-done | bytes 131104 | tf_op jit(solution)/shard_map/ppermute | solution.py:35
  133.6 3.9 %collective-permute-done.41 = bf16[512,128]{1,0:T(8,128)(2,1)S(1)} collective-permute-done((bf16[512,128]{1,0:T(8,128)(2,1)S(1)}, bf16[512,128]{1,0:T(8,128)(2,1)S(1)}, u32[]{:S(2)}, u32[]{:S(2)}) %collective-permute-start.41) | collective-permute-done | bytes 131104 | tf_op jit(solution)/shard_map/ppermute | solution.py:35
  (102 shorter events, 51.5 us)
Async XLA Ops:
  18.2 19.1 %collective-permute-start.8 = (bf16[5,128,512]{2,1,0:T(8,128)(2,1)S(1)}, bf16[5,128,512]{2,1,0:T(8,128)(2,1)S(1)}, u32[]{:S(2)}, u32[]{:S(2)}) collective-permute-start(bf16[5,128,512]{2,1,0:T(8,128)(2,1)S(1)} %join_parts.4.refs_0_), channel_id=1, source_target_pairs={{0,7},{1,0},{2,1},{3,2},{4,3},{5,4},{6,5},{7,6},{8,15},{9,8},{10,9... | collective-permute-start | bytes 1966088 | tf_op jit(solution)/shard_map/ppermute | solution.py:30
  23.1 15.3 %collective-permute-start.7 = (bf16[5,128,512]{2,1,0:T(8,128)(2,1)S(1)}, bf16[5,128,512]{2,1,0:T(8,128)(2,1)S(1)}, u32[]{:S(2)}, u32[]{:S(2)}) collective-permute-start(bf16[5,128,512]{2,1,0:T(8,128)(2,1)S(1)} %join_parts.4.refs_0_), channel_id=1, source_target_pairs={{0,1},{1,2},{2,3},{3,4},{4,5},{5,6},{6,7},{7,0},{8,9},{9,10},{10,1... | collective-permute-start | bytes 1966088 | tf_op jit(solution)/shard_map/ppermute | solution.py:30
  24.5 10.3 %collective-permute-start.12 = (bf16[1,128,512]{2,1,0:T(8,128)(2,1)S(1)}, bf16[1,128,512]{2,1,0:T(8,128)(2,1)S(1)}, u32[]{:S(2)}, u32[]{:S(2)}) collective-permute-start(bf16[1,128,512]{2,1,0:T(8,128)(2,1)S(1)} %bitcast.17), channel_id=1, source_target_pairs={{0,16},{1,17},{2,18},{3,19},{4,20},{5,21},{6,22},{7,23},{8,24},{9,... | collective-permute-start | bytes 393224 | tf_op jit(solution)/shard_map/ppermute | solution.py:25
  38.4 18.4 %collective-permute-start.13 = (bf16[5,128,512]{2,1,0:T(8,128)(2,1)S(1)}, bf16[5,128,512]{2,1,0:T(8,128)(2,1)S(1)}, u32[]{:S(2)}, u32[]{:S(2)}) collective-permute-start(bf16[5,128,512]{2,1,0:T(8,128)(2,1)S(1)} %collective-permute-done.7.refs_0_.refs_1_), channel_id=1, source_target_pairs={{0,1},{1,2},{2,3},{3,4},{4,5},{5,6},{6,7},{7,0},{8,9},{9,10},{10,1... | collective-permute-start | bytes 1966088 | tf_op jit(solution)/shard_map/ppermute | solution.py:30
  38.4 18.4 %collective-permute-start.14 = (bf16[5,128,512]{2,1,0:T(8,128)(2,1)S(1)}, bf16[5,128,512]{2,1,0:T(8,128)(2,1)S(1)}, u32[]{:S(2)}, u32[]{:S(2)}) collective-permute-start(bf16[5,128,512]{2,1,0:T(8,128)(2,1)S(1)} %collective-permute-done.8.refs_1_.refs_2_), channel_id=1, source_target_pairs={{0,7},{1,0},{2,1},{3,2},{4,3},{5,4},{6,5},{7,6},{8,15},{9,8},{10,9... | collective-permute-start | bytes 1966088 | tf_op jit(solution)/shard_map/ppermute | solution.py:30
  41.1 10.8 %collective-permute-start.17 = (bf16[2,128,512]{2,1,0:T(8,128)(2,1)S(1)}, bf16[2,128,512]{2,1,0:T(8,128)(2,1)S(1)}, u32[]{:S(2)}, u32[]{:S(2)}) collective-permute-start(bf16[2,128,512]{2,1,0:T(8,128)(2,1)S(1)} %join_parts.5.refs_0_.refs_4_), channel_id=1, source_target_pairs={{0,16},{1,17},{2,18},{3,19},{4,20},{5,21},{6,22},{7,23},{8,24},{9,... | collective-permute-start | bytes 786440 | tf_op jit(solution)/shard_map/ppermute | solution.py:25
  45.5 11.1 %collective-permute-start.16 = (bf16[2,128,512]{2,1,0:T(8,128)(2,1)S(1)}, bf16[2,128,512]{2,1,0:T(8,128)(2,1)S(1)}, u32[]{:S(2)}, u32[]{:S(2)}) collective-permute-start(bf16[2,128,512]{2,1,0:T(8,128)(2,1)S(1)} %join_parts.5.refs_0_.refs_4_), channel_id=1, source_target_pairs={{0,24},{1,25},{2,26},{3,27},{4,28},{5,29},{6,30},{7,31},{8,0},{9,1... | collective-permute-start | bytes 786440 | tf_op jit(solution)/shard_map/ppermute | solution.py:25
  56.8 18.3 %collective-permute-start.18 = (bf16[5,128,512]{2,1,0:T(8,128)(2,1)S(1)}, bf16[5,128,512]{2,1,0:T(8,128)(2,1)S(1)}, u32[]{:S(2)}, u32[]{:S(2)}) collective-permute-start(bf16[5,128,512]{2,1,0:T(8,128)(2,1)S(1)} %collective-permute-done.13.refs_3_.refs_0_), channel_id=1, source_target_pairs={{0,1},{1,2},{2,3},{3,4},{4,5},{5,6},{6,7},{7,0},{8,9},{9,10},{10,1... | collective-permute-start | bytes 1966088 | tf_op jit(solution)/shard_map/ppermute | solution.py:30
  56.8 18.3 %collective-permute-start.19 = (bf16[5,128,512]{2,1,0:T(8,128)(2,1)S(1)}, bf16[5,128,512]{2,1,0:T(8,128)(2,1)S(1)}, u32[]{:S(2)}, u32[]{:S(2)}) collective-permute-start(bf16[5,128,512]{2,1,0:T(8,128)(2,1)S(1)} %collective-permute-done.14.refs_4_.refs_1_), channel_id=1, source_target_pairs={{0,7},{1,0},{2,1},{3,2},{4,3},{5,4},{6,5},{7,6},{8,15},{9,8},{10,9... | collective-permute-start | bytes 1966088 | tf_op jit(solution)/shard_map/ppermute | solution.py:30
  63.0 11.8 %collective-permute-start.21 = (bf16[2,128,512]{2,1,0:T(8,128)(2,1)S(1)}, bf16[2,128,512]{2,1,0:T(8,128)(2,1)S(1)}, u32[]{:S(2)}, u32[]{:S(2)}) collective-permute-start(bf16[2,128,512]{2,1,0:T(8,128)(2,1)S(1)} %join_parts.6.refs_4_.refs_8_), channel_id=1, source_target_pairs={{0,24},{1,25},{2,26},{3,27},{4,28},{5,29},{6,30},{7,31},{8,0},{9,1... | collective-permute-start | bytes 786440 | tf_op jit(solution)/shard_map/ppermute | solution.py:25
  75.2 10.4 %collective-permute-start.24 = (bf16[3,128,512]{2,1,0:T(8,128)(2,1)S(1)}, bf16[3,128,512]{2,1,0:T(8,128)(2,1)S(1)}, u32[]{:S(2)}, u32[]{:S(2)}) collective-permute-start(bf16[3,128,512]{2,1,0:T(8,128)(2,1)S(1)} %slice.18), channel_id=1, source_target_pairs={{0,7},{1,0},{2,1},{3,2},{4,3},{5,4},{6,5},{7,6},{8,15},{9,8},{10,9... | collective-permute-start | bytes 1179656 | tf_op jit(solution)/shard_map/ppermute | solution.py:30
  75.3 10.2 %collective-permute-start.23 = (bf16[2,128,512]{2,1,0:T(8,128)(2,1)S(1)}, bf16[2,128,512]{2,1,0:T(8,128)(2,1)S(1)}, u32[]{:S(2)}, u32[]{:S(2)}) collective-permute-start(bf16[2,128,512]{2,1,0:T(8,128)(2,1)S(1)} %slice.17), channel_id=1, source_target_pairs={{0,1},{1,2},{2,3},{3,4},{4,5},{5,6},{6,7},{7,0},{8,9},{9,10},{10,1... | collective-permute-start | bytes 786440 | tf_op jit(solution)/shard_map/ppermute | solution.py:30
  76.8 13.2 %collective-permute-start.30 = (bf16[2,128,512]{2,1,0:T(8,128)(2,1)S(1)}, bf16[2,128,512]{2,1,0:T(8,128)(2,1)S(1)}, u32[]{:S(2)}, u32[]{:S(2)}) collective-permute-start(bf16[2,128,512]{2,1,0:T(8,128)(2,1)S(1)} %join_parts.7.refs_0_.refs_12_), channel_id=1, source_target_pairs={{0,16},{1,17},{2,18},{3,19},{4,20},{5,21},{6,22},{7,23},{8,24},{9,... | collective-permute-start | bytes 786440 | tf_op jit(solution)/shard_map/ppermute | solution.py:25
  80.2 12.6 %collective-permute-start.29 = (bf16[2,128,512]{2,1,0:T(8,128)(2,1)S(1)}, bf16[2,128,512]{2,1,0:T(8,128)(2,1)S(1)}, u32[]{:S(2)}, u32[]{:S(2)}) collective-permute-start(bf16[2,128,512]{2,1,0:T(8,128)(2,1)S(1)} %join_parts.7.refs_0_.refs_12_), channel_id=1, source_target_pairs={{0,24},{1,25},{2,26},{3,27},{4,28},{5,29},{6,30},{7,31},{8,0},{9,1... | collective-permute-start | bytes 786440 | tf_op jit(solution)/shard_map/ppermute | solution.py:25
  81.7 11.4 %collective-permute-start.28 = (bf16[2,128,512]{2,1,0:T(8,128)(2,1)S(1)}, bf16[2,128,512]{2,1,0:T(8,128)(2,1)S(1)}, u32[]{:S(2)}, u32[]{:S(2)}) collective-permute-start(bf16[2,128,512]{2,1,0:T(8,128)(2,1)S(1)} %join_parts.7.refs_0_.refs_12_), channel_id=1, source_target_pairs={{0,8},{1,9},{2,10},{3,11},{4,12},{5,13},{6,14},{7,15},{8,16},{9,17... | collective-permute-start | bytes 786440 | tf_op jit(solution)/shard_map/ppermute | solution.py:25
  85.6 11.2 %collective-permute-start.33 = (bf16[1,128,512]{2,1,0:T(8,128)(2,1)S(1)}, bf16[1,128,512]{2,1,0:T(8,128)(2,1)S(1)}, u32[]{:S(2)}, u32[]{:S(2)}) collective-permute-start(bf16[1,128,512]{2,1,0:T(8,128)(2,1)S(1)} %slice.19.refs_16_.refs_4_), channel_id=1, source_target_pairs={{0,16},{1,17},{2,18},{3,19},{4,20},{5,21},{6,22},{7,23},{8,24},{9,... | collective-permute-start | bytes 393224 | tf_op jit(solution)/shard_map/ppermute | solution.py:25
  89.9 14.5 %collective-permute-start.25 = (f32[512,128]{1,0:T(8,128)S(1)}, f32[512,128]{1,0:T(8,128)S(1)}, u32[]{:S(2)}, u32[]{:S(2)}) collective-permute-start(f32[512,128]{1,0:T(8,128)S(1)} %get-tuple-element.117), channel_id=1, source_target_pairs={{0,64},{32,96},{64,128},{96,160},{128,192},{160,224},{192,0},{224,... | collective-permute-start | bytes 786440 | tf_op jit(solution)/shard_map/ppermute | solution.py:35
  90.0 14.4 %collective-permute-start.26 = (f32[512,128]{1,0:T(8,128)S(1)}, f32[512,128]{1,0:T(8,128)S(1)}, u32[]{:S(2)}, u32[]{:S(2)}) collective-permute-start(f32[512,128]{1,0:T(8,128)S(1)} %get-tuple-element.118), channel_id=1, source_target_pairs={{0,128},{32,160},{64,192},{96,224},{128,0},{160,32},{192,64},{224,... | collective-permute-start | bytes 786440 | tf_op jit(solution)/shard_map/ppermute | solution.py:35
  92.8 11.8 %collective-permute-start.27 = (f32[512,128]{1,0:T(8,128)S(1)}, f32[512,128]{1,0:T(8,128)S(1)}, u32[]{:S(2)}, u32[]{:S(2)}) collective-permute-start(f32[512,128]{1,0:T(8,128)S(1)} %get-tuple-element.119), channel_id=1, source_target_pairs={{0,192},{32,224},{64,0},{96,32},{128,64},{160,96},{192,128},{224,1... | collective-permute-start | bytes 786440 | tf_op jit(solution)/shard_map/ppermute | solution.py:35
  99.0 32.3 %collective-permute-start.44 = (bf16[4,128,1024]{2,1,0:T(8,128)(2,1)S(1)}, bf16[4,128,1024]{2,1,0:T(8,128)(2,1)S(1)}, u32[]{:S(2)}, u32[]{:S(2)}) collective-permute-start(bf16[4,128,1024]{2,1,0:T(8,128)(2,1)S(1)} %pad_maximum_fusion.inverse), channel_id=1, source_target_pairs={{0,32},{32,0},{64,96},{96,64},{128,160},{160,128},{192,224},{224,1... | collective-permute-start | bytes 3145736 | tf_op jit(solution)/shard_map/ppermute | solution.py:43
  108.7 11.1 %collective-permute-start.35 = (bf16[512,128]{1,0:T(8,128)(2,1)S(1)}, bf16[512,128]{1,0:T(8,128)(2,1)S(1)}, u32[]{:S(2)}, u32[]{:S(2)}) collective-permute-start(bf16[512,128]{1,0:T(8,128)(2,1)S(1)} %get-tuple-element.154), channel_id=1, source_target_pairs={{0,128},{32,160},{64,192},{96,224},{128,0},{160,32},{192,64},{224,... | collective-permute-start | bytes 393224 | tf_op jit(solution)/shard_map/ppermute | solution.py:35
  108.8 16.4 %collective-permute-start.37 = (bf16[1024,128]{1,0:T(8,128)(2,1)S(1)}, bf16[1024,128]{1,0:T(8,128)(2,1)S(1)}, u32[]{:S(2)}, u32[]{:S(2)}) collective-permute-start(bf16[1024,128]{1,0:T(8,128)(2,1)S(1)} %get-tuple-element.132), channel_id=1, source_target_pairs={{0,64},{32,96},{1,65},{33,97},{2,66},{34,98},{3,67},{35,99},{4,68}... | collective-permute-start | bytes 786440 | tf_op jit(solution)/shard_map/ppermute | solution.py:39
  111.2 13.9 %collective-permute-start.38 = (bf16[1024,128]{1,0:T(8,128)(2,1)S(1)}, bf16[1024,128]{1,0:T(8,128)(2,1)S(1)}, u32[]{:S(2)}, u32[]{:S(2)}) collective-permute-start(bf16[1024,128]{1,0:T(8,128)(2,1)S(1)} %get-tuple-element.133), channel_id=1, source_target_pairs={{0,128},{32,160},{1,129},{33,161},{2,130},{34,162},{3,131},{35,163... | collective-permute-start | bytes 786440 | tf_op jit(solution)/shard_map/ppermute | solution.py:39
  114.3 10.8 %collective-permute-start.39 = (bf16[1024,128]{1,0:T(8,128)(2,1)S(1)}, bf16[1024,128]{1,0:T(8,128)(2,1)S(1)}, u32[]{:S(2)}, u32[]{:S(2)}) collective-permute-start(bf16[1024,128]{1,0:T(8,128)(2,1)S(1)} %get-tuple-element.134), channel_id=1, source_target_pairs={{0,192},{32,224},{1,193},{33,225},{2,194},{34,226},{3,195},{35,227... | collective-permute-start | bytes 786440 | tf_op jit(solution)/shard_map/ppermute | solution.py:39
  (26 other events, 251.9 us)

commit v8 on v7

--- a/solution.py
+++ b/solution.py
@@ -12,6 +12,9 @@
 SUB = 64
 PAIR = 2 * SUB
 HALF = 512
+ROW = 16
+ONE = PAIR // ROW + 1
+TWO = NX * PAIR // ROW
 F32, BF16 = jnp.float32, jnp.bfloat16
 VMEM = pl.BlockSpec(memory_space=pltpu.VMEM)
 SMEM = pl.BlockSpec(memory_space=pltpu.SMEM)
@@ -82,20 +85,66 @@
     )(pos, two, one)
 
 
-def join_kernel(picks, *refs):
-    for n, pick in enumerate(picks):
-        refs[-1][n] = refs[n][...] if pick is None else refs[n][pick]
-
-
-def join(parts, picks):
-    return pl.pallas_call(
-        functools.partial(join_kernel, picks),
-        out_shape=jax.ShapeDtypeStruct((len(parts), PAIR, HALF), BF16),
-        in_specs=[VMEM] * len(parts),
+def top_kernel(pos, own, taken, *outs):
+    first = pos[3] == 0
+    for y, out in enumerate(outs):
+        at = slice(y * 128, y * 128 + 128)
+        out[...] = jnp.where(first, own[1, :, at], taken[1, :, at])
+
+
+def top(pos, own, taken):
+    return pl.pallas_call(
+        top_kernel,
+        out_shape=(jax.ShapeDtypeStruct((SUB, 128), BF16),) * NY,
+        in_specs=[SMEM, VMEM, VMEM],
+        out_specs=(VMEM,) * NY,
+        compiler_params=SMALL,
+        name="diagonal_blocks",
+    )(pos, own, taken)
+
+
+def message_kernel(pos, two, down, up, far, one, own, b1, b2, b3, out, part):
+    for n, ref in enumerate((two, down, up, far)):
+        out[n * 8:n * 8 + 8] = ref[...].reshape(8, ROW, HALF)
+    rows = one[...].reshape(8, ROW, HALF)
+    out[TWO:TWO + 8] = rows
+    part[0, :8] = rows
+    sent = (b1[...] + b2[...]) + b3[...]
+    columns = jnp.where(pos[2] == 0, own[...], sent)
+    for q in range(NY):
+        at = slice(q * 128, q * 128 + 128)
+        out[TWO + 8, :, at] = columns[q * ROW:(q + 1) * ROW]
+        part[0, 8, :, at] = columns[q * ROW:(q + 1) * ROW]
+
+
+def message(pos, twos, one, blocks):
+    return pl.pallas_call(
+        message_kernel,
+        out_shape=(
+            jax.ShapeDtypeStruct((TWO + ONE, ROW, HALF), BF16),
+            jax.ShapeDtypeStruct((1, ONE, ROW, HALF), BF16),
+        ),
+        in_specs=[SMEM] + [VMEM] * 9,
+        out_specs=(VMEM, VMEM),
+        compiler_params=SMALL,
+        name="ring_message",
+    )(pos, *twos, one, *blocks)
+
+
+def join_kernel(*refs):
+    for n, ref in enumerate(refs[:-1]):
+        refs[-1][n] = ref[TWO:]
+
+
+def join(*messages):
+    return pl.pallas_call(
+        join_kernel,
+        out_shape=jax.ShapeDtypeStruct((len(messages), ONE, ROW, HALF), BF16),
+        in_specs=[VMEM] * len(messages),
         out_specs=VMEM,
         compiler_params=SMALL,
         name="join_parts",
-    )(*parts)
+    )(*messages)
 
 
 def prepare_kernel(pos, taper, mine, other, for_two, for_one, rows):
@@ -154,8 +203,10 @@
     for n, (_, parts) in enumerate(items):
         to = 0
         for index, start, size in parts:
-            pltpu.make_async_copy(
-                panels[index].at[pl.ds(start, size)], held.at[n, pl.ds(to, size)], sems.at[n]).start()
+            panel = panels[index].at[pl.ds(start, size)]
+            if len(held.shape) == 5:
+                panel = panel.at[:, pl.ds(0, PAIR // ROW)]
+            pltpu.make_async_copy(panel, held.at[n, pl.ds(to, size)], sems.at[n]).start()
             to += size
     if first:
         total[...] = jnp.zeros_like(total)
@@ -178,10 +229,11 @@
 
 def product(pos, adjoint, panels, items, before=None, kind=None):
     last = kind is not None
+    shape = (TWO,) if panels[0].ndim == 3 else (2 * NX, PAIR // ROW)
     column = jax.ShapeDtypeStruct((512, 128), F32)
     scratch = [pltpu.VMEM((512, HALF), F32)] if last else []
     scratch += [
-        pltpu.VMEM((len(items), adjoint.shape[2] // PAIR, PAIR, HALF), BF16),
+        pltpu.VMEM((len(items),) + shape + (ROW, HALF), BF16),
         pltpu.SemaphoreType.DMA((len(items),)),
     ]
     extra = [] if before is None else [before]
@@ -198,44 +250,22 @@
     )(pos, adjoint, *panels, *extra)
 
 
-def diagonal_kernel(where, pos, *refs):
-    panels, outs, held, sem = refs[:-6], refs[-6:-2], refs[-2], refs[-1]
-    half = jnp.where(pos[3] == 0, 0, SUB)
-
-    @pl.when(pos[2] == 0)
-    def _():
-        for i in range(NX):
-            x = source(pos, i, 0)[0]
-
-            @pl.when(x < 2)
-            def _(i=i, x=x):
-                for j in range(NZ):
-                    index, at = where[i][j]
-                    z = source(pos, i, j)[1]
-                    pltpu.make_async_copy(
-                        panels[index].at[at, pl.ds(half, SUB), :], held.at[x * NZ + z], sem.at[0]
-                    ).start()
-
-        pltpu.make_async_copy(held, held, sem.at[0]).wait()
-        for d, out in enumerate(outs):
-            out[...] = held[:, :, d * 128:(d + 1) * 128].reshape(2 * NZ * SUB, 128)
-
-
-def diagonal(pos, panels, where):
-    return pl.pallas_call(
-        functools.partial(diagonal_kernel, where),
-        out_shape=(jax.ShapeDtypeStruct((1024, 128), BF16),) * 4,
-        in_specs=[SMEM] + [ANY] * len(panels),
-        out_specs=(VMEM,) * 4,
-        scratch_shapes=[pltpu.VMEM((2 * NZ, SUB, HALF), BF16), pltpu.SemaphoreType.DMA((1,))],
-        compiler_params=SMALL,
-        name="diagonal_columns",
-    )(pos, *panels)
-
-
-def factor_kernel(pos, inverse, inverse_other, own, one, two, three, out, out_other):
-    sent = (one[...] + two[...]) + three[...]
-    columns = jnp.where(pos[2] == 0, own[...], sent)
+def factor_kernel(where, pos, inverse, inverse_other, *refs):
+    panels, (out, out_other, held, diagonal, sem) = refs[:-5], refs[-5:]
+    for i in range(NX):
+        x = source(pos, i, 0)[0]
+
+        @pl.when(x < 2)
+        def _(i=i, x=x):
+            for j in range(NZ):
+                index, at = where[i][j]
+                z = source(pos, i, j)[1]
+                pltpu.make_async_copy(panels[index].at[at, ONE - 1], held.at[x * NZ + z], sem.at[0]).start()
+
+    pltpu.make_async_copy(held, held, sem.at[0]).wait()
+    for q in range(NY):
+        diagonal[:, q] = held[:, :, q * 128:(q + 1) * 128]
+    columns = diagonal[...].reshape(2 * NZ * SUB, 128)
     for left, result in ((inverse, out), (inverse_other, out_other)):
         value = jnp.dot(left[...].reshape(512, 1024), columns, preferred_element_type=F32)
         high = value.astype(BF16)
@@ -244,15 +274,20 @@
         result[:, :, 128:] = low.reshape(NY, 128, 128)
 
 
-def factor(pos, inverse, inverse_other, parts):
-    return pl.pallas_call(
-        factor_kernel,
+def factor(pos, inverse, inverse_other, panels, where):
+    return pl.pallas_call(
+        functools.partial(factor_kernel, where),
         out_shape=(jax.ShapeDtypeStruct((NY, 128, 256), BF16),) * 2,
-        in_specs=[SMEM] + [VMEM] * 6,
+        in_specs=[SMEM, VMEM, VMEM] + [ANY] * len(panels),
         out_specs=(VMEM, VMEM),
+        scratch_shapes=[
+            pltpu.VMEM((2 * NZ, ROW, HALF), BF16),
+            pltpu.VMEM((2 * NZ, NY, ROW, 128), BF16),
+            pltpu.SemaphoreType.DMA((1,)),
+        ],
         compiler_params=SMALL,
         name="inverse_times_diagonal",
-    )(pos, inverse, inverse_other, *parts)
+    )(pos, inverse, inverse_other, *panels)
 
 
 def carried_kernel(mine, other, factors, factors_other, out, total):
@@ -287,64 +322,58 @@
     own, give = pack(pos, panel_two, panel_one)
     taken = core_swap(give)
     shards = jnp.concatenate([own, taken], axis=1)
-
+    block, *blocks = top(pos, own, taken)
     two, one = shards[0], shards[1]
 
     def x_all(part):
         return [part] + [x_shift(part, d) for d in (1, -1, 2)]
-
-    def of_one(*messages):
-        return x_all(join(messages, (NX,) * len(messages)))
 
     two, one, swapped = together(two, one, core_swap(adjoint))
     *two, inverse1, inverse3 = together(
         *x_all(two), y_shift(inverse_factor, 1), y_shift(inverse_factor, 3))
-    own = join(two + [one], (None,) * 5)
-    own, later = together(own, inverse_factor)
+    blocks = [y_first(part, d + 1) for d, part in enumerate(blocks)]
+    own, part = message(pos, two, one, [block] + blocks)
+    own, part, later = together(own, part, inverse_factor)
     inverse = jnp.stack([inverse_factor, inverse1, y_shift(later, 2), inverse3])
     down1, up1, inverse, *first_x = together(
-        z_shift(own, 1), z_shift(own, -1), inverse, *x_all(one[None]))
+        z_shift(own, 1), z_shift(own, -1), inverse, *x_all(part))
 
     for_two, for_one = prepare(pos, taper, adjoint, swapped)
     down2, up2, for_two, for_one, *near = together(
-        z_shift(down1, 1), z_shift(up1, -1), for_two, for_one, *of_one(down1, up1))
+        z_shift(down1, 1), z_shift(up1, -1), for_two, for_one, *x_all(join(down1, up1)))
     inverse, down2, up2 = together(inverse, down2, up2)
     inverse_other = core_swap(inverse)
     sums = product(
-        pos, for_two, [own, down1, up1, down2, up2], [(j, [(j, 0, 4)]) for j in range(5)])
+        pos, for_two, [own, down1, up1, down2, up2], [(j, [(j, 0, TWO)]) for j in range(5)])
     down3, up3, sums, *middle = together(
-        z_shift(down2, 1), z_shift(up2, -1), sums, *of_one(down2, up2))
-    sums = product(pos, for_two, [down3, up3], [(5 + j, [(j, 0, 4)]) for j in range(2)], sums)
+        z_shift(down2, 1), z_shift(up2, -1), sums, *x_all(join(down2, up2)))
+    sums = product(pos, for_two, [down3, up3], [(5 + j, [(j, 0, TWO)]) for j in range(2)], sums)
     sums_one = product(
         pos, for_one, near + middle,
         [(1 + c, [(NX * c + i, 0, 2) for i in range(NX)]) for c in range(2)])
-    third = of_one(down3, up3)
+    third = x_all(join(down3, up3))
     far_low, far_high, sums, sums_one = together(
-        z_shift(down3[:2], 1), z_shift(up3[2:], -1), sums, sums_one)
+        z_shift(down3[:TWO // 2], 1), z_shift(up3[TWO // 2:], -1), sums, sums_one)
 
     mine, *sent = product(
-        pos, for_two, [far_low, far_high], [(7, [(0, 0, 2), (1, 0, 2)])], sums, F32)
-    last = x_all(far_high[2:])
+        pos, for_two, [far_low, far_high], [(7, [(0, 0, TWO // 2), (1, 0, TWO // 2)])], sums, F32)
+    last = x_all(far_high[None, TWO // 2:])
     sums_one = product(pos, for_one, third, [(3, [(i, 0, 2) for i in range(NX)])], sums_one)
-    where = tuple(
-        ((i, 0),) + tuple((NX * (1 + j // 2) + i, j % 2) for j in range(7)) for i in range(NX))
-    columns = diagonal(pos, first_x + near + middle + third + last, where)
-    r1, r2, r3, sums_one, *columns = together(
-        *[y_shift(part, d + 1) for d, part in enumerate(sent)], sums_one, *columns)
+    r1, r2, r3, sums_one, *last = together(
+        *[y_shift(part, d + 1) for d, part in enumerate(sent)], sums_one, *last)
     second_grad = incoming + ((mine + r1) + (r2 + r3))
     rounded = second_grad.astype(BF16)
 
     sums_one = product(
         pos, for_one, first_x + last,
         [(0, [(NX * s + i, 0, 1) for i in range(NX) for s in range(2)])], sums_one, BF16)
-    first, *rest = columns
-    rest = [y_first(part, d + 1) for d, part in enumerate(rest)]
-    s1, s2, s3, *rest = together(*[y_shift(rounded, d) for d in range(1, NY)], *rest, *sums_one)
-    rest, (mine, *sent) = rest[:3], rest[3:]
+    where = tuple(
+        ((i, 0),) + tuple((NX * (1 + j // 2) + i, j % 2) for j in range(7)) for i in range(NX))
+    factors = factor(pos, inverse, inverse_other, first_x + near + middle + third + last, where)
+    s1, s2, s3, mine, *sent = together(*[y_shift(rounded, d) for d in range(1, NY)], *sums_one)
     rounded = jnp.stack([rounded, s1, s2, s3])
     rounded_other = core_swap(rounded)
     r1, r2, r3 = [y_shift(part, d + 1).astype(F32) for d, part in enumerate(sent)]
-    factors = factor(pos, inverse, inverse_other, [first] + rest)
     term = carried(rounded, rounded_other, *factors)
     return second_grad, (mine + r1) + (r2 + r3) - term
 

time: 138 us -> 132 us (0.957)
  starting transfers between devices: 78 us -> 68.7 us
  waiting for transfers between devices: 31.8 us -> 35.6 us
    ppermute x3, starting transfers between devices: 11 us -> 5.01 us  [y_first(): return lax.ppermute(value, 'row', [(k, y * 2 + k) for k in range(2)])]
    ppermute x18, starting transfers between devices: 34 us -> 29.7 us  [x_shift(): return lax.ppermute(value, 'col', pairs)]
    ppermute x18, waiting for transfers between devices: 18 us -> 20 us  [x_shift(): return lax.ppermute(value, 'col', pairs)]
    ppermute x8, waiting for transfers between devices: 1.18 us -> 3.05 us  [z_shift(): return lax.ppermute(value, 'col', pairs)]
  transfers between devices with their start and end apart: 45 -> 45, of which waited for: 17 -> 17; matrix products, arithmetic and copies ran while one was open for 1% -> 2% of each run, Pallas kernels for 16% -> 16%
where the time goes in v8:
time: 132 us
  starting transfers between devices  68.7 us (52%)
  waiting for transfers between devices  35.6 us (27%)
  Pallas kernels  22.2 us (17%)
  other arithmetic  2.78 us (2%)
  local copies, waits for them, and re-layouts  1.92 us (1%)
    ppermute x18, starting transfers between devices, x_shift(): return lax.ppermute(value, 'col', pairs)  29.7 us
    ppermute x18, waiting for transfers between devices, x_shift(): return lax.ppermute(value, 'col', pairs)  20 us
    ppermute x12, starting transfers between devices, y_shift(): return lax.ppermute(value, 'row', pairs)  13.2 us
    ppermute x8, starting transfers between devices, z_shift(): return lax.ppermute(value, 'col', pairs)  12.7 us
    pallas_call x6, Pallas kernels, product(): pl.pallas_call(kernel, out_shape=(column,) + (jax.ShapeDtypeStruct((512,...  12.3 us
    ppermute x12, waiting for transfers between devices, y_shift(): return lax.ppermute(value, 'row', pairs)  11.7 us
    ppermute x4, starting transfers between devices, core_swap(): return lax.ppermute(value, 'row', [(r, r ^ 1) for r in range(2 * NY)])  8.1 us
    ppermute x3, starting transfers between devices, y_first(): return lax.ppermute(value, 'row', [(k, y * 2 + k) for k in range(2)])  5.01 us
  transfers between devices with their start and end apart: 45, of which 17 were waited for; matrix products, arithmetic and copies ran while one was open for 2% of the time, Pallas kernels for 16%

profile of v8, /device:TPU:1, one launch (start us, length us, event | category | flops | bytes accessed | tf_op | source)
XLA Modules:
  0.0 132.2 jit_solution(2111339159021394679)
XLA Ops:
  0.6 3.3 %collective-permute-start.1 = (bf16[2048,512]{1,0:T(8,128)(2,1)}, bf16[2048,512]{1,0:T(8,128)(2,1)}, u32[]{:S(2)}, u32[]{:S(2)}) collective-permute-start(bf16[2048,512]{1,0:T(8,128)(2,1)} %mine.1), channel_id=1, source_target_pairs={{0,32},{32,0},{64,96},{96,64},{128,160},{160,128},{192,224},{224,1... | collective-permute-start | bytes 6291464 | tf_op jit(solution)/shard_map/ppermute | solution.py:46
  8.6 2.4 %collective-permute-start.4 = (bf16[128,512]{1,0:T(8,128)(2,1)S(1)}, bf16[128,512]{1,0:T(8,128)(2,1)S(1)}, u32[]{:S(2)}, u32[]{:S(2)}) collective-permute-start(bf16[128,512]{1,0:T(8,128)(2,1)S(1)} %get-tuple-element.81.two), channel_id=1, source_target_pairs={{0,16},{1,17},{2,18},{3,19},{4,20},{5,21},{6,22},{7,23},{8,24},{9,... | collective-permute-start | bytes 393224 | tf_op jit(solution)/shard_map/ppermute | solution.py:28
  21.7 5.7 %collective-permute-start.11 = (bf16[41,16,512]{2,1,0:T(8,128)(2,1)S(1)}, bf16[41,16,512]{2,1,0:T(8,128)(2,1)S(1)}, u32[]{:S(2)}, u32[]{:S(2)}) collective-permute-start(bf16[41,16,512]{2,1,0:T(8,128)(2,1)S(1)} %get-tuple-element.92.refs_0_), channel_id=1, source_target_pairs={{0,7},{1,0},{2,1},{3,2},{4,3},{5,4},{6,5},{7,6},{8,15},{9,8},{10,9... | collective-permute-start | bytes 2015240 | tf_op jit(solution)/shard_map/ppermute | solution.py:33
  28.9 2.7 %collective-permute-start.15 = (bf16[1,9,16,512]{3,2,1,0:T(8,128)(2,1)S(1)}, bf16[1,9,16,512]{3,2,1,0:T(8,128)(2,1)S(1)}, u32[]{:S(2)}, u32[]{:S(2)}) collective-permute-start(bf16[1,9,16,512]{3,2,1,0:T(8,128)(2,1)S(1)} %get-tuple-element.131.refs_0_), channel_id=1, source_target_pairs={{0,16},{1,17},{2,18},{3,19},{4,20},{5,21},{6,22},{7,23},{8,24},{9,... | collective-permute-start | bytes 442376 | tf_op jit(solution)/shard_map/ppermute | solution.py:28
  36.7 3.2 %collective-permute-done.13.refs_1_ = bf16[1,9,16,512]{3,2,1,0:T(8,128)(2,1)S(1)} collective-permute-done((bf16[1,9,16,512]{3,2,1,0:T(8,128)(2,1)S(1)}, bf16[1,9,16,512]{3,2,1,0:T(8,128)(2,1)S(1)}, u32[]{:S(2)}, u32[]{:S(2)}) %collective-permute-start.13) | collective-permute-done | bytes 147488 | tf_op jit(solution)/shard_map/ppermute | solution.py:28
  39.8 3.0 %collective-permute-done.10.refs_0_.refs_1_ = bf16[41,16,512]{2,1,0:T(8,128)(2,1)S(1)} collective-permute-done((bf16[41,16,512]{2,1,0:T(8,128)(2,1)S(1)}, bf16[41,16,512]{2,1,0:T(8,128)(2,1)S(1)}, u32[]{:S(2)}, u32[]{:S(2)}) %collective-permute-start.10) | collective-permute-done | bytes 671776 | tf_op jit(solution)/shard_map/ppermute | solution.py:33
  42.9 2.7 %collective-permute-start.17 = (bf16[41,16,512]{2,1,0:T(8,128)(2,1)S(1)}, bf16[41,16,512]{2,1,0:T(8,128)(2,1)S(1)}, u32[]{:S(2)}, u32[]{:S(2)}) collective-permute-start(bf16[41,16,512]{2,1,0:T(8,128)(2,1)S(1)} %collective-permute-done.11.refs_1_.refs_2_), channel_id=1, source_target_pairs={{0,7},{1,0},{2,1},{3,2},{4,3},{5,4},{6,5},{7,6},{8,15},{9,8},{10,9... | collective-permute-start | bytes 2015240 | tf_op jit(solution)/shard_map/ppermute | solution.py:33
  45.6 2.7 %collective-permute-start.20 = (bf16[2,9,16,512]{3,2,1,0:T(8,128)(2,1)S(1)}, bf16[2,9,16,512]{3,2,1,0:T(8,128)(2,1)S(1)}, u32[]{:S(2)}, u32[]{:S(2)}) collective-permute-start(bf16[2,9,16,512]{3,2,1,0:T(8,128)(2,1)S(1)} %join_parts.3.refs_0_.refs_4_), channel_id=1, source_target_pairs={{0,16},{1,17},{2,18},{3,19},{4,20},{5,21},{6,22},{7,23},{8,24},{9,... | collective-permute-start | bytes 884744 | tf_op jit(solution)/shard_map/ppermute | solution.py:28
  49.8 4.9 %prepare_adjoint.1 = (bf16[8,512,512]{2,1,0:T(8,128)(2,1)S(1)}, bf16[4,512,1024]{2,1,0:T(8,128)(2,1)S(1)}) custom-call(s32[4]{0:T(128)S(1)} %pad_add_fusion.pos, s32[64,64]{1,0:T(8,128)S(1)} %copy-done.3, bf16[2048,512]{1,0:T(8,128)(2,1)S(1)} %copy-done, bf16[2048,512]{1,0:T(8,128)(2,1)} %collective-permute-done.1.other), custom_call_target="tpu_custom_call" | custom-call | tf_op jit(solution)/shard_map/prepare_adjoint/pallas_call | solution.py:184
  54.7 4.7 %collective-permute-done.19.refs_2_.refs_6_ = bf16[2,9,16,512]{3,2,1,0:T(8,128)(2,1)S(1)} collective-permute-done((bf16[2,9,16,512]{3,2,1,0:T(8,128)(2,1)S(1)}, bf16[2,9,16,512]{3,2,1,0:T(8,128)(2,1)S(1)}, u32[]{:S(2)}, u32[]{:S(2)}) %collective-permute-start.19) | collective-permute-done | bytes 294944 | tf_op jit(solution)/shard_map/ppermute | solution.py:28
  59.5 2.7 %collective-permute-start.22 = (bf16[41,16,512]{2,1,0:T(8,128)(2,1)S(1)}, bf16[41,16,512]{2,1,0:T(8,128)(2,1)S(1)}, u32[]{:S(2)}, u32[]{:S(2)}) collective-permute-start(bf16[41,16,512]{2,1,0:T(8,128)(2,1)S(1)} %collective-permute-done.17.refs_4_.refs_1_), channel_id=1, source_target_pairs={{0,7},{1,0},{2,1},{3,2},{4,3},{5,4},{6,5},{7,6},{8,15},{9,8},{10,9... | collective-permute-start | bytes 2015240 | tf_op jit(solution)/shard_map/ppermute | solution.py:33
  62.2 3.9 %collective-permute-start.25 = (bf16[2,9,16,512]{3,2,1,0:T(8,128)(2,1)S(1)}, bf16[2,9,16,512]{3,2,1,0:T(8,128)(2,1)S(1)}, u32[]{:S(2)}, u32[]{:S(2)}) collective-permute-start(bf16[2,9,16,512]{3,2,1,0:T(8,128)(2,1)S(1)} %join_parts.4.refs_4_.refs_8_), channel_id=1, source_target_pairs={{0,16},{1,17},{2,18},{3,19},{4,20},{5,21},{6,22},{7,23},{8,24},{9,... | collective-permute-start | bytes 884744 | tf_op jit(solution)/shard_map/ppermute | solution.py:28
  67.6 3.0 %masked_product.6.refs_2_ = f32[512,512]{1,0:T(8,128)S(1)} custom-call(s32[4]{0:T(128)S(1)} %pad_add_fusion.pos, bf16[8,512,512]{2,1,0:T(8,128)(2,1)S(1)} %get-tuple-element.102.adjoint, bf16[41,16,512]{2,1,0:T(8,128)(2,1)S(1)} %get-tuple-element.92.refs_0_, bf16[41,16,512]{2,1,0:T(8,128)(2,1)S(1)} %collective-permute-done.10.refs_0_.refs_1_, ...), custom_call_target="tpu_custom_call" | custom-call | tf_op jit(solution)/shard_map/masked_product/pallas_call | solution.py:241
  70.6 7.8 %collective-permute-done.24.refs_6_.refs_10_ = bf16[2,9,16,512]{3,2,1,0:T(8,128)(2,1)S(1)} collective-permute-done((bf16[2,9,16,512]{3,2,1,0:T(8,128)(2,1)S(1)}, bf16[2,9,16,512]{3,2,1,0:T(8,128)(2,1)S(1)}, u32[]{:S(2)}, u32[]{:S(2)}) %collective-permute-start.24) | collective-permute-done | bytes 294944 | tf_op jit(solution)/shard_map/ppermute | solution.py:28
  80.3 3.6 %collective-permute-start.33 = (bf16[2,9,16,512]{3,2,1,0:T(8,128)(2,1)S(1)}, bf16[2,9,16,512]{3,2,1,0:T(8,128)(2,1)S(1)}, u32[]{:S(2)}, u32[]{:S(2)}) collective-permute-start(bf16[2,9,16,512]{3,2,1,0:T(8,128)(2,1)S(1)} %join_parts.5.refs_0_.refs_12_), channel_id=1, source_target_pairs={{0,16},{1,17},{2,18},{3,19},{4,20},{5,21},{6,22},{7,23},{8,24},{9,... | collective-permute-start | bytes 884744 | tf_op jit(solution)/shard_map/ppermute | solution.py:28
  87.1 2.2 %masked_product.8.refs_4_ = f32[512,512]{1,0:T(8,128)S(1)} custom-call(s32[4]{0:T(128)S(1)} %pad_add_fusion.pos, bf16[4,512,1024]{2,1,0:T(8,128)(2,1)S(1)} %get-tuple-element.111.adjoint, bf16[2,9,16,512]{3,2,1,0:T(8,128)(2,1)S(1)} %join_parts.3.refs_0_.refs_4_, bf16[2,9,16,512]{3,2,1,0:T(8,128)(2,1)S(1)} %collective-permute-done.18.refs_1_.refs_5_, ...), custom_call_target="tpu_custom_call" | custom-call | tf_op jit(solution)/shard_map/masked_product/pallas_call | solution.py:241
  89.4 2.7 %collective-permute-start.36 = (bf16[1,9,16,512]{3,2,1,0:T(8,128)(2,1)S(1)}, bf16[1,9,16,512]{3,2,1,0:T(8,128)(2,1)S(1)}, u32[]{:S(2)}, u32[]{:S(2)}) collective-permute-start(bf16[1,9,16,512]{3,2,1,0:T(8,128)(2,1)S(1)} %slice_bitcast_fusion.refs_4_.refs_16_), channel_id=1, source_target_pairs={{0,16},{1,17},{2,18},{3,19},{4,20},{5,21},{6,22},{7,23},{8,24},{9,... | collective-permute-start | bytes 442376 | tf_op jit(solution)/shard_map/ppermute | solution.py:28
  93.5 2.9 %collective-permute-start.29 = (f32[512,128]{1,0:T(8,128)S(1)}, f32[512,128]{1,0:T(8,128)S(1)}, u32[]{:S(2)}, u32[]{:S(2)}) collective-permute-start(f32[512,128]{1,0:T(8,128)S(1)} %get-tuple-element.125), channel_id=1, source_target_pairs={{0,128},{32,160},{64,192},{96,224},{128,0},{160,32},{192,64},{224,... | collective-permute-start | bytes 786440 | tf_op jit(solution)/shard_map/ppermute | solution.py:38
  96.4 2.0 %collective-permute-done.32.refs_2_.refs_14_ = bf16[2,9,16,512]{3,2,1,0:T(8,128)(2,1)S(1)} collective-permute-done((bf16[2,9,16,512]{3,2,1,0:T(8,128)(2,1)S(1)}, bf16[2,9,16,512]{3,2,1,0:T(8,128)(2,1)S(1)}, u32[]{:S(2)}, u32[]{:S(2)}) %collective-permute-start.32) | collective-permute-done | bytes 294944 | tf_op jit(solution)/shard_map/ppermute | solution.py:28
  100.4 3.6 %collective-permute-start.35 = (bf16[1,9,16,512]{3,2,1,0:T(8,128)(2,1)S(1)}, bf16[1,9,16,512]{3,2,1,0:T(8,128)(2,1)S(1)}, u32[]{:S(2)}, u32[]{:S(2)}) collective-permute-start(bf16[1,9,16,512]{3,2,1,0:T(8,128)(2,1)S(1)} %slice_bitcast_fusion.refs_4_.refs_16_), channel_id=1, source_target_pairs={{0,24},{1,25},{2,26},{3,27},{4,28},{5,29},{6,30},{7,31},{8,0},{9,1... | collective-permute-start | bytes 442376 | tf_op jit(solution)/shard_map/ppermute | solution.py:28
  109.9 2.0 %collective-permute-start.39 = (bf16[512,128]{1,0:T(8,128)(2,1)S(1)}, bf16[512,128]{1,0:T(8,128)(2,1)S(1)}, u32[]{:S(2)}, u32[]{:S(2)}) collective-permute-start(bf16[512,128]{1,0:T(8,128)(2,1)S(1)} %get-tuple-element.154), channel_id=1, source_target_pairs={{0,192},{32,224},{64,0},{96,32},{128,64},{160,96},{192,128},{224,1... | collective-permute-start | bytes 393224 | tf_op jit(solution)/shard_map/ppermute | solution.py:38
  112.5 2.8 %masked_product.11 = (f32[512,128]{1,0:T(8,128)S(1)}, bf16[512,128]{1,0:T(8,128)(2,1)S(1)}, bf16[512,128]{1,0:T(8,128)(2,1)S(1)}, bf16[512,128]{1,0:T(8,128)(2,1)S(1)}) custom-call(s32[4]{0:T(128)S(1)} %pad_add_fusion.pos, bf16[4,512,1024]{2,1,0:T(8,128)(2,1)S(1)} %get-tuple-element.111.adjoint, bf16[1,9,16,512]{3,2,1,0:T(8,128)(2,1)S(1)} %get-tuple-element.131.refs_0_, ...), custom_call_target="tpu_custom_call" | custom-call | tf_op jit(solution)/shard_map/masked_product/pallas_call | solution.py:241
  119.2 2.8 %collective-permute-start.43 = (bf16[4,512,128]{2,1,0:T(8,128)(2,1)S(1)}, bf16[4,512,128]{2,1,0:T(8,128)(2,1)S(1)}, u32[]{:S(2)}, u32[]{:S(2)}) collective-permute-start(bf16[4,512,128]{2,1,0:T(8,128)(2,1)S(1)} %pad_maximum_fusion.1.mine), channel_id=1, source_target_pairs={{0,32},{32,0},{64,96},{96,64},{128,160},{160,128},{192,224},{224,1... | collective-permute-start | bytes 1572872 | tf_op jit(solution)/shard_map/ppermute | solution.py:46
  127.5 3.5 %collective-permute-done.40 = bf16[512,128]{1,0:T(8,128)(2,1)S(1)} collective-permute-done((bf16[512,128]{1,0:T(8,128)(2,1)S(1)}, bf16[512,128]{1,0:T(8,128)(2,1)S(1)}, u32[]{:S(2)}, u32[]{:S(2)}) %collective-permute-start.40) | collective-permute-done | bytes 131104 | tf_op jit(solution)/shard_map/ppermute | solution.py:38
  (102 shorter events, 50.3 us)
Async XLA Ops:
  8.6 10.0 %collective-permute-start.4 = (bf16[128,512]{1,0:T(8,128)(2,1)S(1)}, bf16[128,512]{1,0:T(8,128)(2,1)S(1)}, u32[]{:S(2)}, u32[]{:S(2)}) collective-permute-start(bf16[128,512]{1,0:T(8,128)(2,1)S(1)} %get-tuple-element.81.two), channel_id=1, source_target_pairs={{0,16},{1,17},{2,18},{3,19},{4,20},{5,21},{6,22},{7,23},{8,24},{9,... | collective-permute-start | bytes 393224 | tf_op jit(solution)/shard_map/ppermute | solution.py:28
  11.0 9.3 %collective-permute-start.3 = (bf16[128,512]{1,0:T(8,128)(2,1)S(1)}, bf16[128,512]{1,0:T(8,128)(2,1)S(1)}, u32[]{:S(2)}, u32[]{:S(2)}) collective-permute-start(bf16[128,512]{1,0:T(8,128)(2,1)S(1)} %get-tuple-element.81.two), channel_id=1, source_target_pairs={{0,24},{1,25},{2,26},{3,27},{4,28},{5,29},{6,30},{7,31},{8,0},{9,1... | collective-permute-start | bytes 393224 | tf_op jit(solution)/shard_map/ppermute | solution.py:28
  21.7 18.1 %collective-permute-start.11 = (bf16[41,16,512]{2,1,0:T(8,128)(2,1)S(1)}, bf16[41,16,512]{2,1,0:T(8,128)(2,1)S(1)}, u32[]{:S(2)}, u32[]{:S(2)}) collective-permute-start(bf16[41,16,512]{2,1,0:T(8,128)(2,1)S(1)} %get-tuple-element.92.refs_0_), channel_id=1, source_target_pairs={{0,7},{1,0},{2,1},{3,2},{4,3},{5,4},{6,5},{7,6},{8,15},{9,8},{10,9... | collective-permute-start | bytes 2015240 | tf_op jit(solution)/shard_map/ppermute | solution.py:33
  27.4 15.5 %collective-permute-start.10 = (bf16[41,16,512]{2,1,0:T(8,128)(2,1)S(1)}, bf16[41,16,512]{2,1,0:T(8,128)(2,1)S(1)}, u32[]{:S(2)}, u32[]{:S(2)}) collective-permute-start(bf16[41,16,512]{2,1,0:T(8,128)(2,1)S(1)} %get-tuple-element.92.refs_0_), channel_id=1, source_target_pairs={{0,1},{1,2},{2,3},{3,4},{4,5},{5,6},{6,7},{7,0},{8,9},{9,10},{10,1... | collective-permute-start | bytes 2015240 | tf_op jit(solution)/shard_map/ppermute | solution.py:33
  42.9 16.5 %collective-permute-start.16 = (bf16[41,16,512]{2,1,0:T(8,128)(2,1)S(1)}, bf16[41,16,512]{2,1,0:T(8,128)(2,1)S(1)}, u32[]{:S(2)}, u32[]{:S(2)}) collective-permute-start(bf16[41,16,512]{2,1,0:T(8,128)(2,1)S(1)} %collective-permute-done.10.refs_0_.refs_1_), channel_id=1, source_target_pairs={{0,1},{1,2},{2,3},{3,4},{4,5},{5,6},{6,7},{7,0},{8,9},{9,10},{10,1... | collective-permute-start | bytes 2015240 | tf_op jit(solution)/shard_map/ppermute | solution.py:33
  42.9 16.5 %collective-permute-start.17 = (bf16[41,16,512]{2,1,0:T(8,128)(2,1)S(1)}, bf16[41,16,512]{2,1,0:T(8,128)(2,1)S(1)}, u32[]{:S(2)}, u32[]{:S(2)}) collective-permute-start(bf16[41,16,512]{2,1,0:T(8,128)(2,1)S(1)} %collective-permute-done.11.refs_1_.refs_2_), channel_id=1, source_target_pairs={{0,7},{1,0},{2,1},{3,2},{4,3},{5,4},{6,5},{7,6},{8,15},{9,8},{10,9... | collective-permute-start | bytes 2015240 | tf_op jit(solution)/shard_map/ppermute | solution.py:33
  45.6 9.1 %collective-permute-start.20 = (bf16[2,9,16,512]{3,2,1,0:T(8,128)(2,1)S(1)}, bf16[2,9,16,512]{3,2,1,0:T(8,128)(2,1)S(1)}, u32[]{:S(2)}, u32[]{:S(2)}) collective-permute-start(bf16[2,9,16,512]{3,2,1,0:T(8,128)(2,1)S(1)} %join_parts.3.refs_0_.refs_4_), channel_id=1, source_target_pairs={{0,16},{1,17},{2,18},{3,19},{4,20},{5,21},{6,22},{7,23},{8,24},{9,... | collective-permute-start | bytes 884744 | tf_op jit(solution)/shard_map/ppermute | solution.py:28
  48.3 11.1 %collective-permute-start.19 = (bf16[2,9,16,512]{3,2,1,0:T(8,128)(2,1)S(1)}, bf16[2,9,16,512]{3,2,1,0:T(8,128)(2,1)S(1)}, u32[]{:S(2)}, u32[]{:S(2)}) collective-permute-start(bf16[2,9,16,512]{3,2,1,0:T(8,128)(2,1)S(1)} %join_parts.3.refs_0_.refs_4_), channel_id=1, source_target_pairs={{0,24},{1,25},{2,26},{3,27},{4,28},{5,29},{6,30},{7,31},{8,0},{9,1... | collective-permute-start | bytes 884744 | tf_op jit(solution)/shard_map/ppermute | solution.py:28
  49.1 10.3 %collective-permute-start.18 = (bf16[2,9,16,512]{3,2,1,0:T(8,128)(2,1)S(1)}, bf16[2,9,16,512]{3,2,1,0:T(8,128)(2,1)S(1)}, u32[]{:S(2)}, u32[]{:S(2)}) collective-permute-start(bf16[2,9,16,512]{3,2,1,0:T(8,128)(2,1)S(1)} %join_parts.3.refs_0_.refs_4_), channel_id=1, source_target_pairs={{0,8},{1,9},{2,10},{3,11},{4,12},{5,13},{6,14},{7,15},{8,16},{9,17... | collective-permute-start | bytes 884744 | tf_op jit(solution)/shard_map/ppermute | solution.py:28
  59.4 19.3 %collective-permute-start.21 = (bf16[41,16,512]{2,1,0:T(8,128)(2,1)S(1)}, bf16[41,16,512]{2,1,0:T(8,128)(2,1)S(1)}, u32[]{:S(2)}, u32[]{:S(2)}) collective-permute-start(bf16[41,16,512]{2,1,0:T(8,128)(2,1)S(1)} %collective-permute-done.16.refs_3_.refs_0_), channel_id=1, source_target_pairs={{0,1},{1,2},{2,3},{3,4},{4,5},{5,6},{6,7},{7,0},{8,9},{9,10},{10,1... | collective-permute-start | bytes 2015240 | tf_op jit(solution)/shard_map/ppermute | solution.py:33
  59.5 19.2 %collective-permute-start.22 = (bf16[41,16,512]{2,1,0:T(8,128)(2,1)S(1)}, bf16[41,16,512]{2,1,0:T(8,128)(2,1)S(1)}, u32[]{:S(2)}, u32[]{:S(2)}) collective-permute-start(bf16[41,16,512]{2,1,0:T(8,128)(2,1)S(1)} %collective-permute-done.17.refs_4_.refs_1_), channel_id=1, source_target_pairs={{0,7},{1,0},{2,1},{3,2},{4,3},{5,4},{6,5},{7,6},{8,15},{9,8},{10,9... | collective-permute-start | bytes 2015240 | tf_op jit(solution)/shard_map/ppermute | solution.py:33
  66.1 12.3 %collective-permute-start.24 = (bf16[2,9,16,512]{3,2,1,0:T(8,128)(2,1)S(1)}, bf16[2,9,16,512]{3,2,1,0:T(8,128)(2,1)S(1)}, u32[]{:S(2)}, u32[]{:S(2)}) collective-permute-start(bf16[2,9,16,512]{3,2,1,0:T(8,128)(2,1)S(1)} %join_parts.4.refs_4_.refs_8_), channel_id=1, source_target_pairs={{0,24},{1,25},{2,26},{3,27},{4,28},{5,29},{6,30},{7,31},{8,0},{9,1... | collective-permute-start | bytes 884744 | tf_op jit(solution)/shard_map/ppermute | solution.py:28
  67.2 11.5 %collective-permute-start.23 = (bf16[2,9,16,512]{3,2,1,0:T(8,128)(2,1)S(1)}, bf16[2,9,16,512]{3,2,1,0:T(8,128)(2,1)S(1)}, u32[]{:S(2)}, u32[]{:S(2)}) collective-permute-start(bf16[2,9,16,512]{3,2,1,0:T(8,128)(2,1)S(1)} %join_parts.4.refs_4_.refs_8_), channel_id=1, source_target_pairs={{0,8},{1,9},{2,10},{3,11},{4,12},{5,13},{6,14},{7,15},{8,16},{9,17... | collective-permute-start | bytes 884744 | tf_op jit(solution)/shard_map/ppermute | solution.py:28
  78.7 10.7 %collective-permute-start.27 = (bf16[25,16,512]{2,1,0:T(8,128)(2,1)S(1)}, bf16[25,16,512]{2,1,0:T(8,128)(2,1)S(1)}, u32[]{:S(2)}, u32[]{:S(2)}) collective-permute-start(bf16[25,16,512]{2,1,0:T(8,128)(2,1)S(1)} %slice.18), channel_id=1, source_target_pairs={{0,7},{1,0},{2,1},{3,2},{4,3},{5,4},{6,5},{7,6},{8,15},{9,8},{10,9... | collective-permute-start | bytes 1228808 | tf_op jit(solution)/shard_map/ppermute | solution.py:33
  78.8 10.6 %collective-permute-start.26 = (bf16[16,16,512]{2,1,0:T(8,128)(2,1)S(1)}, bf16[16,16,512]{2,1,0:T(8,128)(2,1)S(1)}, u32[]{:S(2)}, u32[]{:S(2)}) collective-permute-start(bf16[16,16,512]{2,1,0:T(8,128)(2,1)S(1)} %slice.17), channel_id=1, source_target_pairs={{0,1},{1,2},{2,3},{3,4},{4,5},{5,6},{6,7},{7,0},{8,9},{9,10},{10,1... | collective-permute-start | bytes 786440 | tf_op jit(solution)/shard_map/ppermute | solution.py:33
  80.3 13.1 %collective-permute-start.33 = (bf16[2,9,16,512]{3,2,1,0:T(8,128)(2,1)S(1)}, bf16[2,9,16,512]{3,2,1,0:T(8,128)(2,1)S(1)}, u32[]{:S(2)}, u32[]{:S(2)}) collective-permute-start(bf16[2,9,16,512]{3,2,1,0:T(8,128)(2,1)S(1)} %join_parts.5.refs_0_.refs_12_), channel_id=1, source_target_pairs={{0,16},{1,17},{2,18},{3,19},{4,20},{5,21},{6,22},{7,23},{8,24},{9,... | collective-permute-start | bytes 884744 | tf_op jit(solution)/shard_map/ppermute | solution.py:28
  83.9 14.4 %collective-permute-start.32 = (bf16[2,9,16,512]{3,2,1,0:T(8,128)(2,1)S(1)}, bf16[2,9,16,512]{3,2,1,0:T(8,128)(2,1)S(1)}, u32[]{:S(2)}, u32[]{:S(2)}) collective-permute-start(bf16[2,9,16,512]{3,2,1,0:T(8,128)(2,1)S(1)} %join_parts.5.refs_0_.refs_12_), channel_id=1, source_target_pairs={{0,24},{1,25},{2,26},{3,27},{4,28},{5,29},{6,30},{7,31},{8,0},{9,1... | collective-permute-start | bytes 884744 | tf_op jit(solution)/shard_map/ppermute | solution.py:28
  85.5 14.8 %collective-permute-start.31 = (bf16[2,9,16,512]{3,2,1,0:T(8,128)(2,1)S(1)}, bf16[2,9,16,512]{3,2,1,0:T(8,128)(2,1)S(1)}, u32[]{:S(2)}, u32[]{:S(2)}) collective-permute-start(bf16[2,9,16,512]{3,2,1,0:T(8,128)(2,1)S(1)} %join_parts.5.refs_0_.refs_12_), channel_id=1, source_target_pairs={{0,8},{1,9},{2,10},{3,11},{4,12},{5,13},{6,14},{7,15},{8,16},{9,17... | collective-permute-start | bytes 884744 | tf_op jit(solution)/shard_map/ppermute | solution.py:28
  89.4 14.5 %collective-permute-start.36 = (bf16[1,9,16,512]{3,2,1,0:T(8,128)(2,1)S(1)}, bf16[1,9,16,512]{3,2,1,0:T(8,128)(2,1)S(1)}, u32[]{:S(2)}, u32[]{:S(2)}) collective-permute-start(bf16[1,9,16,512]{3,2,1,0:T(8,128)(2,1)S(1)} %slice_bitcast_fusion.refs_4_.refs_16_), channel_id=1, source_target_pairs={{0,16},{1,17},{2,18},{3,19},{4,20},{5,21},{6,22},{7,23},{8,24},{9,... | collective-permute-start | bytes 442376 | tf_op jit(solution)/shard_map/ppermute | solution.py:28
  93.4 15.8 %collective-permute-start.28 = (f32[512,128]{1,0:T(8,128)S(1)}, f32[512,128]{1,0:T(8,128)S(1)}, u32[]{:S(2)}, u32[]{:S(2)}) collective-permute-start(f32[512,128]{1,0:T(8,128)S(1)} %get-tuple-element.124), channel_id=1, source_target_pairs={{0,64},{32,96},{64,128},{96,160},{128,192},{160,224},{192,0},{224,... | collective-permute-start | bytes 786440 | tf_op jit(solution)/shard_map/ppermute | solution.py:38
  93.5 15.7 %collective-permute-start.29 = (f32[512,128]{1,0:T(8,128)S(1)}, f32[512,128]{1,0:T(8,128)S(1)}, u32[]{:S(2)}, u32[]{:S(2)}) collective-permute-start(f32[512,128]{1,0:T(8,128)S(1)} %get-tuple-element.125), channel_id=1, source_target_pairs={{0,128},{32,160},{64,192},{96,224},{128,0},{160,32},{192,64},{224,... | collective-permute-start | bytes 786440 | tf_op jit(solution)/shard_map/ppermute | solution.py:38
  98.4 10.8 %collective-permute-start.30 = (f32[512,128]{1,0:T(8,128)S(1)}, f32[512,128]{1,0:T(8,128)S(1)}, u32[]{:S(2)}, u32[]{:S(2)}) collective-permute-start(f32[512,128]{1,0:T(8,128)S(1)} %get-tuple-element.126), channel_id=1, source_target_pairs={{0,192},{32,224},{64,0},{96,32},{128,64},{160,96},{192,128},{224,1... | collective-permute-start | bytes 786440 | tf_op jit(solution)/shard_map/ppermute | solution.py:38
  106.3 18.4 %collective-permute-start.44 = (bf16[4,128,1024]{2,1,0:T(8,128)(2,1)S(1)}, bf16[4,128,1024]{2,1,0:T(8,128)(2,1)S(1)}, u32[]{:S(2)}, u32[]{:S(2)}) collective-permute-start(bf16[4,128,1024]{2,1,0:T(8,128)(2,1)S(1)} %pad_maximum_fusion.inverse), channel_id=1, source_target_pairs={{0,32},{32,0},{64,96},{96,64},{128,160},{160,128},{192,224},{224,1... | collective-permute-start | bytes 3145736 | tf_op jit(solution)/shard_map/ppermute | solution.py:46
  122.0 9.1 %collective-permute-start.40 = (bf16[512,128]{1,0:T(8,128)(2,1)S(1)}, bf16[512,128]{1,0:T(8,128)(2,1)S(1)}, u32[]{:S(2)}, u32[]{:S(2)}) collective-permute-start(bf16[512,128]{1,0:T(8,128)(2,1)S(1)} %get-tuple-element.145), channel_id=1, source_target_pairs={{0,64},{32,96},{64,128},{96,160},{128,192},{160,224},{192,0},{224,... | collective-permute-start | bytes 393224 | tf_op jit(solution)/shard_map/ppermute | solution.py:38
  (26 other events, 244.1 us)

commit v9 on v8

--- a/solution.py
+++ b/solution.py
@@ -103,29 +103,24 @@
     )(pos, own, taken)
 
 
-def message_kernel(pos, two, down, up, far, one, own, b1, b2, b3, out, part):
+def message_kernel(pos, two, down, up, far, one, own, b1, b2, b3, out):
     for n, ref in enumerate((two, down, up, far)):
         out[n * 8:n * 8 + 8] = ref[...].reshape(8, ROW, HALF)
     rows = one[...].reshape(8, ROW, HALF)
     out[TWO:TWO + 8] = rows
-    part[0, :8] = rows
     sent = (b1[...] + b2[...]) + b3[...]
     columns = jnp.where(pos[2] == 0, own[...], sent)
     for q in range(NY):
         at = slice(q * 128, q * 128 + 128)
         out[TWO + 8, :, at] = columns[q * ROW:(q + 1) * ROW]
-        part[0, 8, :, at] = columns[q * ROW:(q + 1) * ROW]
 
 
 def message(pos, twos, one, blocks):
     return pl.pallas_call(
         message_kernel,
-        out_shape=(
-            jax.ShapeDtypeStruct((TWO + ONE, ROW, HALF), BF16),
-            jax.ShapeDtypeStruct((1, ONE, ROW, HALF), BF16),
-        ),
+        out_shape=jax.ShapeDtypeStruct((TWO + ONE, ROW, HALF), BF16),
         in_specs=[SMEM] + [VMEM] * 9,
-        out_specs=(VMEM, VMEM),
+        out_specs=VMEM,
         compiler_params=SMALL,
         name="ring_message",
     )(pos, *twos, one, *blocks)
@@ -133,7 +128,7 @@
 
 def join_kernel(*refs):
     for n, ref in enumerate(refs[:-1]):
-        refs[-1][n] = ref[TWO:]
+        refs[-1][n] = ref[ref.shape[0] - ONE:]
 
 
 def join(*messages):
@@ -329,14 +324,11 @@
         return [part] + [x_shift(part, d) for d in (1, -1, 2)]
 
     two, one, swapped = together(two, one, core_swap(adjoint))
-    *two, inverse1, inverse3 = together(
-        *x_all(two), y_shift(inverse_factor, 1), y_shift(inverse_factor, 3))
+    twos = together(*x_all(two))
     blocks = [y_first(part, d + 1) for d, part in enumerate(blocks)]
-    own, part = message(pos, two, one, [block] + blocks)
-    own, part, later = together(own, part, inverse_factor)
-    inverse = jnp.stack([inverse_factor, inverse1, y_shift(later, 2), inverse3])
-    down1, up1, inverse, *first_x = together(
-        z_shift(own, 1), z_shift(own, -1), inverse, *x_all(part))
+    own, later = together(message(pos, twos, one, [block] + blocks), inverse_factor)
+    inverse = jnp.stack([later] + [y_shift(later, d) for d in range(1, NY)])
+    down1, up1, inverse = together(z_shift(own, 1), z_shift(own, -1), inverse)
 
     for_two, for_one = prepare(pos, taper, adjoint, swapped)
     down2, up2, for_two, for_one, *near = together(
@@ -345,31 +337,28 @@
     inverse_other = core_swap(inverse)
     sums = product(
         pos, for_two, [own, down1, up1, down2, up2], [(j, [(j, 0, TWO)]) for j in range(5)])
-    down3, up3, sums, *middle = together(
-        z_shift(down2, 1), z_shift(up2, -1), sums, *x_all(join(down2, up2)))
+    sums_one = product(pos, for_one, near, [(1, [(i, 0, 2) for i in range(NX)])])
+    down3, up3, sums, sums_one, *middle = together(
+        z_shift(down2, 1), z_shift(up2, -1), sums, sums_one, *x_all(join(down2, up2)))
     sums = product(pos, for_two, [down3, up3], [(5 + j, [(j, 0, TWO)]) for j in range(2)], sums)
-    sums_one = product(
-        pos, for_one, near + middle,
-        [(1 + c, [(NX * c + i, 0, 2) for i in range(NX)]) for c in range(2)])
+    sums_one = product(pos, for_one, middle, [(2, [(i, 0, 2) for i in range(NX)])], sums_one)
     third = x_all(join(down3, up3))
     far_low, far_high, sums, sums_one = together(
         z_shift(down3[:TWO // 2], 1), z_shift(up3[TWO // 2:], -1), sums, sums_one)
 
     mine, *sent = product(
         pos, for_two, [far_low, far_high], [(7, [(0, 0, TWO // 2), (1, 0, TWO // 2)])], sums, F32)
-    last = x_all(far_high[None, TWO // 2:])
+    last = x_all(join(own, far_high))
     sums_one = product(pos, for_one, third, [(3, [(i, 0, 2) for i in range(NX)])], sums_one)
-    r1, r2, r3, sums_one, *last = together(
-        *[y_shift(part, d + 1) for d, part in enumerate(sent)], sums_one, *last)
+    r1, r2, r3, sums_one = together(*[y_shift(part, d + 1) for d, part in enumerate(sent)], sums_one)
     second_grad = incoming + ((mine + r1) + (r2 + r3))
     rounded = second_grad.astype(BF16)
 
-    sums_one = product(
-        pos, for_one, first_x + last,
-        [(0, [(NX * s + i, 0, 1) for i in range(NX) for s in range(2)])], sums_one, BF16)
+    sums_one = product(pos, for_one, last, [(0, [(i, 0, 2) for i in range(NX)])], sums_one, BF16)
     where = tuple(
-        ((i, 0),) + tuple((NX * (1 + j // 2) + i, j % 2) for j in range(7)) for i in range(NX))
-    factors = factor(pos, inverse, inverse_other, first_x + near + middle + third + last, where)
+        ((3 * NX + i, 0),) + tuple((NX * (j // 2) + i, j % 2) for j in range(6)) + ((3 * NX + i, 1),)
+        for i in range(NX))
+    factors = factor(pos, inverse, inverse_other, near + middle + third + last, where)
     s1, s2, s3, mine, *sent = together(*[y_shift(rounded, d) for d in range(1, NY)], *sums_one)
     rounded = jnp.stack([rounded, s1, s2, s3])
     rounded_other = core_swap(rounded)

time: 132 us -> 135 us (1.023)
  waiting for transfers between devices: 35.6 us -> 50.4 us
  starting transfers between devices: 68.7 us -> 56.3 us
    ppermute x18 -> x15, starting transfers between devices: 29.7 us -> 20.2 us  [x_shift(): return lax.ppermute(value, 'col', pairs)]
    ppermute x12, waiting for transfers between devices: 11.7 us -> 20.5 us  [y_shift(): return lax.ppermute(value, 'row', pairs)]
    ppermute x18 -> x15, waiting for transfers between devices: 20 us -> 26.7 us  [x_shift(): return lax.ppermute(value, 'col', pairs)]
    ppermute x12, starting transfers between devices: 13.2 us -> 9.02 us  [y_shift(): return lax.ppermute(value, 'row', pairs)]
    ppermute x8, waiting for transfers between devices: 3.05 us -> 1.27 us  [z_shift(): return lax.ppermute(value, 'col', pairs)]
    ppermute x3, starting transfers between devices: 5.01 us -> 6.77 us  [y_first(): return lax.ppermute(value, 'row', [(k, y * 2 + k) for k in range(2)])]
    pallas_call x6 -> x7, Pallas kernels: 12.3 us -> 11.6 us  [product(): pl.pallas_call(kernel, out_shape=(column,) + (jax.ShapeDtypeStruct((512,...]
  transfers between devices with their start and end apart: 45 -> 42, of which waited for: 17 -> 19; matrix products, arithmetic and copies ran while one was open for 2% -> 2% of each run, Pallas kernels for 16% -> 16%
where the time goes in v9:
time: 135 us; the launch traced here: 134 us
  starting transfers between devices  56.3 us (42%)
  waiting for transfers between devices  50.4 us (37%)
  Pallas kernels  21.5 us (16%)
  other arithmetic  2.79 us (2%)
  local copies, waits for them, and re-layouts  1.91 us (1%)
    ppermute x15, waiting for transfers between devices, x_shift(): return lax.ppermute(value, 'col', pairs)  26.7 us
    ppermute x12, waiting for transfers between devices, y_shift(): return lax.ppermute(value, 'row', pairs)  20.5 us
    ppermute x15, starting transfers between devices, x_shift(): return lax.ppermute(value, 'col', pairs)  20.2 us
    ppermute x8, starting transfers between devices, z_shift(): return lax.ppermute(value, 'col', pairs)  12.6 us
    pallas_call x7, Pallas kernels, product(): pl.pallas_call(kernel, out_shape=(column,) + (jax.ShapeDtypeStruct((512,...  11.6 us
    ppermute x12, starting transfers between devices, y_shift(): return lax.ppermute(value, 'row', pairs)  9.02 us
    ppermute x4, starting transfers between devices, core_swap(): return lax.ppermute(value, 'row', [(r, r ^ 1) for r in range(2 * NY)])  7.77 us
    ppermute x3, starting transfers between devices, y_first(): return lax.ppermute(value, 'row', [(k, y * 2 + k) for k in range(2)])  6.77 us
  transfers between devices with their start and end apart: 42, of which 19 were waited for; matrix products, arithmetic and copies ran while one was open for 2% of the time, Pallas kernels for 16%

profile of v9, /device:TPU:1, one launch (start us, length us, event | category | flops | bytes accessed | tf_op | source)
XLA Modules:
  0.0 133.9 jit_solution(6554494787212148474)
XLA Ops:
  0.6 3.3 %collective-permute-start.1 = (bf16[2048,512]{1,0:T(8,128)(2,1)}, bf16[2048,512]{1,0:T(8,128)(2,1)}, u32[]{:S(2)}, u32[]{:S(2)}) collective-permute-start(bf16[2048,512]{1,0:T(8,128)(2,1)} %mine.1), channel_id=1, source_target_pairs={{0,32},{32,0},{64,96},{96,64},{128,160},{160,128},{192,224},{224,1... | collective-permute-start | bytes 6291464 | tf_op jit(solution)/shard_map/ppermute | solution.py:46
  11.4 3.2 %collective-permute-start.5 = (bf16[64,128]{1,0:T(8,128)(2,1)S(1)}, bf16[64,128]{1,0:T(8,128)(2,1)S(1)}, u32[]{:S(2)}, u32[]{:S(2)}) collective-permute-start(bf16[64,128]{1,0:T(8,128)(2,1)S(1)} %get-tuple-element.75), channel_id=1, source_target_pairs={{0,64},{32,96},{1,65},{33,97},{2,66},{34,98},{3,67},{35,99},{4,68}... | collective-permute-start | bytes 49160 | tf_op jit(solution)/shard_map/ppermute | solution.py:42
  14.6 2.3 %collective-permute-start.6 = (bf16[64,128]{1,0:T(8,128)(2,1)S(1)}, bf16[64,128]{1,0:T(8,128)(2,1)S(1)}, u32[]{:S(2)}, u32[]{:S(2)}) collective-permute-start(bf16[64,128]{1,0:T(8,128)(2,1)S(1)} %get-tuple-element.76), channel_id=1, source_target_pairs={{0,128},{32,160},{1,129},{33,161},{2,130},{34,162},{3,131},{35,163... | collective-permute-start | bytes 49160 | tf_op jit(solution)/shard_map/ppermute | solution.py:42
  19.7 5.7 %collective-permute-start.9 = (bf16[41,16,512]{2,1,0:T(8,128)(2,1)S(1)}, bf16[41,16,512]{2,1,0:T(8,128)(2,1)S(1)}, u32[]{:S(2)}, u32[]{:S(2)}) collective-permute-start(bf16[41,16,512]{2,1,0:T(8,128)(2,1)S(1)} %ring_message.1.refs_0_), channel_id=1, source_target_pairs={{0,7},{1,0},{2,1},{3,2},{4,3},{5,4},{6,5},{7,6},{8,15},{9,8},{10,9... | collective-permute-start | bytes 2015240 | tf_op jit(solution)/shard_map/ppermute | solution.py:33
  25.3 2.9 %collective-permute-start.12 = (bf16[128,1024]{1,0:T(8,128)(2,1)}, bf16[128,1024]{1,0:T(8,128)(2,1)S(1)}, u32[]{:S(2)}, u32[]{:S(2)}) collective-permute-start(bf16[128,1024]{1,0:T(8,128)(2,1)} %param.11), channel_id=1, source_target_pairs={{0,192},{32,224},{64,0},{96,32},{128,64},{160,96},{192,128},{224,1... | collective-permute-start | bytes 786440 | tf_op jit(solution)/shard_map/ppermute | solution.py:38
  28.8 5.6 %collective-permute-done.12 = bf16[128,1024]{1,0:T(8,128)(2,1)S(1)} collective-permute-done((bf16[128,1024]{1,0:T(8,128)(2,1)}, bf16[128,1024]{1,0:T(8,128)(2,1)S(1)}, u32[]{:S(2)}, u32[]{:S(2)}) %collective-permute-start.12) | collective-permute-done | bytes 262176 | tf_op jit(solution)/shard_map/ppermute | solution.py:38
  35.3 7.9 %collective-permute-done.10 = bf16[128,1024]{1,0:T(8,128)(2,1)S(1)} collective-permute-done((bf16[128,1024]{1,0:T(8,128)(2,1)}, bf16[128,1024]{1,0:T(8,128)(2,1)S(1)}, u32[]{:S(2)}, u32[]{:S(2)}) %collective-permute-start.10) | collective-permute-done | bytes 262176 | tf_op jit(solution)/shard_map/ppermute | solution.py:38
  44.4 2.7 %collective-permute-start.14 = (bf16[41,16,512]{2,1,0:T(8,128)(2,1)S(1)}, bf16[41,16,512]{2,1,0:T(8,128)(2,1)S(1)}, u32[]{:S(2)}, u32[]{:S(2)}) collective-permute-start(bf16[41,16,512]{2,1,0:T(8,128)(2,1)S(1)} %collective-permute-done.9.refs_1_.refs_2_), channel_id=1, source_target_pairs={{0,7},{1,0},{2,1},{3,2},{4,3},{5,4},{6,5},{7,6},{8,15},{9,8},{10,9... | collective-permute-start | bytes 2015240 | tf_op jit(solution)/shard_map/ppermute | solution.py:33
  50.4 4.9 %prepare_adjoint.1 = (bf16[8,512,512]{2,1,0:T(8,128)(2,1)S(1)}, bf16[4,512,1024]{2,1,0:T(8,128)(2,1)S(1)}) custom-call(s32[4]{0:T(128)S(1)} %pad_add_fusion.pos, s32[64,64]{1,0:T(8,128)S(1)} %copy-done.3, bf16[2048,512]{1,0:T(8,128)(2,1)S(1)} %copy-done, bf16[2048,512]{1,0:T(8,128)(2,1)} %collective-permute-done.1.other), custom_call_target="tpu_custom_call" | custom-call | tf_op jit(solution)/shard_map/prepare_adjoint/pallas_call | solution.py:179
  55.8 6.4 %collective-permute-done.16.refs_2_ = bf16[2,9,16,512]{3,2,1,0:T(8,128)(2,1)S(1)} collective-permute-done((bf16[2,9,16,512]{3,2,1,0:T(8,128)(2,1)S(1)}, bf16[2,9,16,512]{3,2,1,0:T(8,128)(2,1)S(1)}, u32[]{:S(2)}, u32[]{:S(2)}) %collective-permute-start.16) | collective-permute-done | bytes 294944 | tf_op jit(solution)/shard_map/ppermute | solution.py:28
  63.5 2.7 %collective-permute-start.19 = (bf16[41,16,512]{2,1,0:T(8,128)(2,1)S(1)}, bf16[41,16,512]{2,1,0:T(8,128)(2,1)S(1)}, u32[]{:S(2)}, u32[]{:S(2)}) collective-permute-start(bf16[41,16,512]{2,1,0:T(8,128)(2,1)S(1)} %collective-permute-done.14.refs_4_.refs_1_), channel_id=1, source_target_pairs={{0,7},{1,0},{2,1},{3,2},{4,3},{5,4},{6,5},{7,6},{8,15},{9,8},{10,9... | collective-permute-start | bytes 2015240 | tf_op jit(solution)/shard_map/ppermute | solution.py:33
  66.1 2.3 %collective-permute-start.22 = (bf16[2,9,16,512]{3,2,1,0:T(8,128)(2,1)S(1)}, bf16[2,9,16,512]{3,2,1,0:T(8,128)(2,1)S(1)}, u32[]{:S(2)}, u32[]{:S(2)}) collective-permute-start(bf16[2,9,16,512]{3,2,1,0:T(8,128)(2,1)S(1)} %join_parts.5.refs_0_.refs_4_), channel_id=1, source_target_pairs={{0,16},{1,17},{2,18},{3,19},{4,20},{5,21},{6,22},{7,23},{8,24},{9,... | collective-permute-start | bytes 884744 | tf_op jit(solution)/shard_map/ppermute | solution.py:28
  69.9 3.0 %masked_product.7.refs_2_ = f32[512,512]{1,0:T(8,128)S(1)} custom-call(s32[4]{0:T(128)S(1)} %pad_add_fusion.pos, bf16[8,512,512]{2,1,0:T(8,128)(2,1)S(1)} %get-tuple-element.85.adjoint, bf16[41,16,512]{2,1,0:T(8,128)(2,1)S(1)} %ring_message.1.refs_0_, bf16[41,16,512]{2,1,0:T(8,128)(2,1)S(1)} %collective-permute-done.8.refs_0_.refs_1_, ...), custom_call_target="tpu_custom_call" | custom-call | tf_op jit(solution)/shard_map/masked_product/pallas_call | solution.py:236
  74.7 7.2 %collective-permute-done.21.refs_2_.refs_6_ = bf16[2,9,16,512]{3,2,1,0:T(8,128)(2,1)S(1)} collective-permute-done((bf16[2,9,16,512]{3,2,1,0:T(8,128)(2,1)S(1)}, bf16[2,9,16,512]{3,2,1,0:T(8,128)(2,1)S(1)}, u32[]{:S(2)}, u32[]{:S(2)}) %collective-permute-start.21) | collective-permute-done | bytes 294944 | tf_op jit(solution)/shard_map/ppermute | solution.py:28
  82.8 2.8 %collective-permute-start.30 = (bf16[2,9,16,512]{3,2,1,0:T(8,128)(2,1)S(1)}, bf16[2,9,16,512]{3,2,1,0:T(8,128)(2,1)S(1)}, u32[]{:S(2)}, u32[]{:S(2)}) collective-permute-start(bf16[2,9,16,512]{3,2,1,0:T(8,128)(2,1)S(1)} %join_parts.6.refs_0_.refs_8_), channel_id=1, source_target_pairs={{0,16},{1,17},{2,18},{3,19},{4,20},{5,21},{6,22},{7,23},{8,24},{9,... | collective-permute-start | bytes 884744 | tf_op jit(solution)/shard_map/ppermute | solution.py:28
  94.2 2.6 %collective-permute-start.27 = (f32[512,128]{1,0:T(8,128)S(1)}, f32[512,128]{1,0:T(8,128)S(1)}, u32[]{:S(2)}, u32[]{:S(2)}) collective-permute-start(f32[512,128]{1,0:T(8,128)S(1)} %get-tuple-element.110), channel_id=1, source_target_pairs={{0,192},{32,224},{64,0},{96,32},{128,64},{160,96},{192,128},{224,1... | collective-permute-start | bytes 786440 | tf_op jit(solution)/shard_map/ppermute | solution.py:38
  96.8 2.3 %collective-permute-done.29.refs_2_.refs_10_ = bf16[2,9,16,512]{3,2,1,0:T(8,128)(2,1)S(1)} collective-permute-done((bf16[2,9,16,512]{3,2,1,0:T(8,128)(2,1)S(1)}, bf16[2,9,16,512]{3,2,1,0:T(8,128)(2,1)S(1)}, u32[]{:S(2)}, u32[]{:S(2)}) %collective-permute-start.29) | collective-permute-done | bytes 294944 | tf_op jit(solution)/shard_map/ppermute | solution.py:28
  100.7 2.8 %collective-permute-start.35 = (bf16[2,9,16,512]{3,2,1,0:T(8,128)(2,1)S(1)}, bf16[2,9,16,512]{3,2,1,0:T(8,128)(2,1)S(1)}, u32[]{:S(2)}, u32[]{:S(2)}) collective-permute-start(bf16[2,9,16,512]{3,2,1,0:T(8,128)(2,1)S(1)} %join_parts.7.refs_0_.refs_12_), channel_id=1, source_target_pairs={{0,24},{1,25},{2,26},{3,27},{4,28},{5,29},{6,30},{7,31},{8,0},{9,1... | collective-permute-start | bytes 884744 | tf_op jit(solution)/shard_map/ppermute | solution.py:28
  104.9 2.3 %collective-permute-done.25 = f32[512,128]{1,0:T(8,128)S(1)} collective-permute-done((f32[512,128]{1,0:T(8,128)S(1)}, f32[512,128]{1,0:T(8,128)S(1)}, u32[]{:S(2)}, u32[]{:S(2)}) %collective-permute-start.25) | collective-permute-done | bytes 262176 | tf_op jit(solution)/shard_map/ppermute | solution.py:38
  107.2 2.4 %collective-permute-start.41 = (bf16[4,128,1024]{2,1,0:T(8,128)(2,1)S(1)}, bf16[4,128,1024]{2,1,0:T(8,128)(2,1)S(1)}, u32[]{:S(2)}, u32[]{:S(2)}) collective-permute-start(bf16[4,128,1024]{2,1,0:T(8,128)(2,1)S(1)} %pad_maximum_fusion.inverse), channel_id=1, source_target_pairs={{0,32},{32,0},{64,96},{96,64},{128,160},{160,128},{192,224},{224,1... | collective-permute-start | bytes 3145736 | tf_op jit(solution)/shard_map/ppermute | solution.py:46
  109.6 1.9 %collective-permute-start.34 = (bf16[2,9,16,512]{3,2,1,0:T(8,128)(2,1)S(1)}, bf16[2,9,16,512]{3,2,1,0:T(8,128)(2,1)S(1)}, u32[]{:S(2)}, u32[]{:S(2)}) collective-permute-start(bf16[2,9,16,512]{3,2,1,0:T(8,128)(2,1)S(1)} %join_parts.7.refs_0_.refs_12_), channel_id=1, source_target_pairs={{0,8},{1,9},{2,10},{3,11},{4,12},{5,13},{6,14},{7,15},{8,16},{9,17... | collective-permute-start | bytes 884744 | tf_op jit(solution)/shard_map/ppermute | solution.py:28
  112.3 3.8 %collective-permute-done.35.refs_2_.refs_14_ = bf16[2,9,16,512]{3,2,1,0:T(8,128)(2,1)S(1)} collective-permute-done((bf16[2,9,16,512]{3,2,1,0:T(8,128)(2,1)S(1)}, bf16[2,9,16,512]{3,2,1,0:T(8,128)(2,1)S(1)}, u32[]{:S(2)}, u32[]{:S(2)}) %collective-permute-start.35) | collective-permute-done | bytes 294944 | tf_op jit(solution)/shard_map/ppermute | solution.py:28
  116.1 4.2 %collective-permute-done.34.refs_1_.refs_13_ = bf16[2,9,16,512]{3,2,1,0:T(8,128)(2,1)S(1)} collective-permute-done((bf16[2,9,16,512]{3,2,1,0:T(8,128)(2,1)S(1)}, bf16[2,9,16,512]{3,2,1,0:T(8,128)(2,1)S(1)}, u32[]{:S(2)}, u32[]{:S(2)}) %collective-permute-start.34) | collective-permute-done | bytes 294944 | tf_op jit(solution)/shard_map/ppermute | solution.py:28
  129.3 3.5 %collective-permute-done.37 = bf16[512,128]{1,0:T(8,128)(2,1)S(1)} collective-permute-done((bf16[512,128]{1,0:T(8,128)(2,1)S(1)}, bf16[512,128]{1,0:T(8,128)(2,1)S(1)}, u32[]{:S(2)}, u32[]{:S(2)}) %collective-permute-start.37) | collective-permute-done | bytes 131104 | tf_op jit(solution)/shard_map/ppermute | solution.py:38
  (97 shorter events, 44.3 us)
Async XLA Ops:
  19.7 24.6 %collective-permute-start.9 = (bf16[41,16,512]{2,1,0:T(8,128)(2,1)S(1)}, bf16[41,16,512]{2,1,0:T(8,128)(2,1)S(1)}, u32[]{:S(2)}, u32[]{:S(2)}) collective-permute-start(bf16[41,16,512]{2,1,0:T(8,128)(2,1)S(1)} %ring_message.1.refs_0_), channel_id=1, source_target_pairs={{0,7},{1,0},{2,1},{3,2},{4,3},{5,4},{6,5},{7,6},{8,15},{9,8},{10,9... | collective-permute-start | bytes 2015240 | tf_op jit(solution)/shard_map/ppermute | solution.py:33
  25.3 18.9 %collective-permute-start.8 = (bf16[41,16,512]{2,1,0:T(8,128)(2,1)S(1)}, bf16[41,16,512]{2,1,0:T(8,128)(2,1)S(1)}, u32[]{:S(2)}, u32[]{:S(2)}) collective-permute-start(bf16[41,16,512]{2,1,0:T(8,128)(2,1)S(1)} %ring_message.1.refs_0_), channel_id=1, source_target_pairs={{0,1},{1,2},{2,3},{3,4},{4,5},{5,6},{6,7},{7,0},{8,9},{9,10},{10,1... | collective-permute-start | bytes 2015240 | tf_op jit(solution)/shard_map/ppermute | solution.py:33
  28.3 14.9 %collective-permute-start.10 = (bf16[128,1024]{1,0:T(8,128)(2,1)}, bf16[128,1024]{1,0:T(8,128)(2,1)S(1)}, u32[]{:S(2)}, u32[]{:S(2)}) collective-permute-start(bf16[128,1024]{1,0:T(8,128)(2,1)} %param.11), channel_id=1, source_target_pairs={{0,64},{32,96},{64,128},{96,160},{128,192},{160,224},{192,0},{224,... | collective-permute-start | bytes 786440 | tf_op jit(solution)/shard_map/ppermute | solution.py:38
  44.3 19.2 %collective-permute-start.13 = (bf16[41,16,512]{2,1,0:T(8,128)(2,1)S(1)}, bf16[41,16,512]{2,1,0:T(8,128)(2,1)S(1)}, u32[]{:S(2)}, u32[]{:S(2)}) collective-permute-start(bf16[41,16,512]{2,1,0:T(8,128)(2,1)S(1)} %collective-permute-done.8.refs_0_.refs_1_), channel_id=1, source_target_pairs={{0,1},{1,2},{2,3},{3,4},{4,5},{5,6},{6,7},{7,0},{8,9},{9,10},{10,1... | collective-permute-start | bytes 2015240 | tf_op jit(solution)/shard_map/ppermute | solution.py:33
  44.4 19.1 %collective-permute-start.14 = (bf16[41,16,512]{2,1,0:T(8,128)(2,1)S(1)}, bf16[41,16,512]{2,1,0:T(8,128)(2,1)S(1)}, u32[]{:S(2)}, u32[]{:S(2)}) collective-permute-start(bf16[41,16,512]{2,1,0:T(8,128)(2,1)S(1)} %collective-permute-done.9.refs_1_.refs_2_), channel_id=1, source_target_pairs={{0,7},{1,0},{2,1},{3,2},{4,3},{5,4},{6,5},{7,6},{8,15},{9,8},{10,9... | collective-permute-start | bytes 2015240 | tf_op jit(solution)/shard_map/ppermute | solution.py:33
  48.9 13.2 %collective-permute-start.16 = (bf16[2,9,16,512]{3,2,1,0:T(8,128)(2,1)S(1)}, bf16[2,9,16,512]{3,2,1,0:T(8,128)(2,1)S(1)}, u32[]{:S(2)}, u32[]{:S(2)}) collective-permute-start(bf16[2,9,16,512]{3,2,1,0:T(8,128)(2,1)S(1)} %join_parts.4.refs_0_), channel_id=1, source_target_pairs={{0,24},{1,25},{2,26},{3,27},{4,28},{5,29},{6,30},{7,31},{8,0},{9,1... | collective-permute-start | bytes 884744 | tf_op jit(solution)/shard_map/ppermute | solution.py:28
  49.8 13.7 %collective-permute-start.15 = (bf16[2,9,16,512]{3,2,1,0:T(8,128)(2,1)S(1)}, bf16[2,9,16,512]{3,2,1,0:T(8,128)(2,1)S(1)}, u32[]{:S(2)}, u32[]{:S(2)}) collective-permute-start(bf16[2,9,16,512]{3,2,1,0:T(8,128)(2,1)S(1)} %join_parts.4.refs_0_), channel_id=1, source_target_pairs={{0,8},{1,9},{2,10},{3,11},{4,12},{5,13},{6,14},{7,15},{8,16},{9,17... | collective-permute-start | bytes 884744 | tf_op jit(solution)/shard_map/ppermute | solution.py:28
  63.4 19.1 %collective-permute-start.18 = (bf16[41,16,512]{2,1,0:T(8,128)(2,1)S(1)}, bf16[41,16,512]{2,1,0:T(8,128)(2,1)S(1)}, u32[]{:S(2)}, u32[]{:S(2)}) collective-permute-start(bf16[41,16,512]{2,1,0:T(8,128)(2,1)S(1)} %collective-permute-done.13.refs_3_.refs_0_), channel_id=1, source_target_pairs={{0,1},{1,2},{2,3},{3,4},{4,5},{5,6},{6,7},{7,0},{8,9},{9,10},{10,1... | collective-permute-start | bytes 2015240 | tf_op jit(solution)/shard_map/ppermute | solution.py:33
  63.5 19.1 %collective-permute-start.19 = (bf16[41,16,512]{2,1,0:T(8,128)(2,1)S(1)}, bf16[41,16,512]{2,1,0:T(8,128)(2,1)S(1)}, u32[]{:S(2)}, u32[]{:S(2)}) collective-permute-start(bf16[41,16,512]{2,1,0:T(8,128)(2,1)S(1)} %collective-permute-done.14.refs_4_.refs_1_), channel_id=1, source_target_pairs={{0,7},{1,0},{2,1},{3,2},{4,3},{5,4},{6,5},{7,6},{8,15},{9,8},{10,9... | collective-permute-start | bytes 2015240 | tf_op jit(solution)/shard_map/ppermute | solution.py:33
  68.4 13.5 %collective-permute-start.21 = (bf16[2,9,16,512]{3,2,1,0:T(8,128)(2,1)S(1)}, bf16[2,9,16,512]{3,2,1,0:T(8,128)(2,1)S(1)}, u32[]{:S(2)}, u32[]{:S(2)}) collective-permute-start(bf16[2,9,16,512]{3,2,1,0:T(8,128)(2,1)S(1)} %join_parts.5.refs_0_.refs_4_), channel_id=1, source_target_pairs={{0,24},{1,25},{2,26},{3,27},{4,28},{5,29},{6,30},{7,31},{8,0},{9,1... | collective-permute-start | bytes 884744 | tf_op jit(solution)/shard_map/ppermute | solution.py:28
  69.6 13.0 %collective-permute-start.20 = (bf16[2,9,16,512]{3,2,1,0:T(8,128)(2,1)S(1)}, bf16[2,9,16,512]{3,2,1,0:T(8,128)(2,1)S(1)}, u32[]{:S(2)}, u32[]{:S(2)}) collective-permute-start(bf16[2,9,16,512]{3,2,1,0:T(8,128)(2,1)S(1)} %join_parts.5.refs_0_.refs_4_), channel_id=1, source_target_pairs={{0,8},{1,9},{2,10},{3,11},{4,12},{5,13},{6,14},{7,15},{8,16},{9,17... | collective-permute-start | bytes 884744 | tf_op jit(solution)/shard_map/ppermute | solution.py:28
  82.6 10.1 %collective-permute-start.24 = (bf16[25,16,512]{2,1,0:T(8,128)(2,1)S(1)}, bf16[25,16,512]{2,1,0:T(8,128)(2,1)S(1)}, u32[]{:S(2)}, u32[]{:S(2)}) collective-permute-start(bf16[25,16,512]{2,1,0:T(8,128)(2,1)S(1)} %slice.15), channel_id=1, source_target_pairs={{0,7},{1,0},{2,1},{3,2},{4,3},{5,4},{6,5},{7,6},{8,15},{9,8},{10,9... | collective-permute-start | bytes 1228808 | tf_op jit(solution)/shard_map/ppermute | solution.py:33
  82.8 11.3 %collective-permute-start.30 = (bf16[2,9,16,512]{3,2,1,0:T(8,128)(2,1)S(1)}, bf16[2,9,16,512]{3,2,1,0:T(8,128)(2,1)S(1)}, u32[]{:S(2)}, u32[]{:S(2)}) collective-permute-start(bf16[2,9,16,512]{3,2,1,0:T(8,128)(2,1)S(1)} %join_parts.6.refs_0_.refs_8_), channel_id=1, source_target_pairs={{0,16},{1,17},{2,18},{3,19},{4,20},{5,21},{6,22},{7,23},{8,24},{9,... | collective-permute-start | bytes 884744 | tf_op jit(solution)/shard_map/ppermute | solution.py:28
  87.0 12.1 %collective-permute-start.29 = (bf16[2,9,16,512]{3,2,1,0:T(8,128)(2,1)S(1)}, bf16[2,9,16,512]{3,2,1,0:T(8,128)(2,1)S(1)}, u32[]{:S(2)}, u32[]{:S(2)}) collective-permute-start(bf16[2,9,16,512]{3,2,1,0:T(8,128)(2,1)S(1)} %join_parts.6.refs_0_.refs_8_), channel_id=1, source_target_pairs={{0,24},{1,25},{2,26},{3,27},{4,28},{5,29},{6,30},{7,31},{8,0},{9,1... | collective-permute-start | bytes 884744 | tf_op jit(solution)/shard_map/ppermute | solution.py:28
  88.2 12.5 %collective-permute-start.28 = (bf16[2,9,16,512]{3,2,1,0:T(8,128)(2,1)S(1)}, bf16[2,9,16,512]{3,2,1,0:T(8,128)(2,1)S(1)}, u32[]{:S(2)}, u32[]{:S(2)}) collective-permute-start(bf16[2,9,16,512]{3,2,1,0:T(8,128)(2,1)S(1)} %join_parts.6.refs_0_.refs_8_), channel_id=1, source_target_pairs={{0,8},{1,9},{2,10},{3,11},{4,12},{5,13},{6,14},{7,15},{8,16},{9,17... | collective-permute-start | bytes 884744 | tf_op jit(solution)/shard_map/ppermute | solution.py:28
  94.0 13.2 %collective-permute-start.25 = (f32[512,128]{1,0:T(8,128)S(1)}, f32[512,128]{1,0:T(8,128)S(1)}, u32[]{:S(2)}, u32[]{:S(2)}) collective-permute-start(f32[512,128]{1,0:T(8,128)S(1)} %get-tuple-element.108), channel_id=1, source_target_pairs={{0,64},{32,96},{64,128},{96,160},{128,192},{160,224},{192,0},{224,... | collective-permute-start | bytes 786440 | tf_op jit(solution)/shard_map/ppermute | solution.py:38
  94.1 15.5 %collective-permute-start.26 = (f32[512,128]{1,0:T(8,128)S(1)}, f32[512,128]{1,0:T(8,128)S(1)}, u32[]{:S(2)}, u32[]{:S(2)}) collective-permute-start(f32[512,128]{1,0:T(8,128)S(1)} %get-tuple-element.109), channel_id=1, source_target_pairs={{0,128},{32,160},{64,192},{96,224},{128,0},{160,32},{192,64},{224,... | collective-permute-start | bytes 786440 | tf_op jit(solution)/shard_map/ppermute | solution.py:38
  94.2 17.3 %collective-permute-start.27 = (f32[512,128]{1,0:T(8,128)S(1)}, f32[512,128]{1,0:T(8,128)S(1)}, u32[]{:S(2)}, u32[]{:S(2)}) collective-permute-start(f32[512,128]{1,0:T(8,128)S(1)} %get-tuple-element.110), channel_id=1, source_target_pairs={{0,192},{32,224},{64,0},{96,32},{128,64},{160,96},{192,128},{224,1... | collective-permute-start | bytes 786440 | tf_op jit(solution)/shard_map/ppermute | solution.py:38
  99.1 13.2 %collective-permute-start.36 = (bf16[2,9,16,512]{3,2,1,0:T(8,128)(2,1)S(1)}, bf16[2,9,16,512]{3,2,1,0:T(8,128)(2,1)S(1)}, u32[]{:S(2)}, u32[]{:S(2)}) collective-permute-start(bf16[2,9,16,512]{3,2,1,0:T(8,128)(2,1)S(1)} %join_parts.7.refs_0_.refs_12_), channel_id=1, source_target_pairs={{0,16},{1,17},{2,18},{3,19},{4,20},{5,21},{6,22},{7,23},{8,24},{9,... | collective-permute-start | bytes 884744 | tf_op jit(solution)/shard_map/ppermute | solution.py:28
  100.7 15.4 %collective-permute-start.35 = (bf16[2,9,16,512]{3,2,1,0:T(8,128)(2,1)S(1)}, bf16[2,9,16,512]{3,2,1,0:T(8,128)(2,1)S(1)}, u32[]{:S(2)}, u32[]{:S(2)}) collective-permute-start(bf16[2,9,16,512]{3,2,1,0:T(8,128)(2,1)S(1)} %join_parts.7.refs_0_.refs_12_), channel_id=1, source_target_pairs={{0,24},{1,25},{2,26},{3,27},{4,28},{5,29},{6,30},{7,31},{8,0},{9,1... | collective-permute-start | bytes 884744 | tf_op jit(solution)/shard_map/ppermute | solution.py:28
  107.2 19.2 %collective-permute-start.41 = (bf16[4,128,1024]{2,1,0:T(8,128)(2,1)S(1)}, bf16[4,128,1024]{2,1,0:T(8,128)(2,1)S(1)}, u32[]{:S(2)}, u32[]{:S(2)}) collective-permute-start(bf16[4,128,1024]{2,1,0:T(8,128)(2,1)S(1)} %pad_maximum_fusion.inverse), channel_id=1, source_target_pairs={{0,32},{32,0},{64,96},{96,64},{128,160},{160,128},{192,224},{224,1... | collective-permute-start | bytes 3145736 | tf_op jit(solution)/shard_map/ppermute | solution.py:46
  109.6 10.7 %collective-permute-start.34 = (bf16[2,9,16,512]{3,2,1,0:T(8,128)(2,1)S(1)}, bf16[2,9,16,512]{3,2,1,0:T(8,128)(2,1)S(1)}, u32[]{:S(2)}, u32[]{:S(2)}) collective-permute-start(bf16[2,9,16,512]{3,2,1,0:T(8,128)(2,1)S(1)} %join_parts.7.refs_0_.refs_12_), channel_id=1, source_target_pairs={{0,8},{1,9},{2,10},{3,11},{4,12},{5,13},{6,14},{7,15},{8,16},{9,17... | collective-permute-start | bytes 884744 | tf_op jit(solution)/shard_map/ppermute | solution.py:28
  112.3 9.6 %collective-permute-start.33 = (bf16[512,128]{1,0:T(8,128)(2,1)S(1)}, bf16[512,128]{1,0:T(8,128)(2,1)S(1)}, u32[]{:S(2)}, u32[]{:S(2)}) collective-permute-start(bf16[512,128]{1,0:T(8,128)(2,1)S(1)} %get-tuple-element.130), channel_id=1, source_target_pairs={{0,192},{32,224},{64,0},{96,32},{128,64},{160,96},{192,128},{224,1... | collective-permute-start | bytes 393224 | tf_op jit(solution)/shard_map/ppermute | solution.py:38
  112.3 9.6 %collective-permute-start.32 = (bf16[512,128]{1,0:T(8,128)(2,1)S(1)}, bf16[512,128]{1,0:T(8,128)(2,1)S(1)}, u32[]{:S(2)}, u32[]{:S(2)}) collective-permute-start(bf16[512,128]{1,0:T(8,128)(2,1)S(1)} %get-tuple-element.130), channel_id=1, source_target_pairs={{0,128},{32,160},{64,192},{96,224},{128,0},{160,32},{192,64},{224,... | collective-permute-start | bytes 393224 | tf_op jit(solution)/shard_map/ppermute | solution.py:38
  (23 other events, 239.5 us)

commit v10 on v8

--- a/solution.py
+++ b/solution.py
@@ -133,7 +133,7 @@
 
 def join_kernel(*refs):
     for n, ref in enumerate(refs[:-1]):
-        refs[-1][n] = ref[TWO:]
+        refs[-1][n] = ref[ref.shape[0] - ONE:]
 
 
 def join(*messages):
@@ -351,25 +351,25 @@
     sums_one = product(
         pos, for_one, near + middle,
         [(1 + c, [(NX * c + i, 0, 2) for i in range(NX)]) for c in range(2)])
-    third = x_all(join(down3, up3))
     far_low, far_high, sums, sums_one = together(
         z_shift(down3[:TWO // 2], 1), z_shift(up3[TWO // 2:], -1), sums, sums_one)
 
     mine, *sent = product(
         pos, for_two, [far_low, far_high], [(7, [(0, 0, TWO // 2), (1, 0, TWO // 2)])], sums, F32)
-    last = x_all(far_high[None, TWO // 2:])
-    sums_one = product(pos, for_one, third, [(3, [(i, 0, 2) for i in range(NX)])], sums_one)
-    r1, r2, r3, sums_one, *last = together(
-        *[y_shift(part, d + 1) for d, part in enumerate(sent)], sums_one, *last)
+    sent = [y_shift(part, d + 1) for d, part in enumerate(sent)]
+    third = x_all(join(down3, up3, far_high))
+    r1, r2, r3 = together(*sent)
     second_grad = incoming + ((mine + r1) + (r2 + r3))
     rounded = second_grad.astype(BF16)
 
+    sums_one = product(pos, for_one, third, [(3, [(i, 0, 2) for i in range(NX)])], sums_one)
     sums_one = product(
-        pos, for_one, first_x + last,
-        [(0, [(NX * s + i, 0, 1) for i in range(NX) for s in range(2)])], sums_one, BF16)
+        pos, for_one, first_x + third,
+        [(0, [(NX * s + i, 2 * s, 1) for i in range(NX) for s in range(2)])], sums_one, BF16)
     where = tuple(
-        ((i, 0),) + tuple((NX * (1 + j // 2) + i, j % 2) for j in range(7)) for i in range(NX))
-    factors = factor(pos, inverse, inverse_other, first_x + near + middle + third + last, where)
+        ((i, 0),) + tuple((NX * (1 + j // 2) + i, j % 2) for j in range(6)) + ((3 * NX + i, 2),)
+        for i in range(NX))
+    factors = factor(pos, inverse, inverse_other, first_x + near + middle + third, where)
     s1, s2, s3, mine, *sent = together(*[y_shift(rounded, d) for d in range(1, NY)], *sums_one)
     rounded = jnp.stack([rounded, s1, s2, s3])
     rounded_other = core_swap(rounded)

time: 132 us -> 134 us (1.015)
  waiting for transfers between devices: 35.6 us -> 39.6 us
  starting transfers between devices: 68.7 us -> 66.4 us
    ppermute x18 -> x15, waiting for transfers between devices: 20 us -> 24.7 us  [x_shift(): return lax.ppermute(value, 'col', pairs)]
    ppermute x12, waiting for transfers between devices: 11.7 us -> 7.73 us  [y_shift(): return lax.ppermute(value, 'row', pairs)]
    ppermute x8, waiting for transfers between devices: 3.05 us -> 6.28 us  [z_shift(): return lax.ppermute(value, 'col', pairs)]
    ppermute x4, starting transfers between devices: 8.1 us -> 10.7 us  [core_swap(): return lax.ppermute(value, 'row', [(r, r ^ 1) for r in range(2 * NY)])]
    ppermute x12, starting transfers between devices: 13.2 us -> 10.7 us  [y_shift(): return lax.ppermute(value, 'row', pairs)]
    ppermute x18 -> x15, starting transfers between devices: 29.7 us -> 27.2 us  [x_shift(): return lax.ppermute(value, 'col', pairs)]
  transfers between devices with their start and end apart: 45 -> 42, of which waited for: 17 -> 15; matrix products, arithmetic and copies ran while one was open for 2% -> 2% of each run, Pallas kernels for 16% -> 15%
where the time goes in v10:
time: 134 us
  starting transfers between devices  66.4 us (50%)
  waiting for transfers between devices  39.6 us (30%)
  Pallas kernels  22.2 us (17%)
  other arithmetic  2.82 us (2%)
  local copies, waits for them, and re-layouts  1.91 us (1%)
    ppermute x15, starting transfers between devices, x_shift(): return lax.ppermute(value, 'col', pairs)  27.2 us
    ppermute x15, waiting for transfers between devices, x_shift(): return lax.ppermute(value, 'col', pairs)  24.7 us
    ppermute x8, starting transfers between devices, z_shift(): return lax.ppermute(value, 'col', pairs)  12.7 us
    pallas_call x6, Pallas kernels, product(): pl.pallas_call(kernel, out_shape=(column,) + (jax.ShapeDtypeStruct((512,...  12.3 us
    ppermute x12, starting transfers between devices, y_shift(): return lax.ppermute(value, 'row', pairs)  10.7 us
    ppermute x4, starting transfers between devices, core_swap(): return lax.ppermute(value, 'row', [(r, r ^ 1) for r in range(2 * NY)])  10.7 us
    ppermute x12, waiting for transfers between devices, y_shift(): return lax.ppermute(value, 'row', pairs)  7.73 us
    ppermute x8, waiting for transfers between devices, z_shift(): return lax.ppermute(value, 'col', pairs)  6.28 us
  transfers between devices with their start and end apart: 42, of which 15 were waited for; matrix products, arithmetic and copies ran while one was open for 2% of the time, Pallas kernels for 15%

profile of v10, /device:TPU:1, one launch (start us, length us, event | category | flops | bytes accessed | tf_op | source)
XLA Modules:
  0.0 133.9 jit_solution(14018899019918775914)
XLA Ops:
  0.6 3.3 %collective-permute-start.1 = (bf16[2048,512]{1,0:T(8,128)(2,1)}, bf16[2048,512]{1,0:T(8,128)(2,1)}, u32[]{:S(2)}, u32[]{:S(2)}) collective-permute-start(bf16[2048,512]{1,0:T(8,128)(2,1)} %mine.1), channel_id=1, source_target_pairs={{0,32},{32,0},{64,96},{96,64},{128,160},{160,128},{192,224},{224,1... | collective-permute-start | bytes 6291464 | tf_op jit(solution)/shard_map/ppermute | solution.py:46
  8.6 2.4 %collective-permute-start.4 = (bf16[128,512]{1,0:T(8,128)(2,1)S(1)}, bf16[128,512]{1,0:T(8,128)(2,1)S(1)}, u32[]{:S(2)}, u32[]{:S(2)}) collective-permute-start(bf16[128,512]{1,0:T(8,128)(2,1)S(1)} %get-tuple-element.76.two), channel_id=1, source_target_pairs={{0,16},{1,17},{2,18},{3,19},{4,20},{5,21},{6,22},{7,23},{8,24},{9,... | collective-permute-start | bytes 393224 | tf_op jit(solution)/shard_map/ppermute | solution.py:28
  21.7 5.7 %collective-permute-start.11 = (bf16[41,16,512]{2,1,0:T(8,128)(2,1)S(1)}, bf16[41,16,512]{2,1,0:T(8,128)(2,1)S(1)}, u32[]{:S(2)}, u32[]{:S(2)}) collective-permute-start(bf16[41,16,512]{2,1,0:T(8,128)(2,1)S(1)} %get-tuple-element.87.refs_0_), channel_id=1, source_target_pairs={{0,7},{1,0},{2,1},{3,2},{4,3},{5,4},{6,5},{7,6},{8,15},{9,8},{10,9... | collective-permute-start | bytes 2015240 | tf_op jit(solution)/shard_map/ppermute | solution.py:33
  28.9 2.7 %collective-permute-start.15 = (bf16[1,9,16,512]{3,2,1,0:T(8,128)(2,1)S(1)}, bf16[1,9,16,512]{3,2,1,0:T(8,128)(2,1)S(1)}, u32[]{:S(2)}, u32[]{:S(2)}) collective-permute-start(bf16[1,9,16,512]{3,2,1,0:T(8,128)(2,1)S(1)} %get-tuple-element.125.refs_0_), channel_id=1, source_target_pairs={{0,16},{1,17},{2,18},{3,19},{4,20},{5,21},{6,22},{7,23},{8,24},{9,... | collective-permute-start | bytes 442376 | tf_op jit(solution)/shard_map/ppermute | solution.py:28
  36.7 3.2 %collective-permute-done.13.refs_1_ = bf16[1,9,16,512]{3,2,1,0:T(8,128)(2,1)S(1)} collective-permute-done((bf16[1,9,16,512]{3,2,1,0:T(8,128)(2,1)S(1)}, bf16[1,9,16,512]{3,2,1,0:T(8,128)(2,1)S(1)}, u32[]{:S(2)}, u32[]{:S(2)}) %collective-permute-start.13) | collective-permute-done | bytes 147488 | tf_op jit(solution)/shard_map/ppermute | solution.py:28
  39.8 3.0 %collective-permute-done.10.refs_0_.refs_1_ = bf16[41,16,512]{2,1,0:T(8,128)(2,1)S(1)} collective-permute-done((bf16[41,16,512]{2,1,0:T(8,128)(2,1)S(1)}, bf16[41,16,512]{2,1,0:T(8,128)(2,1)S(1)}, u32[]{:S(2)}, u32[]{:S(2)}) %collective-permute-start.10) | collective-permute-done | bytes 671776 | tf_op jit(solution)/shard_map/ppermute | solution.py:33
  42.9 2.7 %collective-permute-start.17 = (bf16[41,16,512]{2,1,0:T(8,128)(2,1)S(1)}, bf16[41,16,512]{2,1,0:T(8,128)(2,1)S(1)}, u32[]{:S(2)}, u32[]{:S(2)}) collective-permute-start(bf16[41,16,512]{2,1,0:T(8,128)(2,1)S(1)} %collective-permute-done.11.refs_1_.refs_2_), channel_id=1, source_target_pairs={{0,7},{1,0},{2,1},{3,2},{4,3},{5,4},{6,5},{7,6},{8,15},{9,8},{10,9... | collective-permute-start | bytes 2015240 | tf_op jit(solution)/shard_map/ppermute | solution.py:33
  45.6 2.7 %collective-permute-start.20 = (bf16[2,9,16,512]{3,2,1,0:T(8,128)(2,1)S(1)}, bf16[2,9,16,512]{3,2,1,0:T(8,128)(2,1)S(1)}, u32[]{:S(2)}, u32[]{:S(2)}) collective-permute-start(bf16[2,9,16,512]{3,2,1,0:T(8,128)(2,1)S(1)} %join_parts.3.refs_0_.refs_4_), channel_id=1, source_target_pairs={{0,16},{1,17},{2,18},{3,19},{4,20},{5,21},{6,22},{7,23},{8,24},{9,... | collective-permute-start | bytes 884744 | tf_op jit(solution)/shard_map/ppermute | solution.py:28
  49.8 4.9 %prepare_adjoint.1 = (bf16[8,512,512]{2,1,0:T(8,128)(2,1)S(1)}, bf16[4,512,1024]{2,1,0:T(8,128)(2,1)S(1)}) custom-call(s32[4]{0:T(128)S(1)} %pad_add_fusion.pos, s32[64,64]{1,0:T(8,128)S(1)} %copy-done.3, bf16[2048,512]{1,0:T(8,128)(2,1)S(1)} %copy-done, bf16[2048,512]{1,0:T(8,128)(2,1)} %collective-permute-done.1.other), custom_call_target="tpu_custom_call" | custom-call | tf_op jit(solution)/shard_map/prepare_adjoint/pallas_call | solution.py:184
  54.7 4.7 %collective-permute-done.19.refs_2_.refs_6_ = bf16[2,9,16,512]{3,2,1,0:T(8,128)(2,1)S(1)} collective-permute-done((bf16[2,9,16,512]{3,2,1,0:T(8,128)(2,1)S(1)}, bf16[2,9,16,512]{3,2,1,0:T(8,128)(2,1)S(1)}, u32[]{:S(2)}, u32[]{:S(2)}) %collective-permute-start.19) | collective-permute-done | bytes 294944 | tf_op jit(solution)/shard_map/ppermute | solution.py:28
  59.5 2.7 %collective-permute-start.22 = (bf16[41,16,512]{2,1,0:T(8,128)(2,1)S(1)}, bf16[41,16,512]{2,1,0:T(8,128)(2,1)S(1)}, u32[]{:S(2)}, u32[]{:S(2)}) collective-permute-start(bf16[41,16,512]{2,1,0:T(8,128)(2,1)S(1)} %collective-permute-done.17.refs_4_.refs_1_), channel_id=1, source_target_pairs={{0,7},{1,0},{2,1},{3,2},{4,3},{5,4},{6,5},{7,6},{8,15},{9,8},{10,9... | collective-permute-start | bytes 2015240 | tf_op jit(solution)/shard_map/ppermute | solution.py:33
  62.2 3.9 %collective-permute-start.25 = (bf16[2,9,16,512]{3,2,1,0:T(8,128)(2,1)S(1)}, bf16[2,9,16,512]{3,2,1,0:T(8,128)(2,1)S(1)}, u32[]{:S(2)}, u32[]{:S(2)}) collective-permute-start(bf16[2,9,16,512]{3,2,1,0:T(8,128)(2,1)S(1)} %join_parts.4.refs_4_.refs_8_), channel_id=1, source_target_pairs={{0,16},{1,17},{2,18},{3,19},{4,20},{5,21},{6,22},{7,23},{8,24},{9,... | collective-permute-start | bytes 884744 | tf_op jit(solution)/shard_map/ppermute | solution.py:28
  67.6 3.0 %masked_product.6.refs_2_ = f32[512,512]{1,0:T(8,128)S(1)} custom-call(s32[4]{0:T(128)S(1)} %pad_add_fusion.pos, bf16[8,512,512]{2,1,0:T(8,128)(2,1)S(1)} %get-tuple-element.97.adjoint, bf16[41,16,512]{2,1,0:T(8,128)(2,1)S(1)} %get-tuple-element.87.refs_0_, bf16[41,16,512]{2,1,0:T(8,128)(2,1)S(1)} %collective-permute-done.10.refs_0_.refs_1_, ...), custom_call_target="tpu_custom_call" | custom-call | tf_op jit(solution)/shard_map/masked_product/pallas_call | solution.py:241
  70.6 7.8 %collective-permute-done.24.refs_6_.refs_10_ = bf16[2,9,16,512]{3,2,1,0:T(8,128)(2,1)S(1)} collective-permute-done((bf16[2,9,16,512]{3,2,1,0:T(8,128)(2,1)S(1)}, bf16[2,9,16,512]{3,2,1,0:T(8,128)(2,1)S(1)}, u32[]{:S(2)}, u32[]{:S(2)}) %collective-permute-start.24) | collective-permute-done | bytes 294944 | tf_op jit(solution)/shard_map/ppermute | solution.py:28
  81.9 2.2 %masked_product.8.refs_4_ = f32[512,512]{1,0:T(8,128)S(1)} custom-call(s32[4]{0:T(128)S(1)} %pad_add_fusion.pos, bf16[4,512,1024]{2,1,0:T(8,128)(2,1)S(1)} %get-tuple-element.106.adjoint, bf16[2,9,16,512]{3,2,1,0:T(8,128)(2,1)S(1)} %join_parts.3.refs_0_.refs_4_, bf16[2,9,16,512]{3,2,1,0:T(8,128)(2,1)S(1)} %collective-permute-done.18.refs_1_.refs_5_, ...), custom_call_target="tpu_custom_call" | custom-call | tf_op jit(solution)/shard_map/masked_product/pallas_call | solution.py:241
  88.7 2.9 %collective-permute-start.29 = (f32[512,128]{1,0:T(8,128)S(1)}, f32[512,128]{1,0:T(8,128)S(1)}, u32[]{:S(2)}, u32[]{:S(2)}) collective-permute-start(f32[512,128]{1,0:T(8,128)S(1)} %get-tuple-element.120), channel_id=1, source_target_pairs={{0,128},{32,160},{64,192},{96,224},{128,0},{160,32},{192,64},{224,... | collective-permute-start | bytes 786440 | tf_op jit(solution)/shard_map/ppermute | solution.py:38
  91.8 4.6 %collective-permute-start.36 = (bf16[3,9,16,512]{3,2,1,0:T(8,128)(2,1)S(1)}, bf16[3,9,16,512]{3,2,1,0:T(8,128)(2,1)S(1)}, u32[]{:S(2)}, u32[]{:S(2)}) collective-permute-start(bf16[3,9,16,512]{3,2,1,0:T(8,128)(2,1)S(1)} %join_parts.5.refs_0_.refs_4_.refs_12_), channel_id=1, source_target_pairs={{0,16},{1,17},{2,18},{3,19},{4,20},{5,21},{6,22},{7,23},{8,24},{9,... | collective-permute-start | bytes 1327112 | tf_op jit(solution)/shard_map/ppermute | solution.py:28
  96.4 2.1 %collective-permute-start.35 = (bf16[3,9,16,512]{3,2,1,0:T(8,128)(2,1)S(1)}, bf16[3,9,16,512]{3,2,1,0:T(8,128)(2,1)S(1)}, u32[]{:S(2)}, u32[]{:S(2)}) collective-permute-start(bf16[3,9,16,512]{3,2,1,0:T(8,128)(2,1)S(1)} %join_parts.5.refs_0_.refs_4_.refs_12_), channel_id=1, source_target_pairs={{0,24},{1,25},{2,26},{3,27},{4,28},{5,29},{6,30},{7,31},{8,0},{9,1... | collective-permute-start | bytes 1327112 | tf_op jit(solution)/shard_map/ppermute | solution.py:28
  98.5 2.3 %collective-permute-start.34 = (bf16[3,9,16,512]{3,2,1,0:T(8,128)(2,1)S(1)}, bf16[3,9,16,512]{3,2,1,0:T(8,128)(2,1)S(1)}, u32[]{:S(2)}, u32[]{:S(2)}) collective-permute-start(bf16[3,9,16,512]{3,2,1,0:T(8,128)(2,1)S(1)} %join_parts.5.refs_0_.refs_4_.refs_12_), channel_id=1, source_target_pairs={{0,8},{1,9},{2,10},{3,11},{4,12},{5,13},{6,14},{7,15},{8,16},{9,17... | collective-permute-start | bytes 1327112 | tf_op jit(solution)/shard_map/ppermute | solution.py:28
  100.8 4.9 %collective-permute-start.41 = (bf16[4,128,1024]{2,1,0:T(8,128)(2,1)S(1)}, bf16[4,128,1024]{2,1,0:T(8,128)(2,1)S(1)}, u32[]{:S(2)}, u32[]{:S(2)}) collective-permute-start(bf16[4,128,1024]{2,1,0:T(8,128)(2,1)S(1)} %pad_maximum_fusion.inverse), channel_id=1, source_target_pairs={{0,32},{32,0},{64,96},{96,64},{128,160},{160,128},{192,224},{224,1... | collective-permute-start | bytes 3145736 | tf_op jit(solution)/shard_map/ppermute | solution.py:46
  107.0 8.8 %collective-permute-done.35.refs_2_.refs_6_.refs_14_ = bf16[3,9,16,512]{3,2,1,0:T(8,128)(2,1)S(1)} collective-permute-done((bf16[3,9,16,512]{3,2,1,0:T(8,128)(2,1)S(1)}, bf16[3,9,16,512]{3,2,1,0:T(8,128)(2,1)S(1)}, u32[]{:S(2)}, u32[]{:S(2)}) %collective-permute-start.35) | collective-permute-done | bytes 442400 | tf_op jit(solution)/shard_map/ppermute | solution.py:28
  118.5 2.8 %masked_product.11 = (f32[512,128]{1,0:T(8,128)S(1)}, bf16[512,128]{1,0:T(8,128)(2,1)S(1)}, bf16[512,128]{1,0:T(8,128)(2,1)S(1)}, bf16[512,128]{1,0:T(8,128)(2,1)S(1)}) custom-call(s32[4]{0:T(128)S(1)} %pad_add_fusion.pos, bf16[4,512,1024]{2,1,0:T(8,128)(2,1)S(1)} %get-tuple-element.106.adjoint, bf16[1,9,16,512]{3,2,1,0:T(8,128)(2,1)S(1)} %get-tuple-element.125.refs_0_, ...), custom_call_target="tpu_custom_call" | custom-call | tf_op jit(solution)/shard_map/masked_product/pallas_call | solution.py:241
  121.5 2.2 %collective-permute-start.40 = (bf16[4,512,128]{2,1,0:T(8,128)(2,1)S(1)}, bf16[4,512,128]{2,1,0:T(8,128)(2,1)S(1)}, u32[]{:S(2)}, u32[]{:S(2)}) collective-permute-start(bf16[4,512,128]{2,1,0:T(8,128)(2,1)S(1)} %pad_maximum_fusion.1.mine), channel_id=1, source_target_pairs={{0,32},{32,0},{64,96},{96,64},{128,160},{160,128},{192,224},{224,1... | collective-permute-start | bytes 1572872 | tf_op jit(solution)/shard_map/ppermute | solution.py:46
  123.8 2.1 %collective-permute-start.38 = (bf16[512,128]{1,0:T(8,128)(2,1)S(1)}, bf16[512,128]{1,0:T(8,128)(2,1)S(1)}, u32[]{:S(2)}, u32[]{:S(2)}) collective-permute-start(bf16[512,128]{1,0:T(8,128)(2,1)S(1)} %get-tuple-element.136), channel_id=1, source_target_pairs={{0,128},{32,160},{64,192},{96,224},{128,0},{160,32},{192,64},{224,... | collective-permute-start | bytes 393224 | tf_op jit(solution)/shard_map/ppermute | solution.py:38
  (95 shorter events, 45.2 us)
Async XLA Ops:
  8.1 8.7 %collective-permute-start.5 = (bf16[128,1024]{1,0:T(8,128)(2,1)}, bf16[128,1024]{1,0:T(8,128)(2,1)S(1)}, u32[]{:S(2)}, u32[]{:S(2)}) collective-permute-start(bf16[128,1024]{1,0:T(8,128)(2,1)} %param.11), channel_id=1, source_target_pairs={{0,64},{32,96},{64,128},{96,160},{128,192},{160,224},{192,0},{224,... | collective-permute-start | bytes 786440 | tf_op jit(solution)/shard_map/ppermute | solution.py:38
  8.6 10.0 %collective-permute-start.4 = (bf16[128,512]{1,0:T(8,128)(2,1)S(1)}, bf16[128,512]{1,0:T(8,128)(2,1)S(1)}, u32[]{:S(2)}, u32[]{:S(2)}) collective-permute-start(bf16[128,512]{1,0:T(8,128)(2,1)S(1)} %get-tuple-element.76.two), channel_id=1, source_target_pairs={{0,16},{1,17},{2,18},{3,19},{4,20},{5,21},{6,22},{7,23},{8,24},{9,... | collective-permute-start | bytes 393224 | tf_op jit(solution)/shard_map/ppermute | solution.py:28
  11.0 9.3 %collective-permute-start.3 = (bf16[128,512]{1,0:T(8,128)(2,1)S(1)}, bf16[128,512]{1,0:T(8,128)(2,1)S(1)}, u32[]{:S(2)}, u32[]{:S(2)}) collective-permute-start(bf16[128,512]{1,0:T(8,128)(2,1)S(1)} %get-tuple-element.76.two), channel_id=1, source_target_pairs={{0,24},{1,25},{2,26},{3,27},{4,28},{5,29},{6,30},{7,31},{8,0},{9,1... | collective-permute-start | bytes 393224 | tf_op jit(solution)/shard_map/ppermute | solution.py:28
  21.7 18.1 %collective-permute-start.11 = (bf16[41,16,512]{2,1,0:T(8,128)(2,1)S(1)}, bf16[41,16,512]{2,1,0:T(8,128)(2,1)S(1)}, u32[]{:S(2)}, u32[]{:S(2)}) collective-permute-start(bf16[41,16,512]{2,1,0:T(8,128)(2,1)S(1)} %get-tuple-element.87.refs_0_), channel_id=1, source_target_pairs={{0,7},{1,0},{2,1},{3,2},{4,3},{5,4},{6,5},{7,6},{8,15},{9,8},{10,9... | collective-permute-start | bytes 2015240 | tf_op jit(solution)/shard_map/ppermute | solution.py:33
  27.4 15.5 %collective-permute-start.10 = (bf16[41,16,512]{2,1,0:T(8,128)(2,1)S(1)}, bf16[41,16,512]{2,1,0:T(8,128)(2,1)S(1)}, u32[]{:S(2)}, u32[]{:S(2)}) collective-permute-start(bf16[41,16,512]{2,1,0:T(8,128)(2,1)S(1)} %get-tuple-element.87.refs_0_), channel_id=1, source_target_pairs={{0,1},{1,2},{2,3},{3,4},{4,5},{5,6},{6,7},{7,0},{8,9},{9,10},{10,1... | collective-permute-start | bytes 2015240 | tf_op jit(solution)/shard_map/ppermute | solution.py:33
  42.9 16.5 %collective-permute-start.16 = (bf16[41,16,512]{2,1,0:T(8,128)(2,1)S(1)}, bf16[41,16,512]{2,1,0:T(8,128)(2,1)S(1)}, u32[]{:S(2)}, u32[]{:S(2)}) collective-permute-start(bf16[41,16,512]{2,1,0:T(8,128)(2,1)S(1)} %collective-permute-done.10.refs_0_.refs_1_), channel_id=1, source_target_pairs={{0,1},{1,2},{2,3},{3,4},{4,5},{5,6},{6,7},{7,0},{8,9},{9,10},{10,1... | collective-permute-start | bytes 2015240 | tf_op jit(solution)/shard_map/ppermute | solution.py:33
  42.9 16.5 %collective-permute-start.17 = (bf16[41,16,512]{2,1,0:T(8,128)(2,1)S(1)}, bf16[41,16,512]{2,1,0:T(8,128)(2,1)S(1)}, u32[]{:S(2)}, u32[]{:S(2)}) collective-permute-start(bf16[41,16,512]{2,1,0:T(8,128)(2,1)S(1)} %collective-permute-done.11.refs_1_.refs_2_), channel_id=1, source_target_pairs={{0,7},{1,0},{2,1},{3,2},{4,3},{5,4},{6,5},{7,6},{8,15},{9,8},{10,9... | collective-permute-start | bytes 2015240 | tf_op jit(solution)/shard_map/ppermute | solution.py:33
  45.6 9.1 %collective-permute-start.20 = (bf16[2,9,16,512]{3,2,1,0:T(8,128)(2,1)S(1)}, bf16[2,9,16,512]{3,2,1,0:T(8,128)(2,1)S(1)}, u32[]{:S(2)}, u32[]{:S(2)}) collective-permute-start(bf16[2,9,16,512]{3,2,1,0:T(8,128)(2,1)S(1)} %join_parts.3.refs_0_.refs_4_), channel_id=1, source_target_pairs={{0,16},{1,17},{2,18},{3,19},{4,20},{5,21},{6,22},{7,23},{8,24},{9,... | collective-permute-start | bytes 884744 | tf_op jit(solution)/shard_map/ppermute | solution.py:28
  48.3 11.1 %collective-permute-start.19 = (bf16[2,9,16,512]{3,2,1,0:T(8,128)(2,1)S(1)}, bf16[2,9,16,512]{3,2,1,0:T(8,128)(2,1)S(1)}, u32[]{:S(2)}, u32[]{:S(2)}) collective-permute-start(bf16[2,9,16,512]{3,2,1,0:T(8,128)(2,1)S(1)} %join_parts.3.refs_0_.refs_4_), channel_id=1, source_target_pairs={{0,24},{1,25},{2,26},{3,27},{4,28},{5,29},{6,30},{7,31},{8,0},{9,1... | collective-permute-start | bytes 884744 | tf_op jit(solution)/shard_map/ppermute | solution.py:28
  49.1 10.3 %collective-permute-start.18 = (bf16[2,9,16,512]{3,2,1,0:T(8,128)(2,1)S(1)}, bf16[2,9,16,512]{3,2,1,0:T(8,128)(2,1)S(1)}, u32[]{:S(2)}, u32[]{:S(2)}) collective-permute-start(bf16[2,9,16,512]{3,2,1,0:T(8,128)(2,1)S(1)} %join_parts.3.refs_0_.refs_4_), channel_id=1, source_target_pairs={{0,8},{1,9},{2,10},{3,11},{4,12},{5,13},{6,14},{7,15},{8,16},{9,17... | collective-permute-start | bytes 884744 | tf_op jit(solution)/shard_map/ppermute | solution.py:28
  59.4 19.3 %collective-permute-start.21 = (bf16[41,16,512]{2,1,0:T(8,128)(2,1)S(1)}, bf16[41,16,512]{2,1,0:T(8,128)(2,1)S(1)}, u32[]{:S(2)}, u32[]{:S(2)}) collective-permute-start(bf16[41,16,512]{2,1,0:T(8,128)(2,1)S(1)} %collective-permute-done.16.refs_3_.refs_0_), channel_id=1, source_target_pairs={{0,1},{1,2},{2,3},{3,4},{4,5},{5,6},{6,7},{7,0},{8,9},{9,10},{10,1... | collective-permute-start | bytes 2015240 | tf_op jit(solution)/shard_map/ppermute | solution.py:33
  59.5 19.2 %collective-permute-start.22 = (bf16[41,16,512]{2,1,0:T(8,128)(2,1)S(1)}, bf16[41,16,512]{2,1,0:T(8,128)(2,1)S(1)}, u32[]{:S(2)}, u32[]{:S(2)}) collective-permute-start(bf16[41,16,512]{2,1,0:T(8,128)(2,1)S(1)} %collective-permute-done.17.refs_4_.refs_1_), channel_id=1, source_target_pairs={{0,7},{1,0},{2,1},{3,2},{4,3},{5,4},{6,5},{7,6},{8,15},{9,8},{10,9... | collective-permute-start | bytes 2015240 | tf_op jit(solution)/shard_map/ppermute | solution.py:33
  66.1 12.3 %collective-permute-start.24 = (bf16[2,9,16,512]{3,2,1,0:T(8,128)(2,1)S(1)}, bf16[2,9,16,512]{3,2,1,0:T(8,128)(2,1)S(1)}, u32[]{:S(2)}, u32[]{:S(2)}) collective-permute-start(bf16[2,9,16,512]{3,2,1,0:T(8,128)(2,1)S(1)} %join_parts.4.refs_4_.refs_8_), channel_id=1, source_target_pairs={{0,24},{1,25},{2,26},{3,27},{4,28},{5,29},{6,30},{7,31},{8,0},{9,1... | collective-permute-start | bytes 884744 | tf_op jit(solution)/shard_map/ppermute | solution.py:28
  67.2 11.5 %collective-permute-start.23 = (bf16[2,9,16,512]{3,2,1,0:T(8,128)(2,1)S(1)}, bf16[2,9,16,512]{3,2,1,0:T(8,128)(2,1)S(1)}, u32[]{:S(2)}, u32[]{:S(2)}) collective-permute-start(bf16[2,9,16,512]{3,2,1,0:T(8,128)(2,1)S(1)} %join_parts.4.refs_4_.refs_8_), channel_id=1, source_target_pairs={{0,8},{1,9},{2,10},{3,11},{4,12},{5,13},{6,14},{7,15},{8,16},{9,17... | collective-permute-start | bytes 884744 | tf_op jit(solution)/shard_map/ppermute | solution.py:28
  78.7 8.7 %collective-permute-start.27 = (bf16[25,16,512]{2,1,0:T(8,128)(2,1)S(1)}, bf16[25,16,512]{2,1,0:T(8,128)(2,1)S(1)}, u32[]{:S(2)}, u32[]{:S(2)}) collective-permute-start(bf16[25,16,512]{2,1,0:T(8,128)(2,1)S(1)} %slice.15), channel_id=1, source_target_pairs={{0,7},{1,0},{2,1},{3,2},{4,3},{5,4},{6,5},{7,6},{8,15},{9,8},{10,9... | collective-permute-start | bytes 1228808 | tf_op jit(solution)/shard_map/ppermute | solution.py:33
  88.6 9.9 %collective-permute-start.28 = (f32[512,128]{1,0:T(8,128)S(1)}, f32[512,128]{1,0:T(8,128)S(1)}, u32[]{:S(2)}, u32[]{:S(2)}) collective-permute-start(f32[512,128]{1,0:T(8,128)S(1)} %get-tuple-element.119), channel_id=1, source_target_pairs={{0,64},{32,96},{64,128},{96,160},{128,192},{160,224},{192,0},{224,... | collective-permute-start | bytes 786440 | tf_op jit(solution)/shard_map/ppermute | solution.py:38
  88.7 12.1 %collective-permute-start.29 = (f32[512,128]{1,0:T(8,128)S(1)}, f32[512,128]{1,0:T(8,128)S(1)}, u32[]{:S(2)}, u32[]{:S(2)}) collective-permute-start(f32[512,128]{1,0:T(8,128)S(1)} %get-tuple-element.120), channel_id=1, source_target_pairs={{0,128},{32,160},{64,192},{96,224},{128,0},{160,32},{192,64},{224,... | collective-permute-start | bytes 786440 | tf_op jit(solution)/shard_map/ppermute | solution.py:38
  91.6 14.1 %collective-permute-start.30 = (f32[512,128]{1,0:T(8,128)S(1)}, f32[512,128]{1,0:T(8,128)S(1)}, u32[]{:S(2)}, u32[]{:S(2)}) collective-permute-start(f32[512,128]{1,0:T(8,128)S(1)} %get-tuple-element.121), channel_id=1, source_target_pairs={{0,192},{32,224},{64,0},{96,32},{128,64},{160,96},{192,128},{224,1... | collective-permute-start | bytes 786440 | tf_op jit(solution)/shard_map/ppermute | solution.py:38
  91.8 15.2 %collective-permute-start.36 = (bf16[3,9,16,512]{3,2,1,0:T(8,128)(2,1)S(1)}, bf16[3,9,16,512]{3,2,1,0:T(8,128)(2,1)S(1)}, u32[]{:S(2)}, u32[]{:S(2)}) collective-permute-start(bf16[3,9,16,512]{3,2,1,0:T(8,128)(2,1)S(1)} %join_parts.5.refs_0_.refs_4_.refs_12_), channel_id=1, source_target_pairs={{0,16},{1,17},{2,18},{3,19},{4,20},{5,21},{6,22},{7,23},{8,24},{9,... | collective-permute-start | bytes 1327112 | tf_op jit(solution)/shard_map/ppermute | solution.py:28
  96.4 19.4 %collective-permute-start.35 = (bf16[3,9,16,512]{3,2,1,0:T(8,128)(2,1)S(1)}, bf16[3,9,16,512]{3,2,1,0:T(8,128)(2,1)S(1)}, u32[]{:S(2)}, u32[]{:S(2)}) collective-permute-start(bf16[3,9,16,512]{3,2,1,0:T(8,128)(2,1)S(1)} %join_parts.5.refs_0_.refs_4_.refs_12_), channel_id=1, source_target_pairs={{0,24},{1,25},{2,26},{3,27},{4,28},{5,29},{6,30},{7,31},{8,0},{9,1... | collective-permute-start | bytes 1327112 | tf_op jit(solution)/shard_map/ppermute | solution.py:28
  98.5 18.6 %collective-permute-start.34 = (bf16[3,9,16,512]{3,2,1,0:T(8,128)(2,1)S(1)}, bf16[3,9,16,512]{3,2,1,0:T(8,128)(2,1)S(1)}, u32[]{:S(2)}, u32[]{:S(2)}) collective-permute-start(bf16[3,9,16,512]{3,2,1,0:T(8,128)(2,1)S(1)} %join_parts.5.refs_0_.refs_4_.refs_12_), channel_id=1, source_target_pairs={{0,8},{1,9},{2,10},{3,11},{4,12},{5,13},{6,14},{7,15},{8,16},{9,17... | collective-permute-start | bytes 1327112 | tf_op jit(solution)/shard_map/ppermute | solution.py:28
  100.8 25.7 %collective-permute-start.41 = (bf16[4,128,1024]{2,1,0:T(8,128)(2,1)S(1)}, bf16[4,128,1024]{2,1,0:T(8,128)(2,1)S(1)}, u32[]{:S(2)}, u32[]{:S(2)}) collective-permute-start(bf16[4,128,1024]{2,1,0:T(8,128)(2,1)S(1)} %pad_maximum_fusion.inverse), channel_id=1, source_target_pairs={{0,32},{32,0},{64,96},{96,64},{128,160},{160,128},{192,224},{224,1... | collective-permute-start | bytes 3145736 | tf_op jit(solution)/shard_map/ppermute | solution.py:46
  106.5 14.8 %collective-permute-start.33 = (bf16[512,128]{1,0:T(8,128)(2,1)S(1)}, bf16[512,128]{1,0:T(8,128)(2,1)S(1)}, u32[]{:S(2)}, u32[]{:S(2)}) collective-permute-start(bf16[512,128]{1,0:T(8,128)(2,1)S(1)} %get-tuple-element.144), channel_id=1, source_target_pairs={{0,192},{32,224},{64,0},{96,32},{128,64},{160,96},{192,128},{224,1... | collective-permute-start | bytes 393224 | tf_op jit(solution)/shard_map/ppermute | solution.py:38
  107.0 14.4 %collective-permute-start.32 = (bf16[512,128]{1,0:T(8,128)(2,1)S(1)}, bf16[512,128]{1,0:T(8,128)(2,1)S(1)}, u32[]{:S(2)}, u32[]{:S(2)}) collective-permute-start(bf16[512,128]{1,0:T(8,128)(2,1)S(1)} %get-tuple-element.144), channel_id=1, source_target_pairs={{0,128},{32,160},{64,192},{96,224},{128,0},{160,32},{192,64},{224,... | collective-permute-start | bytes 393224 | tf_op jit(solution)/shard_map/ppermute | solution.py:38
  (23 other events, 229.1 us)

commit v11 on v10

--- a/solution.py
+++ b/solution.py
@@ -351,25 +351,30 @@
     sums_one = product(
         pos, for_one, near + middle,
         [(1 + c, [(NX * c + i, 0, 2) for i in range(NX)]) for c in range(2)])
-    far_low, far_high, sums, sums_one = together(
-        z_shift(down3[:TWO // 2], 1), z_shift(up3[TWO // 2:], -1), sums, sums_one)
+    third = join(down3, up3)
+    third = [third, x_shift(third, 1), x_shift(third, -1)]
+    far_low, far_high, sums, sums_one, *third = together(
+        z_shift(down3[:TWO // 2], 1), z_shift(up3[TWO // 2:], -1), sums, sums_one, *third)
 
     mine, *sent = product(
         pos, for_two, [far_low, far_high], [(7, [(0, 0, TWO // 2), (1, 0, TWO // 2)])], sums, F32)
-    sent = [y_shift(part, d + 1) for d, part in enumerate(sent)]
-    third = x_all(join(down3, up3, far_high))
-    r1, r2, r3 = together(*sent)
+    last = far_high[None, TWO // 2:]
+    last = [last, x_shift(last, 1), x_shift(last, -1)]
+    third.append(x_shift(join(down3, up3, far_high), 2))
+    r1, r2, r3 = together(*[y_shift(part, d + 1) for d, part in enumerate(sent)])
     second_grad = incoming + ((mine + r1) + (r2 + r3))
     rounded = second_grad.astype(BF16)
 
     sums_one = product(pos, for_one, third, [(3, [(i, 0, 2) for i in range(NX)])], sums_one)
-    sums_one = product(
-        pos, for_one, first_x + third,
-        [(0, [(NX * s + i, 2 * s, 1) for i in range(NX) for s in range(2)])], sums_one, BF16)
+    parts = []
+    for i in range(NX):
+        parts += [(i, 0, 1), (NX + 1 + i, 0, 1) if i < 3 else (NX, 2, 1)]
+    sums_one = product(pos, for_one, first_x + third[3:] + last, [(0, parts)], sums_one, BF16)
     where = tuple(
-        ((i, 0),) + tuple((NX * (1 + j // 2) + i, j % 2) for j in range(6)) + ((3 * NX + i, 2),)
+        ((i, 0),) + tuple((NX * (1 + j // 2) + i, j % 2) for j in range(6))
+        + ((4 * NX + i, 0) if i < 3 else (4 * NX - 1, 2),)
         for i in range(NX))
-    factors = factor(pos, inverse, inverse_other, first_x + near + middle + third, where)
+    factors = factor(pos, inverse, inverse_other, first_x + near + middle + third + last, where)
     s1, s2, s3, mine, *sent = together(*[y_shift(rounded, d) for d in range(1, NY)], *sums_one)
     rounded = jnp.stack([rounded, s1, s2, s3])
     rounded_other = core_swap(rounded)

time: 134 us -> 136 us (1.015)
    ppermute x12, waiting for transfers between devices: 7.73 us -> 10.5 us  [y_shift(): return lax.ppermute(value, 'row', pairs)]
    ppermute x8, waiting for transfers between devices: 6.28 us -> 4.21 us  [z_shift(): return lax.ppermute(value, 'col', pairs)]
    ppermute x12, starting transfers between devices: 10.7 us -> 12.3 us  [y_shift(): return lax.ppermute(value, 'row', pairs)]
    ppermute x15 -> x17, waiting for transfers between devices: 24.7 us -> 25.3 us  [x_shift(): return lax.ppermute(value, 'col', pairs)]
    ppermute x15 -> x17, starting transfers between devices: 27.2 us -> 27.7 us  [x_shift(): return lax.ppermute(value, 'col', pairs)]
  transfers between devices with their start and end apart: 42 -> 44, of which waited for: 15 -> 15; matrix products, arithmetic and copies ran while one was open for 2% -> 2% of each run, Pallas kernels for 15% -> 15%
where the time goes in v11:
time: 136 us
  starting transfers between devices  67.4 us (50%)
  waiting for transfers between devices  40.8 us (30%)
  Pallas kernels  22.2 us (16%)
  other arithmetic  2.78 us (2%)
  local copies, waits for them, and re-layouts  1.92 us (1%)
    ppermute x17, starting transfers between devices, x_shift(): return lax.ppermute(value, 'col', pairs)  27.7 us
    ppermute x17, waiting for transfers between devices, x_shift(): return lax.ppermute(value, 'col', pairs)  25.3 us
    ppermute x8, starting transfers between devices, z_shift(): return lax.ppermute(value, 'col', pairs)  12.7 us
    ppermute x12, starting transfers between devices, y_shift(): return lax.ppermute(value, 'row', pairs)  12.3 us
    pallas_call x6, Pallas kernels, product(): pl.pallas_call(kernel, out_shape=(column,) + (jax.ShapeDtypeStruct((512,...  12.3 us
    ppermute x12, waiting for transfers between devices, y_shift(): return lax.ppermute(value, 'row', pairs)  10.5 us
    ppermute x4, starting transfers between devices, core_swap(): return lax.ppermute(value, 'row', [(r, r ^ 1) for r in range(2 * NY)])  9.61 us
    ppermute x3, starting transfers between devices, y_first(): return lax.ppermute(value, 'row', [(k, y * 2 + k) for k in range(2)])  5.01 us
  transfers between devices with their start and end apart: 44, of which 15 were waited for; matrix products, arithmetic and copies ran while one was open for 2% of the time, Pallas kernels for 15%

profile of v11, /device:TPU:1, one launch (start us, length us, event | category | flops | bytes accessed | tf_op | source)
XLA Modules:
  0.0 136.1 jit_solution(3592965995202588313)
XLA Ops:
  0.6 3.3 %collective-permute-start.1 = (bf16[2048,512]{1,0:T(8,128)(2,1)}, bf16[2048,512]{1,0:T(8,128)(2,1)}, u32[]{:S(2)}, u32[]{:S(2)}) collective-permute-start(bf16[2048,512]{1,0:T(8,128)(2,1)} %mine.1), channel_id=1, source_target_pairs={{0,32},{32,0},{64,96},{96,64},{128,160},{160,128},{192,224},{224,1... | collective-permute-start | bytes 6291464 | tf_op jit(solution)/shard_map/ppermute | solution.py:46
  8.6 2.4 %collective-permute-start.4 = (bf16[128,512]{1,0:T(8,128)(2,1)S(1)}, bf16[128,512]{1,0:T(8,128)(2,1)S(1)}, u32[]{:S(2)}, u32[]{:S(2)}) collective-permute-start(bf16[128,512]{1,0:T(8,128)(2,1)S(1)} %get-tuple-element.79.two), channel_id=1, source_target_pairs={{0,16},{1,17},{2,18},{3,19},{4,20},{5,21},{6,22},{7,23},{8,24},{9,... | collective-permute-start | bytes 393224 | tf_op jit(solution)/shard_map/ppermute | solution.py:28
  21.7 5.7 %collective-permute-start.11 = (bf16[41,16,512]{2,1,0:T(8,128)(2,1)S(1)}, bf16[41,16,512]{2,1,0:T(8,128)(2,1)S(1)}, u32[]{:S(2)}, u32[]{:S(2)}) collective-permute-start(bf16[41,16,512]{2,1,0:T(8,128)(2,1)S(1)} %get-tuple-element.90.refs_0_), channel_id=1, source_target_pairs={{0,7},{1,0},{2,1},{3,2},{4,3},{5,4},{6,5},{7,6},{8,15},{9,8},{10,9... | collective-permute-start | bytes 2015240 | tf_op jit(solution)/shard_map/ppermute | solution.py:33
  28.9 2.7 %collective-permute-start.15 = (bf16[1,9,16,512]{3,2,1,0:T(8,128)(2,1)S(1)}, bf16[1,9,16,512]{3,2,1,0:T(8,128)(2,1)S(1)}, u32[]{:S(2)}, u32[]{:S(2)}) collective-permute-start(bf16[1,9,16,512]{3,2,1,0:T(8,128)(2,1)S(1)} %get-tuple-element.128.refs_0_), channel_id=1, source_target_pairs={{0,16},{1,17},{2,18},{3,19},{4,20},{5,21},{6,22},{7,23},{8,24},{9,... | collective-permute-start | bytes 442376 | tf_op jit(solution)/shard_map/ppermute | solution.py:28
  36.7 3.2 %collective-permute-done.13.refs_1_ = bf16[1,9,16,512]{3,2,1,0:T(8,128)(2,1)S(1)} collective-permute-done((bf16[1,9,16,512]{3,2,1,0:T(8,128)(2,1)S(1)}, bf16[1,9,16,512]{3,2,1,0:T(8,128)(2,1)S(1)}, u32[]{:S(2)}, u32[]{:S(2)}) %collective-permute-start.13) | collective-permute-done | bytes 147488 | tf_op jit(solution)/shard_map/ppermute | solution.py:28
  39.8 3.0 %collective-permute-done.10.refs_0_.refs_1_ = bf16[41,16,512]{2,1,0:T(8,128)(2,1)S(1)} collective-permute-done((bf16[41,16,512]{2,1,0:T(8,128)(2,1)S(1)}, bf16[41,16,512]{2,1,0:T(8,128)(2,1)S(1)}, u32[]{:S(2)}, u32[]{:S(2)}) %collective-permute-start.10) | collective-permute-done | bytes 671776 | tf_op jit(solution)/shard_map/ppermute | solution.py:33
  42.9 2.7 %collective-permute-start.17 = (bf16[41,16,512]{2,1,0:T(8,128)(2,1)S(1)}, bf16[41,16,512]{2,1,0:T(8,128)(2,1)S(1)}, u32[]{:S(2)}, u32[]{:S(2)}) collective-permute-start(bf16[41,16,512]{2,1,0:T(8,128)(2,1)S(1)} %collective-permute-done.11.refs_1_.refs_2_), channel_id=1, source_target_pairs={{0,7},{1,0},{2,1},{3,2},{4,3},{5,4},{6,5},{7,6},{8,15},{9,8},{10,9... | collective-permute-start | bytes 2015240 | tf_op jit(solution)/shard_map/ppermute | solution.py:33
  45.6 2.7 %collective-permute-start.20 = (bf16[2,9,16,512]{3,2,1,0:T(8,128)(2,1)S(1)}, bf16[2,9,16,512]{3,2,1,0:T(8,128)(2,1)S(1)}, u32[]{:S(2)}, u32[]{:S(2)}) collective-permute-start(bf16[2,9,16,512]{3,2,1,0:T(8,128)(2,1)S(1)} %join_parts.4.refs_0_.refs_4_), channel_id=1, source_target_pairs={{0,16},{1,17},{2,18},{3,19},{4,20},{5,21},{6,22},{7,23},{8,24},{9,... | collective-permute-start | bytes 884744 | tf_op jit(solution)/shard_map/ppermute | solution.py:28
  49.8 4.9 %prepare_adjoint.1 = (bf16[8,512,512]{2,1,0:T(8,128)(2,1)S(1)}, bf16[4,512,1024]{2,1,0:T(8,128)(2,1)S(1)}) custom-call(s32[4]{0:T(128)S(1)} %pad_add_fusion.pos, s32[64,64]{1,0:T(8,128)S(1)} %copy-done.3, bf16[2048,512]{1,0:T(8,128)(2,1)S(1)} %copy-done, bf16[2048,512]{1,0:T(8,128)(2,1)} %collective-permute-done.1.other), custom_call_target="tpu_custom_call" | custom-call | tf_op jit(solution)/shard_map/prepare_adjoint/pallas_call | solution.py:184
  54.7 4.7 %collective-permute-done.19.refs_2_.refs_6_ = bf16[2,9,16,512]{3,2,1,0:T(8,128)(2,1)S(1)} collective-permute-done((bf16[2,9,16,512]{3,2,1,0:T(8,128)(2,1)S(1)}, bf16[2,9,16,512]{3,2,1,0:T(8,128)(2,1)S(1)}, u32[]{:S(2)}, u32[]{:S(2)}) %collective-permute-start.19) | collective-permute-done | bytes 294944 | tf_op jit(solution)/shard_map/ppermute | solution.py:28
  59.5 2.7 %collective-permute-start.22 = (bf16[41,16,512]{2,1,0:T(8,128)(2,1)S(1)}, bf16[41,16,512]{2,1,0:T(8,128)(2,1)S(1)}, u32[]{:S(2)}, u32[]{:S(2)}) collective-permute-start(bf16[41,16,512]{2,1,0:T(8,128)(2,1)S(1)} %collective-permute-done.17.refs_4_.refs_1_), channel_id=1, source_target_pairs={{0,7},{1,0},{2,1},{3,2},{4,3},{5,4},{6,5},{7,6},{8,15},{9,8},{10,9... | collective-permute-start | bytes 2015240 | tf_op jit(solution)/shard_map/ppermute | solution.py:33
  62.2 3.9 %collective-permute-start.25 = (bf16[2,9,16,512]{3,2,1,0:T(8,128)(2,1)S(1)}, bf16[2,9,16,512]{3,2,1,0:T(8,128)(2,1)S(1)}, u32[]{:S(2)}, u32[]{:S(2)}) collective-permute-start(bf16[2,9,16,512]{3,2,1,0:T(8,128)(2,1)S(1)} %join_parts.5.refs_4_.refs_8_), channel_id=1, source_target_pairs={{0,16},{1,17},{2,18},{3,19},{4,20},{5,21},{6,22},{7,23},{8,24},{9,... | collective-permute-start | bytes 884744 | tf_op jit(solution)/shard_map/ppermute | solution.py:28
  67.6 3.0 %masked_product.6.refs_2_ = f32[512,512]{1,0:T(8,128)S(1)} custom-call(s32[4]{0:T(128)S(1)} %pad_add_fusion.pos, bf16[8,512,512]{2,1,0:T(8,128)(2,1)S(1)} %get-tuple-element.100.adjoint, bf16[41,16,512]{2,1,0:T(8,128)(2,1)S(1)} %get-tuple-element.90.refs_0_, bf16[41,16,512]{2,1,0:T(8,128)(2,1)S(1)} %collective-permute-done.10.refs_0_.refs_1_, ...), custom_call_target="tpu_custom_call" | custom-call | tf_op jit(solution)/shard_map/masked_product/pallas_call | solution.py:241
  70.6 7.8 %collective-permute-done.24.refs_6_.refs_10_ = bf16[2,9,16,512]{3,2,1,0:T(8,128)(2,1)S(1)} collective-permute-done((bf16[2,9,16,512]{3,2,1,0:T(8,128)(2,1)S(1)}, bf16[2,9,16,512]{3,2,1,0:T(8,128)(2,1)S(1)}, u32[]{:S(2)}, u32[]{:S(2)}) %collective-permute-start.24) | collective-permute-done | bytes 294944 | tf_op jit(solution)/shard_map/ppermute | solution.py:28
  78.8 3.2 %collective-permute-start.29 = (bf16[2,9,16,512]{3,2,1,0:T(8,128)(2,1)S(1)}, bf16[2,9,16,512]{3,2,1,0:T(8,128)(2,1)S(1)}, u32[]{:S(2)}, u32[]{:S(2)}) collective-permute-start(bf16[2,9,16,512]{3,2,1,0:T(8,128)(2,1)S(1)} %join_parts.6.refs_0_.refs_12_), channel_id=1, source_target_pairs={{0,24},{1,25},{2,26},{3,27},{4,28},{5,29},{6,30},{7,31},{8,0},{9,1... | collective-permute-start | bytes 884744 | tf_op jit(solution)/shard_map/ppermute | solution.py:28
  85.2 2.2 %masked_product.8.refs_4_ = f32[512,512]{1,0:T(8,128)S(1)} custom-call(s32[4]{0:T(128)S(1)} %pad_add_fusion.pos, bf16[4,512,1024]{2,1,0:T(8,128)(2,1)S(1)} %get-tuple-element.109.adjoint, bf16[2,9,16,512]{3,2,1,0:T(8,128)(2,1)S(1)} %join_parts.4.refs_0_.refs_4_, bf16[2,9,16,512]{3,2,1,0:T(8,128)(2,1)S(1)} %collective-permute-done.18.refs_1_.refs_5_, ...), custom_call_target="tpu_custom_call" | custom-call | tf_op jit(solution)/shard_map/masked_product/pallas_call | solution.py:241
  90.2 3.2 %collective-permute-start.31 = (f32[512,128]{1,0:T(8,128)S(1)}, f32[512,128]{1,0:T(8,128)S(1)}, u32[]{:S(2)}, u32[]{:S(2)}) collective-permute-start(f32[512,128]{1,0:T(8,128)S(1)} %get-tuple-element.123), channel_id=1, source_target_pairs={{0,128},{32,160},{64,192},{96,224},{128,0},{160,32},{192,64},{224,... | collective-permute-start | bytes 786440 | tf_op jit(solution)/shard_map/ppermute | solution.py:38
  93.4 5.2 %collective-permute-start.43 = (bf16[4,128,1024]{2,1,0:T(8,128)(2,1)S(1)}, bf16[4,128,1024]{2,1,0:T(8,128)(2,1)S(1)}, u32[]{:S(2)}, u32[]{:S(2)}) collective-permute-start(bf16[4,128,1024]{2,1,0:T(8,128)(2,1)S(1)} %pad_maximum_fusion.inverse), channel_id=1, source_target_pairs={{0,32},{32,0},{64,96},{96,64},{128,160},{160,128},{192,224},{224,1... | collective-permute-start | bytes 3145736 | tf_op jit(solution)/shard_map/ppermute | solution.py:46
  101.7 3.2 %collective-permute-start.37 = (bf16[1,9,16,512]{3,2,1,0:T(8,128)(2,1)S(1)}, bf16[1,9,16,512]{3,2,1,0:T(8,128)(2,1)S(1)}, u32[]{:S(2)}, u32[]{:S(2)}) collective-permute-start(bf16[1,9,16,512]{3,2,1,0:T(8,128)(2,1)S(1)} %slice_bitcast_fusion.refs_5_.refs_16_), channel_id=1, source_target_pairs={{0,8},{1,9},{2,10},{3,11},{4,12},{5,13},{6,14},{7,15},{8,16},{9,17... | collective-permute-start | bytes 442376 | tf_op jit(solution)/shard_map/ppermute | solution.py:28
  106.4 9.1 %collective-permute-done.38.refs_7_.refs_18_ = bf16[1,9,16,512]{3,2,1,0:T(8,128)(2,1)S(1)} collective-permute-done((bf16[1,9,16,512]{3,2,1,0:T(8,128)(2,1)S(1)}, bf16[1,9,16,512]{3,2,1,0:T(8,128)(2,1)S(1)}, u32[]{:S(2)}, u32[]{:S(2)}) %collective-permute-start.38) | collective-permute-done | bytes 147488 | tf_op jit(solution)/shard_map/ppermute | solution.py:28
  118.7 2.8 %masked_product.11 = (f32[512,128]{1,0:T(8,128)S(1)}, bf16[512,128]{1,0:T(8,128)(2,1)S(1)}, bf16[512,128]{1,0:T(8,128)(2,1)S(1)}, bf16[512,128]{1,0:T(8,128)(2,1)S(1)}) custom-call(s32[4]{0:T(128)S(1)} %pad_add_fusion.pos, bf16[4,512,1024]{2,1,0:T(8,128)(2,1)S(1)} %get-tuple-element.109.adjoint, bf16[1,9,16,512]{3,2,1,0:T(8,128)(2,1)S(1)} %get-tuple-element.128.refs_0_, ...), custom_call_target="tpu_custom_call" | custom-call | tf_op jit(solution)/shard_map/masked_product/pallas_call | solution.py:241
  121.6 3.5 %collective-permute-done.33 = bf16[512,128]{1,0:T(8,128)(2,1)S(1)} collective-permute-done((bf16[512,128]{1,0:T(8,128)(2,1)S(1)}, bf16[512,128]{1,0:T(8,128)(2,1)S(1)}, u32[]{:S(2)}, u32[]{:S(2)}) %collective-permute-start.33) | collective-permute-done | bytes 131104 | tf_op jit(solution)/shard_map/ppermute | solution.py:38
  127.4 2.1 %collective-permute-start.41 = (bf16[512,128]{1,0:T(8,128)(2,1)S(1)}, bf16[512,128]{1,0:T(8,128)(2,1)S(1)}, u32[]{:S(2)}, u32[]{:S(2)}) collective-permute-start(bf16[512,128]{1,0:T(8,128)(2,1)S(1)} %get-tuple-element.143), channel_id=1, source_target_pairs={{0,192},{32,224},{64,0},{96,32},{128,64},{160,96},{192,128},{224,1... | collective-permute-start | bytes 393224 | tf_op jit(solution)/shard_map/ppermute | solution.py:38
  132.3 2.7 %collective-permute-done.39 = bf16[512,128]{1,0:T(8,128)(2,1)S(1)} collective-permute-done((bf16[512,128]{1,0:T(8,128)(2,1)S(1)}, bf16[512,128]{1,0:T(8,128)(2,1)S(1)}, u32[]{:S(2)}, u32[]{:S(2)}) %collective-permute-start.39) | collective-permute-done | bytes 131104 | tf_op jit(solution)/shard_map/ppermute | solution.py:38
  (101 shorter events, 45.1 us)
Async XLA Ops:
  8.6 10.0 %collective-permute-start.4 = (bf16[128,512]{1,0:T(8,128)(2,1)S(1)}, bf16[128,512]{1,0:T(8,128)(2,1)S(1)}, u32[]{:S(2)}, u32[]{:S(2)}) collective-permute-start(bf16[128,512]{1,0:T(8,128)(2,1)S(1)} %get-tuple-element.79.two), channel_id=1, source_target_pairs={{0,16},{1,17},{2,18},{3,19},{4,20},{5,21},{6,22},{7,23},{8,24},{9,... | collective-permute-start | bytes 393224 | tf_op jit(solution)/shard_map/ppermute | solution.py:28
  11.0 9.3 %collective-permute-start.3 = (bf16[128,512]{1,0:T(8,128)(2,1)S(1)}, bf16[128,512]{1,0:T(8,128)(2,1)S(1)}, u32[]{:S(2)}, u32[]{:S(2)}) collective-permute-start(bf16[128,512]{1,0:T(8,128)(2,1)S(1)} %get-tuple-element.79.two), channel_id=1, source_target_pairs={{0,24},{1,25},{2,26},{3,27},{4,28},{5,29},{6,30},{7,31},{8,0},{9,1... | collective-permute-start | bytes 393224 | tf_op jit(solution)/shard_map/ppermute | solution.py:28
  21.7 18.1 %collective-permute-start.11 = (bf16[41,16,512]{2,1,0:T(8,128)(2,1)S(1)}, bf16[41,16,512]{2,1,0:T(8,128)(2,1)S(1)}, u32[]{:S(2)}, u32[]{:S(2)}) collective-permute-start(bf16[41,16,512]{2,1,0:T(8,128)(2,1)S(1)} %get-tuple-element.90.refs_0_), channel_id=1, source_target_pairs={{0,7},{1,0},{2,1},{3,2},{4,3},{5,4},{6,5},{7,6},{8,15},{9,8},{10,9... | collective-permute-start | bytes 2015240 | tf_op jit(solution)/shard_map/ppermute | solution.py:33
  27.4 15.5 %collective-permute-start.10 = (bf16[41,16,512]{2,1,0:T(8,128)(2,1)S(1)}, bf16[41,16,512]{2,1,0:T(8,128)(2,1)S(1)}, u32[]{:S(2)}, u32[]{:S(2)}) collective-permute-start(bf16[41,16,512]{2,1,0:T(8,128)(2,1)S(1)} %get-tuple-element.90.refs_0_), channel_id=1, source_target_pairs={{0,1},{1,2},{2,3},{3,4},{4,5},{5,6},{6,7},{7,0},{8,9},{9,10},{10,1... | collective-permute-start | bytes 2015240 | tf_op jit(solution)/shard_map/ppermute | solution.py:33
  42.9 16.5 %collective-permute-start.16 = (bf16[41,16,512]{2,1,0:T(8,128)(2,1)S(1)}, bf16[41,16,512]{2,1,0:T(8,128)(2,1)S(1)}, u32[]{:S(2)}, u32[]{:S(2)}) collective-permute-start(bf16[41,16,512]{2,1,0:T(8,128)(2,1)S(1)} %collective-permute-done.10.refs_0_.refs_1_), channel_id=1, source_target_pairs={{0,1},{1,2},{2,3},{3,4},{4,5},{5,6},{6,7},{7,0},{8,9},{9,10},{10,1... | collective-permute-start | bytes 2015240 | tf_op jit(solution)/shard_map/ppermute | solution.py:33
  42.9 16.5 %collective-permute-start.17 = (bf16[41,16,512]{2,1,0:T(8,128)(2,1)S(1)}, bf16[41,16,512]{2,1,0:T(8,128)(2,1)S(1)}, u32[]{:S(2)}, u32[]{:S(2)}) collective-permute-start(bf16[41,16,512]{2,1,0:T(8,128)(2,1)S(1)} %collective-permute-done.11.refs_1_.refs_2_), channel_id=1, source_target_pairs={{0,7},{1,0},{2,1},{3,2},{4,3},{5,4},{6,5},{7,6},{8,15},{9,8},{10,9... | collective-permute-start | bytes 2015240 | tf_op jit(solution)/shard_map/ppermute | solution.py:33
  45.6 9.1 %collective-permute-start.20 = (bf16[2,9,16,512]{3,2,1,0:T(8,128)(2,1)S(1)}, bf16[2,9,16,512]{3,2,1,0:T(8,128)(2,1)S(1)}, u32[]{:S(2)}, u32[]{:S(2)}) collective-permute-start(bf16[2,9,16,512]{3,2,1,0:T(8,128)(2,1)S(1)} %join_parts.4.refs_0_.refs_4_), channel_id=1, source_target_pairs={{0,16},{1,17},{2,18},{3,19},{4,20},{5,21},{6,22},{7,23},{8,24},{9,... | collective-permute-start | bytes 884744 | tf_op jit(solution)/shard_map/ppermute | solution.py:28
  48.3 11.1 %collective-permute-start.19 = (bf16[2,9,16,512]{3,2,1,0:T(8,128)(2,1)S(1)}, bf16[2,9,16,512]{3,2,1,0:T(8,128)(2,1)S(1)}, u32[]{:S(2)}, u32[]{:S(2)}) collective-permute-start(bf16[2,9,16,512]{3,2,1,0:T(8,128)(2,1)S(1)} %join_parts.4.refs_0_.refs_4_), channel_id=1, source_target_pairs={{0,24},{1,25},{2,26},{3,27},{4,28},{5,29},{6,30},{7,31},{8,0},{9,1... | collective-permute-start | bytes 884744 | tf_op jit(solution)/shard_map/ppermute | solution.py:28
  49.1 10.3 %collective-permute-start.18 = (bf16[2,9,16,512]{3,2,1,0:T(8,128)(2,1)S(1)}, bf16[2,9,16,512]{3,2,1,0:T(8,128)(2,1)S(1)}, u32[]{:S(2)}, u32[]{:S(2)}) collective-permute-start(bf16[2,9,16,512]{3,2,1,0:T(8,128)(2,1)S(1)} %join_parts.4.refs_0_.refs_4_), channel_id=1, source_target_pairs={{0,8},{1,9},{2,10},{3,11},{4,12},{5,13},{6,14},{7,15},{8,16},{9,17... | collective-permute-start | bytes 884744 | tf_op jit(solution)/shard_map/ppermute | solution.py:28
  59.4 19.3 %collective-permute-start.21 = (bf16[41,16,512]{2,1,0:T(8,128)(2,1)S(1)}, bf16[41,16,512]{2,1,0:T(8,128)(2,1)S(1)}, u32[]{:S(2)}, u32[]{:S(2)}) collective-permute-start(bf16[41,16,512]{2,1,0:T(8,128)(2,1)S(1)} %collective-permute-done.16.refs_3_.refs_0_), channel_id=1, source_target_pairs={{0,1},{1,2},{2,3},{3,4},{4,5},{5,6},{6,7},{7,0},{8,9},{9,10},{10,1... | collective-permute-start | bytes 2015240 | tf_op jit(solution)/shard_map/ppermute | solution.py:33
  59.5 19.2 %collective-permute-start.22 = (bf16[41,16,512]{2,1,0:T(8,128)(2,1)S(1)}, bf16[41,16,512]{2,1,0:T(8,128)(2,1)S(1)}, u32[]{:S(2)}, u32[]{:S(2)}) collective-permute-start(bf16[41,16,512]{2,1,0:T(8,128)(2,1)S(1)} %collective-permute-done.17.refs_4_.refs_1_), channel_id=1, source_target_pairs={{0,7},{1,0},{2,1},{3,2},{4,3},{5,4},{6,5},{7,6},{8,15},{9,8},{10,9... | collective-permute-start | bytes 2015240 | tf_op jit(solution)/shard_map/ppermute | solution.py:33
  66.1 12.3 %collective-permute-start.24 = (bf16[2,9,16,512]{3,2,1,0:T(8,128)(2,1)S(1)}, bf16[2,9,16,512]{3,2,1,0:T(8,128)(2,1)S(1)}, u32[]{:S(2)}, u32[]{:S(2)}) collective-permute-start(bf16[2,9,16,512]{3,2,1,0:T(8,128)(2,1)S(1)} %join_parts.5.refs_4_.refs_8_), channel_id=1, source_target_pairs={{0,24},{1,25},{2,26},{3,27},{4,28},{5,29},{6,30},{7,31},{8,0},{9,1... | collective-permute-start | bytes 884744 | tf_op jit(solution)/shard_map/ppermute | solution.py:28
  67.2 11.5 %collective-permute-start.23 = (bf16[2,9,16,512]{3,2,1,0:T(8,128)(2,1)S(1)}, bf16[2,9,16,512]{3,2,1,0:T(8,128)(2,1)S(1)}, u32[]{:S(2)}, u32[]{:S(2)}) collective-permute-start(bf16[2,9,16,512]{3,2,1,0:T(8,128)(2,1)S(1)} %join_parts.5.refs_4_.refs_8_), channel_id=1, source_target_pairs={{0,8},{1,9},{2,10},{3,11},{4,12},{5,13},{6,14},{7,15},{8,16},{9,17... | collective-permute-start | bytes 884744 | tf_op jit(solution)/shard_map/ppermute | solution.py:28
  78.7 10.2 %collective-permute-start.27 = (bf16[25,16,512]{2,1,0:T(8,128)(2,1)S(1)}, bf16[25,16,512]{2,1,0:T(8,128)(2,1)S(1)}, u32[]{:S(2)}, u32[]{:S(2)}) collective-permute-start(bf16[25,16,512]{2,1,0:T(8,128)(2,1)S(1)} %slice.18), channel_id=1, source_target_pairs={{0,7},{1,0},{2,1},{3,2},{4,3},{5,4},{6,5},{7,6},{8,15},{9,8},{10,9... | collective-permute-start | bytes 1228808 | tf_op jit(solution)/shard_map/ppermute | solution.py:33
  78.8 9.8 %collective-permute-start.29 = (bf16[2,9,16,512]{3,2,1,0:T(8,128)(2,1)S(1)}, bf16[2,9,16,512]{3,2,1,0:T(8,128)(2,1)S(1)}, u32[]{:S(2)}, u32[]{:S(2)}) collective-permute-start(bf16[2,9,16,512]{3,2,1,0:T(8,128)(2,1)S(1)} %join_parts.6.refs_0_.refs_12_), channel_id=1, source_target_pairs={{0,24},{1,25},{2,26},{3,27},{4,28},{5,29},{6,30},{7,31},{8,0},{9,1... | collective-permute-start | bytes 884744 | tf_op jit(solution)/shard_map/ppermute | solution.py:28
  90.1 10.4 %collective-permute-start.30 = (f32[512,128]{1,0:T(8,128)S(1)}, f32[512,128]{1,0:T(8,128)S(1)}, u32[]{:S(2)}, u32[]{:S(2)}) collective-permute-start(f32[512,128]{1,0:T(8,128)S(1)} %get-tuple-element.122), channel_id=1, source_target_pairs={{0,64},{32,96},{64,128},{96,160},{128,192},{160,224},{192,0},{224,... | collective-permute-start | bytes 786440 | tf_op jit(solution)/shard_map/ppermute | solution.py:38
  90.2 11.5 %collective-permute-start.31 = (f32[512,128]{1,0:T(8,128)S(1)}, f32[512,128]{1,0:T(8,128)S(1)}, u32[]{:S(2)}, u32[]{:S(2)}) collective-permute-start(f32[512,128]{1,0:T(8,128)S(1)} %get-tuple-element.123), channel_id=1, source_target_pairs={{0,128},{32,160},{64,192},{96,224},{128,0},{160,32},{192,64},{224,... | collective-permute-start | bytes 786440 | tf_op jit(solution)/shard_map/ppermute | solution.py:38
  93.4 11.5 %collective-permute-start.32 = (f32[512,128]{1,0:T(8,128)S(1)}, f32[512,128]{1,0:T(8,128)S(1)}, u32[]{:S(2)}, u32[]{:S(2)}) collective-permute-start(f32[512,128]{1,0:T(8,128)S(1)} %get-tuple-element.124), channel_id=1, source_target_pairs={{0,192},{32,224},{64,0},{96,32},{128,64},{160,96},{192,128},{224,1... | collective-permute-start | bytes 786440 | tf_op jit(solution)/shard_map/ppermute | solution.py:38
  93.4 36.1 %collective-permute-start.43 = (bf16[4,128,1024]{2,1,0:T(8,128)(2,1)S(1)}, bf16[4,128,1024]{2,1,0:T(8,128)(2,1)S(1)}, u32[]{:S(2)}, u32[]{:S(2)}) collective-permute-start(bf16[4,128,1024]{2,1,0:T(8,128)(2,1)S(1)} %pad_maximum_fusion.inverse), channel_id=1, source_target_pairs={{0,32},{32,0},{64,96},{96,64},{128,160},{160,128},{192,224},{224,1... | collective-permute-start | bytes 3145736 | tf_op jit(solution)/shard_map/ppermute | solution.py:46
  98.6 18.7 %collective-permute-start.36 = (bf16[3,9,16,512]{3,2,1,0:T(8,128)(2,1)S(1)}, bf16[3,9,16,512]{3,2,1,0:T(8,128)(2,1)S(1)}, u32[]{:S(2)}, u32[]{:S(2)}) collective-permute-start(bf16[3,9,16,512]{3,2,1,0:T(8,128)(2,1)S(1)} %join_parts.7), channel_id=1, source_target_pairs={{0,16},{1,17},{2,18},{3,19},{4,20},{5,21},{6,22},{7,23},{8,24},{9,... | collective-permute-start | bytes 1327112 | tf_op jit(solution)/shard_map/ppermute | solution.py:28
  100.5 15.1 %collective-permute-start.38 = (bf16[1,9,16,512]{3,2,1,0:T(8,128)(2,1)S(1)}, bf16[1,9,16,512]{3,2,1,0:T(8,128)(2,1)S(1)}, u32[]{:S(2)}, u32[]{:S(2)}) collective-permute-start(bf16[1,9,16,512]{3,2,1,0:T(8,128)(2,1)S(1)} %slice_bitcast_fusion.refs_5_.refs_16_), channel_id=1, source_target_pairs={{0,24},{1,25},{2,26},{3,27},{4,28},{5,29},{6,30},{7,31},{8,0},{9,1... | collective-permute-start | bytes 442376 | tf_op jit(solution)/shard_map/ppermute | solution.py:28
  101.7 17.0 %collective-permute-start.37 = (bf16[1,9,16,512]{3,2,1,0:T(8,128)(2,1)S(1)}, bf16[1,9,16,512]{3,2,1,0:T(8,128)(2,1)S(1)}, u32[]{:S(2)}, u32[]{:S(2)}) collective-permute-start(bf16[1,9,16,512]{3,2,1,0:T(8,128)(2,1)S(1)} %slice_bitcast_fusion.refs_5_.refs_16_), channel_id=1, source_target_pairs={{0,8},{1,9},{2,10},{3,11},{4,12},{5,13},{6,14},{7,15},{8,16},{9,17... | collective-permute-start | bytes 442376 | tf_op jit(solution)/shard_map/ppermute | solution.py:28
  105.6 15.9 %collective-permute-start.35 = (bf16[512,128]{1,0:T(8,128)(2,1)S(1)}, bf16[512,128]{1,0:T(8,128)(2,1)S(1)}, u32[]{:S(2)}, u32[]{:S(2)}) collective-permute-start(bf16[512,128]{1,0:T(8,128)(2,1)S(1)} %get-tuple-element.150), channel_id=1, source_target_pairs={{0,192},{32,224},{64,0},{96,32},{128,64},{160,96},{192,128},{224,1... | collective-permute-start | bytes 393224 | tf_op jit(solution)/shard_map/ppermute | solution.py:38
  125.9 9.1 %collective-permute-start.39 = (bf16[512,128]{1,0:T(8,128)(2,1)S(1)}, bf16[512,128]{1,0:T(8,128)(2,1)S(1)}, u32[]{:S(2)}, u32[]{:S(2)}) collective-permute-start(bf16[512,128]{1,0:T(8,128)(2,1)S(1)} %get-tuple-element.141), channel_id=1, source_target_pairs={{0,64},{32,96},{64,128},{96,160},{128,192},{160,224},{192,0},{224,... | collective-permute-start | bytes 393224 | tf_op jit(solution)/shard_map/ppermute | solution.py:38
  (25 other events, 242.2 us)

commit v12 on v11

--- a/solution.py
+++ b/solution.py
@@ -360,8 +360,10 @@
         pos, for_two, [far_low, far_high], [(7, [(0, 0, TWO // 2), (1, 0, TWO // 2)])], sums, F32)
     last = far_high[None, TWO // 2:]
     last = [last, x_shift(last, 1), x_shift(last, -1)]
-    third.append(x_shift(join(down3, up3, far_high), 2))
-    r1, r2, r3 = together(*[y_shift(part, d + 1) for d, part in enumerate(sent)])
+    r1, r2, r3 = [y_shift(part, d + 1) for d, part in enumerate(sent)]
+    r1, *last, distant = together(r1, *last, join(down3, up3, far_high))
+    third.append(x_shift(distant, 2))
+    r1, r2, r3, inverse_other = together(r1, r2, r3, inverse_other)
     second_grad = incoming + ((mine + r1) + (r2 + r3))
     rounded = second_grad.astype(BF16)
 

time: 136 us -> 135 us (level)
    ppermute x17, waiting for transfers between devices: 25.3 us -> 16.6 us  [x_shift(): return lax.ppermute(value, 'col', pairs)]
    ppermute x12, waiting for transfers between devices: 10.5 us -> 17.5 us  [y_shift(): return lax.ppermute(value, 'row', pairs)]
    ppermute x17, starting transfers between devices: 27.7 us -> 24.2 us  [x_shift(): return lax.ppermute(value, 'col', pairs)]
    ppermute x4, starting transfers between devices: 9.61 us -> 11.6 us  [core_swap(): return lax.ppermute(value, 'row', [(r, r ^ 1) for r in range(2 * NY)])]
  transfers between devices with their start and end apart: 44 -> 44, of which waited for: 15 -> 17; matrix products, arithmetic and copies ran while one was open for 2% -> 2% of each run, Pallas kernels for 15% -> 16%
where the time goes in v12:
time: 135 us
  starting transfers between devices  66.8 us (49%)
  waiting for transfers between devices  39.8 us (29%)
  Pallas kernels  22.2 us (16%)
  other arithmetic  2.78 us (2%)
  local copies, waits for them, and re-layouts  1.92 us (1%)
    ppermute x17, starting transfers between devices, x_shift(): return lax.ppermute(value, 'col', pairs)  24.2 us
    ppermute x12, waiting for transfers between devices, y_shift(): return lax.ppermute(value, 'row', pairs)  17.5 us
    ppermute x17, waiting for transfers between devices, x_shift(): return lax.ppermute(value, 'col', pairs)  16.6 us
    ppermute x12, starting transfers between devices, y_shift(): return lax.ppermute(value, 'row', pairs)  13.3 us
    ppermute x8, starting transfers between devices, z_shift(): return lax.ppermute(value, 'col', pairs)  12.7 us
    pallas_call x6, Pallas kernels, product(): pl.pallas_call(kernel, out_shape=(column,) + (jax.ShapeDtypeStruct((512,...  12.3 us
    ppermute x4, starting transfers between devices, core_swap(): return lax.ppermute(value, 'row', [(r, r ^ 1) for r in range(2 * NY)])  11.6 us
    ppermute x3, starting transfers between devices, y_first(): return lax.ppermute(value, 'row', [(k, y * 2 + k) for k in range(2)])  5.01 us
  transfers between devices with their start and end apart: 44, of which 17 were waited for; matrix products, arithmetic and copies ran while one was open for 2% of the time, Pallas kernels for 16%

profile of v12, /device:TPU:1, one launch (start us, length us, event | category | flops | bytes accessed | tf_op | source)
XLA Modules:
  0.0 134.5 jit_solution(4603147886556167876)
XLA Ops:
  0.6 3.3 %collective-permute-start.1 = (bf16[2048,512]{1,0:T(8,128)(2,1)}, bf16[2048,512]{1,0:T(8,128)(2,1)}, u32[]{:S(2)}, u32[]{:S(2)}) collective-permute-start(bf16[2048,512]{1,0:T(8,128)(2,1)} %mine.1), channel_id=1, source_target_pairs={{0,32},{32,0},{64,96},{96,64},{128,160},{160,128},{192,224},{224,1... | collective-permute-start | bytes 6291464 | tf_op jit(solution)/shard_map/ppermute | solution.py:46
  8.6 2.4 %collective-permute-start.4 = (bf16[128,512]{1,0:T(8,128)(2,1)S(1)}, bf16[128,512]{1,0:T(8,128)(2,1)S(1)}, u32[]{:S(2)}, u32[]{:S(2)}) collective-permute-start(bf16[128,512]{1,0:T(8,128)(2,1)S(1)} %get-tuple-element.85.two), channel_id=1, source_target_pairs={{0,16},{1,17},{2,18},{3,19},{4,20},{5,21},{6,22},{7,23},{8,24},{9,... | collective-permute-start | bytes 393224 | tf_op jit(solution)/shard_map/ppermute | solution.py:28
  21.7 5.7 %collective-permute-start.11 = (bf16[41,16,512]{2,1,0:T(8,128)(2,1)S(1)}, bf16[41,16,512]{2,1,0:T(8,128)(2,1)S(1)}, u32[]{:S(2)}, u32[]{:S(2)}) collective-permute-start(bf16[41,16,512]{2,1,0:T(8,128)(2,1)S(1)} %get-tuple-element.96.refs_0_), channel_id=1, source_target_pairs={{0,7},{1,0},{2,1},{3,2},{4,3},{5,4},{6,5},{7,6},{8,15},{9,8},{10,9... | collective-permute-start | bytes 2015240 | tf_op jit(solution)/shard_map/ppermute | solution.py:33
  28.9 2.7 %collective-permute-start.15 = (bf16[1,9,16,512]{3,2,1,0:T(8,128)(2,1)S(1)}, bf16[1,9,16,512]{3,2,1,0:T(8,128)(2,1)S(1)}, u32[]{:S(2)}, u32[]{:S(2)}) collective-permute-start(bf16[1,9,16,512]{3,2,1,0:T(8,128)(2,1)S(1)} %get-tuple-element.136.refs_0_), channel_id=1, source_target_pairs={{0,16},{1,17},{2,18},{3,19},{4,20},{5,21},{6,22},{7,23},{8,24},{9,... | collective-permute-start | bytes 442376 | tf_op jit(solution)/shard_map/ppermute | solution.py:28
  36.7 3.2 %collective-permute-done.13.refs_1_ = bf16[1,9,16,512]{3,2,1,0:T(8,128)(2,1)S(1)} collective-permute-done((bf16[1,9,16,512]{3,2,1,0:T(8,128)(2,1)S(1)}, bf16[1,9,16,512]{3,2,1,0:T(8,128)(2,1)S(1)}, u32[]{:S(2)}, u32[]{:S(2)}) %collective-permute-start.13) | collective-permute-done | bytes 147488 | tf_op jit(solution)/shard_map/ppermute | solution.py:28
  39.8 3.0 %collective-permute-done.10.refs_0_.refs_1_ = bf16[41,16,512]{2,1,0:T(8,128)(2,1)S(1)} collective-permute-done((bf16[41,16,512]{2,1,0:T(8,128)(2,1)S(1)}, bf16[41,16,512]{2,1,0:T(8,128)(2,1)S(1)}, u32[]{:S(2)}, u32[]{:S(2)}) %collective-permute-start.10) | collective-permute-done | bytes 671776 | tf_op jit(solution)/shard_map/ppermute | solution.py:33
  42.9 2.7 %collective-permute-start.17 = (bf16[41,16,512]{2,1,0:T(8,128)(2,1)S(1)}, bf16[41,16,512]{2,1,0:T(8,128)(2,1)S(1)}, u32[]{:S(2)}, u32[]{:S(2)}) collective-permute-start(bf16[41,16,512]{2,1,0:T(8,128)(2,1)S(1)} %collective-permute-done.11.refs_1_.refs_2_), channel_id=1, source_target_pairs={{0,7},{1,0},{2,1},{3,2},{4,3},{5,4},{6,5},{7,6},{8,15},{9,8},{10,9... | collective-permute-start | bytes 2015240 | tf_op jit(solution)/shard_map/ppermute | solution.py:33
  45.6 2.7 %collective-permute-start.20 = (bf16[2,9,16,512]{3,2,1,0:T(8,128)(2,1)S(1)}, bf16[2,9,16,512]{3,2,1,0:T(8,128)(2,1)S(1)}, u32[]{:S(2)}, u32[]{:S(2)}) collective-permute-start(bf16[2,9,16,512]{3,2,1,0:T(8,128)(2,1)S(1)} %join_parts.4.refs_0_.refs_4_), channel_id=1, source_target_pairs={{0,16},{1,17},{2,18},{3,19},{4,20},{5,21},{6,22},{7,23},{8,24},{9,... | collective-permute-start | bytes 884744 | tf_op jit(solution)/shard_map/ppermute | solution.py:28
  49.8 4.9 %prepare_adjoint.1 = (bf16[8,512,512]{2,1,0:T(8,128)(2,1)S(1)}, bf16[4,512,1024]{2,1,0:T(8,128)(2,1)S(1)}) custom-call(s32[4]{0:T(128)S(1)} %pad_add_fusion.pos, s32[64,64]{1,0:T(8,128)S(1)} %copy-done.3, bf16[2048,512]{1,0:T(8,128)(2,1)S(1)} %copy-done, bf16[2048,512]{1,0:T(8,128)(2,1)} %collective-permute-done.1.other), custom_call_target="tpu_custom_call" | custom-call | tf_op jit(solution)/shard_map/prepare_adjoint/pallas_call | solution.py:184
  54.7 4.7 %collective-permute-done.19.refs_2_.refs_6_ = bf16[2,9,16,512]{3,2,1,0:T(8,128)(2,1)S(1)} collective-permute-done((bf16[2,9,16,512]{3,2,1,0:T(8,128)(2,1)S(1)}, bf16[2,9,16,512]{3,2,1,0:T(8,128)(2,1)S(1)}, u32[]{:S(2)}, u32[]{:S(2)}) %collective-permute-start.19) | collective-permute-done | bytes 294944 | tf_op jit(solution)/shard_map/ppermute | solution.py:28
  59.5 2.7 %collective-permute-start.22 = (bf16[41,16,512]{2,1,0:T(8,128)(2,1)S(1)}, bf16[41,16,512]{2,1,0:T(8,128)(2,1)S(1)}, u32[]{:S(2)}, u32[]{:S(2)}) collective-permute-start(bf16[41,16,512]{2,1,0:T(8,128)(2,1)S(1)} %collective-permute-done.17.refs_4_.refs_1_), channel_id=1, source_target_pairs={{0,7},{1,0},{2,1},{3,2},{4,3},{5,4},{6,5},{7,6},{8,15},{9,8},{10,9... | collective-permute-start | bytes 2015240 | tf_op jit(solution)/shard_map/ppermute | solution.py:33
  62.2 3.9 %collective-permute-start.25 = (bf16[2,9,16,512]{3,2,1,0:T(8,128)(2,1)S(1)}, bf16[2,9,16,512]{3,2,1,0:T(8,128)(2,1)S(1)}, u32[]{:S(2)}, u32[]{:S(2)}) collective-permute-start(bf16[2,9,16,512]{3,2,1,0:T(8,128)(2,1)S(1)} %join_parts.5.refs_4_.refs_8_), channel_id=1, source_target_pairs={{0,16},{1,17},{2,18},{3,19},{4,20},{5,21},{6,22},{7,23},{8,24},{9,... | collective-permute-start | bytes 884744 | tf_op jit(solution)/shard_map/ppermute | solution.py:28
  67.6 2.6 %collective-permute-done.25.refs_7_.refs_11_ = bf16[2,9,16,512]{3,2,1,0:T(8,128)(2,1)S(1)} collective-permute-done((bf16[2,9,16,512]{3,2,1,0:T(8,128)(2,1)S(1)}, bf16[2,9,16,512]{3,2,1,0:T(8,128)(2,1)S(1)}, u32[]{:S(2)}, u32[]{:S(2)}) %collective-permute-start.25) | collective-permute-done | bytes 294944 | tf_op jit(solution)/shard_map/ppermute | solution.py:28
  70.2 7.1 %collective-permute-start.35 = (bf16[4,128,1024]{2,1,0:T(8,128)(2,1)S(1)}, bf16[4,128,1024]{2,1,0:T(8,128)(2,1)S(1)}, u32[]{:S(2)}, u32[]{:S(2)}) collective-permute-start(bf16[4,128,1024]{2,1,0:T(8,128)(2,1)S(1)} %pad_maximum_fusion.inverse), channel_id=1, source_target_pairs={{0,32},{32,0},{64,96},{96,64},{128,160},{160,128},{192,224},{224,1... | collective-permute-start | bytes 3145736 | tf_op jit(solution)/shard_map/ppermute | solution.py:46
  77.3 3.0 %masked_product.6.refs_2_ = f32[512,512]{1,0:T(8,128)S(1)} custom-call(s32[4]{0:T(128)S(1)} %pad_add_fusion.pos, bf16[8,512,512]{2,1,0:T(8,128)(2,1)S(1)} %get-tuple-element.106.adjoint, bf16[41,16,512]{2,1,0:T(8,128)(2,1)S(1)} %get-tuple-element.96.refs_0_, bf16[41,16,512]{2,1,0:T(8,128)(2,1)S(1)} %collective-permute-done.10.refs_0_.refs_1_, ...), custom_call_target="tpu_custom_call" | custom-call | tf_op jit(solution)/shard_map/masked_product/pallas_call | solution.py:241
  80.6 2.7 %collective-permute-start.29 = (bf16[2,9,16,512]{3,2,1,0:T(8,128)(2,1)S(1)}, bf16[2,9,16,512]{3,2,1,0:T(8,128)(2,1)S(1)}, u32[]{:S(2)}, u32[]{:S(2)}) collective-permute-start(bf16[2,9,16,512]{3,2,1,0:T(8,128)(2,1)S(1)} %join_parts.6.refs_0_.refs_12_), channel_id=1, source_target_pairs={{0,24},{1,25},{2,26},{3,27},{4,28},{5,29},{6,30},{7,31},{8,0},{9,1... | collective-permute-start | bytes 884744 | tf_op jit(solution)/shard_map/ppermute | solution.py:28
  91.1 3.2 %collective-permute-start.32 = (bf16[1,9,16,512]{3,2,1,0:T(8,128)(2,1)S(1)}, bf16[1,9,16,512]{3,2,1,0:T(8,128)(2,1)S(1)}, u32[]{:S(2)}, u32[]{:S(2)}) collective-permute-start(bf16[1,9,16,512]{3,2,1,0:T(8,128)(2,1)S(1)} %slice_bitcast_fusion.refs_5_.refs_16_), channel_id=1, source_target_pairs={{0,24},{1,25},{2,26},{3,27},{4,28},{5,29},{6,30},{7,31},{8,0},{9,1... | collective-permute-start | bytes 442376 | tf_op jit(solution)/shard_map/ppermute | solution.py:28
  95.7 3.6 %collective-permute-start.33 = (f32[512,128]{1,0:T(8,128)S(1)}, f32[512,128]{1,0:T(8,128)S(1)}, u32[]{:S(2)}, u32[]{:S(2)}) collective-permute-start(f32[512,128]{1,0:T(8,128)S(1)} %get-tuple-element.130), channel_id=1, source_target_pairs={{0,128},{32,160},{64,192},{96,224},{128,0},{160,32},{192,64},{224,... | collective-permute-start | bytes 786440 | tf_op jit(solution)/shard_map/ppermute | solution.py:38
  99.3 5.5 %collective-permute-done.31.refs_6_.refs_17_ = bf16[1,9,16,512]{3,2,1,0:T(8,128)(2,1)S(1)} collective-permute-done((bf16[1,9,16,512]{3,2,1,0:T(8,128)(2,1)S(1)}, bf16[1,9,16,512]{3,2,1,0:T(8,128)(2,1)S(1)}, u32[]{:S(2)}, u32[]{:S(2)}) %collective-permute-start.31) | collective-permute-done | bytes 147488 | tf_op jit(solution)/shard_map/ppermute | solution.py:28
  104.7 4.4 %collective-permute-done.33 = f32[512,128]{1,0:T(8,128)S(1)} collective-permute-done((f32[512,128]{1,0:T(8,128)S(1)}, f32[512,128]{1,0:T(8,128)S(1)}, u32[]{:S(2)}, u32[]{:S(2)}) %collective-permute-start.33) | collective-permute-done | bytes 262176 | tf_op jit(solution)/shard_map/ppermute | solution.py:38
  110.9 3.4 %collective-permute-start.38 = (bf16[512,128]{1,0:T(8,128)(2,1)S(1)}, bf16[512,128]{1,0:T(8,128)(2,1)S(1)}, u32[]{:S(2)}, u32[]{:S(2)}) collective-permute-start(bf16[512,128]{1,0:T(8,128)(2,1)S(1)} %get-tuple-element.162), channel_id=1, source_target_pairs={{0,192},{32,224},{64,0},{96,32},{128,64},{160,96},{192,128},{224,1... | collective-permute-start | bytes 393224 | tf_op jit(solution)/shard_map/ppermute | solution.py:38
  116.3 2.8 %masked_product.11 = (f32[512,128]{1,0:T(8,128)S(1)}, bf16[512,128]{1,0:T(8,128)(2,1)S(1)}, bf16[512,128]{1,0:T(8,128)(2,1)S(1)}, bf16[512,128]{1,0:T(8,128)(2,1)S(1)}) custom-call(s32[4]{0:T(128)S(1)} %pad_add_fusion.pos, bf16[4,512,1024]{2,1,0:T(8,128)(2,1)S(1)} %get-tuple-element.115.adjoint, bf16[1,9,16,512]{3,2,1,0:T(8,128)(2,1)S(1)} %get-tuple-element.136.refs_0_, ...), custom_call_target="tpu_custom_call" | custom-call | tf_op jit(solution)/shard_map/masked_product/pallas_call | solution.py:241
  119.7 3.7 %collective-permute-done.36 = bf16[512,128]{1,0:T(8,128)(2,1)S(1)} collective-permute-done((bf16[512,128]{1,0:T(8,128)(2,1)S(1)}, bf16[512,128]{1,0:T(8,128)(2,1)S(1)}, u32[]{:S(2)}, u32[]{:S(2)}) %collective-permute-start.36) | collective-permute-done | bytes 131104 | tf_op jit(solution)/shard_map/ppermute | solution.py:38
  129.9 3.5 %collective-permute-done.40 = bf16[512,128]{1,0:T(8,128)(2,1)S(1)} collective-permute-done((bf16[512,128]{1,0:T(8,128)(2,1)S(1)}, bf16[512,128]{1,0:T(8,128)(2,1)S(1)}, u32[]{:S(2)}, u32[]{:S(2)}) %collective-permute-start.40) | collective-permute-done | bytes 131104 | tf_op jit(solution)/shard_map/ppermute | solution.py:38
  (101 shorter events, 46.1 us)
Async XLA Ops:
  8.1 8.7 %collective-permute-start.5 = (bf16[128,1024]{1,0:T(8,128)(2,1)}, bf16[128,1024]{1,0:T(8,128)(2,1)S(1)}, u32[]{:S(2)}, u32[]{:S(2)}) collective-permute-start(bf16[128,1024]{1,0:T(8,128)(2,1)} %param.11), channel_id=1, source_target_pairs={{0,64},{32,96},{64,128},{96,160},{128,192},{160,224},{192,0},{224,... | collective-permute-start | bytes 786440 | tf_op jit(solution)/shard_map/ppermute | solution.py:38
  8.6 10.0 %collective-permute-start.4 = (bf16[128,512]{1,0:T(8,128)(2,1)S(1)}, bf16[128,512]{1,0:T(8,128)(2,1)S(1)}, u32[]{:S(2)}, u32[]{:S(2)}) collective-permute-start(bf16[128,512]{1,0:T(8,128)(2,1)S(1)} %get-tuple-element.85.two), channel_id=1, source_target_pairs={{0,16},{1,17},{2,18},{3,19},{4,20},{5,21},{6,22},{7,23},{8,24},{9,... | collective-permute-start | bytes 393224 | tf_op jit(solution)/shard_map/ppermute | solution.py:28
  11.0 9.3 %collective-permute-start.3 = (bf16[128,512]{1,0:T(8,128)(2,1)S(1)}, bf16[128,512]{1,0:T(8,128)(2,1)S(1)}, u32[]{:S(2)}, u32[]{:S(2)}) collective-permute-start(bf16[128,512]{1,0:T(8,128)(2,1)S(1)} %get-tuple-element.85.two), channel_id=1, source_target_pairs={{0,24},{1,25},{2,26},{3,27},{4,28},{5,29},{6,30},{7,31},{8,0},{9,1... | collective-permute-start | bytes 393224 | tf_op jit(solution)/shard_map/ppermute | solution.py:28
  21.7 18.1 %collective-permute-start.11 = (bf16[41,16,512]{2,1,0:T(8,128)(2,1)S(1)}, bf16[41,16,512]{2,1,0:T(8,128)(2,1)S(1)}, u32[]{:S(2)}, u32[]{:S(2)}) collective-permute-start(bf16[41,16,512]{2,1,0:T(8,128)(2,1)S(1)} %get-tuple-element.96.refs_0_), channel_id=1, source_target_pairs={{0,7},{1,0},{2,1},{3,2},{4,3},{5,4},{6,5},{7,6},{8,15},{9,8},{10,9... | collective-permute-start | bytes 2015240 | tf_op jit(solution)/shard_map/ppermute | solution.py:33
  27.4 15.5 %collective-permute-start.10 = (bf16[41,16,512]{2,1,0:T(8,128)(2,1)S(1)}, bf16[41,16,512]{2,1,0:T(8,128)(2,1)S(1)}, u32[]{:S(2)}, u32[]{:S(2)}) collective-permute-start(bf16[41,16,512]{2,1,0:T(8,128)(2,1)S(1)} %get-tuple-element.96.refs_0_), channel_id=1, source_target_pairs={{0,1},{1,2},{2,3},{3,4},{4,5},{5,6},{6,7},{7,0},{8,9},{9,10},{10,1... | collective-permute-start | bytes 2015240 | tf_op jit(solution)/shard_map/ppermute | solution.py:33
  42.9 16.5 %collective-permute-start.16 = (bf16[41,16,512]{2,1,0:T(8,128)(2,1)S(1)}, bf16[41,16,512]{2,1,0:T(8,128)(2,1)S(1)}, u32[]{:S(2)}, u32[]{:S(2)}) collective-permute-start(bf16[41,16,512]{2,1,0:T(8,128)(2,1)S(1)} %collective-permute-done.10.refs_0_.refs_1_), channel_id=1, source_target_pairs={{0,1},{1,2},{2,3},{3,4},{4,5},{5,6},{6,7},{7,0},{8,9},{9,10},{10,1... | collective-permute-start | bytes 2015240 | tf_op jit(solution)/shard_map/ppermute | solution.py:33
  42.9 16.5 %collective-permute-start.17 = (bf16[41,16,512]{2,1,0:T(8,128)(2,1)S(1)}, bf16[41,16,512]{2,1,0:T(8,128)(2,1)S(1)}, u32[]{:S(2)}, u32[]{:S(2)}) collective-permute-start(bf16[41,16,512]{2,1,0:T(8,128)(2,1)S(1)} %collective-permute-done.11.refs_1_.refs_2_), channel_id=1, source_target_pairs={{0,7},{1,0},{2,1},{3,2},{4,3},{5,4},{6,5},{7,6},{8,15},{9,8},{10,9... | collective-permute-start | bytes 2015240 | tf_op jit(solution)/shard_map/ppermute | solution.py:33
  45.6 9.1 %collective-permute-start.20 = (bf16[2,9,16,512]{3,2,1,0:T(8,128)(2,1)S(1)}, bf16[2,9,16,512]{3,2,1,0:T(8,128)(2,1)S(1)}, u32[]{:S(2)}, u32[]{:S(2)}) collective-permute-start(bf16[2,9,16,512]{3,2,1,0:T(8,128)(2,1)S(1)} %join_parts.4.refs_0_.refs_4_), channel_id=1, source_target_pairs={{0,16},{1,17},{2,18},{3,19},{4,20},{5,21},{6,22},{7,23},{8,24},{9,... | collective-permute-start | bytes 884744 | tf_op jit(solution)/shard_map/ppermute | solution.py:28
  48.3 11.1 %collective-permute-start.19 = (bf16[2,9,16,512]{3,2,1,0:T(8,128)(2,1)S(1)}, bf16[2,9,16,512]{3,2,1,0:T(8,128)(2,1)S(1)}, u32[]{:S(2)}, u32[]{:S(2)}) collective-permute-start(bf16[2,9,16,512]{3,2,1,0:T(8,128)(2,1)S(1)} %join_parts.4.refs_0_.refs_4_), channel_id=1, source_target_pairs={{0,24},{1,25},{2,26},{3,27},{4,28},{5,29},{6,30},{7,31},{8,0},{9,1... | collective-permute-start | bytes 884744 | tf_op jit(solution)/shard_map/ppermute | solution.py:28
  49.1 10.3 %collective-permute-start.18 = (bf16[2,9,16,512]{3,2,1,0:T(8,128)(2,1)S(1)}, bf16[2,9,16,512]{3,2,1,0:T(8,128)(2,1)S(1)}, u32[]{:S(2)}, u32[]{:S(2)}) collective-permute-start(bf16[2,9,16,512]{3,2,1,0:T(8,128)(2,1)S(1)} %join_parts.4.refs_0_.refs_4_), channel_id=1, source_target_pairs={{0,8},{1,9},{2,10},{3,11},{4,12},{5,13},{6,14},{7,15},{8,16},{9,17... | collective-permute-start | bytes 884744 | tf_op jit(solution)/shard_map/ppermute | solution.py:28
  59.4 21.0 %collective-permute-start.21 = (bf16[41,16,512]{2,1,0:T(8,128)(2,1)S(1)}, bf16[41,16,512]{2,1,0:T(8,128)(2,1)S(1)}, u32[]{:S(2)}, u32[]{:S(2)}) collective-permute-start(bf16[41,16,512]{2,1,0:T(8,128)(2,1)S(1)} %collective-permute-done.16.refs_3_.refs_0_), channel_id=1, source_target_pairs={{0,1},{1,2},{2,3},{3,4},{4,5},{5,6},{6,7},{7,0},{8,9},{9,10},{10,1... | collective-permute-start | bytes 2015240 | tf_op jit(solution)/shard_map/ppermute | solution.py:33
  59.5 20.9 %collective-permute-start.22 = (bf16[41,16,512]{2,1,0:T(8,128)(2,1)S(1)}, bf16[41,16,512]{2,1,0:T(8,128)(2,1)S(1)}, u32[]{:S(2)}, u32[]{:S(2)}) collective-permute-start(bf16[41,16,512]{2,1,0:T(8,128)(2,1)S(1)} %collective-permute-done.17.refs_4_.refs_1_), channel_id=1, source_target_pairs={{0,7},{1,0},{2,1},{3,2},{4,3},{5,4},{6,5},{7,6},{8,15},{9,8},{10,9... | collective-permute-start | bytes 2015240 | tf_op jit(solution)/shard_map/ppermute | solution.py:33
  66.1 14.3 %collective-permute-start.24 = (bf16[2,9,16,512]{3,2,1,0:T(8,128)(2,1)S(1)}, bf16[2,9,16,512]{3,2,1,0:T(8,128)(2,1)S(1)}, u32[]{:S(2)}, u32[]{:S(2)}) collective-permute-start(bf16[2,9,16,512]{3,2,1,0:T(8,128)(2,1)S(1)} %join_parts.5.refs_4_.refs_8_), channel_id=1, source_target_pairs={{0,24},{1,25},{2,26},{3,27},{4,28},{5,29},{6,30},{7,31},{8,0},{9,1... | collective-permute-start | bytes 884744 | tf_op jit(solution)/shard_map/ppermute | solution.py:28
  67.2 13.2 %collective-permute-start.23 = (bf16[2,9,16,512]{3,2,1,0:T(8,128)(2,1)S(1)}, bf16[2,9,16,512]{3,2,1,0:T(8,128)(2,1)S(1)}, u32[]{:S(2)}, u32[]{:S(2)}) collective-permute-start(bf16[2,9,16,512]{3,2,1,0:T(8,128)(2,1)S(1)} %join_parts.5.refs_4_.refs_8_), channel_id=1, source_target_pairs={{0,8},{1,9},{2,10},{3,11},{4,12},{5,13},{6,14},{7,15},{8,16},{9,17... | collective-permute-start | bytes 884744 | tf_op jit(solution)/shard_map/ppermute | solution.py:28
  70.2 34.5 %collective-permute-start.35 = (bf16[4,128,1024]{2,1,0:T(8,128)(2,1)S(1)}, bf16[4,128,1024]{2,1,0:T(8,128)(2,1)S(1)}, u32[]{:S(2)}, u32[]{:S(2)}) collective-permute-start(bf16[4,128,1024]{2,1,0:T(8,128)(2,1)S(1)} %pad_maximum_fusion.inverse), channel_id=1, source_target_pairs={{0,32},{32,0},{64,96},{96,64},{128,160},{160,128},{192,224},{224,1... | collective-permute-start | bytes 3145736 | tf_op jit(solution)/shard_map/ppermute | solution.py:46
  80.5 10.6 %collective-permute-start.27 = (bf16[25,16,512]{2,1,0:T(8,128)(2,1)S(1)}, bf16[25,16,512]{2,1,0:T(8,128)(2,1)S(1)}, u32[]{:S(2)}, u32[]{:S(2)}) collective-permute-start(bf16[25,16,512]{2,1,0:T(8,128)(2,1)S(1)} %slice.18), channel_id=1, source_target_pairs={{0,7},{1,0},{2,1},{3,2},{4,3},{5,4},{6,5},{7,6},{8,15},{9,8},{10,9... | collective-permute-start | bytes 1228808 | tf_op jit(solution)/shard_map/ppermute | solution.py:33
  80.6 9.9 %collective-permute-start.29 = (bf16[2,9,16,512]{3,2,1,0:T(8,128)(2,1)S(1)}, bf16[2,9,16,512]{3,2,1,0:T(8,128)(2,1)S(1)}, u32[]{:S(2)}, u32[]{:S(2)}) collective-permute-start(bf16[2,9,16,512]{3,2,1,0:T(8,128)(2,1)S(1)} %join_parts.6.refs_0_.refs_12_), channel_id=1, source_target_pairs={{0,24},{1,25},{2,26},{3,27},{4,28},{5,29},{6,30},{7,31},{8,0},{9,1... | collective-permute-start | bytes 884744 | tf_op jit(solution)/shard_map/ppermute | solution.py:28
  95.6 9.2 %collective-permute-start.30 = (f32[512,128]{1,0:T(8,128)S(1)}, f32[512,128]{1,0:T(8,128)S(1)}, u32[]{:S(2)}, u32[]{:S(2)}) collective-permute-start(f32[512,128]{1,0:T(8,128)S(1)} %get-tuple-element.128), channel_id=1, source_target_pairs={{0,64},{32,96},{64,128},{96,160},{128,192},{160,224},{192,0},{224,... | collective-permute-start | bytes 786440 | tf_op jit(solution)/shard_map/ppermute | solution.py:38
  95.7 13.5 %collective-permute-start.33 = (f32[512,128]{1,0:T(8,128)S(1)}, f32[512,128]{1,0:T(8,128)S(1)}, u32[]{:S(2)}, u32[]{:S(2)}) collective-permute-start(f32[512,128]{1,0:T(8,128)S(1)} %get-tuple-element.130), channel_id=1, source_target_pairs={{0,128},{32,160},{64,192},{96,224},{128,0},{160,32},{192,64},{224,... | collective-permute-start | bytes 786440 | tf_op jit(solution)/shard_map/ppermute | solution.py:38
  99.2 10.9 %collective-permute-start.34 = (f32[512,128]{1,0:T(8,128)S(1)}, f32[512,128]{1,0:T(8,128)S(1)}, u32[]{:S(2)}, u32[]{:S(2)}) collective-permute-start(f32[512,128]{1,0:T(8,128)S(1)} %get-tuple-element.131), channel_id=1, source_target_pairs={{0,192},{32,224},{64,0},{96,32},{128,64},{160,96},{192,128},{224,1... | collective-permute-start | bytes 786440 | tf_op jit(solution)/shard_map/ppermute | solution.py:38
  104.7 10.1 %collective-permute-start.39 = (bf16[3,9,16,512]{3,2,1,0:T(8,128)(2,1)S(1)}, bf16[3,9,16,512]{3,2,1,0:T(8,128)(2,1)S(1)}, u32[]{:S(2)}, u32[]{:S(2)}) collective-permute-start(bf16[3,9,16,512]{3,2,1,0:T(8,128)(2,1)S(1)} %join_parts.7), channel_id=1, source_target_pairs={{0,16},{1,17},{2,18},{3,19},{4,20},{5,21},{6,22},{7,23},{8,24},{9,... | collective-permute-start | bytes 1327112 | tf_op jit(solution)/shard_map/ppermute | solution.py:28
  114.3 9.1 %collective-permute-start.36 = (bf16[512,128]{1,0:T(8,128)(2,1)S(1)}, bf16[512,128]{1,0:T(8,128)(2,1)S(1)}, u32[]{:S(2)}, u32[]{:S(2)}) collective-permute-start(bf16[512,128]{1,0:T(8,128)(2,1)S(1)} %get-tuple-element.162), channel_id=1, source_target_pairs={{0,64},{32,96},{64,128},{96,160},{128,192},{160,224},{192,0},{224,... | collective-permute-start | bytes 393224 | tf_op jit(solution)/shard_map/ppermute | solution.py:38
  124.4 9.1 %collective-permute-start.40 = (bf16[512,128]{1,0:T(8,128)(2,1)S(1)}, bf16[512,128]{1,0:T(8,128)(2,1)S(1)}, u32[]{:S(2)}, u32[]{:S(2)}) collective-permute-start(bf16[512,128]{1,0:T(8,128)(2,1)S(1)} %get-tuple-element.153), channel_id=1, source_target_pairs={{0,64},{32,96},{64,128},{96,160},{128,192},{160,224},{192,0},{224,... | collective-permute-start | bytes 393224 | tf_op jit(solution)/shard_map/ppermute | solution.py:38
  124.6 8.9 %collective-permute-start.41 = (bf16[512,128]{1,0:T(8,128)(2,1)S(1)}, bf16[512,128]{1,0:T(8,128)(2,1)S(1)}, u32[]{:S(2)}, u32[]{:S(2)}) collective-permute-start(bf16[512,128]{1,0:T(8,128)(2,1)S(1)} %get-tuple-element.154), channel_id=1, source_target_pairs={{0,128},{32,160},{64,192},{96,224},{128,0},{160,32},{192,64},{224,... | collective-permute-start | bytes 393224 | tf_op jit(solution)/shard_map/ppermute | solution.py:38
  (25 other events, 242.5 us)

commit v13 on v8

--- a/solution.py
+++ b/solution.py
@@ -358,12 +358,13 @@
     mine, *sent = product(
         pos, for_two, [far_low, far_high], [(7, [(0, 0, TWO // 2), (1, 0, TWO // 2)])], sums, F32)
     last = x_all(far_high[None, TWO // 2:])
-    sums_one = product(pos, for_one, third, [(3, [(i, 0, 2) for i in range(NX)])], sums_one)
-    r1, r2, r3, sums_one, *last = together(
-        *[y_shift(part, d + 1) for d, part in enumerate(sent)], sums_one, *last)
+    r1, r2, r3, *last = together(
+        *[y_shift(part, d + 1) for d, part in enumerate(sent)], *last, *third)
+    last, third = last[:NX], last[NX:]
     second_grad = incoming + ((mine + r1) + (r2 + r3))
     rounded = second_grad.astype(BF16)
 
+    sums_one = product(pos, for_one, third, [(3, [(i, 0, 2) for i in range(NX)])], sums_one)
     sums_one = product(
         pos, for_one, first_x + last,
         [(0, [(NX * s + i, 0, 1) for i in range(NX) for s in range(2)])], sums_one, BF16)

time: 132 us -> 132 us (level)
    ppermute x12, waiting for transfers between devices: 11.7 us -> 10.3 us  [y_shift(): return lax.ppermute(value, 'row', pairs)]
    ppermute x18, waiting for transfers between devices: 20 us -> 21.4 us  [x_shift(): return lax.ppermute(value, 'col', pairs)]
  transfers between devices with their start and end apart: 45 -> 45, of which waited for: 17 -> 16; matrix products, arithmetic and copies ran while one was open for 2% -> 2% of each run, Pallas kernels for 16% -> 16%
where the time goes in v13:
time: 132 us
  starting transfers between devices  68.7 us (52%)
  waiting for transfers between devices  35.5 us (27%)
  Pallas kernels  22.2 us (17%)
  other arithmetic  2.78 us (2%)
  local copies, waits for them, and re-layouts  1.92 us (1%)
    ppermute x18, starting transfers between devices, x_shift(): return lax.ppermute(value, 'col', pairs)  29.7 us
    ppermute x18, waiting for transfers between devices, x_shift(): return lax.ppermute(value, 'col', pairs)  21.4 us
    ppermute x12, starting transfers between devices, y_shift(): return lax.ppermute(value, 'row', pairs)  13.2 us
    ppermute x8, starting transfers between devices, z_shift(): return lax.ppermute(value, 'col', pairs)  12.7 us
    pallas_call x6, Pallas kernels, product(): pl.pallas_call(kernel, out_shape=(column,) + (jax.ShapeDtypeStruct((512,...  12.3 us
    ppermute x12, waiting for transfers between devices, y_shift(): return lax.ppermute(value, 'row', pairs)  10.3 us
    ppermute x4, starting transfers between devices, core_swap(): return lax.ppermute(value, 'row', [(r, r ^ 1) for r in range(2 * NY)])  8.12 us
    ppermute x3, starting transfers between devices, y_first(): return lax.ppermute(value, 'row', [(k, y * 2 + k) for k in range(2)])  5.01 us
  transfers between devices with their start and end apart: 45, of which 16 were waited for; matrix products, arithmetic and copies ran while one was open for 2% of the time, Pallas kernels for 16%

profile of v13, /device:TPU:1, one launch (start us, length us, event | category | flops | bytes accessed | tf_op | source)
XLA Modules:
  0.0 132.2 jit_solution(6500514742768037461)
XLA Ops:
  0.6 3.3 %collective-permute-start.1 = (bf16[2048,512]{1,0:T(8,128)(2,1)}, bf16[2048,512]{1,0:T(8,128)(2,1)}, u32[]{:S(2)}, u32[]{:S(2)}) collective-permute-start(bf16[2048,512]{1,0:T(8,128)(2,1)} %mine.1), channel_id=1, source_target_pairs={{0,32},{32,0},{64,96},{96,64},{128,160},{160,128},{192,224},{224,1... | collective-permute-start | bytes 6291464 | tf_op jit(solution)/shard_map/ppermute | solution.py:46
  8.6 2.4 %collective-permute-start.4 = (bf16[128,512]{1,0:T(8,128)(2,1)S(1)}, bf16[128,512]{1,0:T(8,128)(2,1)S(1)}, u32[]{:S(2)}, u32[]{:S(2)}) collective-permute-start(bf16[128,512]{1,0:T(8,128)(2,1)S(1)} %get-tuple-element.84.two), channel_id=1, source_target_pairs={{0,16},{1,17},{2,18},{3,19},{4,20},{5,21},{6,22},{7,23},{8,24},{9,... | collective-permute-start | bytes 393224 | tf_op jit(solution)/shard_map/ppermute | solution.py:28
  21.7 5.7 %collective-permute-start.11 = (bf16[41,16,512]{2,1,0:T(8,128)(2,1)S(1)}, bf16[41,16,512]{2,1,0:T(8,128)(2,1)S(1)}, u32[]{:S(2)}, u32[]{:S(2)}) collective-permute-start(bf16[41,16,512]{2,1,0:T(8,128)(2,1)S(1)} %get-tuple-element.95.refs_0_), channel_id=1, source_target_pairs={{0,7},{1,0},{2,1},{3,2},{4,3},{5,4},{6,5},{7,6},{8,15},{9,8},{10,9... | collective-permute-start | bytes 2015240 | tf_op jit(solution)/shard_map/ppermute | solution.py:33
  28.9 2.7 %collective-permute-start.15 = (bf16[1,9,16,512]{3,2,1,0:T(8,128)(2,1)S(1)}, bf16[1,9,16,512]{3,2,1,0:T(8,128)(2,1)S(1)}, u32[]{:S(2)}, u32[]{:S(2)}) collective-permute-start(bf16[1,9,16,512]{3,2,1,0:T(8,128)(2,1)S(1)} %get-tuple-element.133.refs_0_), channel_id=1, source_target_pairs={{0,16},{1,17},{2,18},{3,19},{4,20},{5,21},{6,22},{7,23},{8,24},{9,... | collective-permute-start | bytes 442376 | tf_op jit(solution)/shard_map/ppermute | solution.py:28
  36.7 3.2 %collective-permute-done.13.refs_1_ = bf16[1,9,16,512]{3,2,1,0:T(8,128)(2,1)S(1)} collective-permute-done((bf16[1,9,16,512]{3,2,1,0:T(8,128)(2,1)S(1)}, bf16[1,9,16,512]{3,2,1,0:T(8,128)(2,1)S(1)}, u32[]{:S(2)}, u32[]{:S(2)}) %collective-permute-start.13) | collective-permute-done | bytes 147488 | tf_op jit(solution)/shard_map/ppermute | solution.py:28
  39.8 3.0 %collective-permute-done.10.refs_0_.refs_1_ = bf16[41,16,512]{2,1,0:T(8,128)(2,1)S(1)} collective-permute-done((bf16[41,16,512]{2,1,0:T(8,128)(2,1)S(1)}, bf16[41,16,512]{2,1,0:T(8,128)(2,1)S(1)}, u32[]{:S(2)}, u32[]{:S(2)}) %collective-permute-start.10) | collective-permute-done | bytes 671776 | tf_op jit(solution)/shard_map/ppermute | solution.py:33
  42.9 2.7 %collective-permute-start.17 = (bf16[41,16,512]{2,1,0:T(8,128)(2,1)S(1)}, bf16[41,16,512]{2,1,0:T(8,128)(2,1)S(1)}, u32[]{:S(2)}, u32[]{:S(2)}) collective-permute-start(bf16[41,16,512]{2,1,0:T(8,128)(2,1)S(1)} %collective-permute-done.11.refs_1_.refs_2_), channel_id=1, source_target_pairs={{0,7},{1,0},{2,1},{3,2},{4,3},{5,4},{6,5},{7,6},{8,15},{9,8},{10,9... | collective-permute-start | bytes 2015240 | tf_op jit(solution)/shard_map/ppermute | solution.py:33
  45.6 2.7 %collective-permute-start.20 = (bf16[2,9,16,512]{3,2,1,0:T(8,128)(2,1)S(1)}, bf16[2,9,16,512]{3,2,1,0:T(8,128)(2,1)S(1)}, u32[]{:S(2)}, u32[]{:S(2)}) collective-permute-start(bf16[2,9,16,512]{3,2,1,0:T(8,128)(2,1)S(1)} %join_parts.3.refs_0_.refs_4_), channel_id=1, source_target_pairs={{0,16},{1,17},{2,18},{3,19},{4,20},{5,21},{6,22},{7,23},{8,24},{9,... | collective-permute-start | bytes 884744 | tf_op jit(solution)/shard_map/ppermute | solution.py:28
  49.8 4.9 %prepare_adjoint.1 = (bf16[8,512,512]{2,1,0:T(8,128)(2,1)S(1)}, bf16[4,512,1024]{2,1,0:T(8,128)(2,1)S(1)}) custom-call(s32[4]{0:T(128)S(1)} %pad_add_fusion.pos, s32[64,64]{1,0:T(8,128)S(1)} %copy-done.3, bf16[2048,512]{1,0:T(8,128)(2,1)S(1)} %copy-done, bf16[2048,512]{1,0:T(8,128)(2,1)} %collective-permute-done.1.other), custom_call_target="tpu_custom_call" | custom-call | tf_op jit(solution)/shard_map/prepare_adjoint/pallas_call | solution.py:184
  54.7 4.7 %collective-permute-done.19.refs_2_.refs_6_ = bf16[2,9,16,512]{3,2,1,0:T(8,128)(2,1)S(1)} collective-permute-done((bf16[2,9,16,512]{3,2,1,0:T(8,128)(2,1)S(1)}, bf16[2,9,16,512]{3,2,1,0:T(8,128)(2,1)S(1)}, u32[]{:S(2)}, u32[]{:S(2)}) %collective-permute-start.19) | collective-permute-done | bytes 294944 | tf_op jit(solution)/shard_map/ppermute | solution.py:28
  59.5 2.7 %collective-permute-start.22 = (bf16[41,16,512]{2,1,0:T(8,128)(2,1)S(1)}, bf16[41,16,512]{2,1,0:T(8,128)(2,1)S(1)}, u32[]{:S(2)}, u32[]{:S(2)}) collective-permute-start(bf16[41,16,512]{2,1,0:T(8,128)(2,1)S(1)} %collective-permute-done.17.refs_4_.refs_1_), channel_id=1, source_target_pairs={{0,7},{1,0},{2,1},{3,2},{4,3},{5,4},{6,5},{7,6},{8,15},{9,8},{10,9... | collective-permute-start | bytes 2015240 | tf_op jit(solution)/shard_map/ppermute | solution.py:33
  62.2 3.9 %collective-permute-start.25 = (bf16[2,9,16,512]{3,2,1,0:T(8,128)(2,1)S(1)}, bf16[2,9,16,512]{3,2,1,0:T(8,128)(2,1)S(1)}, u32[]{:S(2)}, u32[]{:S(2)}) collective-permute-start(bf16[2,9,16,512]{3,2,1,0:T(8,128)(2,1)S(1)} %join_parts.4.refs_4_.refs_8_), channel_id=1, source_target_pairs={{0,16},{1,17},{2,18},{3,19},{4,20},{5,21},{6,22},{7,23},{8,24},{9,... | collective-permute-start | bytes 884744 | tf_op jit(solution)/shard_map/ppermute | solution.py:28
  67.6 3.0 %masked_product.6.refs_2_ = f32[512,512]{1,0:T(8,128)S(1)} custom-call(s32[4]{0:T(128)S(1)} %pad_add_fusion.pos, bf16[8,512,512]{2,1,0:T(8,128)(2,1)S(1)} %get-tuple-element.105.adjoint, bf16[41,16,512]{2,1,0:T(8,128)(2,1)S(1)} %get-tuple-element.95.refs_0_, bf16[41,16,512]{2,1,0:T(8,128)(2,1)S(1)} %collective-permute-done.10.refs_0_.refs_1_, ...), custom_call_target="tpu_custom_call" | custom-call | tf_op jit(solution)/shard_map/masked_product/pallas_call | solution.py:241
  70.6 7.8 %collective-permute-done.24.refs_6_.refs_10_ = bf16[2,9,16,512]{3,2,1,0:T(8,128)(2,1)S(1)} collective-permute-done((bf16[2,9,16,512]{3,2,1,0:T(8,128)(2,1)S(1)}, bf16[2,9,16,512]{3,2,1,0:T(8,128)(2,1)S(1)}, u32[]{:S(2)}, u32[]{:S(2)}) %collective-permute-start.24) | collective-permute-done | bytes 294944 | tf_op jit(solution)/shard_map/ppermute | solution.py:28
  80.3 3.6 %collective-permute-start.36 = (bf16[2,9,16,512]{3,2,1,0:T(8,128)(2,1)S(1)}, bf16[2,9,16,512]{3,2,1,0:T(8,128)(2,1)S(1)}, u32[]{:S(2)}, u32[]{:S(2)}) collective-permute-start(bf16[2,9,16,512]{3,2,1,0:T(8,128)(2,1)S(1)} %join_parts.5.refs_0_.refs_12_), channel_id=1, source_target_pairs={{0,16},{1,17},{2,18},{3,19},{4,20},{5,21},{6,22},{7,23},{8,24},{9,... | collective-permute-start | bytes 884744 | tf_op jit(solution)/shard_map/ppermute | solution.py:28
  87.1 2.2 %masked_product.8.refs_4_ = f32[512,512]{1,0:T(8,128)S(1)} custom-call(s32[4]{0:T(128)S(1)} %pad_add_fusion.pos, bf16[4,512,1024]{2,1,0:T(8,128)(2,1)S(1)} %get-tuple-element.114.adjoint, bf16[2,9,16,512]{3,2,1,0:T(8,128)(2,1)S(1)} %join_parts.3.refs_0_.refs_4_, bf16[2,9,16,512]{3,2,1,0:T(8,128)(2,1)S(1)} %collective-permute-done.18.refs_1_.refs_5_, ...), custom_call_target="tpu_custom_call" | custom-call | tf_op jit(solution)/shard_map/masked_product/pallas_call | solution.py:241
  89.4 2.7 %collective-permute-start.33 = (bf16[1,9,16,512]{3,2,1,0:T(8,128)(2,1)S(1)}, bf16[1,9,16,512]{3,2,1,0:T(8,128)(2,1)S(1)}, u32[]{:S(2)}, u32[]{:S(2)}) collective-permute-start(bf16[1,9,16,512]{3,2,1,0:T(8,128)(2,1)S(1)} %slice_bitcast_fusion.refs_4_.refs_16_), channel_id=1, source_target_pairs={{0,16},{1,17},{2,18},{3,19},{4,20},{5,21},{6,22},{7,23},{8,24},{9,... | collective-permute-start | bytes 442376 | tf_op jit(solution)/shard_map/ppermute | solution.py:28
  93.5 2.9 %collective-permute-start.29 = (f32[512,128]{1,0:T(8,128)S(1)}, f32[512,128]{1,0:T(8,128)S(1)}, u32[]{:S(2)}, u32[]{:S(2)}) collective-permute-start(f32[512,128]{1,0:T(8,128)S(1)} %get-tuple-element.128), channel_id=1, source_target_pairs={{0,128},{32,160},{64,192},{96,224},{128,0},{160,32},{192,64},{224,... | collective-permute-start | bytes 786440 | tf_op jit(solution)/shard_map/ppermute | solution.py:38
  96.4 2.0 %collective-permute-done.35.refs_2_.refs_14_ = bf16[2,9,16,512]{3,2,1,0:T(8,128)(2,1)S(1)} collective-permute-done((bf16[2,9,16,512]{3,2,1,0:T(8,128)(2,1)S(1)}, bf16[2,9,16,512]{3,2,1,0:T(8,128)(2,1)S(1)}, u32[]{:S(2)}, u32[]{:S(2)}) %collective-permute-start.35) | collective-permute-done | bytes 294944 | tf_op jit(solution)/shard_map/ppermute | solution.py:28
  100.4 3.6 %collective-permute-start.32 = (bf16[1,9,16,512]{3,2,1,0:T(8,128)(2,1)S(1)}, bf16[1,9,16,512]{3,2,1,0:T(8,128)(2,1)S(1)}, u32[]{:S(2)}, u32[]{:S(2)}) collective-permute-start(bf16[1,9,16,512]{3,2,1,0:T(8,128)(2,1)S(1)} %slice_bitcast_fusion.refs_4_.refs_16_), channel_id=1, source_target_pairs={{0,24},{1,25},{2,26},{3,27},{4,28},{5,29},{6,30},{7,31},{8,0},{9,1... | collective-permute-start | bytes 442376 | tf_op jit(solution)/shard_map/ppermute | solution.py:28
  103.9 2.3 %collective-permute-done.32.refs_6_.refs_18_ = bf16[1,9,16,512]{3,2,1,0:T(8,128)(2,1)S(1)} collective-permute-done((bf16[1,9,16,512]{3,2,1,0:T(8,128)(2,1)S(1)}, bf16[1,9,16,512]{3,2,1,0:T(8,128)(2,1)S(1)}, u32[]{:S(2)}, u32[]{:S(2)}) %collective-permute-start.32) | collective-permute-done | bytes 147488 | tf_op jit(solution)/shard_map/ppermute | solution.py:28
  113.9 2.8 %masked_product.11 = (f32[512,128]{1,0:T(8,128)S(1)}, bf16[512,128]{1,0:T(8,128)(2,1)S(1)}, bf16[512,128]{1,0:T(8,128)(2,1)S(1)}, bf16[512,128]{1,0:T(8,128)(2,1)S(1)}) custom-call(s32[4]{0:T(128)S(1)} %pad_add_fusion.pos, bf16[4,512,1024]{2,1,0:T(8,128)(2,1)S(1)} %get-tuple-element.114.adjoint, bf16[1,9,16,512]{3,2,1,0:T(8,128)(2,1)S(1)} %get-tuple-element.133.refs_0_, ...), custom_call_target="tpu_custom_call" | custom-call | tf_op jit(solution)/shard_map/masked_product/pallas_call | solution.py:241
  119.2 2.8 %collective-permute-start.43 = (bf16[4,512,128]{2,1,0:T(8,128)(2,1)S(1)}, bf16[4,512,128]{2,1,0:T(8,128)(2,1)S(1)}, u32[]{:S(2)}, u32[]{:S(2)}) collective-permute-start(bf16[4,512,128]{2,1,0:T(8,128)(2,1)S(1)} %pad_maximum_fusion.1.mine), channel_id=1, source_target_pairs={{0,32},{32,0},{64,96},{96,64},{128,160},{160,128},{192,224},{224,1... | collective-permute-start | bytes 1572872 | tf_op jit(solution)/shard_map/ppermute | solution.py:46
  127.5 3.5 %collective-permute-done.40 = bf16[512,128]{1,0:T(8,128)(2,1)S(1)} collective-permute-done((bf16[512,128]{1,0:T(8,128)(2,1)S(1)}, bf16[512,128]{1,0:T(8,128)(2,1)S(1)}, u32[]{:S(2)}, u32[]{:S(2)}) %collective-permute-start.40) | collective-permute-done | bytes 131104 | tf_op jit(solution)/shard_map/ppermute | solution.py:38
  (102 shorter events, 50.0 us)
Async XLA Ops:
  8.6 10.0 %collective-permute-start.4 = (bf16[128,512]{1,0:T(8,128)(2,1)S(1)}, bf16[128,512]{1,0:T(8,128)(2,1)S(1)}, u32[]{:S(2)}, u32[]{:S(2)}) collective-permute-start(bf16[128,512]{1,0:T(8,128)(2,1)S(1)} %get-tuple-element.84.two), channel_id=1, source_target_pairs={{0,16},{1,17},{2,18},{3,19},{4,20},{5,21},{6,22},{7,23},{8,24},{9,... | collective-permute-start | bytes 393224 | tf_op jit(solution)/shard_map/ppermute | solution.py:28
  11.0 9.3 %collective-permute-start.3 = (bf16[128,512]{1,0:T(8,128)(2,1)S(1)}, bf16[128,512]{1,0:T(8,128)(2,1)S(1)}, u32[]{:S(2)}, u32[]{:S(2)}) collective-permute-start(bf16[128,512]{1,0:T(8,128)(2,1)S(1)} %get-tuple-element.84.two), channel_id=1, source_target_pairs={{0,24},{1,25},{2,26},{3,27},{4,28},{5,29},{6,30},{7,31},{8,0},{9,1... | collective-permute-start | bytes 393224 | tf_op jit(solution)/shard_map/ppermute | solution.py:28
  21.7 18.1 %collective-permute-start.11 = (bf16[41,16,512]{2,1,0:T(8,128)(2,1)S(1)}, bf16[41,16,512]{2,1,0:T(8,128)(2,1)S(1)}, u32[]{:S(2)}, u32[]{:S(2)}) collective-permute-start(bf16[41,16,512]{2,1,0:T(8,128)(2,1)S(1)} %get-tuple-element.95.refs_0_), channel_id=1, source_target_pairs={{0,7},{1,0},{2,1},{3,2},{4,3},{5,4},{6,5},{7,6},{8,15},{9,8},{10,9... | collective-permute-start | bytes 2015240 | tf_op jit(solution)/shard_map/ppermute | solution.py:33
  27.4 15.5 %collective-permute-start.10 = (bf16[41,16,512]{2,1,0:T(8,128)(2,1)S(1)}, bf16[41,16,512]{2,1,0:T(8,128)(2,1)S(1)}, u32[]{:S(2)}, u32[]{:S(2)}) collective-permute-start(bf16[41,16,512]{2,1,0:T(8,128)(2,1)S(1)} %get-tuple-element.95.refs_0_), channel_id=1, source_target_pairs={{0,1},{1,2},{2,3},{3,4},{4,5},{5,6},{6,7},{7,0},{8,9},{9,10},{10,1... | collective-permute-start | bytes 2015240 | tf_op jit(solution)/shard_map/ppermute | solution.py:33
  42.9 16.5 %collective-permute-start.16 = (bf16[41,16,512]{2,1,0:T(8,128)(2,1)S(1)}, bf16[41,16,512]{2,1,0:T(8,128)(2,1)S(1)}, u32[]{:S(2)}, u32[]{:S(2)}) collective-permute-start(bf16[41,16,512]{2,1,0:T(8,128)(2,1)S(1)} %collective-permute-done.10.refs_0_.refs_1_), channel_id=1, source_target_pairs={{0,1},{1,2},{2,3},{3,4},{4,5},{5,6},{6,7},{7,0},{8,9},{9,10},{10,1... | collective-permute-start | bytes 2015240 | tf_op jit(solution)/shard_map/ppermute | solution.py:33
  42.9 16.5 %collective-permute-start.17 = (bf16[41,16,512]{2,1,0:T(8,128)(2,1)S(1)}, bf16[41,16,512]{2,1,0:T(8,128)(2,1)S(1)}, u32[]{:S(2)}, u32[]{:S(2)}) collective-permute-start(bf16[41,16,512]{2,1,0:T(8,128)(2,1)S(1)} %collective-permute-done.11.refs_1_.refs_2_), channel_id=1, source_target_pairs={{0,7},{1,0},{2,1},{3,2},{4,3},{5,4},{6,5},{7,6},{8,15},{9,8},{10,9... | collective-permute-start | bytes 2015240 | tf_op jit(solution)/shard_map/ppermute | solution.py:33
  45.6 9.1 %collective-permute-start.20 = (bf16[2,9,16,512]{3,2,1,0:T(8,128)(2,1)S(1)}, bf16[2,9,16,512]{3,2,1,0:T(8,128)(2,1)S(1)}, u32[]{:S(2)}, u32[]{:S(2)}) collective-permute-start(bf16[2,9,16,512]{3,2,1,0:T(8,128)(2,1)S(1)} %join_parts.3.refs_0_.refs_4_), channel_id=1, source_target_pairs={{0,16},{1,17},{2,18},{3,19},{4,20},{5,21},{6,22},{7,23},{8,24},{9,... | collective-permute-start | bytes 884744 | tf_op jit(solution)/shard_map/ppermute | solution.py:28
  48.3 11.1 %collective-permute-start.19 = (bf16[2,9,16,512]{3,2,1,0:T(8,128)(2,1)S(1)}, bf16[2,9,16,512]{3,2,1,0:T(8,128)(2,1)S(1)}, u32[]{:S(2)}, u32[]{:S(2)}) collective-permute-start(bf16[2,9,16,512]{3,2,1,0:T(8,128)(2,1)S(1)} %join_parts.3.refs_0_.refs_4_), channel_id=1, source_target_pairs={{0,24},{1,25},{2,26},{3,27},{4,28},{5,29},{6,30},{7,31},{8,0},{9,1... | collective-permute-start | bytes 884744 | tf_op jit(solution)/shard_map/ppermute | solution.py:28
  49.1 10.3 %collective-permute-start.18 = (bf16[2,9,16,512]{3,2,1,0:T(8,128)(2,1)S(1)}, bf16[2,9,16,512]{3,2,1,0:T(8,128)(2,1)S(1)}, u32[]{:S(2)}, u32[]{:S(2)}) collective-permute-start(bf16[2,9,16,512]{3,2,1,0:T(8,128)(2,1)S(1)} %join_parts.3.refs_0_.refs_4_), channel_id=1, source_target_pairs={{0,8},{1,9},{2,10},{3,11},{4,12},{5,13},{6,14},{7,15},{8,16},{9,17... | collective-permute-start | bytes 884744 | tf_op jit(solution)/shard_map/ppermute | solution.py:28
  59.4 19.3 %collective-permute-start.21 = (bf16[41,16,512]{2,1,0:T(8,128)(2,1)S(1)}, bf16[41,16,512]{2,1,0:T(8,128)(2,1)S(1)}, u32[]{:S(2)}, u32[]{:S(2)}) collective-permute-start(bf16[41,16,512]{2,1,0:T(8,128)(2,1)S(1)} %collective-permute-done.16.refs_3_.refs_0_), channel_id=1, source_target_pairs={{0,1},{1,2},{2,3},{3,4},{4,5},{5,6},{6,7},{7,0},{8,9},{9,10},{10,1... | collective-permute-start | bytes 2015240 | tf_op jit(solution)/shard_map/ppermute | solution.py:33
  59.5 19.2 %collective-permute-start.22 = (bf16[41,16,512]{2,1,0:T(8,128)(2,1)S(1)}, bf16[41,16,512]{2,1,0:T(8,128)(2,1)S(1)}, u32[]{:S(2)}, u32[]{:S(2)}) collective-permute-start(bf16[41,16,512]{2,1,0:T(8,128)(2,1)S(1)} %collective-permute-done.17.refs_4_.refs_1_), channel_id=1, source_target_pairs={{0,7},{1,0},{2,1},{3,2},{4,3},{5,4},{6,5},{7,6},{8,15},{9,8},{10,9... | collective-permute-start | bytes 2015240 | tf_op jit(solution)/shard_map/ppermute | solution.py:33
  66.1 12.3 %collective-permute-start.24 = (bf16[2,9,16,512]{3,2,1,0:T(8,128)(2,1)S(1)}, bf16[2,9,16,512]{3,2,1,0:T(8,128)(2,1)S(1)}, u32[]{:S(2)}, u32[]{:S(2)}) collective-permute-start(bf16[2,9,16,512]{3,2,1,0:T(8,128)(2,1)S(1)} %join_parts.4.refs_4_.refs_8_), channel_id=1, source_target_pairs={{0,24},{1,25},{2,26},{3,27},{4,28},{5,29},{6,30},{7,31},{8,0},{9,1... | collective-permute-start | bytes 884744 | tf_op jit(solution)/shard_map/ppermute | solution.py:28
  67.2 11.5 %collective-permute-start.23 = (bf16[2,9,16,512]{3,2,1,0:T(8,128)(2,1)S(1)}, bf16[2,9,16,512]{3,2,1,0:T(8,128)(2,1)S(1)}, u32[]{:S(2)}, u32[]{:S(2)}) collective-permute-start(bf16[2,9,16,512]{3,2,1,0:T(8,128)(2,1)S(1)} %join_parts.4.refs_4_.refs_8_), channel_id=1, source_target_pairs={{0,8},{1,9},{2,10},{3,11},{4,12},{5,13},{6,14},{7,15},{8,16},{9,17... | collective-permute-start | bytes 884744 | tf_op jit(solution)/shard_map/ppermute | solution.py:28
  78.7 10.7 %collective-permute-start.27 = (bf16[25,16,512]{2,1,0:T(8,128)(2,1)S(1)}, bf16[25,16,512]{2,1,0:T(8,128)(2,1)S(1)}, u32[]{:S(2)}, u32[]{:S(2)}) collective-permute-start(bf16[25,16,512]{2,1,0:T(8,128)(2,1)S(1)} %slice.18), channel_id=1, source_target_pairs={{0,7},{1,0},{2,1},{3,2},{4,3},{5,4},{6,5},{7,6},{8,15},{9,8},{10,9... | collective-permute-start | bytes 1228808 | tf_op jit(solution)/shard_map/ppermute | solution.py:33
  78.8 10.6 %collective-permute-start.26 = (bf16[16,16,512]{2,1,0:T(8,128)(2,1)S(1)}, bf16[16,16,512]{2,1,0:T(8,128)(2,1)S(1)}, u32[]{:S(2)}, u32[]{:S(2)}) collective-permute-start(bf16[16,16,512]{2,1,0:T(8,128)(2,1)S(1)} %slice.17), channel_id=1, source_target_pairs={{0,1},{1,2},{2,3},{3,4},{4,5},{5,6},{6,7},{7,0},{8,9},{9,10},{10,1... | collective-permute-start | bytes 786440 | tf_op jit(solution)/shard_map/ppermute | solution.py:33
  80.3 13.1 %collective-permute-start.36 = (bf16[2,9,16,512]{3,2,1,0:T(8,128)(2,1)S(1)}, bf16[2,9,16,512]{3,2,1,0:T(8,128)(2,1)S(1)}, u32[]{:S(2)}, u32[]{:S(2)}) collective-permute-start(bf16[2,9,16,512]{3,2,1,0:T(8,128)(2,1)S(1)} %join_parts.5.refs_0_.refs_12_), channel_id=1, source_target_pairs={{0,16},{1,17},{2,18},{3,19},{4,20},{5,21},{6,22},{7,23},{8,24},{9,... | collective-permute-start | bytes 884744 | tf_op jit(solution)/shard_map/ppermute | solution.py:28
  83.9 14.4 %collective-permute-start.35 = (bf16[2,9,16,512]{3,2,1,0:T(8,128)(2,1)S(1)}, bf16[2,9,16,512]{3,2,1,0:T(8,128)(2,1)S(1)}, u32[]{:S(2)}, u32[]{:S(2)}) collective-permute-start(bf16[2,9,16,512]{3,2,1,0:T(8,128)(2,1)S(1)} %join_parts.5.refs_0_.refs_12_), channel_id=1, source_target_pairs={{0,24},{1,25},{2,26},{3,27},{4,28},{5,29},{6,30},{7,31},{8,0},{9,1... | collective-permute-start | bytes 884744 | tf_op jit(solution)/shard_map/ppermute | solution.py:28
  85.5 14.8 %collective-permute-start.34 = (bf16[2,9,16,512]{3,2,1,0:T(8,128)(2,1)S(1)}, bf16[2,9,16,512]{3,2,1,0:T(8,128)(2,1)S(1)}, u32[]{:S(2)}, u32[]{:S(2)}) collective-permute-start(bf16[2,9,16,512]{3,2,1,0:T(8,128)(2,1)S(1)} %join_parts.5.refs_0_.refs_12_), channel_id=1, source_target_pairs={{0,8},{1,9},{2,10},{3,11},{4,12},{5,13},{6,14},{7,15},{8,16},{9,17... | collective-permute-start | bytes 884744 | tf_op jit(solution)/shard_map/ppermute | solution.py:28
  89.4 14.5 %collective-permute-start.33 = (bf16[1,9,16,512]{3,2,1,0:T(8,128)(2,1)S(1)}, bf16[1,9,16,512]{3,2,1,0:T(8,128)(2,1)S(1)}, u32[]{:S(2)}, u32[]{:S(2)}) collective-permute-start(bf16[1,9,16,512]{3,2,1,0:T(8,128)(2,1)S(1)} %slice_bitcast_fusion.refs_4_.refs_16_), channel_id=1, source_target_pairs={{0,16},{1,17},{2,18},{3,19},{4,20},{5,21},{6,22},{7,23},{8,24},{9,... | collective-permute-start | bytes 442376 | tf_op jit(solution)/shard_map/ppermute | solution.py:28
  93.4 15.8 %collective-permute-start.28 = (f32[512,128]{1,0:T(8,128)S(1)}, f32[512,128]{1,0:T(8,128)S(1)}, u32[]{:S(2)}, u32[]{:S(2)}) collective-permute-start(f32[512,128]{1,0:T(8,128)S(1)} %get-tuple-element.127), channel_id=1, source_target_pairs={{0,64},{32,96},{64,128},{96,160},{128,192},{160,224},{192,0},{224,... | collective-permute-start | bytes 786440 | tf_op jit(solution)/shard_map/ppermute | solution.py:38
  93.5 15.7 %collective-permute-start.29 = (f32[512,128]{1,0:T(8,128)S(1)}, f32[512,128]{1,0:T(8,128)S(1)}, u32[]{:S(2)}, u32[]{:S(2)}) collective-permute-start(f32[512,128]{1,0:T(8,128)S(1)} %get-tuple-element.128), channel_id=1, source_target_pairs={{0,128},{32,160},{64,192},{96,224},{128,0},{160,32},{192,64},{224,... | collective-permute-start | bytes 786440 | tf_op jit(solution)/shard_map/ppermute | solution.py:38
  98.4 10.8 %collective-permute-start.30 = (f32[512,128]{1,0:T(8,128)S(1)}, f32[512,128]{1,0:T(8,128)S(1)}, u32[]{:S(2)}, u32[]{:S(2)}) collective-permute-start(f32[512,128]{1,0:T(8,128)S(1)} %get-tuple-element.129), channel_id=1, source_target_pairs={{0,192},{32,224},{64,0},{96,32},{128,64},{160,96},{192,128},{224,1... | collective-permute-start | bytes 786440 | tf_op jit(solution)/shard_map/ppermute | solution.py:38
  106.3 18.4 %collective-permute-start.44 = (bf16[4,128,1024]{2,1,0:T(8,128)(2,1)S(1)}, bf16[4,128,1024]{2,1,0:T(8,128)(2,1)S(1)}, u32[]{:S(2)}, u32[]{:S(2)}) collective-permute-start(bf16[4,128,1024]{2,1,0:T(8,128)(2,1)S(1)} %pad_maximum_fusion.inverse), channel_id=1, source_target_pairs={{0,32},{32,0},{64,96},{96,64},{128,160},{160,128},{192,224},{224,1... | collective-permute-start | bytes 3145736 | tf_op jit(solution)/shard_map/ppermute | solution.py:46
  122.0 9.1 %collective-permute-start.40 = (bf16[512,128]{1,0:T(8,128)(2,1)S(1)}, bf16[512,128]{1,0:T(8,128)(2,1)S(1)}, u32[]{:S(2)}, u32[]{:S(2)}) collective-permute-start(bf16[512,128]{1,0:T(8,128)(2,1)S(1)} %get-tuple-element.151), channel_id=1, source_target_pairs={{0,64},{32,96},{64,128},{96,160},{128,192},{160,224},{192,0},{224,... | collective-permute-start | bytes 393224 | tf_op jit(solution)/shard_map/ppermute | solution.py:38
  (26 other events, 249.1 us)
